TPU v7x, 256 devices: a whole 4x4x8 slice. The times are simulated.
256 devices in a mesh: island: 8 (over y, x_lo), fsdp: 32 (over z, x_hi, core).
Axes of the slice: x: 4 (x_hi: 2, x_lo: 2; x = x_hi * 2 + x_lo), y: 4, z: 8, core: 2. Of those that a mesh axis runs over, the one named last changes fastest.
Arguments:
- tokens: bfloat16 [65536, 4096], P(('island', 'fsdp')), may hold values from -6 to 6
- upstream: bfloat16 [65536, 1024], P(('island', 'fsdp')), may hold values from -6 to 6
- params: float32 [4096, 1024], P('fsdp'), may hold values from -6 to 6
- momentum: float32 [4096, 1024], P('fsdp'), may hold values from -4 to 4
- projection: float32 [1024, 512], replicated, may hold values from -6 to 6
Outputs:
- values: bfloat16 [65536, 1024], P(('island', 'fsdp'))
- token_grads: bfloat16 [65536, 4096], P(('island', 'fsdp'))
- new_params: float32 [4096, 1024], P('fsdp')
- new_momentum: float32 [4096, 1024], P('fsdp')
All inputs are finite; a program needn't handle non-finite values.
Results may differ from a plain program's by a relative error of at most 0.012.
Values may be sent and summed in bfloat16 or wider, within the bound.
No kernel may reach another device: no remote copies, remote signals or barrier semaphores. Data moves between devices by JAX's collectives and lax.ppermute only.
A program may use at most 128 MiB of HBM per device.

v0:
```python
import math

import jax
import jax.numpy as jnp
from jax import lax
from jax.sharding import PartitionSpec as P


def local(tokens, upstream, params, momentum, projection):
    half_weight = params.astype(jnp.bfloat16)
    inv_width = 1.0 / math.sqrt(tokens.shape[1])
    dims_feat = (((1,), (1,)), ((), ()))
    dims_rows = (((0,), (0,)), ((), ()))
    forward_sum = jnp.dot(
        tokens,
        lax.all_gather(half_weight, "fsdp", axis=0, tiled=True),
        preferred_element_type=jnp.float32,
    )
    product = lax.dot_general(
        upstream,
        lax.all_gather(half_weight, "fsdp", axis=0, tiled=True),
        dims_feat,
        preferred_element_type=jnp.float32,
    )
    token_grads = (product * inv_width).astype(jnp.bfloat16)
    values = (forward_sum * inv_width).astype(jnp.bfloat16)
    fsdp_count = lax.axis_size("fsdp")
    scale_tok = 1.0 / math.sqrt(tokens.shape[0] * fsdp_count)
    local_grad = lax.dot_general(tokens, upstream, dims_rows, preferred_element_type=jnp.float32)
    shard_grad = lax.psum_scatter(local_grad, "fsdp", scatter_dimension=0, tiled=True) * scale_tok
    compressed = jnp.dot(shard_grad, projection, precision=lax.Precision.HIGHEST)
    island_total = lax.psum(compressed.astype(jnp.bfloat16), "island").astype(jnp.float32)
    outer = jnp.dot(island_total, projection.T, precision=lax.Precision.HIGHEST) / (
        projection.shape[1] * lax.axis_size("island")
    )
    new_momentum = 0.9 * momentum + outer
    new_params = params - 0.7 * (outer + 0.9 * new_momentum)
    return (values, token_grads, new_params, new_momentum)


def solution(mesh):
    in_specs = (
        P(("island", "fsdp"), None),
        P(("island", "fsdp"), None),
        P("fsdp", None),
        P("fsdp", None),
        P(),
    )
    out_specs = (
        P(("island", "fsdp"), None),
        P(("island", "fsdp"), None),
        P("fsdp", None),
        P("fsdp", None),
    )
    return jax.shard_map(local, mesh=mesh, in_specs=in_specs, out_specs=out_specs, check_vma=False)
```

profile of v0, /device:TPU:1, one launch (start us, length us, event | category | flops | bytes accessed | tf_op | source)
XLA Modules:
  0.0 444.7 jit_solution(7758417855345706923)
XLA Ops:
  7.2 0.0 copy-start
  7.2 0.0 reduce-scatter.2.cloned.1.call-start
  7.2 1.5 copy-done
  8.8 9.2 %fusion.5 = f32[4096,1024]{1,0:T(8,128)} fusion(bf16[256,4096]{1,0:T(8,128)(2,1)S(1)} %copy-done, bf16[256,1024]{1,0:T(8,128)(2,1)} %param.6), kind=kOutput, calls=%fused_computation.11 | convolution fusion | flops 2147483648 | bytes 19398656 | tf_op jit(solution)/shard_map/dot_general | solution.py:29
  17.9 0.0 reduce-scatter.2.cloned.1.call-update
  17.9 0.0 copy-start.1
  18.0 0.0 copy-start.2
  18.0 0.0 all-reduce.2.cloned.1.call-start
  18.0 219.4 %reduce-scatter.2.cloned.1.call-done = f32[128,1024]{1,0:T(8,128)} async-done(((f32[4096,1024]{1,0:T(8,128)}), f32[128,1024]{1,0:T(8,128)}) %reduce-scatter.2.cloned.1.call-update) | async-done | bytes 524304 | tf_op jit(solution)/shard_map/reduce_scatter | solution.py:30
  237.4 3.7 convolution_convert_fusion
  241.1 0.0 all-reduce.2.cloned.1.call-update
  241.1 0.0 all-gather.2.cloned.1.call-start
  241.2 76.1 %all-reduce.2.cloned.1.call-done = bf16[128,512]{1,0:T(8,128)(2,1)} async-done(((bf16[128,512]{1,0:T(8,128)(2,1)}), bf16[128,512]{1,0:T(8,128)(2,1)}) %all-reduce.2.cloned.1.call-update) | async-done | bytes 131088 | tf_op jit(solution)/shard_map/psum | solution.py:32
  317.3 0.0 copy-done.1
  317.3 0.0 copy-done.2
  317.3 4.0 multiply_subtract_fusion
  321.3 0.0 all-gather.2.cloned.1.call-update
  321.4 0.0 copy-start.3
  321.4 106.3 %all-gather.2.cloned.1.call-done = bf16[4096,1024]{1,0:T(8,128)(2,1)} async-done(((bf16[128,1024]{1,0:T(8,128)(2,1)}), bf16[4096,1024]{1,0:T(8,128)(2,1)}) %all-gather.2.cloned.1.call-update) | async-done | bytes 8388624 | tf_op jit(solution)/shard_map/all_gather | solution.py:16
  427.7 0.0 copy-start.4
  427.7 6.7 %fusion.1 = bf16[256,1024]{1,0:T(8,128)(2,1)} fusion(bf16[256,4096]{1,0:T(8,128)(2,1)S(1)} %copy-done, bf16[4096,1024]{1,0:T(8,128)(2,1)} %all-gather.2.cloned.1.call-done), kind=kOutput, calls=%fused_computation.3 | convolution fusion | flops 2148007936 | bytes 11010048 | tf_op jit(solution)/shard_map/dot_general | solution.py:14
  434.4 0.0 copy-done.3
  434.4 0.0 copy-done.4
  434.4 3.8 fusion
Async XLA Ops:
  7.2 1.6 copy-start
  7.2 230.2 %reduce-scatter.2.cloned.1.call-start = ((), (), s32[]{:S(2)}) async-start(), calls=%async_computation.2 | async-start | bytes 17301504 | tf_op jit(solution)/shard_map/reduce_scatter | solution.py:30
  17.9 299.3 %copy-start.1 = (f32[128,1024]{1,0:T(8,128)S(1)}, f32[128,1024]{1,0:T(8,128)}, u32[]{:S(2)}) copy-start(f32[128,1024]{1,0:T(8,128)} %param.7) | copy-start | bytes 1572868
  18.0 299.3 %copy-start.2 = (f32[128,1024]{1,0:T(8,128)S(1)}, f32[128,1024]{1,0:T(8,128)}, u32[]{:S(2)}) copy-start(f32[128,1024]{1,0:T(8,128)} %param.8) | copy-start | bytes 1572868
  18.0 299.3 %all-reduce.2.cloned.1.call-start = ((), (), s32[]{:S(2)}) async-start(), calls=%async_computation.3 | async-start | bytes 262144 | tf_op jit(solution)/shard_map/psum | solution.py:32
  241.1 186.6 %all-gather.2.cloned.1.call-start = ((), (), s32[]{:S(2)}) async-start(), calls=%async_computation.1 | async-start | bytes 8650752 | tf_op jit(solution)/shard_map/all_gather | solution.py:16
  321.4 113.0 %copy-start.3 = (bf16[256,1024]{1,0:T(8,128)(2,1)S(1)}, bf16[256,1024]{1,0:T(8,128)(2,1)}, u32[]{:S(2)}) copy-start(bf16[256,1024]{1,0:T(8,128)(2,1)} %param.6) | copy-start | bytes 1572868
  427.7 6.7 %copy-start.4 = (bf16[4096,1024]{1,0:T(8,128)(2,1)S(1)}, bf16[4096,1024]{1,0:T(8,128)(2,1)}, u32[]{:S(2)}) copy-start(bf16[4096,1024]{1,0:T(8,128)(2,1)} %all-gather.2.cloned.1.call-done) | copy-start | bytes 25165828
Sparse Core Ops, SparseCore 0:
  18.1 219.2 reduce-scatter.1
  241.3 75.9 all-reduce.1
  321.5 106.1 all-gather.1
where the time goes:
time: 445 us
  waiting for transfers between devices  402 us (90%)
  matrix products  27.4 us (6%)
  between operations  13.8 us (3%)
    reduce_scatter x1, waiting for transfers between devices, local(): lax.psum_scatter(local_grad, 'fsdp', scatter_dimension=0, tiled=True)  219 us
    all_gather x1, waiting for transfers between devices, local(): lax.all_gather(half_weight, 'fsdp', axis=0, tiled=True)  106 us
    psum x1, waiting for transfers between devices, local(): lax.psum(compressed.astype(jnp.bfloat16), 'island').astype(jnp.float32)  76.1 us
    dot_general x1, matrix products, local(): lax.dot_general(tokens, upstream, dims_rows, preferred_element_type=jnp.f...  9.16 us
  transfers between devices with their start and end apart: 3, of which 3 were waited for; matrix products, arithmetic and copies ran while one was open for 0% of the time, Pallas kernels for 0%

commit v1 on v0

v1 whole, which is shorter than its diff:
```python
import functools
import math

import jax
import jax.numpy as jnp
from jax import lax
from jax.experimental import pallas as pl
from jax.experimental.pallas import tpu as pltpu
from jax.sharding import Mesh
from jax.sharding import PartitionSpec as P

ISLAND = ("y", "xl")
FSDP = ("z", "xh", "c")
PLANE = ("y", "xl", "xh")
F32, BF16 = jnp.float32, jnp.bfloat16
LANES = 128


def two_parts(x):
    head = x.astype(BF16)
    return head, (x - head.astype(F32)).astype(BF16)


def pick_kernel(c_ref, tokens_ref, params_ref, out_ref, half_ref):
    skip = 1 - c_ref[0]
    half_ref[...] = params_ref[...].astype(BF16)
    for k in range(out_ref.shape[1] // LANES):
        at = pl.multiple_of((2 * k + skip) * LANES, LANES)
        out_ref[:, k * LANES : (k + 1) * LANES] = tokens_ref[:, pl.ds(at, LANES)]


def pick(c, tokens, params):
    t, d = tokens.shape
    vm = pl.BlockSpec(memory_space=pltpu.VMEM)
    return pl.pallas_call(
        pick_kernel,
        out_shape=(
            jax.ShapeDtypeStruct((t, d // 2), BF16),
            jax.ShapeDtypeStruct(params.shape, BF16),
        ),
        in_specs=[pl.BlockSpec(memory_space=pltpu.SMEM), vm, vm],
        out_specs=(vm, vm),
        name="pick",
    )(c, tokens, params)


def q_kernel(up_ref, proj_ref, q_ref):
    head, rest = two_parts(proj_ref[...])
    q = jnp.dot(up_ref[...], head, preferred_element_type=F32)
    q += jnp.dot(up_ref[...], rest, preferred_element_type=F32)
    q_ref[...] = q.astype(BF16)


def make_q(upstream, projection):
    vm = pl.BlockSpec(memory_space=pltpu.VMEM)
    return pl.pallas_call(
        q_kernel,
        out_shape=jax.ShapeDtypeStruct((upstream.shape[0], projection.shape[1]), BF16),
        in_specs=[vm, vm],
        out_specs=vm,
        name="make_q",
    )(upstream, projection)


def sketch_kernel(c_ref, tok_ref, got_ref, q_ref, got_q_ref, out_ref):
    pieces, n_xh, _, part, proj = out_ref.shape
    z = pl.program_id(0)
    dims = (((0,), (0,)), ((), ()))
    for h in range(n_xh):
        k = z * n_xh + h
        mine = tok_ref[:, pl.ds(pl.multiple_of((2 * k + c_ref[0]) * LANES, LANES), LANES)]
        theirs = got_ref[:, pl.ds(pl.multiple_of(k * LANES, LANES), LANES)]
        s = lax.dot_general(mine, q_ref[...], dims, preferred_element_type=F32)
        s += lax.dot_general(theirs, got_q_ref[...], dims, preferred_element_type=F32)
        out_ref[:, h, 0] = s.astype(BF16).reshape(pieces, part, proj)


def make_sketch(c, tokens, got, q, got_q, pieces, n_xh, n_z):
    t, d = tokens.shape
    proj = q.shape[1]
    part = LANES // pieces
    vm = pl.BlockSpec(memory_space=pltpu.VMEM)
    return pl.pallas_call(
        sketch_kernel,
        grid=(n_z,),
        out_shape=jax.ShapeDtypeStruct((pieces, n_xh, n_z, part, proj), BF16),
        in_specs=[pl.BlockSpec(memory_space=pltpu.SMEM), vm, vm, vm, vm],
        out_specs=pl.BlockSpec((pieces, n_xh, 1, part, proj), lambda z: (0, 0, z, 0, 0)),
        name="make_sketch",
    )(c, tokens, got, q, got_q)


def local(tokens, upstream, params, momentum, projection):
    rows, feat = params.shape
    n_z, n_xh, n_c = (lax.axis_size(a) for a in FSDP)
    n_isl = lax.axis_size("y") * lax.axis_size("xl")
    fsdp_count = n_z * n_xh * n_c
    width = tokens.shape[1]
    proj = projection.shape[1]
    part = rows // n_isl
    inv_width = 1.0 / math.sqrt(width)
    scale_tok = 1.0 / math.sqrt(tokens.shape[0] * fsdp_count)
    c = lax.axis_index("c").astype(jnp.int32).reshape(1)
    swap = functools.partial(lax.ppermute, axis_name="c", perm=[(0, 1), (1, 0)])

    other, half = pick(c, tokens, params)
    got = swap(other)
    weight = lax.all_gather(half, FSDP, axis=0, tiled=True)

    q = make_q(upstream, projection)
    got_q = swap(q)
    pair = make_sketch(c, tokens, got, q, got_q, n_isl, n_xh, n_z)
    pair = pair.reshape(n_isl * n_xh, n_z * part, proj)
    pair = lax.all_to_all(pair, PLANE, 0, 0, tiled=True)
    plane = jnp.sum(pair.astype(F32), axis=0).astype(BF16)
    plane = lax.all_to_all(plane.reshape(n_z, part, proj), "z", 0, 0, tiled=True)
    total = jnp.sum(plane.astype(F32), axis=0).astype(BF16)
    total = jnp.broadcast_to(total[None], (n_isl, part, proj))
    total = lax.all_to_all(total, ISLAND, 0, 0, tiled=True).reshape(rows, proj)

    dims = (((1,), (1,)), ((), ()))
    head, rest = two_parts(projection)
    outer = lax.dot_general(total, head, dims, preferred_element_type=F32)
    outer = outer + lax.dot_general(total, rest, dims, preferred_element_type=F32)
    outer = outer * (scale_tok / (proj * n_isl))
    new_momentum = 0.9 * momentum + outer
    new_params = params - 0.7 * (outer + 0.9 * new_momentum)

    forward_sum = jnp.dot(tokens, weight, preferred_element_type=F32)
    values = (forward_sum * inv_width).astype(BF16)
    product = lax.dot_general(upstream, weight, dims, preferred_element_type=F32)
    token_grads = (product * inv_width).astype(BF16)
    return (values, token_grads, new_params, new_momentum)


def solution(mesh):
    fine = Mesh(mesh.devices.reshape(4, 2, 8, 2, 2), ISLAND + FSDP)
    both = ISLAND + FSDP
    in_specs = (P(both, None), P(both, None), P(FSDP, None), P(FSDP, None), P())
    out_specs = (P(both, None), P(both, None), P(FSDP, None), P(FSDP, None))
    return jax.shard_map(local, mesh=fine, in_specs=in_specs, out_specs=out_specs, check_vma=False)
```

time: 445 us -> 142 us (0.32)
  waiting for transfers between devices: 402 us -> 30.3 us
  blocking collectives: 0 us -> 58.9 us
  matrix products: 27.4 us -> 14.1 us
  Pallas kernels: 0 us -> 12.8 us
    reduce_scatter x1 -> x0, waiting for transfers between devices: 219 us -> none  [local(): lax.psum_scatter(local_grad, 'fsdp', scatter_dimension=0, tiled=True)]
    all_gather x1, waiting for transfers between devices: 106 us -> 28.5 us  [local(): weight = lax.all_gather(half, FSDP, axis=0, tiled=True)]
    psum x1 -> x0, waiting for transfers between devices: 76.1 us -> none  [local(): lax.psum(compressed.astype(jnp.bfloat16), 'island').astype(jnp.float32)]
    all_to_all x0 -> x3, blocking collectives: none -> 58.9 us  [the longest x1 31.6 us: local(): pair = lax.all_to_all(pair, PLANE, 0, 0, tiled=True)]
    dot_general x5 -> x4, matrix products: 27.4 us -> 14.1 us  [the longest x1 6.37 us: local(): forward_sum = jnp.dot(tokens, weight, preferred_element_type=F32)]
    pallas_call x0 -> x3, Pallas kernels: none -> 12.8 us  [the longest x1 6.51 us: make_sketch(): pl.pallas_call(sketch_kernel, grid=(n_z,), out_shape=jax.ShapeDtypeStruct...]
  transfers between devices with their start and end apart: 3 -> 3, of which waited for: 3 -> 2; matrix products, arithmetic and copies ran while one was open for 0% -> 3% of each run, Pallas kernels for 0% -> 7%
where the time goes in v1:
time: 142 us; the launch traced here: 141 us
  blocking collectives  58.9 us (41%)
  waiting for transfers between devices  30.3 us (21%)
  matrix products  14.1 us (10%)
  between operations  14.1 us (10%)
  Pallas kernels  12.8 us (9%)
  local copies, waits for them, and re-layouts  5.64 us (4%)
  starting transfers between devices  3.34 us (2%)
  other arithmetic  2.07 us (1%)
    all_to_all x1, blocking collectives, local(): pair = lax.all_to_all(pair, PLANE, 0, 0, tiled=True)  31.6 us
    all_gather x1, waiting for transfers between devices, local(): weight = lax.all_gather(half, FSDP, axis=0, tiled=True)  28.5 us
    all_to_all x1, blocking collectives, local(): lax.all_to_all(plane.reshape(n_z, part, proj), 'z', 0, 0, tiled=True)  16.6 us
    all_to_all x1, blocking collectives, local(): total = lax.all_to_all(total, ISLAND, 0, 0, tiled=True).reshape(rows, proj)  10.6 us
    pallas_call x1, Pallas kernels, make_sketch(): pl.pallas_call(sketch_kernel, grid=(n_z,), out_shape=jax.ShapeDtypeStruct...  6.51 us
    dot_general x1, matrix products, local(): forward_sum = jnp.dot(tokens, weight, preferred_element_type=F32)  6.37 us
    dot_general x1, matrix products, local(): lax.dot_general(upstream, weight, dims, preferred_element_type=F32)  5.76 us
    unnamed x14, local copies, waits for them, and re-layouts  5.63 us
  transfers between devices with their start and end apart: 3, of which 2 were waited for; matrix products, arithmetic and copies ran while one was open for 3% of the time, Pallas kernels for 7%

profile of v1, /device:TPU:1, one launch (start us, length us, event | category | flops | bytes accessed | tf_op | source)
XLA Modules:
  0.0 141.2 jit_solution(7627043314401418664)
XLA Ops:
  7.2 0.0 all-gather.2.cloned.1.call-start
  7.2 3.0 %pick.1 = (bf16[256,2048]{1,0:T(8,128)(2,1)}, bf16[128,1024]{1,0:T(8,128)(2,1)}) custom-call(s32[1]{0:T(128)} %bitcast.c_ref, bf16[256,4096]{1,0:T(8,128)(2,1)} %tok_ref.1, f32[128,1024]{1,0:T(8,128)} %params_ref.1), custom_call_target="tpu_custom_call" | custom-call | tf_op jit(solution)/shard_map/pick/pallas_call | solution.py:35
  10.3 0.0 all-gather.2.cloned.1.call-update
  10.3 3.3 %collective-permute-start = (bf16[256,2048]{1,0:T(8,128)(2,1)}, bf16[256,2048]{1,0:T(8,128)(2,1)S(1)}, u32[]{:S(2)}, u32[]{:S(2)}) collective-permute-start(bf16[256,2048]{1,0:T(8,128)(2,1)} %get-tuple-element.7), channel_id=1, source_target_pairs={{0,1},{1,0},{2,3},{3,2},{4,5},{5,4},{6,7},{7,6},{8,9},{9,8},{10,11... | collective-permute-start | bytes 3145736 | tf_op jit(solution)/shard_map/ppermute | solution.py:107
  13.6 3.2 %make_q.1.q_ref = bf16[256,512]{1,0:T(8,128)(2,1)} custom-call(bf16[256,1024]{1,0:T(8,128)(2,1)} %up_ref.1, f32[1024,512]{1,0:T(8,128)} %proj_ref.1), custom_call_target="tpu_custom_call" | custom-call | tf_op jit(solution)/shard_map/make_q/pallas_call | solution.py:56
  16.8 0.0 collective-permute-start.1
  16.8 1.7 %collective-permute-done.1.got_q_ref = bf16[256,512]{1,0:T(8,128)(2,1)S(1)} collective-permute-done((bf16[256,512]{1,0:T(8,128)(2,1)}, bf16[256,512]{1,0:T(8,128)(2,1)S(1)}, u32[]{:S(2)}, u32[]{:S(2)}) %collective-permute-start.1) | collective-permute-done | bytes 262176 | tf_op jit(solution)/shard_map/ppermute | solution.py:111
  18.5 0.0 collective-permute-done.got_ref
  18.5 0.7 copy-done.5
  19.2 1.0 copy-done.2
  20.3 6.5 %make_sketch.1 = bf16[8,2,8,16,512]{4,3,2,1,0:T(8,128)(2,1)} custom-call(s32[1]{0:T(128)} %bitcast.c_ref, bf16[256,4096]{1,0:T(8,128)(2,1)} %tok_ref.1, bf16[256,2048]{1,0:T(8,128)(2,1)} %copy-done.2, bf16[256,512]{1,0:T(8,128)(2,1)} %make_q.1.q_ref, bf16[256,512]{1,0:T(8,128)(2,1)} %copy-done.5), custom_call_target="tpu_custom_call" | custom-call | tf_op jit(solution)/shard_map/make_sketch/pallas_call | solution.py:83
  26.8 31.6 %all_to_all.15 = bf16[16,128,512]{2,1,0:T(8,128)(2,1)} all-to-all(bf16[16,128,512]{2,1,0:T(8,128)(2,1)} %bitcast.14), channel_id=1, replica_groups=mesh['y'=4,'xl'=2,'z'=8,'xh'=2,'c'=2] {'y','xl','xh'}, dimensions={0} | all-to-all | bytes 4194304 | tf_op jit(solution)/shard_map/all_to_all | solution.py:114
  58.4 2.0 %reduce_sum.24 = bf16[128,512]{1,0:T(8,128)(2,1)S(1)} reduce(bf16[16,128,512]{2,1,0:T(8,128)(2,1)} %all_to_all.15, bf16[]{:T(256)} %constant.3.clone.1), dimensions={0}, to_apply=%region_0.0 | reduce | flops 983040 | bytes 2228226 | tf_op jit(solution)/shard_map/reduce_sum | solution.py:115
  60.4 0.0 copy-start.1
  60.5 0.0 copy-start.3
  60.5 16.6 %all_to_all.16 = bf16[8,16,512]{2,1,0:T(8,128)(2,1)S(1)} all-to-all(bf16[8,16,512]{2,1,0:T(8,128)(2,1)S(1)} %bitcast.17), channel_id=1, replica_groups=mesh['y'=4,'xl'=2,'z'=8,'xh'=2,'c'=2] {'z'}, dimensions={0} | all-to-all | bytes 262144 | tf_op jit(solution)/shard_map/all_to_all | solution.py:116
  77.1 10.6 %all_to_all.17 = bf16[8,16,512]{2,1,0:T(8,128)(2,1)S(1)} all-to-all(bf16[8,16,512]{2,1,0:T(8,128)(2,1)S(1)} %broadcast_in_dim.2), channel_id=1, replica_groups=mesh['y'=4,'xl'=2,'z'=8,'xh'=2,'c'=2] {'y','xl'}, dimensions={0} | all-to-all | bytes 262144 | tf_op jit(solution)/shard_map/all_to_all | solution.py:119
  87.8 0.5 fusion.6
  88.3 1.5 %multiply_subtract_fusion = (f32[128,1024]{1,0:T(8,128)}, f32[128,1024]{1,0:T(8,128)}) fusion(f32[128,1024]{1,0:T(8,128)S(1)} %copy-done.1, f32[128,1024]{1,0:T(8,128)S(1)} %copy-done.3, f32[128,1024]{1,0:T(8,128)S(1)} %fusion.6, bf16[128,512]{1,0:T(8,128)(2,1)S(1)} %bitcast.16, f32[1024,512]{1,0:T(8,128)S(1)} %copy-done), kind=kOutput, calls=%fused_computation.9 | convolution fusion | flops 137363456 | bytes 4849664 | tf_op jit(solution)/shard_map/dot_general | solution.py:124
  89.8 28.5 %all-gather.2.cloned.1.call-done = bf16[4096,1024]{1,0:T(8,128)(2,1)} async-done(((bf16[128,1024]{1,0:T(8,128)(2,1)}), bf16[4096,1024]{1,0:T(8,128)(2,1)}) %all-gather.2.cloned.1.call-update) | async-done | bytes 8388624 | tf_op jit(solution)/shard_map/all_gather | solution.py:108
  118.4 6.4 %fusion.4 = bf16[256,1024]{0,1:T(8,128)(2,1)S(1)} fusion(bf16[4096,1024]{1,0:T(8,128)(2,1)} %all-gather.2.cloned.1.call-done, bf16[256,4096]{1,0:T(8,128)(2,1)} %tok_ref.1), kind=kOutput, calls=%fused_computation.8 | convolution fusion | flops 2148007936 | bytes 11010048 | tf_op jit(solution)/shard_map/dot_general | solution.py:129
  124.7 1.0 copy.11
  125.7 5.8 %fusion.1 = bf16[256,4096]{0,1:T(8,128)(2,1)S(1)} fusion(bf16[4096,1024]{1,0:T(8,128)(2,1)} %all-gather.2.cloned.1.call-done, bf16[256,1024]{1,0:T(8,128)(2,1)S(1)} %copy-done.4), kind=kOutput, calls=%fused_computation.2 | convolution fusion | flops 2149580800 | bytes 11010048 | tf_op jit(solution)/shard_map/dot_general | solution.py:131
  131.5 2.9 %copy.12 = bf16[256,4096]{1,0:T(8,128)(2,1)} copy(bf16[256,4096]{0,1:T(8,128)(2,1)S(1)} %fusion.1) | data formatting | bytes 4194304
  (10 shorter events, 0.0 us)
Async XLA Ops:
  7.2 111.2 %all-gather.2.cloned.1.call-start = ((), (), s32[]{:S(2)}) async-start(), calls=%async_computation.3 | async-start | bytes 8650752 | tf_op jit(solution)/shard_map/all_gather | solution.py:108
  10.3 8.2 %collective-permute-start = (bf16[256,2048]{1,0:T(8,128)(2,1)}, bf16[256,2048]{1,0:T(8,128)(2,1)S(1)}, u32[]{:S(2)}, u32[]{:S(2)}) collective-permute-start(bf16[256,2048]{1,0:T(8,128)(2,1)} %get-tuple-element.7), channel_id=1, source_target_pairs={{0,1},{1,0},{2,3},{3,2},{4,5},{5,4},{6,7},{7,6},{8,9},{9,8},{10,11... | collective-permute-start | bytes 3145736 | tf_op jit(solution)/shard_map/ppermute | solution.py:107
  16.8 1.7 %collective-permute-start.1 = (bf16[256,512]{1,0:T(8,128)(2,1)}, bf16[256,512]{1,0:T(8,128)(2,1)S(1)}, u32[]{:S(2)}, u32[]{:S(2)}) collective-permute-start(bf16[256,512]{1,0:T(8,128)(2,1)} %make_q.1.q_ref), channel_id=1, source_target_pairs={{0,1},{1,0},{2,3},{3,2},{4,5},{5,4},{6,7},{7,6},{8,9},{9,8},{10,11... | collective-permute-start | bytes 786440 | tf_op jit(solution)/shard_map/ppermute | solution.py:111
  18.5 0.7 copy-start.5
  19.2 1.0 copy-start.2
  58.4 29.4 %copy-start = (f32[1024,512]{1,0:T(8,128)S(1)}, f32[1024,512]{1,0:T(8,128)}, u32[]{:S(2)}) copy-start(f32[1024,512]{1,0:T(8,128)} %proj_ref.1) | copy-start | bytes 6291460
  60.4 27.8 %copy-start.1 = (f32[128,1024]{1,0:T(8,128)S(1)}, f32[128,1024]{1,0:T(8,128)}, u32[]{:S(2)}) copy-start(f32[128,1024]{1,0:T(8,128)} %params_ref.1) | copy-start | bytes 1572868
  60.5 27.8 %copy-start.3 = (f32[128,1024]{1,0:T(8,128)S(1)}, f32[128,1024]{1,0:T(8,128)}, u32[]{:S(2)}) copy-start(f32[128,1024]{1,0:T(8,128)} %param.8) | copy-start | bytes 1572868
  89.8 35.9 %copy-start.4 = (bf16[256,1024]{1,0:T(8,128)(2,1)S(1)}, bf16[256,1024]{1,0:T(8,128)(2,1)}, u32[]{:S(2)}) copy-start(bf16[256,1024]{1,0:T(8,128)(2,1)} %up_ref.1) | copy-start | bytes 1572868
Sparse Core Ops, SparseCore 0:
  11.3 106.9 all-gather.1

commit v2 on v1

v2 whole, which is shorter than its diff:
```python
import functools
import math

import jax
import jax.numpy as jnp
from jax import lax
from jax.experimental import pallas as pl
from jax.experimental.pallas import tpu as pltpu
from jax.sharding import Mesh
from jax.sharding import PartitionSpec as P


ISLAND = ("y", "xl")
FSDP = ("z", "xh", "c")
PLANE = ("y", "xl", "xh")
F32, BF16 = jnp.float32, jnp.bfloat16
LANES = 128
VMEM = pl.BlockSpec(memory_space=pltpu.VMEM)
SMEM = pl.BlockSpec(memory_space=pltpu.SMEM)
LEFT = pl.BlockSpec(memory_space=pl.ANY)


def two_parts(x):
    head = x.astype(BF16)
    return head, (x - head.astype(F32)).astype(BF16)


def pick_kernel(at_ref, tokens_ref, params_ref, out_ref, piece_ref):
    skip = 1 - at_ref[0]
    width = piece_ref.shape[2]
    block = 2 * at_ref[1] + at_ref[3]
    piece = params_ref[:, pl.ds(pl.multiple_of(block * width, width), width)].astype(BF16)
    for z in range(piece_ref.shape[0]):
        piece_ref[z] = piece
    for k in range(out_ref.shape[1] // LANES):
        at = pl.multiple_of((2 * k + skip) * LANES, LANES)
        out_ref[:, k * LANES : (k + 1) * LANES] = tokens_ref[:, pl.ds(at, LANES)]


def pick(at, tokens, params, n_z, pieces):
    t, d = tokens.shape
    rows, kv = params.shape
    return pl.pallas_call(
        pick_kernel,
        out_shape=(
            jax.ShapeDtypeStruct((t, d // 2), BF16),
            jax.ShapeDtypeStruct((n_z, rows, kv // pieces), BF16),
        ),
        in_specs=[SMEM, VMEM, VMEM],
        out_specs=(VMEM, VMEM),
        name="pick",
    )(at, tokens, params)


def q_kernel(up_ref, proj_ref, q_ref):
    head, rest = two_parts(proj_ref[...])
    q = jnp.dot(up_ref[...], head, preferred_element_type=F32)
    q += jnp.dot(up_ref[...], rest, preferred_element_type=F32)
    q_ref[...] = q.astype(BF16)


def make_q(upstream, projection):
    vm = pl.BlockSpec(memory_space=pltpu.VMEM)
    return pl.pallas_call(
        q_kernel,
        out_shape=jax.ShapeDtypeStruct((upstream.shape[0], projection.shape[1]), BF16),
        in_specs=[vm, vm],
        out_specs=vm,
        cost_estimate=pl.CostEstimate(flops=8 * upstream.size * projection.shape[1], bytes_accessed=4 * projection.size + 4 * upstream.size, transcendentals=0),
        name="make_q",
    )(upstream, projection)


def sketch_kernel(at_ref, tok_ref, got_ref, q_ref, got_q_ref, out_ref):
    pieces, n_xh, _, part, proj = out_ref.shape
    z = pl.program_id(0)
    dims = (((0,), (0,)), ((), ()))
    for h in range(n_xh):
        k = z * n_xh + h
        mine = tok_ref[:, pl.ds(pl.multiple_of((2 * k + at_ref[0]) * LANES, LANES), LANES)]
        theirs = got_ref[:, pl.ds(pl.multiple_of(k * LANES, LANES), LANES)]
        s = lax.dot_general(mine, q_ref[...], dims, preferred_element_type=F32)
        s += lax.dot_general(theirs, got_q_ref[...], dims, preferred_element_type=F32)
        out_ref[:, h, 0] = s.astype(BF16).reshape(pieces, part, proj)


def make_sketch(at, tokens, got, q, got_q, pieces, n_xh, n_z):
    proj = q.shape[1]
    part = LANES // pieces
    vm = pl.BlockSpec(memory_space=pltpu.VMEM)
    return pl.pallas_call(
        sketch_kernel,
        grid=(n_z,),
        out_shape=jax.ShapeDtypeStruct((pieces, n_xh, n_z, part, proj), BF16),
        in_specs=[pl.BlockSpec(memory_space=pltpu.SMEM), vm, vm, vm, vm],
        out_specs=pl.BlockSpec((pieces, n_xh, 1, part, proj), lambda z: (0, 0, z, 0, 0)),
        cost_estimate=pl.CostEstimate(flops=8 * tokens.size * proj, bytes_accessed=16 * tokens.size, transcendentals=0),
        name="make_sketch",
    )(at, tokens, got, q, got_q)


GROUPS = ("XALB", "ALBX", "LBXA", "BXAL")
FLIP = {"X": (1, 0, 1), "L": (0, 0, 1), "A": (0, 1, 0), "B": (0, 3, 0)}


def exchange(x, kind):
    if kind == "X":
        return lax.ppermute(x, ("xl", "xh"), [(0, 3), (3, 0), (1, 2), (2, 1)])
    if kind == "L":
        return lax.ppermute(x, "xl", [(0, 1), (1, 0)])
    flip = FLIP[kind][1]
    return lax.ppermute(x, "y", [(i, i ^ flip) for i in range(4)])


def places(n_z):
    table = {}
    each = n_z // len(GROUPS)
    for g, order in enumerate(GROUPS):
        held = [(0, 0, 0)]
        for step, kind in enumerate(order):
            f = FLIP[kind]
            there = [(a ^ f[0], b ^ f[1], l ^ f[2]) for a, b, l in held]
            if step == 3:
                for half, part in enumerate((held, there)):
                    for k in range(each):
                        for a in range(2):
                            table[half, g * each + k, a] = sorted(
                                ((b, l), g, i * each + k) for i, (a_, b, l) in enumerate(part) if a_ == a
                            )
            held = held + there
    return table


def split_kernel(piece_ref, after_ref, *out_refs):
    each = out_refs[0].shape[0]
    for g, out_ref in enumerate(out_refs):
        out_ref[...] = piece_ref[g * each : (g + 1) * each]


def split(piece, after):
    n = len(GROUPS)
    shape = (piece.shape[0] // n,) + piece.shape[1:]
    return pl.pallas_call(
        split_kernel,
        out_shape=(jax.ShapeDtypeStruct(shape, BF16),) * n,
        in_specs=[VMEM, LEFT],
        out_specs=(VMEM,) * n,
        name="split",
    )(piece, after)


def join_kernel(after_ref, *refs):
    n = len(refs) // 3
    for a_ref, b_ref, out_ref in zip(refs[:n], refs[n : 2 * n], refs[2 * n :]):
        k = a_ref.shape[0]
        out_ref[:k] = a_ref[...]
        out_ref[k:] = b_ref[...]


def join(held, more, after):
    n = len(held)
    shapes = tuple(jax.ShapeDtypeStruct((2 * h.shape[0],) + h.shape[1:], BF16) for h in held)
    return pl.pallas_call(
        join_kernel, out_shape=shapes, in_specs=[LEFT] + [VMEM] * (2 * n), out_specs=(VMEM,) * n, name="join"
    )(after, *held, *more)


def lanes(ref, blocks):
    return jnp.concatenate([ref[:, at] for at in blocks], axis=1)


def half_products(half, at_ref, tok_ref, up_ref, w_refs, acc_ref, up_rel, take):
    c, y, xh, xl = (at_ref[i] for i in range(4))
    n = len(GROUPS)
    n_z = tok_ref.shape[1] // (4 * LANES)
    table = places(n_z)
    cols = [
        pl.ds(pl.multiple_of((2 * (y ^ (r // 2)) + (xl ^ (r % 2))) * LANES, LANES), LANES) for r in range(8)
    ]
    for r in range(8):
        up_rel[:, r * LANES : (r + 1) * LANES] = up_ref[:, cols[r]]
    for z in range(n_z):
        for a in range(2):
            shard = 2 * (2 * z + (xh ^ a))
            blocks = [pl.ds(pl.multiple_of((shard + (c ^ o)) * LANES, LANES), LANES) for o in range(2)]
            found = table[half, z, a]
            total = None
            if found:
                w = jnp.concatenate(
                    [
                        jnp.concatenate([w_refs[n * o + g][i] for _, g, i in found], axis=1)
                        for o in range(2)
                    ],
                    axis=0,
                )
                here = [slice((2 * b + l) * LANES, (2 * b + l + 1) * LANES) for (b, l), _, _ in found]
                part = jnp.dot(lanes(tok_ref, blocks), w, preferred_element_type=F32)
                for i, at in enumerate(here):
                    acc_ref[:, at] += part[:, i * LANES : (i + 1) * LANES]
                total = lax.dot_general(
                    lanes(up_rel, here), w, (((1,), (1,)), ((), ())), preferred_element_type=F32
                )
            take(z, a, blocks, total)
    return cols


def near_kernel(at_ref, tok_ref, up_ref, *refs):
    w_refs, (acc_ref, sum_ref, up_rel) = refs[:-3], refs[-3:]
    acc_ref[...] = jnp.zeros(acc_ref.shape, F32)

    def take(z, a, blocks, total):
        if total is not None:
            sum_ref[2 * z + a] = total

    half_products(0, at_ref, tok_ref, up_ref, w_refs, acc_ref, up_rel, take)


def far_kernel(at_ref, tok_ref, up_ref, before_ref, sum_ref, *refs, scale):
    w_refs, (values_ref, grads_ref, acc_ref, up_rel) = refs[:-4], refs[-4:]
    acc_ref[...] = before_ref[...]
    near = places(tok_ref.shape[1] // (4 * LANES))

    def take(z, a, blocks, total):
        if near[0, z, a]:
            total = sum_ref[2 * z + a] if total is None else total + sum_ref[2 * z + a]
        grad = (total * scale).astype(BF16)
        for o in range(2):
            grads_ref[:, blocks[o]] = grad[:, o * LANES : (o + 1) * LANES]

    cols = half_products(1, at_ref, tok_ref, up_ref, w_refs, acc_ref, up_rel, take)
    for r in range(8):
        values_ref[:, cols[r]] = (acc_ref[:, r * LANES : (r + 1) * LANES] * scale).astype(BF16)


def near_products(at, tokens, upstream, weights):
    t, d = tokens.shape
    kv = upstream.shape[1]
    return pl.pallas_call(
        near_kernel,
        out_shape=(
            jax.ShapeDtypeStruct((t, kv), F32),
            jax.ShapeDtypeStruct((d // (2 * LANES), t, 2 * LANES), F32),
        ),
        in_specs=[SMEM] + [VMEM] * (2 + len(weights)),
        out_specs=(VMEM, VMEM),
        scratch_shapes=[pltpu.VMEM((t, kv), BF16)],
        cost_estimate=pl.CostEstimate(flops=2 * t * d * kv, bytes_accessed=d * kv, transcendentals=0),
        name="near_products",
    )(at, tokens, upstream, *weights)


def far_products(at, tokens, upstream, acc, sums, weights, scale):
    t, d = tokens.shape
    kv = upstream.shape[1]
    return pl.pallas_call(
        functools.partial(far_kernel, scale=scale),
        out_shape=(jax.ShapeDtypeStruct((t, kv), BF16), jax.ShapeDtypeStruct((t, d), BF16)),
        in_specs=[SMEM] + [VMEM] * (4 + len(weights)),
        out_specs=(VMEM, VMEM),
        scratch_shapes=[pltpu.VMEM((t, kv), F32), pltpu.VMEM((t, kv), BF16)],
        cost_estimate=pl.CostEstimate(flops=2 * t * d * kv, bytes_accessed=d * kv, transcendentals=0),
        name="far_products",
    )(at, tokens, upstream, acc, sums, *weights)


def step(tokens, upstream, params, momentum, projection):
    rows, _ = params.shape
    n_z, n_xh, n_c = (lax.axis_size(a) for a in FSDP)
    n_isl = lax.axis_size("y") * lax.axis_size("xl")
    fsdp_count = n_z * n_xh * n_c
    width = tokens.shape[1]
    proj = projection.shape[1]
    part = rows // n_isl
    inv_width = 1.0 / math.sqrt(width)
    scale_tok = 1.0 / math.sqrt(tokens.shape[0] * fsdp_count)
    at = jnp.stack([lax.axis_index(a).astype(jnp.int32) for a in ("c", "y", "xh", "xl")])
    swap = functools.partial(lax.ppermute, axis_name="c", perm=[(0, 1), (1, 0)])

    other, piece = pick(at, tokens, params, n_z, n_isl)
    got = swap(other)
    piece = lax.all_to_all(piece, "z", 0, 0, tiled=True)

    q = make_q(upstream, projection)
    got_q = swap(q)
    pair = make_sketch(at, tokens, got, q, got_q, n_isl, n_xh, n_z)
    held = split(piece, pair)
    held = join(held, [exchange(h, order[0]) for h, order in zip(held, GROUPS)], pair)
    more = [exchange(h, order[1]) for h, order in zip(held, GROUPS)]
    pair = pair.reshape(n_isl * n_xh, n_z * part, proj)
    pair = lax.all_to_all(pair, PLANE, 0, 0, tiled=True)
    plane = jnp.sum(pair.astype(F32), axis=0).astype(BF16)
    held = join(held, more, plane)
    more = [exchange(h, order[2]) for h, order in zip(held, GROUPS)]
    plane = lax.all_to_all(plane.reshape(n_z, part, proj), "z", 0, 0, tiled=True)
    total = jnp.sum(plane.astype(F32), axis=0).astype(BF16)
    held = join(held, more, total)
    far = [exchange(h, order[3]) for h, order in zip(held, GROUPS)]
    total = jnp.broadcast_to(total[None], (n_isl, part, proj))
    total = lax.all_to_all(total, ISLAND, 0, 0, tiled=True).reshape(rows, proj)

    held = [*held, *(swap(h) for h in held)]
    acc, sums = near_products(at, tokens, upstream, held)
    far = [*far, *(swap(f) for f in far)]
    values, token_grads = far_products(at, tokens, upstream, acc, sums, far, inv_width)

    dims = (((1,), (1,)), ((), ()))
    head, rest = two_parts(projection)
    outer = lax.dot_general(total, head, dims, preferred_element_type=F32)
    outer = outer + lax.dot_general(total, rest, dims, preferred_element_type=F32)
    outer = outer * (scale_tok / (proj * n_isl))
    new_momentum = 0.9 * momentum + outer
    new_params = params - 0.7 * (outer + 0.9 * new_momentum)

    return (values, token_grads, new_params, new_momentum)


def solution(mesh):
    fine = Mesh(mesh.devices.reshape(4, 2, 8, 2, 2), ISLAND + FSDP)
    both = ISLAND + FSDP
    in_specs = (P(both, None), P(both, None), P(FSDP, None), P(FSDP, None), P())
    out_specs = (P(both, None), P(both, None), P(FSDP, None), P(FSDP, None))
    return jax.shard_map(step, mesh=fine, in_specs=in_specs, out_specs=out_specs, check_vma=False)
```

time: 142 us -> 145 us (1.021)
  blocking collectives: 58.9 us -> 13.2 us
  starting transfers between devices: 3.34 us -> 48.5 us
  Pallas kernels: 12.8 us -> 37.9 us
  between operations: 14.1 us -> 0.82 us
  matrix products: 14.1 us -> 2 us
  waiting for transfers between devices: 30.3 us -> 33.1 us
    all_to_all x3 -> x1, blocking collectives: 58.9 us -> 13.2 us  [step(): lax.all_to_all(plane.reshape(n_z, part, proj), 'z', 0, 0, tiled=True)]
    all_gather x1 -> x0, waiting for transfers between devices: 28.5 us -> none  [local(): weight = lax.all_gather(half, FSDP, axis=0, tiled=True)]
    ppermute x2 -> x26, starting transfers between devices: 3.3 us -> 31.6 us  [the longest x8 7.98 us: exchange(): return lax.ppermute(x, 'y', [(i, i ^ flip) for i in range(4)])]
    pallas_call x0 -> x6, Pallas kernels: none -> 25 us  [the longest x1 8.67 us: far_products(): pl.pallas_call(functools.partial(far_kernel, scale=scale), out_shape=(jax...]
    ppermute x2 -> x26, waiting for transfers between devices: 1.73 us -> 21.6 us  [the longest x8 11 us: exchange(): return lax.ppermute(x, 'y', [(i, i ^ flip) for i in range(4)])]
    all_to_all x0 -> x3, starting transfers between devices: none -> 16.9 us  [the longest x1 6.75 us: step(): pair = lax.all_to_all(pair, PLANE, 0, 0, tiled=True)]
    dot_general x4 -> x2, matrix products: 14.1 us -> 2 us  [the longest x1 1.52 us: step(): lax.dot_general(total, rest, dims, preferred_element_type=F32)]
    all_to_all x0 -> x3, waiting for transfers between devices: none -> 11.5 us  [the longest x1 9.05 us: step(): total = lax.all_to_all(total, ISLAND, 0, 0, tiled=True).reshape(rows, proj)]
  transfers between devices with their start and end apart: 3 -> 29, of which waited for: 2 -> 6; matrix products, arithmetic and copies ran while one was open for 3% -> 3% of each run, Pallas kernels for 7% -> 15%
where the time goes in v2:
time: 145 us; the launch traced here: 144 us
  starting transfers between devices  48.5 us (33%)
  Pallas kernels  37.9 us (26%)
  waiting for transfers between devices  33.1 us (23%)
  blocking collectives  13.2 us (9%)
  local copies, waits for them, and re-layouts  6.55 us (5%)
  other arithmetic  2.19 us (2%)
  matrix products  2 us (1%)
    all_to_all x1, blocking collectives, step(): lax.all_to_all(plane.reshape(n_z, part, proj), 'z', 0, 0, tiled=True)  13.2 us
    ppermute x8, waiting for transfers between devices, exchange(): return lax.ppermute(x, 'y', [(i, i ^ flip) for i in range(4)])  11 us
    ppermute x4, waiting for transfers between devices, exchange(): return lax.ppermute(x, ('xl', 'xh'), [(0, 3), (3, 0), (1, 2), (2, 1)])  10.6 us
    all_to_all x1, waiting for transfers between devices, step(): total = lax.all_to_all(total, ISLAND, 0, 0, tiled=True).reshape(rows, proj)  9.05 us
    pallas_call x1, Pallas kernels, far_products(): pl.pallas_call(functools.partial(far_kernel, scale=scale), out_shape=(jax...  8.67 us
    ppermute x8, starting transfers between devices, exchange(): return lax.ppermute(x, 'y', [(i, i ^ flip) for i in range(4)])  7.98 us
    ppermute x4, starting transfers between devices, step(): held = [*held, *(swap(h) for h in held)]  7.85 us
    pallas_call x1, Pallas kernels, near_products(): pl.pallas_call(near_kernel, out_shape=(jax.ShapeDtypeStruct((t, kv), F32)...  7.69 us
  transfers between devices with their start and end apart: 29, of which 6 were waited for; matrix products, arithmetic and copies ran while one was open for 3% of the time, Pallas kernels for 15%

profile of v2, /device:TPU:1, one launch (start us, length us, event | category | flops | bytes accessed | tf_op | source)
XLA Modules:
  0.0 144.2 jit_solution(5236218076584796012)
XLA Ops:
  1.2 3.0 %pick.1 = (bf16[256,2048]{1,0:T(8,128)(2,1)}, bf16[8,128,128]{2,1,0:T(8,128)(2,1)}) custom-call(s32[4]{0:T(128)} %pad_add_fusion.at_ref, bf16[256,4096]{1,0:T(8,128)(2,1)} %tok_ref.5, f32[128,1024]{1,0:T(8,128)} %params_ref.1), custom_call_target="tpu_custom_call" | custom-call | tf_op jit(solution)/shard_map/pick/pallas_call | solution.py:43
  4.3 3.2 %collective-permute-start = (bf16[256,2048]{1,0:T(8,128)(2,1)}, bf16[256,2048]{1,0:T(8,128)(2,1)S(1)}, u32[]{:S(2)}, u32[]{:S(2)}) collective-permute-start(bf16[256,2048]{1,0:T(8,128)(2,1)} %get-tuple-element.26), channel_id=1, source_target_pairs={{0,1},{1,0},{2,3},{3,2},{4,5},{5,4},{6,7},{7,6},{8,9},{9,8},{10,11... | collective-permute-start | bytes 3145736 | tf_op jit(solution)/shard_map/ppermute | solution.py:280
  7.5 3.2 %make_q.1.q_ref = bf16[256,512]{1,0:T(8,128)(2,1)} custom-call(bf16[256,1024]{1,0:T(8,128)(2,1)} %up_ref.5, f32[1024,512]{1,0:T(8,128)} %proj_ref.1), custom_call_target="tpu_custom_call" | custom-call | flops 1073741824 | bytes 3145728 | tf_op jit(solution)/shard_map/make_q/pallas_call | solution.py:64
  10.7 6.5 %all-to-all-start.2 = ((bf16[8,128,128]{2,1,0:T(8,128)(2,1)}), bf16[8,128,128]{2,1,0:T(8,128)(2,1)S(1)}, u32[]{:S(2)}, u32[]{:S(2)}) async-start(bf16[8,128,128]{2,1,0:T(8,128)(2,1)} %get-tuple-element.27), calls=%async_computation.2 | async-start | bytes 524288 | tf_op jit(solution)/shard_map/all_to_all | solution.py:281
  18.9 6.6 %make_sketch.1.after_ref = bf16[8,2,8,16,512]{4,3,2,1,0:T(8,128)(2,1)} custom-call(s32[4]{0:T(128)} %pad_add_fusion.at_ref, bf16[256,4096]{1,0:T(8,128)(2,1)} %tok_ref.5, bf16[256,2048]{1,0:T(8,128)(2,1)} %copy-done.17, bf16[256,512]{1,0:T(8,128)(2,1)} %make_q.1.q_ref, bf16[256,512]{1,0:T(8,128)(2,1)} %copy-done.18), custom_call_target="tpu_custom_call" | custom-call | flops 4294967296 | bytes 16777216 | tf_op jit(solution)/shard_map/make_sketch/pallas_call | solution.py:91
  25.5 2.4 %all-to-all-done.2.piece_ref = bf16[8,128,128]{2,1,0:T(8,128)(2,1)S(1)} async-done(((bf16[8,128,128]{2,1,0:T(8,128)(2,1)}), bf16[8,128,128]{2,1,0:T(8,128)(2,1)S(1)}, u32[]{:S(2)}, u32[]{:S(2)}) %all-to-all-start.2) | async-done | bytes 262176 | tf_op jit(solution)/shard_map/all_to_all | solution.py:281
  28.6 6.8 %all-to-all-start = ((bf16[16,128,512]{2,1,0:T(8,128)(2,1)}), bf16[16,128,512]{2,1,0:T(8,128)(2,1)S(1)}, u32[]{:S(2)}, u32[]{:S(2)}) async-start(bf16[16,128,512]{2,1,0:T(8,128)(2,1)} %bitcast.9), calls=%async_computation | async-start | bytes 4194304 | tf_op jit(solution)/shard_map/all_to_all | solution.py:290
  37.0 2.6 %collective-permute-start.2 = (bf16[2,128,128]{2,1,0:T(8,128)(2,1)}, bf16[2,128,128]{2,1,0:T(8,128)(2,1)S(1)}, u32[]{:S(2)}, u32[]{:S(2)}) collective-permute-start(bf16[2,128,128]{2,1,0:T(8,128)(2,1)} %get-tuple-element.28.refs_0_), channel_id=1, source_target_pairs={{0,34},{34,0},{2,32},{32,2},{1,35},{35,1},{3,33},{33,3},{4,38},{38... | collective-permute-start | bytes 196616 | tf_op jit(solution)/shard_map/ppermute | solution.py:108
  40.8 1.8 %collective-permute-start.5 = (bf16[2,128,128]{2,1,0:T(8,128)(2,1)}, bf16[2,128,128]{2,1,0:T(8,128)(2,1)S(1)}, u32[]{:S(2)}, u32[]{:S(2)}) collective-permute-start(bf16[2,128,128]{2,1,0:T(8,128)(2,1)} %get-tuple-element.31.refs_3_), channel_id=1, source_target_pairs={{0,192},{64,128},{128,64},{192,0},{1,193},{65,129},{129,65},{193,1... | collective-permute-start | bytes 196616 | tf_op jit(solution)/shard_map/ppermute | solution.py:112
  42.6 8.8 %collective-permute-done.2.refs_4_ = bf16[2,128,128]{2,1,0:T(8,128)(2,1)S(1)} collective-permute-done((bf16[2,128,128]{2,1,0:T(8,128)(2,1)}, bf16[2,128,128]{2,1,0:T(8,128)(2,1)S(1)}, u32[]{:S(2)}, u32[]{:S(2)}) %collective-permute-start.2) | collective-permute-done | bytes 65568 | tf_op jit(solution)/shard_map/ppermute | solution.py:108
  51.4 10.3 %collective-permute-done.3.refs_5_ = bf16[2,128,128]{2,1,0:T(8,128)(2,1)S(1)} collective-permute-done((bf16[2,128,128]{2,1,0:T(8,128)(2,1)}, bf16[2,128,128]{2,1,0:T(8,128)(2,1)S(1)}, u32[]{:S(2)}, u32[]{:S(2)}) %collective-permute-start.3) | collective-permute-done | bytes 65568 | tf_op jit(solution)/shard_map/ppermute | solution.py:112
  63.0 1.9 %join.3 = (bf16[4,128,128]{2,1,0:T(8,128)(2,1)}, bf16[4,128,128]{2,1,0:T(8,128)(2,1)}, bf16[4,128,128]{2,1,0:T(8,128)(2,1)}, bf16[4,128,128]{2,1,0:T(8,128)(2,1)}) custom-call(bf16[8,2,8,16,512]{4,3,2,1,0:T(8,128)(2,1)} %make_sketch.1.after_ref, bf16[2,128,128]{2,1,0:T(8,128)(2,1)} %get-tuple-element.28.refs_0_, ...), custom_call_target="tpu_custom_call" | custom-call | tf_op jit(solution)/shard_map/join/pallas_call | solution.py:163
  68.2 2.1 %collective-permute-start.9 = (bf16[4,128,128]{2,1,0:T(8,128)(2,1)}, bf16[4,128,128]{2,1,0:T(8,128)(2,1)S(1)}, u32[]{:S(2)}, u32[]{:S(2)}) collective-permute-start(bf16[4,128,128]{2,1,0:T(8,128)(2,1)} %get-tuple-element.35.refs_3_), channel_id=1, source_target_pairs={{0,34},{34,0},{2,32},{32,2},{1,35},{35,1},{3,33},{33,3},{4,38},{38... | collective-permute-start | bytes 393224 | tf_op jit(solution)/shard_map/ppermute | solution.py:108
  71.9 1.8 %collective-permute-done.9.refs_7_ = bf16[4,128,128]{2,1,0:T(8,128)(2,1)S(1)} collective-permute-done((bf16[4,128,128]{2,1,0:T(8,128)(2,1)}, bf16[4,128,128]{2,1,0:T(8,128)(2,1)S(1)}, u32[]{:S(2)}, u32[]{:S(2)}) %collective-permute-start.9) | collective-permute-done | bytes 131104 | tf_op jit(solution)/shard_map/ppermute | solution.py:108
  74.4 2.2 %join.4 = (bf16[8,128,128]{2,1,0:T(8,128)(2,1)}, bf16[8,128,128]{2,1,0:T(8,128)(2,1)}, bf16[8,128,128]{2,1,0:T(8,128)(2,1)}, bf16[8,128,128]{2,1,0:T(8,128)(2,1)}) custom-call(bf16[128,512]{1,0:T(8,128)(2,1)} %reduce_sum.24.after_ref, bf16[4,128,128]{2,1,0:T(8,128)(2,1)} %get-tuple-element.32.refs_0_, bf16[4,128,128]{2,1,0:T(8,128)(2,1)} %get-tuple-element.33.refs_1_, ...), custom_call_target="tpu_custom_call" | custom-call | tf_op jit(solution)/shard_map/join/pallas_call | solution.py:163
  77.5 2.2 %collective-permute-start.12 = (bf16[8,128,128]{2,1,0:T(8,128)(2,1)}, bf16[8,128,128]{2,1,0:T(8,128)(2,1)S(1)}, u32[]{:S(2)}, u32[]{:S(2)}) collective-permute-start(bf16[8,128,128]{2,1,0:T(8,128)(2,1)} %get-tuple-element.38.refs_2_), channel_id=1, source_target_pairs={{0,34},{34,0},{2,32},{32,2},{1,35},{35,1},{3,33},{33,3},{4,38},{38... | collective-permute-start | bytes 786440 | tf_op jit(solution)/shard_map/ppermute | solution.py:108
  79.7 13.2 %all_to_all.20 = bf16[8,16,512]{2,1,0:T(8,128)(2,1)S(1)} all-to-all(bf16[8,16,512]{2,1,0:T(8,128)(2,1)} %bitcast.10), channel_id=1, replica_groups=mesh['y'=4,'xl'=2,'z'=8,'xh'=2,'c'=2] {'z'}, dimensions={0} | all-to-all | bytes 262144 | tf_op jit(solution)/shard_map/all_to_all | solution.py:294
  95.2 2.8 %join.5 = (bf16[16,128,128]{2,1,0:T(8,128)(2,1)}, bf16[16,128,128]{2,1,0:T(8,128)(2,1)}, bf16[16,128,128]{2,1,0:T(8,128)(2,1)}, bf16[16,128,128]{2,1,0:T(8,128)(2,1)}) custom-call(bf16[16,512]{1,0:T(8,128)(2,1)} %reduce_sum.25.after_ref, bf16[8,128,128]{2,1,0:T(8,128)(2,1)} %get-tuple-element.36.refs_0_, bf16[8,128,128]{2,1,0:T(8,128)(2,1)} %get-tuple-element.37.refs_1_, ...), custom_call_target="tpu_custom_call" | custom-call | tf_op jit(solution)/shard_map/join/pallas_call | solution.py:163
  98.0 6.2 %collective-permute-start.14 = (bf16[16,128,128]{2,1,0:T(8,128)(2,1)}, bf16[16,128,128]{2,1,0:T(8,128)(2,1)}, u32[]{:S(2)}, u32[]{:S(2)}) collective-permute-start(bf16[16,128,128]{2,1,0:T(8,128)(2,1)} %get-tuple-element.40.refs_0_), channel_id=1, source_target_pairs={{0,1},{1,0},{2,3},{3,2},{4,5},{5,4},{6,7},{7,6},{8,9},{9,8},{10,11... | collective-permute-start | bytes 1572872 | tf_op jit(solution)/shard_map/ppermute | solution.py:301
  109.1 3.7 %all-to-all-start.3 = ((bf16[8,16,512]{2,1,0:T(8,128)(2,1)}), bf16[8,16,512]{2,1,0:T(8,128)(2,1)S(1)}, u32[]{:S(2)}, u32[]{:S(2)}) async-start(bf16[8,16,512]{2,1,0:T(8,128)(2,1)} %broadcast_in_dim.2), calls=%async_computation.3 | async-start | bytes 262144 | tf_op jit(solution)/shard_map/all_to_all | solution.py:299
  114.0 9.1 %all-to-all-done.3 = bf16[8,16,512]{2,1,0:T(8,128)(2,1)S(1)} async-done(((bf16[8,16,512]{2,1,0:T(8,128)(2,1)}), bf16[8,16,512]{2,1,0:T(8,128)(2,1)S(1)}, u32[]{:S(2)}, u32[]{:S(2)}) %all-to-all-start.3) | async-done | bytes 131104 | tf_op jit(solution)/shard_map/all_to_all | solution.py:299
  123.5 2.1 %collective-permute-start.22 = (bf16[16,128,128]{2,1,0:T(8,128)(2,1)}, bf16[16,128,128]{2,1,0:T(8,128)(2,1)}, u32[]{:S(2)}, u32[]{:S(2)}) collective-permute-start(bf16[16,128,128]{2,1,0:T(8,128)(2,1)} %collective-permute-done.18.refs_0_), channel_id=1, source_target_pairs={{0,1},{1,0},{2,3},{3,2},{4,5},{5,4},{6,7},{7,6},{8,9},{9,8},{10,11... | collective-permute-start | bytes 1572872 | tf_op jit(solution)/shard_map/ppermute | solution.py:303
  127.8 7.7 %near_products.1 = (f32[256,1024]{1,0:T(8,128)}, f32[16,256,256]{2,1,0:T(8,128)}) custom-call(s32[4]{0:T(128)} %pad_add_fusion.at_ref, bf16[256,4096]{1,0:T(8,128)(2,1)} %tok_ref.5, bf16[256,1024]{1,0:T(8,128)(2,1)} %up_ref.5, bf16[16,128,128]{2,1,0:T(8,128)(2,1)} %get-tuple-element.40.refs_0_, bf16[16,128,128]{2,1,0:T(8,128)(2,1)} %get-tuple-element.41.refs_1_, ...), custom_call_target="tpu_custom_call" | custom-call | flops 2147483648 | bytes 4194304 | tf_op jit(solution)/shard_map/near_products/pallas_call | solution.py:238
  135.6 8.7 %far_products.1 = (bf16[256,1024]{1,0:T(8,128)(2,1)}, bf16[256,4096]{1,0:T(8,128)(2,1)}) custom-call(s32[4]{0:T(128)} %pad_add_fusion.at_ref, bf16[256,4096]{1,0:T(8,128)(2,1)} %tok_ref.5, bf16[256,1024]{1,0:T(8,128)(2,1)} %up_ref.5, f32[256,1024]{1,0:T(8,128)} %get-tuple-element.44.before_ref, f32[16,256,256]{2,1,0:T(8,128)} %get-tuple-element.45.sum_ref, ...), custom_call_target="tpu_custom_call" | custom-call | flops 2147483648 | bytes 4194304 | tf_op jit(solution)/shard_map/far_products/pallas_call | solution.py:255
  (88 shorter events, 24.6 us)
Async XLA Ops:
  4.3 12.9 %collective-permute-start = (bf16[256,2048]{1,0:T(8,128)(2,1)}, bf16[256,2048]{1,0:T(8,128)(2,1)S(1)}, u32[]{:S(2)}, u32[]{:S(2)}) collective-permute-start(bf16[256,2048]{1,0:T(8,128)(2,1)} %get-tuple-element.26), channel_id=1, source_target_pairs={{0,1},{1,0},{2,3},{3,2},{4,5},{5,4},{6,7},{7,6},{8,9},{9,8},{10,11... | collective-permute-start | bytes 3145736 | tf_op jit(solution)/shard_map/ppermute | solution.py:280
  10.7 6.5 %collective-permute-start.1 = (bf16[256,512]{1,0:T(8,128)(2,1)}, bf16[256,512]{1,0:T(8,128)(2,1)S(1)}, u32[]{:S(2)}, u32[]{:S(2)}) collective-permute-start(bf16[256,512]{1,0:T(8,128)(2,1)} %make_q.1.q_ref), channel_id=1, source_target_pairs={{0,1},{1,0},{2,3},{3,2},{4,5},{5,4},{6,7},{7,6},{8,9},{9,8},{10,11... | collective-permute-start | bytes 786440 | tf_op jit(solution)/shard_map/ppermute | solution.py:284
  10.7 17.2 %all-to-all-start.2 = ((bf16[8,128,128]{2,1,0:T(8,128)(2,1)}), bf16[8,128,128]{2,1,0:T(8,128)(2,1)S(1)}, u32[]{:S(2)}, u32[]{:S(2)}) async-start(bf16[8,128,128]{2,1,0:T(8,128)(2,1)} %get-tuple-element.27), calls=%async_computation.2 | async-start | bytes 524288 | tf_op jit(solution)/shard_map/all_to_all | solution.py:281
  28.6 41.6 %all-to-all-start = ((bf16[16,128,512]{2,1,0:T(8,128)(2,1)}), bf16[16,128,512]{2,1,0:T(8,128)(2,1)S(1)}, u32[]{:S(2)}, u32[]{:S(2)}) async-start(bf16[16,128,512]{2,1,0:T(8,128)(2,1)} %bitcast.9), calls=%async_computation | async-start | bytes 4194304 | tf_op jit(solution)/shard_map/all_to_all | solution.py:290
  37.0 14.3 %collective-permute-start.2 = (bf16[2,128,128]{2,1,0:T(8,128)(2,1)}, bf16[2,128,128]{2,1,0:T(8,128)(2,1)S(1)}, u32[]{:S(2)}, u32[]{:S(2)}) collective-permute-start(bf16[2,128,128]{2,1,0:T(8,128)(2,1)} %get-tuple-element.28.refs_0_), channel_id=1, source_target_pairs={{0,34},{34,0},{2,32},{32,2},{1,35},{35,1},{3,33},{33,3},{4,38},{38... | collective-permute-start | bytes 196616 | tf_op jit(solution)/shard_map/ppermute | solution.py:108
  39.6 22.1 %collective-permute-start.3 = (bf16[2,128,128]{2,1,0:T(8,128)(2,1)}, bf16[2,128,128]{2,1,0:T(8,128)(2,1)S(1)}, u32[]{:S(2)}, u32[]{:S(2)}) collective-permute-start(bf16[2,128,128]{2,1,0:T(8,128)(2,1)} %get-tuple-element.29.refs_1_), channel_id=1, source_target_pairs={{0,64},{64,0},{128,192},{192,128},{1,65},{65,1},{129,193},{193,129... | collective-permute-start | bytes 196616 | tf_op jit(solution)/shard_map/ppermute | solution.py:112
  40.8 20.9 %collective-permute-start.4 = (bf16[2,128,128]{2,1,0:T(8,128)(2,1)}, bf16[2,128,128]{2,1,0:T(8,128)(2,1)S(1)}, u32[]{:S(2)}, u32[]{:S(2)}) collective-permute-start(bf16[2,128,128]{2,1,0:T(8,128)(2,1)} %get-tuple-element.30.refs_2_), channel_id=1, source_target_pairs={{0,32},{32,0},{1,33},{33,1},{2,34},{34,2},{3,35},{35,3},{4,36},{36... | collective-permute-start | bytes 196616 | tf_op jit(solution)/shard_map/ppermute | solution.py:110
  40.8 20.9 %collective-permute-start.5 = (bf16[2,128,128]{2,1,0:T(8,128)(2,1)}, bf16[2,128,128]{2,1,0:T(8,128)(2,1)S(1)}, u32[]{:S(2)}, u32[]{:S(2)}) collective-permute-start(bf16[2,128,128]{2,1,0:T(8,128)(2,1)} %get-tuple-element.31.refs_3_), channel_id=1, source_target_pairs={{0,192},{64,128},{128,64},{192,0},{1,193},{65,129},{129,65},{193,1... | collective-permute-start | bytes 196616 | tf_op jit(solution)/shard_map/ppermute | solution.py:112
  76.6 16.9 %collective-permute-start.10 = (bf16[8,128,128]{2,1,0:T(8,128)(2,1)}, bf16[8,128,128]{2,1,0:T(8,128)(2,1)S(1)}, u32[]{:S(2)}, u32[]{:S(2)}) collective-permute-start(bf16[8,128,128]{2,1,0:T(8,128)(2,1)} %get-tuple-element.36.refs_0_), channel_id=1, source_target_pairs={{0,32},{32,0},{1,33},{33,1},{2,34},{34,2},{3,35},{35,3},{4,36},{36... | collective-permute-start | bytes 786440 | tf_op jit(solution)/shard_map/ppermute | solution.py:110
  76.6 17.0 %collective-permute-start.11 = (bf16[8,128,128]{2,1,0:T(8,128)(2,1)}, bf16[8,128,128]{2,1,0:T(8,128)(2,1)S(1)}, u32[]{:S(2)}, u32[]{:S(2)}) collective-permute-start(bf16[8,128,128]{2,1,0:T(8,128)(2,1)} %get-tuple-element.37.refs_1_), channel_id=1, source_target_pairs={{0,192},{64,128},{128,64},{192,0},{1,193},{65,129},{129,65},{193,1... | collective-permute-start | bytes 786440 | tf_op jit(solution)/shard_map/ppermute | solution.py:112
  77.5 16.0 %collective-permute-start.12 = (bf16[8,128,128]{2,1,0:T(8,128)(2,1)}, bf16[8,128,128]{2,1,0:T(8,128)(2,1)S(1)}, u32[]{:S(2)}, u32[]{:S(2)}) collective-permute-start(bf16[8,128,128]{2,1,0:T(8,128)(2,1)} %get-tuple-element.38.refs_2_), channel_id=1, source_target_pairs={{0,34},{34,0},{2,32},{32,2},{1,35},{35,1},{3,33},{33,3},{4,38},{38... | collective-permute-start | bytes 786440 | tf_op jit(solution)/shard_map/ppermute | solution.py:108
  79.7 13.9 %collective-permute-start.13 = (bf16[8,128,128]{2,1,0:T(8,128)(2,1)}, bf16[8,128,128]{2,1,0:T(8,128)(2,1)S(1)}, u32[]{:S(2)}, u32[]{:S(2)}) collective-permute-start(bf16[8,128,128]{2,1,0:T(8,128)(2,1)} %get-tuple-element.39.refs_3_), channel_id=1, source_target_pairs={{0,64},{64,0},{128,192},{192,128},{1,65},{65,1},{129,193},{193,129... | collective-permute-start | bytes 786440 | tf_op jit(solution)/shard_map/ppermute | solution.py:112
  98.0 8.8 %collective-permute-start.14 = (bf16[16,128,128]{2,1,0:T(8,128)(2,1)}, bf16[16,128,128]{2,1,0:T(8,128)(2,1)}, u32[]{:S(2)}, u32[]{:S(2)}) collective-permute-start(bf16[16,128,128]{2,1,0:T(8,128)(2,1)} %get-tuple-element.40.refs_0_), channel_id=1, source_target_pairs={{0,1},{1,0},{2,3},{3,2},{4,5},{5,4},{6,7},{7,6},{8,9},{9,8},{10,11... | collective-permute-start | bytes 1572872 | tf_op jit(solution)/shard_map/ppermute | solution.py:301
  104.3 8.5 %collective-permute-start.16 = (bf16[16,128,128]{2,1,0:T(8,128)(2,1)}, bf16[16,128,128]{2,1,0:T(8,128)(2,1)}, u32[]{:S(2)}, u32[]{:S(2)}) collective-permute-start(bf16[16,128,128]{2,1,0:T(8,128)(2,1)} %get-tuple-element.42.refs_2_), channel_id=1, source_target_pairs={{0,1},{1,0},{2,3},{3,2},{4,5},{5,4},{6,7},{7,6},{8,9},{9,8},{10,11... | collective-permute-start | bytes 1572872 | tf_op jit(solution)/shard_map/ppermute | solution.py:301
  104.8 18.8 %collective-permute-start.18 = (bf16[16,128,128]{2,1,0:T(8,128)(2,1)}, bf16[16,128,128]{2,1,0:T(8,128)(2,1)}, u32[]{:S(2)}, u32[]{:S(2)}) collective-permute-start(bf16[16,128,128]{2,1,0:T(8,128)(2,1)} %get-tuple-element.40.refs_0_), channel_id=1, source_target_pairs={{0,192},{64,128},{128,64},{192,0},{1,193},{65,129},{129,65},{193,1... | collective-permute-start | bytes 1572872 | tf_op jit(solution)/shard_map/ppermute | solution.py:112
  106.1 19.6 %collective-permute-start.19 = (bf16[16,128,128]{2,1,0:T(8,128)(2,1)}, bf16[16,128,128]{2,1,0:T(8,128)(2,1)}, u32[]{:S(2)}, u32[]{:S(2)}) collective-permute-start(bf16[16,128,128]{2,1,0:T(8,128)(2,1)} %get-tuple-element.41.refs_1_), channel_id=1, source_target_pairs={{0,34},{34,0},{2,32},{32,2},{1,35},{35,1},{3,33},{33,3},{4,38},{38... | collective-permute-start | bytes 1572872 | tf_op jit(solution)/shard_map/ppermute | solution.py:108
  106.8 18.9 %collective-permute-start.20 = (bf16[16,128,128]{2,1,0:T(8,128)(2,1)}, bf16[16,128,128]{2,1,0:T(8,128)(2,1)}, u32[]{:S(2)}, u32[]{:S(2)}) collective-permute-start(bf16[16,128,128]{2,1,0:T(8,128)(2,1)} %get-tuple-element.42.refs_2_), channel_id=1, source_target_pairs={{0,64},{64,0},{128,192},{192,128},{1,65},{65,1},{129,193},{193,129... | collective-permute-start | bytes 1572872 | tf_op jit(solution)/shard_map/ppermute | solution.py:112
  108.0 18.2 %collective-permute-start.21 = (bf16[16,128,128]{2,1,0:T(8,128)(2,1)}, bf16[16,128,128]{2,1,0:T(8,128)(2,1)}, u32[]{:S(2)}, u32[]{:S(2)}) collective-permute-start(bf16[16,128,128]{2,1,0:T(8,128)(2,1)} %get-tuple-element.43.refs_3_), channel_id=1, source_target_pairs={{0,32},{32,0},{1,33},{33,1},{2,34},{34,2},{3,35},{35,3},{4,36},{36... | collective-permute-start | bytes 1572872 | tf_op jit(solution)/shard_map/ppermute | solution.py:110
  109.1 13.9 %all-to-all-start.3 = ((bf16[8,16,512]{2,1,0:T(8,128)(2,1)}), bf16[8,16,512]{2,1,0:T(8,128)(2,1)S(1)}, u32[]{:S(2)}, u32[]{:S(2)}) async-start(bf16[8,16,512]{2,1,0:T(8,128)(2,1)} %broadcast_in_dim.2), calls=%async_computation.3 | async-start | bytes 262144 | tf_op jit(solution)/shard_map/all_to_all | solution.py:299
  112.8 15.0 %collective-permute-start.17 = (bf16[16,128,128]{2,1,0:T(8,128)(2,1)}, bf16[16,128,128]{2,1,0:T(8,128)(2,1)}, u32[]{:S(2)}, u32[]{:S(2)}) collective-permute-start(bf16[16,128,128]{2,1,0:T(8,128)(2,1)} %get-tuple-element.43.refs_3_), channel_id=1, source_target_pairs={{0,1},{1,0},{2,3},{3,2},{4,5},{5,4},{6,7},{7,6},{8,9},{9,8},{10,11... | collective-permute-start | bytes 1572872 | tf_op jit(solution)/shard_map/ppermute | solution.py:301
  123.5 12.0 %collective-permute-start.22 = (bf16[16,128,128]{2,1,0:T(8,128)(2,1)}, bf16[16,128,128]{2,1,0:T(8,128)(2,1)}, u32[]{:S(2)}, u32[]{:S(2)}) collective-permute-start(bf16[16,128,128]{2,1,0:T(8,128)(2,1)} %collective-permute-done.18.refs_0_), channel_id=1, source_target_pairs={{0,1},{1,0},{2,3},{3,2},{4,5},{5,4},{6,7},{7,6},{8,9},{9,8},{10,11... | collective-permute-start | bytes 1572872 | tf_op jit(solution)/shard_map/ppermute | solution.py:303
  125.7 9.9 %collective-permute-start.23 = (bf16[16,128,128]{2,1,0:T(8,128)(2,1)}, bf16[16,128,128]{2,1,0:T(8,128)(2,1)}, u32[]{:S(2)}, u32[]{:S(2)}) collective-permute-start(bf16[16,128,128]{2,1,0:T(8,128)(2,1)} %collective-permute-done.19.refs_1_), channel_id=1, source_target_pairs={{0,1},{1,0},{2,3},{3,2},{4,5},{5,4},{6,7},{7,6},{8,9},{9,8},{10,11... | collective-permute-start | bytes 1572872 | tf_op jit(solution)/shard_map/ppermute | solution.py:303
  125.8 9.7 %collective-permute-start.24 = (bf16[16,128,128]{2,1,0:T(8,128)(2,1)}, bf16[16,128,128]{2,1,0:T(8,128)(2,1)}, u32[]{:S(2)}, u32[]{:S(2)}) collective-permute-start(bf16[16,128,128]{2,1,0:T(8,128)(2,1)} %collective-permute-done.20.refs_2_), channel_id=1, source_target_pairs={{0,1},{1,0},{2,3},{3,2},{4,5},{5,4},{6,7},{7,6},{8,9},{9,8},{10,11... | collective-permute-start | bytes 1572872 | tf_op jit(solution)/shard_map/ppermute | solution.py:303
  126.2 9.4 %collective-permute-start.25 = (bf16[16,128,128]{2,1,0:T(8,128)(2,1)}, bf16[16,128,128]{2,1,0:T(8,128)(2,1)}, u32[]{:S(2)}, u32[]{:S(2)}) collective-permute-start(bf16[16,128,128]{2,1,0:T(8,128)(2,1)} %collective-permute-done.21.refs_3_), channel_id=1, source_target_pairs={{0,1},{1,0},{2,3},{3,2},{4,5},{5,4},{6,7},{7,6},{8,9},{9,8},{10,11... | collective-permute-start | bytes 1572872 | tf_op jit(solution)/shard_map/ppermute | solution.py:303
  (24 other events, 175.7 us)

commit v3 on v1

--- a/solution.py
+++ b/solution.py
@@ -9,11 +9,14 @@
 from jax.sharding import Mesh
 from jax.sharding import PartitionSpec as P
 
+
 ISLAND = ("y", "xl")
 FSDP = ("z", "xh", "c")
 PLANE = ("y", "xl", "xh")
 F32, BF16 = jnp.float32, jnp.bfloat16
 LANES = 128
+VMEM = pl.BlockSpec(memory_space=pltpu.VMEM)
+SMEM = pl.BlockSpec(memory_space=pltpu.SMEM)
 
 
 def two_parts(x):
@@ -58,6 +61,7 @@
         out_shape=jax.ShapeDtypeStruct((upstream.shape[0], projection.shape[1]), BF16),
         in_specs=[vm, vm],
         out_specs=vm,
+        cost_estimate=pl.CostEstimate(flops=8 * upstream.size * projection.shape[1], bytes_accessed=4 * projection.size + 4 * upstream.size, transcendentals=0),
         name="make_q",
     )(upstream, projection)
 
@@ -76,7 +80,6 @@
 
 
 def make_sketch(c, tokens, got, q, got_q, pieces, n_xh, n_z):
-    t, d = tokens.shape
     proj = q.shape[1]
     part = LANES // pieces
     vm = pl.BlockSpec(memory_space=pltpu.VMEM)
@@ -86,12 +89,66 @@
         out_shape=jax.ShapeDtypeStruct((pieces, n_xh, n_z, part, proj), BF16),
         in_specs=[pl.BlockSpec(memory_space=pltpu.SMEM), vm, vm, vm, vm],
         out_specs=pl.BlockSpec((pieces, n_xh, 1, part, proj), lambda z: (0, 0, z, 0, 0)),
+        cost_estimate=pl.CostEstimate(flops=8 * tokens.size * proj, bytes_accessed=16 * tokens.size, transcendentals=0),
         name="make_sketch",
     )(c, tokens, got, q, got_q)
 
 
-def local(tokens, upstream, params, momentum, projection):
-    rows, feat = params.shape
+def share_kernel(at_ref, tok_ref, up_ref, w_ref, acc_ref, grads_ref, *, scale, packed):
+    n = w_ref.shape[0] // LANES
+    acc = jnp.zeros(acc_ref.shape, F32)
+    step = 4
+    for k in range(0, n, step):
+        if packed:
+            toks = tok_ref[:, k * LANES : (k + step) * LANES]
+        else:
+            at = [pl.multiple_of((2 * j + at_ref[0]) * LANES, LANES) for j in range(k, k + step)]
+            toks = jnp.concatenate([tok_ref[:, pl.ds(a, LANES)] for a in at], axis=1)
+        w = w_ref[k * LANES : (k + step) * LANES]
+        acc += jnp.dot(toks, w, preferred_element_type=F32)
+        g = lax.dot_general(up_ref[...], w, (((1,), (1,)), ((), ())), preferred_element_type=F32)
+        grads_ref[:, k * LANES : (k + step) * LANES] = (g * scale).astype(BF16)
+    acc_ref[...] = acc
+
+
+def share(at, tokens, upstream, weight, scale, packed):
+    t, kv = upstream.shape
+    rows = weight.shape[0]
+    return pl.pallas_call(
+        functools.partial(share_kernel, scale=scale, packed=packed),
+        out_shape=(jax.ShapeDtypeStruct((t, kv), F32), jax.ShapeDtypeStruct((t, rows), BF16)),
+        in_specs=[SMEM, VMEM, VMEM, VMEM],
+        out_specs=(VMEM, VMEM),
+        cost_estimate=pl.CostEstimate(
+            flops=4 * t * rows * kv, bytes_accessed=2 * rows * kv + 4 * t * rows, transcendentals=0
+        ),
+        name="their_share" if packed else "my_share",
+    )(at, tokens, upstream, weight)
+
+
+def meet_kernel(at_ref, acc_ref, got_acc_ref, grads_ref, got_ref, values_ref, out_ref, *, scale):
+    values_ref[...] = ((acc_ref[...] + got_acc_ref[...]) * scale).astype(BF16)
+    for k in range(grads_ref.shape[1] // LANES):
+        here = slice(k * LANES, (k + 1) * LANES)
+        mine = pl.ds(pl.multiple_of((2 * k + at_ref[0]) * LANES, LANES), LANES)
+        theirs = pl.ds(pl.multiple_of((2 * k + 1 - at_ref[0]) * LANES, LANES), LANES)
+        out_ref[:, mine] = grads_ref[:, here]
+        out_ref[:, theirs] = got_ref[:, here]
+
+
+def meet(at, acc, got_acc, grads, got, scale):
+    t, kv = acc.shape
+    return pl.pallas_call(
+        functools.partial(meet_kernel, scale=scale),
+        out_shape=(jax.ShapeDtypeStruct((t, kv), BF16), jax.ShapeDtypeStruct((t, 2 * grads.shape[1]), BF16)),
+        in_specs=[SMEM] + [VMEM] * 4,
+        out_specs=(VMEM, VMEM),
+        name="meet",
+    )(at, acc, got_acc, grads, got)
+
+
+def step(tokens, upstream, params, momentum, projection):
+    rows, _ = params.shape
     n_z, n_xh, n_c = (lax.axis_size(a) for a in FSDP)
     n_isl = lax.axis_size("y") * lax.axis_size("xl")
     fsdp_count = n_z * n_xh * n_c
@@ -105,7 +162,8 @@
 
     other, half = pick(c, tokens, params)
     got = swap(other)
-    weight = lax.all_gather(half, FSDP, axis=0, tiled=True)
+    own = lax.all_gather(half, FSDP[:2], axis=0, tiled=True)
+    got_up = swap(upstream)
 
     q = make_q(upstream, projection)
     got_q = swap(q)
@@ -126,10 +184,10 @@
     new_momentum = 0.9 * momentum + outer
     new_params = params - 0.7 * (outer + 0.9 * new_momentum)
 
-    forward_sum = jnp.dot(tokens, weight, preferred_element_type=F32)
-    values = (forward_sum * inv_width).astype(BF16)
-    product = lax.dot_general(upstream, weight, dims, preferred_element_type=F32)
-    token_grads = (product * inv_width).astype(BF16)
+    their_acc, their_grads = share(c, got, got_up, own, inv_width, True)
+    got_acc, got_grads = swap(their_acc), swap(their_grads)
+    acc, grads = share(c, tokens, upstream, own, inv_width, False)
+    values, token_grads = meet(c, acc, got_acc, grads, got_grads, inv_width)
     return (values, token_grads, new_params, new_momentum)
 
 
@@ -138,4 +196,4 @@
     both = ISLAND + FSDP
     in_specs = (P(both, None), P(both, None), P(FSDP, None), P(FSDP, None), P())
     out_specs = (P(both, None), P(both, None), P(FSDP, None), P(FSDP, None))
-    return jax.shard_map(local, mesh=fine, in_specs=in_specs, out_specs=out_specs, check_vma=False)
+    return jax.shard_map(step, mesh=fine, in_specs=in_specs, out_specs=out_specs, check_vma=False)

time: 142 us -> 151 us (1.063)
  blocking collectives: 58.9 us -> 9.36 us
  waiting for transfers between devices: 30.3 us -> 71.4 us
  starting transfers between devices: 3.34 us -> 21.6 us
  Pallas kernels: 12.8 us -> 29.7 us
  matrix products: 14.1 us -> 2.01 us
  local copies, waits for them, and re-layouts: 5.64 us -> 1.7 us
    all_to_all x3 -> x1, blocking collectives: 58.9 us -> 9.36 us  [step(): total = lax.all_to_all(total, ISLAND, 0, 0, tiled=True).reshape(rows, proj)]
    all_to_all x0 -> x2, waiting for transfers between devices: none -> 26.4 us  [the longest x1 26.4 us: step(): pair = lax.all_to_all(pair, PLANE, 0, 0, tiled=True)]
    pallas_call x0 -> x3, Pallas kernels: none -> 16.9 us  [the longest x2 12.6 us: share(): pl.pallas_call(functools.partial(share_kernel, scale=scale, packed=packed...]
    all_gather x1, waiting for transfers between devices: 28.5 us -> 43.3 us  [step(): own = lax.all_gather(half, FSDP[:2], axis=0, tiled=True)]
    all_to_all x0 -> x2, starting transfers between devices: none -> 13.4 us  [the longest x1 8.18 us: step(): lax.all_to_all(plane.reshape(n_z, part, proj), 'z', 0, 0, tiled=True)]
    dot_general x4 -> x2, matrix products: 14.1 us -> 2.01 us  [the longest x1 1.53 us: step(): lax.dot_general(total, rest, dims, preferred_element_type=F32)]
    ppermute x2 -> x5, starting transfers between devices: 3.3 us -> 8.21 us  [the longest x2 4.36 us: step(): got_acc, got_grads = (swap(their_acc), swap(their_grads))]
    unnamed x14, local copies, waits for them, and re-layouts: 5.63 us -> 1.69 us
  transfers between devices with their start and end apart: 3 -> 8, of which waited for: 2 -> 3; matrix products, arithmetic and copies ran while one was open for 3% -> 2% of each run, Pallas kernels for 7% -> 15%
where the time goes in v3:
time: 151 us
  waiting for transfers between devices  71.4 us (47%)
  Pallas kernels  29.7 us (20%)
  starting transfers between devices  21.6 us (14%)
  between operations  14.1 us (9%)
  blocking collectives  9.36 us (6%)
  matrix products  2.01 us (1%)
  local copies, waits for them, and re-layouts  1.7 us (1%)
    all_gather x1, waiting for transfers between devices, step(): own = lax.all_gather(half, FSDP[:2], axis=0, tiled=True)  43.3 us
    all_to_all x1, waiting for transfers between devices, step(): pair = lax.all_to_all(pair, PLANE, 0, 0, tiled=True)  26.4 us
    pallas_call x2, Pallas kernels, share(): pl.pallas_call(functools.partial(share_kernel, scale=scale, packed=packed...  12.6 us
    all_to_all x1, blocking collectives, step(): total = lax.all_to_all(total, ISLAND, 0, 0, tiled=True).reshape(rows, proj)  9.36 us
    all_to_all x1, starting transfers between devices, step(): lax.all_to_all(plane.reshape(n_z, part, proj), 'z', 0, 0, tiled=True)  8.18 us
    pallas_call x1, Pallas kernels, make_sketch(): pl.pallas_call(sketch_kernel, grid=(n_z,), out_shape=jax.ShapeDtypeStruct...  6.52 us
    all_to_all x1, starting transfers between devices, step(): pair = lax.all_to_all(pair, PLANE, 0, 0, tiled=True)  5.18 us
    ppermute x2, starting transfers between devices, step(): got_acc, got_grads = (swap(their_acc), swap(their_grads))  4.36 us
  transfers between devices with their start and end apart: 8, of which 3 were waited for; matrix products, arithmetic and copies ran while one was open for 2% of the time, Pallas kernels for 15%

profile of v3, /device:TPU:1, one launch (start us, length us, event | category | flops | bytes accessed | tf_op | source)
XLA Modules:
  0.0 150.9 jit_solution(9019976106803828275)
XLA Ops:
  7.2 0.0 all-gather.2.cloned.1.call-start
  7.2 3.0 %pick.1 = (bf16[256,2048]{1,0:T(8,128)(2,1)}, bf16[128,1024]{1,0:T(8,128)(2,1)}) custom-call(s32[1]{0:T(128)} %bitcast.c_ref.at_ref, bf16[256,4096]{1,0:T(8,128)(2,1)} %tok_ref.3, f32[128,1024]{1,0:T(8,128)} %params_ref.1), custom_call_target="tpu_custom_call" | custom-call | tf_op jit(solution)/shard_map/pick/pallas_call | solution.py:38
  10.3 0.0 all-gather.2.cloned.1.call-update
  10.3 3.3 %collective-permute-start = (bf16[256,2048]{1,0:T(8,128)(2,1)}, bf16[256,2048]{1,0:T(8,128)(2,1)S(1)}, u32[]{:S(2)}, u32[]{:S(2)}) collective-permute-start(bf16[256,2048]{1,0:T(8,128)(2,1)} %get-tuple-element.14), channel_id=1, source_target_pairs={{0,1},{1,0},{2,3},{3,2},{4,5},{5,4},{6,7},{7,6},{8,9},{9,8},{10,11... | collective-permute-start | bytes 3145736 | tf_op jit(solution)/shard_map/ppermute | solution.py:164
  13.6 3.2 %make_q.1.q_ref = bf16[256,512]{1,0:T(8,128)(2,1)} custom-call(bf16[256,1024]{1,0:T(8,128)(2,1)} %up_ref.3, f32[1024,512]{1,0:T(8,128)} %proj_ref.1), custom_call_target="tpu_custom_call" | custom-call | flops 1073741824 | bytes 3145728 | tf_op jit(solution)/shard_map/make_q/pallas_call | solution.py:59
  16.8 0.0 collective-permute-start.4
  16.8 1.7 %collective-permute-done.4.got_q_ref = bf16[256,512]{1,0:T(8,128)(2,1)S(1)} collective-permute-done((bf16[256,512]{1,0:T(8,128)(2,1)}, bf16[256,512]{1,0:T(8,128)(2,1)S(1)}, u32[]{:S(2)}, u32[]{:S(2)}) %collective-permute-start.4) | collective-permute-done | bytes 262176 | tf_op jit(solution)/shard_map/ppermute | solution.py:169
  18.5 0.7 copy-done.6
  19.2 1.0 copy-done.3
  20.2 6.5 %make_sketch.1 = bf16[8,2,8,16,512]{4,3,2,1,0:T(8,128)(2,1)} custom-call(s32[1]{0:T(128)} %bitcast.c_ref.at_ref, bf16[256,4096]{1,0:T(8,128)(2,1)} %tok_ref.3, bf16[256,2048]{1,0:T(8,128)(2,1)} %copy-done.3, bf16[256,512]{1,0:T(8,128)(2,1)} %make_q.1.q_ref, bf16[256,512]{1,0:T(8,128)(2,1)} %copy-done.6), custom_call_target="tpu_custom_call" | custom-call | flops 4294967296 | bytes 16777216 | tf_op jit(solution)/shard_map/make_sketch/pallas_call | solution.py:86
  26.7 5.2 %all-to-all-start = ((bf16[16,128,512]{2,1,0:T(8,128)(2,1)}), bf16[16,128,512]{2,1,0:T(8,128)(2,1)S(1)}, u32[]{:S(2)}, u32[]{:S(2)}) async-start(bf16[16,128,512]{2,1,0:T(8,128)(2,1)} %bitcast.6), calls=%async_computation | async-start | bytes 4194304 | tf_op jit(solution)/shard_map/all_to_all | solution.py:172
  31.9 0.5 collective-permute-start.1
  32.5 26.4 %all-to-all-done = bf16[16,128,512]{2,1,0:T(8,128)(2,1)S(1)} async-done(((bf16[16,128,512]{2,1,0:T(8,128)(2,1)}), bf16[16,128,512]{2,1,0:T(8,128)(2,1)S(1)}, u32[]{:S(2)}, u32[]{:S(2)}) %all-to-all-start) | async-done | bytes 2097184 | tf_op jit(solution)/shard_map/all_to_all | solution.py:172
  58.8 1.0 reduce_sum.24
  59.8 8.2 %all-to-all-start.1 = ((bf16[8,16,512]{2,1,0:T(8,128)(2,1)}), bf16[8,16,512]{2,1,0:T(8,128)(2,1)S(1)}, u32[]{:S(2)}, u32[]{:S(2)}) async-start(bf16[8,16,512]{2,1,0:T(8,128)(2,1)} %bitcast.2), calls=%async_computation.1 | async-start | bytes 262144 | tf_op jit(solution)/shard_map/all_to_all | solution.py:174
  68.0 43.3 %all-gather.2.cloned.1.call-done.w_ref = bf16[2048,1024]{1,0:T(8,128)(2,1)} async-done(((bf16[128,1024]{1,0:T(8,128)(2,1)}), bf16[2048,1024]{1,0:T(8,128)(2,1)}) %all-gather.2.cloned.1.call-update) | async-done | bytes 4194320 | tf_op jit(solution)/shard_map/all_gather | solution.py:165
  111.3 6.1 %their_share.1 = (f32[256,1024]{1,0:T(8,128)}, bf16[256,2048]{1,0:T(8,128)(2,1)}) custom-call(s32[1]{0:T(128)} %bitcast.c_ref.at_ref, bf16[256,2048]{1,0:T(8,128)(2,1)} %copy-done.3, bf16[256,1024]{1,0:T(8,128)(2,1)} %copy-done.5, bf16[2048,1024]{1,0:T(8,128)(2,1)} %all-gather.2.cloned.1.call-done.w_ref), custom_call_target="tpu_custom_call" | custom-call | flops 2147483648 | bytes 6291456 | tf_op jit(solution)/shard_map/their_share/pallas_call | solution.py:117
  117.4 4.3 %collective-permute-start.2 = (f32[256,1024]{1,0:T(8,128)}, f32[256,1024]{1,0:T(8,128)}, u32[]{:S(2)}, u32[]{:S(2)}) collective-permute-start(f32[256,1024]{1,0:T(8,128)} %get-tuple-element.15), channel_id=1, source_target_pairs={{0,1},{1,0},{2,3},{3,2},{4,5},{5,4},{6,7},{7,6},{8,9},{9,8},{10,11... | collective-permute-start | bytes 3145736 | tf_op jit(solution)/shard_map/ppermute | solution.py:188
  121.7 0.1 collective-permute-start.3
  121.8 9.4 %all_to_all.15 = bf16[8,16,512]{2,1,0:T(8,128)(2,1)S(1)} all-to-all(bf16[8,16,512]{2,1,0:T(8,128)(2,1)S(1)} %broadcast_in_dim.2), channel_id=1, replica_groups=mesh['y'=4,'xl'=2,'z'=8,'xh'=2,'c'=2] {'y','xl'}, dimensions={0} | all-to-all | bytes 262144 | tf_op jit(solution)/shard_map/all_to_all | solution.py:177
  131.2 0.5 fusion.2
  131.7 1.5 %multiply_subtract_fusion = (f32[128,1024]{1,0:T(8,128)}, f32[128,1024]{1,0:T(8,128)}) fusion(f32[128,1024]{1,0:T(8,128)S(1)} %copy-done.1, f32[128,1024]{1,0:T(8,128)S(1)} %copy-done.2, f32[128,1024]{1,0:T(8,128)S(1)} %fusion.2, bf16[128,512]{1,0:T(8,128)(2,1)S(1)} %bitcast.8, f32[1024,512]{1,0:T(8,128)S(1)} %copy-done), kind=kOutput, calls=%fused_computation.3 | convolution fusion | flops 137363456 | bytes 4849664 | tf_op jit(solution)/shard_map/dot_general | solution.py:182
  133.2 6.5 %my_share.1 = (f32[256,1024]{1,0:T(8,128)}, bf16[256,2048]{1,0:T(8,128)(2,1)}) custom-call(s32[1]{0:T(128)} %bitcast.c_ref.at_ref, bf16[256,4096]{1,0:T(8,128)(2,1)} %tok_ref.3, bf16[256,1024]{1,0:T(8,128)(2,1)} %up_ref.3, bf16[2048,1024]{1,0:T(8,128)(2,1)} %all-gather.2.cloned.1.call-done.w_ref), custom_call_target="tpu_custom_call" | custom-call | flops 2147483648 | bytes 6291456 | tf_op jit(solution)/shard_map/my_share/pallas_call | solution.py:117
  139.8 4.3 %meet.1 = (bf16[256,1024]{1,0:T(8,128)(2,1)}, bf16[256,4096]{1,0:T(8,128)(2,1)}) custom-call(s32[1]{0:T(128)} %bitcast.c_ref.at_ref, f32[256,1024]{1,0:T(8,128)} %get-tuple-element.13.acc_ref, f32[256,1024]{1,0:T(8,128)} %collective-permute-done.2.got_acc_ref, bf16[256,2048]{1,0:T(8,128)(2,1)} %get-tuple-element.16.grads_ref, ...), custom_call_target="tpu_custom_call" | custom-call | tf_op jit(solution)/shard_map/meet/pallas_call | solution.py:141
  (19 shorter events, 0.1 us)
Async XLA Ops:
  7.2 104.1 %all-gather.2.cloned.1.call-start = ((), (), s32[]{:S(2)}) async-start(), calls=%async_computation.3 | async-start | bytes 4456448 | tf_op jit(solution)/shard_map/all_gather | solution.py:165
  10.3 8.2 %collective-permute-start = (bf16[256,2048]{1,0:T(8,128)(2,1)}, bf16[256,2048]{1,0:T(8,128)(2,1)S(1)}, u32[]{:S(2)}, u32[]{:S(2)}) collective-permute-start(bf16[256,2048]{1,0:T(8,128)(2,1)} %get-tuple-element.14), channel_id=1, source_target_pairs={{0,1},{1,0},{2,3},{3,2},{4,5},{5,4},{6,7},{7,6},{8,9},{9,8},{10,11... | collective-permute-start | bytes 3145736 | tf_op jit(solution)/shard_map/ppermute | solution.py:164
  16.8 1.7 %collective-permute-start.4 = (bf16[256,512]{1,0:T(8,128)(2,1)}, bf16[256,512]{1,0:T(8,128)(2,1)S(1)}, u32[]{:S(2)}, u32[]{:S(2)}) collective-permute-start(bf16[256,512]{1,0:T(8,128)(2,1)} %make_q.1.q_ref), channel_id=1, source_target_pairs={{0,1},{1,0},{2,3},{3,2},{4,5},{5,4},{6,7},{7,6},{8,9},{9,8},{10,11... | collective-permute-start | bytes 786440 | tf_op jit(solution)/shard_map/ppermute | solution.py:169
  18.5 0.7 copy-start.6
  19.2 1.0 copy-start.3
  26.7 5.2 %copy-start.4 = (bf16[256,1024]{1,0:T(8,128)(2,1)S(1)}, bf16[256,1024]{1,0:T(8,128)(2,1)}, u32[]{:S(2)}) copy-start(bf16[256,1024]{1,0:T(8,128)(2,1)} %up_ref.3) | copy-start | bytes 1572868
  26.7 32.1 %all-to-all-start = ((bf16[16,128,512]{2,1,0:T(8,128)(2,1)}), bf16[16,128,512]{2,1,0:T(8,128)(2,1)S(1)}, u32[]{:S(2)}, u32[]{:S(2)}) async-start(bf16[16,128,512]{2,1,0:T(8,128)(2,1)} %bitcast.6), calls=%async_computation | async-start | bytes 4194304 | tf_op jit(solution)/shard_map/all_to_all | solution.py:172
  31.9 36.1 %collective-permute-start.1 = (bf16[256,1024]{1,0:T(8,128)(2,1)S(1)}, bf16[256,1024]{1,0:T(8,128)(2,1)S(1)}, u32[]{:S(2)}, u32[]{:S(2)}) collective-permute-start(bf16[256,1024]{1,0:T(8,128)(2,1)S(1)} %copy-done.4), channel_id=1, source_target_pairs={{0,1},{1,0},{2,3},{3,2},{4,5},{5,4},{6,7},{7,6},{8,9},{9,8},{10,11... | collective-permute-start | bytes 1572872 | tf_op jit(solution)/shard_map/ppermute | solution.py:166
  59.8 62.0 %all-to-all-start.1 = ((bf16[8,16,512]{2,1,0:T(8,128)(2,1)}), bf16[8,16,512]{2,1,0:T(8,128)(2,1)S(1)}, u32[]{:S(2)}, u32[]{:S(2)}) async-start(bf16[8,16,512]{2,1,0:T(8,128)(2,1)} %bitcast.2), calls=%async_computation.1 | async-start | bytes 262144 | tf_op jit(solution)/shard_map/all_to_all | solution.py:174
  68.0 63.2 %copy-start = (f32[1024,512]{1,0:T(8,128)S(1)}, f32[1024,512]{1,0:T(8,128)}, u32[]{:S(2)}) copy-start(f32[1024,512]{1,0:T(8,128)} %proj_ref.1) | copy-start | bytes 6291460
  68.0 43.3 %copy-start.5 = (bf16[256,1024]{1,0:T(8,128)(2,1)}, bf16[256,1024]{1,0:T(8,128)(2,1)S(1)}, u32[]{:S(2)}) copy-start(bf16[256,1024]{1,0:T(8,128)(2,1)S(1)} %collective-permute-done.1.up_ref) | copy-start | bytes 1572868
  117.4 14.3 %copy-start.1 = (f32[128,1024]{1,0:T(8,128)S(1)}, f32[128,1024]{1,0:T(8,128)}, u32[]{:S(2)}) copy-start(f32[128,1024]{1,0:T(8,128)} %params_ref.1) | copy-start | bytes 1572868
  117.4 14.3 %copy-start.2 = (f32[128,1024]{1,0:T(8,128)S(1)}, f32[128,1024]{1,0:T(8,128)}, u32[]{:S(2)}) copy-start(f32[128,1024]{1,0:T(8,128)} %param.8) | copy-start | bytes 1572868
  117.4 22.3 %collective-permute-start.2 = (f32[256,1024]{1,0:T(8,128)}, f32[256,1024]{1,0:T(8,128)}, u32[]{:S(2)}, u32[]{:S(2)}) collective-permute-start(f32[256,1024]{1,0:T(8,128)} %get-tuple-element.15), channel_id=1, source_target_pairs={{0,1},{1,0},{2,3},{3,2},{4,5},{5,4},{6,7},{7,6},{8,9},{9,8},{10,11... | collective-permute-start | bytes 3145736 | tf_op jit(solution)/shard_map/ppermute | solution.py:188
  121.7 18.1 %collective-permute-start.3 = (bf16[256,2048]{1,0:T(8,128)(2,1)}, bf16[256,2048]{1,0:T(8,128)(2,1)}, u32[]{:S(2)}, u32[]{:S(2)}) collective-permute-start(bf16[256,2048]{1,0:T(8,128)(2,1)} %get-tuple-element.17), channel_id=1, source_target_pairs={{0,1},{1,0},{2,3},{3,2},{4,5},{5,4},{6,7},{7,6},{8,9},{9,8},{10,11... | collective-permute-start | bytes 3145736 | tf_op jit(solution)/shard_map/ppermute | solution.py:188
Sparse Core Ops, SparseCore 0:
  11.1 100.1 all-gather.1

commit v4 on v3

--- a/solution.py
+++ b/solution.py
@@ -12,11 +12,12 @@
 
 ISLAND = ("y", "xl")
 FSDP = ("z", "xh", "c")
-PLANE = ("y", "xl", "xh")
+PLANE = ("xh", "y", "xl")
 F32, BF16 = jnp.float32, jnp.bfloat16
 LANES = 128
 VMEM = pl.BlockSpec(memory_space=pltpu.VMEM)
 SMEM = pl.BlockSpec(memory_space=pltpu.SMEM)
+LEFT = pl.BlockSpec(memory_space=pl.ANY)
 
 
 def two_parts(x):
@@ -24,27 +25,30 @@
     return head, (x - head.astype(F32)).astype(BF16)
 
 
-def pick_kernel(c_ref, tokens_ref, params_ref, out_ref, half_ref):
-    skip = 1 - c_ref[0]
-    half_ref[...] = params_ref[...].astype(BF16)
+def pick_kernel(at_ref, tokens_ref, params_ref, out_ref, piece_ref):
+    skip = 1 - at_ref[0]
+    width = piece_ref.shape[2]
+    piece = params_ref[:, pl.ds(pl.multiple_of(at_ref[1] * width, width), width)].astype(BF16)
+    for z in range(piece_ref.shape[0]):
+        piece_ref[z] = piece
     for k in range(out_ref.shape[1] // LANES):
         at = pl.multiple_of((2 * k + skip) * LANES, LANES)
         out_ref[:, k * LANES : (k + 1) * LANES] = tokens_ref[:, pl.ds(at, LANES)]
 
 
-def pick(c, tokens, params):
+def pick(at, tokens, params, n_z, pieces):
     t, d = tokens.shape
-    vm = pl.BlockSpec(memory_space=pltpu.VMEM)
+    rows, kv = params.shape
     return pl.pallas_call(
         pick_kernel,
         out_shape=(
             jax.ShapeDtypeStruct((t, d // 2), BF16),
-            jax.ShapeDtypeStruct(params.shape, BF16),
+            jax.ShapeDtypeStruct((n_z, rows, kv // pieces), BF16),
         ),
-        in_specs=[pl.BlockSpec(memory_space=pltpu.SMEM), vm, vm],
-        out_specs=(vm, vm),
+        in_specs=[SMEM, VMEM, VMEM],
+        out_specs=(VMEM, VMEM),
         name="pick",
-    )(c, tokens, params)
+    )(at, tokens, params)
 
 
 def q_kernel(up_ref, proj_ref, q_ref):
@@ -66,36 +70,56 @@
     )(upstream, projection)
 
 
-def sketch_kernel(c_ref, tok_ref, got_ref, q_ref, got_q_ref, out_ref):
-    pieces, n_xh, _, part, proj = out_ref.shape
-    z = pl.program_id(0)
+def sketch_kernel(at_ref, tok_ref, got_ref, q_ref, got_q_ref, after_ref, *out_refs):
+    n_z = len(out_refs)
+    n_xh = out_refs[0].shape[0]
     dims = (((0,), (0,)), ((), ()))
-    for h in range(n_xh):
-        k = z * n_xh + h
-        mine = tok_ref[:, pl.ds(pl.multiple_of((2 * k + c_ref[0]) * LANES, LANES), LANES)]
-        theirs = got_ref[:, pl.ds(pl.multiple_of(k * LANES, LANES), LANES)]
-        s = lax.dot_general(mine, q_ref[...], dims, preferred_element_type=F32)
-        s += lax.dot_general(theirs, got_q_ref[...], dims, preferred_element_type=F32)
-        out_ref[:, h, 0] = s.astype(BF16).reshape(pieces, part, proj)
-
-
-def make_sketch(c, tokens, got, q, got_q, pieces, n_xh, n_z):
+    for r, out_ref in enumerate(out_refs):
+        z = lax.rem(at_ref[2] + r, n_z)
+        for h in range(n_xh):
+            k = z * n_xh + h
+            mine = tok_ref[:, pl.ds(pl.multiple_of((2 * k + at_ref[0]) * LANES, LANES), LANES)]
+            theirs = got_ref[:, pl.ds(pl.multiple_of(k * LANES, LANES), LANES)]
+            s = lax.dot_general(mine, q_ref[...], dims, preferred_element_type=F32)
+            s += lax.dot_general(theirs, got_q_ref[...], dims, preferred_element_type=F32)
+            out_ref[h] = s.astype(BF16)
+
+
+def make_sketch(at, tokens, got, q, got_q, n_z, n_xh, after):
     proj = q.shape[1]
-    part = LANES // pieces
-    vm = pl.BlockSpec(memory_space=pltpu.VMEM)
     return pl.pallas_call(
         sketch_kernel,
-        grid=(n_z,),
-        out_shape=jax.ShapeDtypeStruct((pieces, n_xh, n_z, part, proj), BF16),
-        in_specs=[pl.BlockSpec(memory_space=pltpu.SMEM), vm, vm, vm, vm],
-        out_specs=pl.BlockSpec((pieces, n_xh, 1, part, proj), lambda z: (0, 0, z, 0, 0)),
-        cost_estimate=pl.CostEstimate(flops=8 * tokens.size * proj, bytes_accessed=16 * tokens.size, transcendentals=0),
+        out_shape=(jax.ShapeDtypeStruct((n_xh, LANES, proj), BF16),) * n_z,
+        in_specs=[SMEM] + [VMEM] * 4 + [LEFT],
+        out_specs=(VMEM,) * n_z,
+        cost_estimate=pl.CostEstimate(
+            flops=8 * tokens.size * proj, bytes_accessed=16 * tokens.size, transcendentals=0
+        ),
         name="make_sketch",
-    )(c, tokens, got, q, got_q)
+    )(at, tokens, got, q, got_q, after)
+
+
+def spread_kernel(piece_ref, *refs):
+    out_ref = refs[-1]
+    out_ref[0] = piece_ref[...]
+
+
+def spread(piece, n, *after):
+    shape = piece.shape
+    return pl.pallas_call(
+        spread_kernel,
+        grid=(n,),
+        out_shape=jax.ShapeDtypeStruct((n,) + shape, BF16),
+        in_specs=[VMEM] + [LEFT] * len(after),
+        out_specs=pl.BlockSpec((1,) + shape, lambda i: (i, 0, 0, 0)),
+        name="spread",
+    )(piece, *after)
 
 
 def share_kernel(at_ref, tok_ref, up_ref, w_ref, acc_ref, grads_ref, *, scale, packed):
-    n = w_ref.shape[0] // LANES
+    pieces = acc_ref.shape[1] // w_ref.shape[3]
+    n_xh = w_ref.shape[0] // pieces
+    n = n_xh * w_ref.shape[1]
     acc = jnp.zeros(acc_ref.shape, F32)
     step = 4
     for k in range(0, n, step):
@@ -104,7 +128,11 @@
         else:
             at = [pl.multiple_of((2 * j + at_ref[0]) * LANES, LANES) for j in range(k, k + step)]
             toks = jnp.concatenate([tok_ref[:, pl.ds(a, LANES)] for a in at], axis=1)
-        w = w_ref[k * LANES : (k + step) * LANES]
+        rows = []
+        for j in range(k, k + step):
+            z, h = j // n_xh, j % n_xh
+            rows.append(jnp.concatenate([w_ref[h * pieces + p, z] for p in range(pieces)], axis=1))
+        w = jnp.concatenate(rows, axis=0)
         acc += jnp.dot(toks, w, preferred_element_type=F32)
         g = lax.dot_general(up_ref[...], w, (((1,), (1,)), ((), ())), preferred_element_type=F32)
         grads_ref[:, k * LANES : (k + step) * LANES] = (g * scale).astype(BF16)
@@ -113,7 +141,7 @@
 
 def share(at, tokens, upstream, weight, scale, packed):
     t, kv = upstream.shape
-    rows = weight.shape[0]
+    rows = weight.size // kv
     return pl.pallas_call(
         functools.partial(share_kernel, scale=scale, packed=packed),
         out_shape=(jax.ShapeDtypeStruct((t, kv), F32), jax.ShapeDtypeStruct((t, rows), BF16)),
@@ -157,21 +185,27 @@
     part = rows // n_isl
     inv_width = 1.0 / math.sqrt(width)
     scale_tok = 1.0 / math.sqrt(tokens.shape[0] * fsdp_count)
-    c = lax.axis_index("c").astype(jnp.int32).reshape(1)
+    at = jnp.stack([lax.axis_index("c"), lax.axis_index(ISLAND), lax.axis_index("z")]).astype(jnp.int32)
     swap = functools.partial(lax.ppermute, axis_name="c", perm=[(0, 1), (1, 0)])
 
-    other, half = pick(c, tokens, params)
+    other, piece = pick(at, tokens, params, n_z, n_isl)
     got = swap(other)
-    own = lax.all_gather(half, FSDP[:2], axis=0, tiled=True)
-    got_up = swap(upstream)
-
+    piece = lax.all_to_all(piece, "z", 0, 0, tiled=True)
     q = make_q(upstream, projection)
     got_q = swap(q)
-    pair = make_sketch(c, tokens, got, q, got_q, n_isl, n_xh, n_z)
-    pair = pair.reshape(n_isl * n_xh, n_z * part, proj)
-    pair = lax.all_to_all(pair, PLANE, 0, 0, tiled=True)
-    plane = jnp.sum(pair.astype(F32), axis=0).astype(BF16)
-    plane = lax.all_to_all(plane.reshape(n_z, part, proj), "z", 0, 0, tiled=True)
+    got_up = swap(upstream)
+
+    wide = spread(piece, n_xh * n_isl, got, got_q)
+    own = lax.all_to_all(wide, PLANE, 0, 0, tiled=True)
+
+    pair = make_sketch(at, tokens, got, q, got_q, n_z, n_xh, wide)
+    along = pair[0].astype(F32)
+    for k in sorted(range(1, n_z), key=lambda k: -min(k, n_z - k)):
+        shift = [(i, (i + k) % n_z) for i in range(n_z)]
+        came = lax.ppermute(pair[k], "z", shift)
+        along += came.astype(F32)
+    along = along.astype(BF16)
+    plane = lax.all_to_all(along.reshape(n_xh * n_isl, part, proj), PLANE, 0, 0, tiled=True)
     total = jnp.sum(plane.astype(F32), axis=0).astype(BF16)
     total = jnp.broadcast_to(total[None], (n_isl, part, proj))
     total = lax.all_to_all(total, ISLAND, 0, 0, tiled=True).reshape(rows, proj)
@@ -184,10 +218,10 @@
     new_momentum = 0.9 * momentum + outer
     new_params = params - 0.7 * (outer + 0.9 * new_momentum)
 
-    their_acc, their_grads = share(c, got, got_up, own, inv_width, True)
+    their_acc, their_grads = share(at, got, got_up, own, inv_width, True)
     got_acc, got_grads = swap(their_acc), swap(their_grads)
-    acc, grads = share(c, tokens, upstream, own, inv_width, False)
-    values, token_grads = meet(c, acc, got_acc, grads, got_grads, inv_width)
+    acc, grads = share(at, tokens, upstream, own, inv_width, False)
+    values, token_grads = meet(at, acc, got_acc, grads, got_grads, inv_width)
     return (values, token_grads, new_params, new_momentum)
 
 

time: 151 us -> 146 us (0.967)
  waiting for transfers between devices: 71.4 us -> 50.4 us
  starting transfers between devices: 21.6 us -> 42.3 us
  between operations: 14.1 us -> 0.74 us
  Pallas kernels: 29.7 us -> 34.4 us
  other arithmetic: 0.99 us -> 2.58 us
    all_gather x1 -> x0, waiting for transfers between devices: 43.3 us -> none  [step(): own = lax.all_gather(half, FSDP[:2], axis=0, tiled=True)]
    ppermute x0 -> x7, waiting for transfers between devices: none -> 29.5 us  [step(): came = lax.ppermute(pair[k], 'z', shift)]
    ppermute x0 -> x7, starting transfers between devices: none -> 10.7 us  [step(): came = lax.ppermute(pair[k], 'z', shift)]
    all_to_all x2 -> x3, waiting for transfers between devices: 26.4 us -> 19.5 us  [the longest x1 12.1 us: step(): own = lax.all_to_all(wide, PLANE, 0, 0, tiled=True)]
    ppermute x1, starting transfers between devices: 0.54 us -> 6.7 us  [step(): got_up = swap(upstream)]
    all_to_all x2 -> x3, starting transfers between devices: 13.4 us -> 19.4 us  [the longest x1 6.8 us: step(): own = lax.all_to_all(wide, PLANE, 0, 0, tiled=True)]
    pallas_call x1 -> x2, Pallas kernels: 6.52 us -> 11.1 us  [the longest x1 6.86 us: spread(): pl.pallas_call(spread_kernel, grid=(n,), out_shape=jax.ShapeDtypeStruct((...]
    ppermute x2, starting transfers between devices: 4.36 us -> 1.99 us  [step(): got_acc, got_grads = (swap(their_acc), swap(their_grads))]
  transfers between devices with their start and end apart: 8 -> 15, of which waited for: 3 -> 7; matrix products, arithmetic and copies ran while one was open for 2% -> 3% of each run, Pallas kernels for 15% -> 14%
where the time goes in v4:
time: 146 us
  waiting for transfers between devices  50.4 us (35%)
  starting transfers between devices  42.3 us (29%)
  Pallas kernels  34.4 us (24%)
  blocking collectives  10.7 us (7%)
  other arithmetic  2.58 us (2%)
  local copies, waits for them, and re-layouts  2.48 us (2%)
  matrix products  2.02 us (1%)
    ppermute x7, waiting for transfers between devices, step(): came = lax.ppermute(pair[k], 'z', shift)  29.5 us
    pallas_call x2, Pallas kernels, share(): pl.pallas_call(functools.partial(share_kernel, scale=scale, packed=packed...  12.8 us
    all_to_all x1, waiting for transfers between devices, step(): own = lax.all_to_all(wide, PLANE, 0, 0, tiled=True)  12.1 us
    ppermute x7, starting transfers between devices, step(): came = lax.ppermute(pair[k], 'z', shift)  10.7 us
    all_to_all x1, blocking collectives, step(): total = lax.all_to_all(total, ISLAND, 0, 0, tiled=True).reshape(rows, proj)  10.7 us
    all_to_all x1, waiting for transfers between devices, step(): piece = lax.all_to_all(piece, 'z', 0, 0, tiled=True)  7.41 us
    pallas_call x1, Pallas kernels, spread(): pl.pallas_call(spread_kernel, grid=(n,), out_shape=jax.ShapeDtypeStruct((...  6.86 us
    all_to_all x1, starting transfers between devices, step(): own = lax.all_to_all(wide, PLANE, 0, 0, tiled=True)  6.8 us
  transfers between devices with their start and end apart: 15, of which 7 were waited for; matrix products, arithmetic and copies ran while one was open for 3% of the time, Pallas kernels for 14%

profile of v4, /device:TPU:1, one launch (start us, length us, event | category | flops | bytes accessed | tf_op | source)
XLA Modules:
  0.0 145.6 jit_solution(7330727168135678409)
XLA Ops:
  1.2 3.0 %pick.1 = (bf16[256,2048]{1,0:T(8,128)(2,1)}, bf16[8,128,128]{2,1,0:T(8,128)(2,1)}) custom-call(s32[3]{0:T(128)} %pad_add_fusion.at_ref, bf16[256,4096]{1,0:T(8,128)(2,1)} %tok_ref.3, f32[128,1024]{1,0:T(8,128)} %params_ref.1), custom_call_target="tpu_custom_call" | custom-call | tf_op jit(solution)/shard_map/pick/pallas_call | solution.py:42
  4.3 3.2 %collective-permute-start = (bf16[256,2048]{1,0:T(8,128)(2,1)}, bf16[256,2048]{1,0:T(8,128)(2,1)S(1)}, u32[]{:S(2)}, u32[]{:S(2)}) collective-permute-start(bf16[256,2048]{1,0:T(8,128)(2,1)} %get-tuple-element.21), channel_id=1, source_target_pairs={{0,1},{1,0},{2,3},{3,2},{4,5},{5,4},{6,7},{7,6},{8,9},{9,8},{10,11... | collective-permute-start | bytes 3145736 | tf_op jit(solution)/shard_map/ppermute | solution.py:192
  7.5 6.5 %all-to-all-start = ((bf16[8,128,128]{2,1,0:T(8,128)(2,1)}), bf16[8,128,128]{2,1,0:T(8,128)(2,1)S(1)}, u32[]{:S(2)}, u32[]{:S(2)}) async-start(bf16[8,128,128]{2,1,0:T(8,128)(2,1)} %get-tuple-element.20), calls=%async_computation | async-start | bytes 524288 | tf_op jit(solution)/shard_map/all_to_all | solution.py:193
  14.0 3.2 %make_q.1.q_ref = bf16[256,512]{1,0:T(8,128)(2,1)} custom-call(bf16[256,1024]{1,0:T(8,128)(2,1)} %up_ref.3, f32[1024,512]{1,0:T(8,128)} %proj_ref.1), custom_call_target="tpu_custom_call" | custom-call | flops 1073741824 | bytes 3145728 | tf_op jit(solution)/shard_map/make_q/pallas_call | solution.py:63
  18.9 7.4 %all-to-all-done.piece_ref = bf16[8,128,128]{2,1,0:T(8,128)(2,1)S(1)} async-done(((bf16[8,128,128]{2,1,0:T(8,128)(2,1)}), bf16[8,128,128]{2,1,0:T(8,128)(2,1)S(1)}, u32[]{:S(2)}, u32[]{:S(2)}) %all-to-all-start) | async-done | bytes 262176 | tf_op jit(solution)/shard_map/all_to_all | solution.py:193
  28.0 6.9 %spread.1.after_ref = bf16[16,8,128,128]{3,2,1,0:T(8,128)(2,1)} custom-call(bf16[8,128,128]{2,1,0:T(8,128)(2,1)} %copy-done.2, bf16[256,2048]{1,0:T(8,128)(2,1)} %copy-done.3, bf16[256,512]{1,0:T(8,128)(2,1)} %copy-done.5), custom_call_target="tpu_custom_call" | custom-call | tf_op jit(solution)/shard_map/spread/pallas_call | solution.py:109
  34.9 6.8 %all-to-all-start.1 = ((bf16[16,8,128,128]{3,2,1,0:T(8,128)(2,1)}), bf16[16,8,128,128]{3,2,1,0:T(8,128)(2,1)}, u32[]{:S(2)}, u32[]{:S(2)}) async-start(bf16[16,8,128,128]{3,2,1,0:T(8,128)(2,1)} %spread.1.after_ref), calls=%async_computation.1 | async-start | bytes 8388608 | tf_op jit(solution)/shard_map/all_to_all | solution.py:199
  41.7 4.3 %make_sketch.1 = (bf16[2,128,512]{2,1,0:T(8,128)(2,1)}, bf16[2,128,512]{2,1,0:T(8,128)(2,1)}, bf16[2,128,512]{2,1,0:T(8,128)(2,1)}, bf16[2,128,512]{2,1,0:T(8,12...) custom-call(s32[3]{0:T(128)} %pad_add_fusion.at_ref, ...), custom_call_target="tpu_custom_call" | custom-call | flops 4294967296 | bytes 16777216 | tf_op jit(solution)/shard_map/make_sketch/pallas_call | solution.py:90
  46.0 2.7 %collective-permute-start.11 = (bf16[2,128,512]{2,1,0:T(8,128)(2,1)}, bf16[2,128,512]{2,1,0:T(8,128)(2,1)S(1)}, u32[]{:S(2)}, u32[]{:S(2)}) collective-permute-start(bf16[2,128,512]{2,1,0:T(8,128)(2,1)} %get-tuple-element.35), channel_id=1, source_target_pairs={{0,28},{4,0},{8,4},{12,8},{16,12},{20,16},{24,20},{28,24},{1,29},{... | collective-permute-start | bytes 786440 | tf_op jit(solution)/shard_map/ppermute | solution.py:205
  48.6 3.0 %collective-permute-start.6 = (bf16[2,128,512]{2,1,0:T(8,128)(2,1)}, bf16[2,128,512]{2,1,0:T(8,128)(2,1)S(1)}, u32[]{:S(2)}, u32[]{:S(2)}) collective-permute-start(bf16[2,128,512]{2,1,0:T(8,128)(2,1)} %get-tuple-element.30), channel_id=1, source_target_pairs={{0,12},{4,16},{8,20},{12,24},{16,28},{20,0},{24,4},{28,8},{1,13},{... | collective-permute-start | bytes 786440 | tf_op jit(solution)/shard_map/ppermute | solution.py:205
  53.1 17.1 %collective-permute-done.10 = bf16[2,128,512]{2,1,0:T(8,128)(2,1)S(1)} collective-permute-done((bf16[2,128,512]{2,1,0:T(8,128)(2,1)}, bf16[2,128,512]{2,1,0:T(8,128)(2,1)S(1)}, u32[]{:S(2)}, u32[]{:S(2)}) %collective-permute-start.10) | collective-permute-done | bytes 262176 | tf_op jit(solution)/shard_map/ppermute | solution.py:205
  70.2 3.6 %collective-permute-start.9 = (bf16[2,128,512]{2,1,0:T(8,128)(2,1)}, bf16[2,128,512]{2,1,0:T(8,128)(2,1)S(1)}, u32[]{:S(2)}, u32[]{:S(2)}) collective-permute-start(bf16[2,128,512]{2,1,0:T(8,128)(2,1)} %get-tuple-element.33), channel_id=1, source_target_pairs={{0,24},{4,28},{8,0},{12,4},{16,8},{20,12},{24,16},{28,20},{1,25},{... | collective-permute-start | bytes 786440 | tf_op jit(solution)/shard_map/ppermute | solution.py:205
  73.8 6.7 %collective-permute-start.2 = (bf16[256,1024]{1,0:T(8,128)(2,1)S(1)}, bf16[256,1024]{1,0:T(8,128)(2,1)S(1)}, u32[]{:S(2)}, u32[]{:S(2)}) collective-permute-start(bf16[256,1024]{1,0:T(8,128)(2,1)S(1)} %copy-done.6), channel_id=1, source_target_pairs={{0,1},{1,0},{2,3},{3,2},{4,5},{5,4},{6,7},{7,6},{8,9},{9,8},{10,11... | collective-permute-start | bytes 1572872 | tf_op jit(solution)/shard_map/ppermute | solution.py:196
  80.5 2.2 %collective-permute-done.6 = bf16[2,128,512]{2,1,0:T(8,128)(2,1)S(1)} collective-permute-done((bf16[2,128,512]{2,1,0:T(8,128)(2,1)}, bf16[2,128,512]{2,1,0:T(8,128)(2,1)S(1)}, u32[]{:S(2)}, u32[]{:S(2)}) %collective-permute-start.6) | collective-permute-done | bytes 262176 | tf_op jit(solution)/shard_map/ppermute | solution.py:205
  82.7 2.6 %collective-permute-done.8 = bf16[2,128,512]{2,1,0:T(8,128)(2,1)S(1)} collective-permute-done((bf16[2,128,512]{2,1,0:T(8,128)(2,1)}, bf16[2,128,512]{2,1,0:T(8,128)(2,1)S(1)}, u32[]{:S(2)}, u32[]{:S(2)}) %collective-permute-start.8) | collective-permute-done | bytes 262176 | tf_op jit(solution)/shard_map/ppermute | solution.py:205
  85.3 7.6 %collective-permute-done.9 = bf16[2,128,512]{2,1,0:T(8,128)(2,1)S(1)} collective-permute-done((bf16[2,128,512]{2,1,0:T(8,128)(2,1)}, bf16[2,128,512]{2,1,0:T(8,128)(2,1)S(1)}, u32[]{:S(2)}, u32[]{:S(2)}) %collective-permute-start.9) | collective-permute-done | bytes 262176 | tf_op jit(solution)/shard_map/ppermute | solution.py:205
  92.9 1.9 %add_convert_fusion = bf16[2,128,512]{2,1,0:T(8,128)(2,1)} fusion(bf16[2,128,512]{2,1,0:T(8,128)(2,1)S(1)} %collective-permute-done.11, bf16[2,128,512]{2,1,0:T(8,128)(2,1)S(1)} %collective-permute-done.10, bf16[2,128,512]{2,1,0:T(8,128)(2,1)S(1)} %collective-permute-done.9, bf16[2,128,512]{2,1,0:T(8,128)(2,1)S(1)} %collective-permute-done.8, ...), kind=kLoop, calls=%fused_computation.8 | loop fusion | flops 2097152 | bytes 2359296 | tf_op jit(solution)/shard_map/convert_element_type | solution.py:207
  94.8 12.1 %all-to-all-done.1.w_ref = bf16[16,8,128,128]{3,2,1,0:T(8,128)(2,1)} async-done(((bf16[16,8,128,128]{3,2,1,0:T(8,128)(2,1)}), bf16[16,8,128,128]{3,2,1,0:T(8,128)(2,1)}, u32[]{:S(2)}, u32[]{:S(2)}) %all-to-all-start.1) | async-done | bytes 4194336 | tf_op jit(solution)/shard_map/all_to_all | solution.py:199
  106.9 6.1 %all-to-all-start.2 = ((bf16[16,16,512]{2,1,0:T(8,128)(2,1)}), bf16[16,16,512]{2,1,0:T(8,128)(2,1)S(1)}, u32[]{:S(2)}, u32[]{:S(2)}) async-start(bf16[16,16,512]{2,1,0:T(8,128)(2,1)} %bitcast.3), calls=%async_computation.2 | async-start | bytes 524288 | tf_op jit(solution)/shard_map/all_to_all | solution.py:208
  113.8 6.3 %their_share.1 = (f32[256,1024]{1,0:T(8,128)}, bf16[256,2048]{1,0:T(8,128)(2,1)}) custom-call(s32[3]{0:T(128)} %pad_add_fusion.at_ref, bf16[256,2048]{1,0:T(8,128)(2,1)} %copy-done.3, bf16[256,1024]{1,0:T(8,128)(2,1)} %copy-done.7, bf16[16,8,128,128]{3,2,1,0:T(8,128)(2,1)} %all-to-all-done.1.w_ref), custom_call_target="tpu_custom_call" | custom-call | flops 2147483648 | bytes 6291456 | tf_op jit(solution)/shard_map/their_share/pallas_call | solution.py:145
  120.1 1.9 %collective-permute-start.3 = (f32[256,1024]{1,0:T(8,128)}, f32[256,1024]{1,0:T(8,128)}, u32[]{:S(2)}, u32[]{:S(2)}) collective-permute-start(f32[256,1024]{1,0:T(8,128)} %get-tuple-element.23), channel_id=1, source_target_pairs={{0,1},{1,0},{2,3},{3,2},{4,5},{5,4},{6,7},{7,6},{8,9},{9,8},{10,11... | collective-permute-start | bytes 3145736 | tf_op jit(solution)/shard_map/ppermute | solution.py:222
  122.1 10.7 %all_to_all.20 = bf16[8,16,512]{2,1,0:T(8,128)(2,1)S(1)} all-to-all(bf16[8,16,512]{2,1,0:T(8,128)(2,1)S(1)} %broadcast_in_dim.2), channel_id=1, replica_groups=mesh['y'=4,'xl'=2,'z'=8,'xh'=2,'c'=2] {'y','xl'}, dimensions={0} | all-to-all | bytes 262144 | tf_op jit(solution)/shard_map/all_to_all | solution.py:211
  134.8 6.5 %my_share.1 = (f32[256,1024]{1,0:T(8,128)}, bf16[256,2048]{1,0:T(8,128)(2,1)}) custom-call(s32[3]{0:T(128)} %pad_add_fusion.at_ref, bf16[256,4096]{1,0:T(8,128)(2,1)} %tok_ref.3, bf16[256,1024]{1,0:T(8,128)(2,1)} %up_ref.3, bf16[16,8,128,128]{3,2,1,0:T(8,128)(2,1)} %all-to-all-done.1.w_ref), custom_call_target="tpu_custom_call" | custom-call | flops 2147483648 | bytes 6291456 | tf_op jit(solution)/shard_map/my_share/pallas_call | solution.py:145
  141.3 4.3 %meet.1 = (bf16[256,1024]{1,0:T(8,128)(2,1)}, bf16[256,4096]{1,0:T(8,128)(2,1)}) custom-call(s32[3]{0:T(128)} %pad_add_fusion.at_ref, f32[256,1024]{1,0:T(8,128)} %get-tuple-element.22.acc_ref, f32[256,1024]{1,0:T(8,128)} %collective-permute-done.3.got_acc_ref, bf16[256,2048]{1,0:T(8,128)(2,1)} %get-tuple-element.24.grads_ref, ...), custom_call_target="tpu_custom_call" | custom-call | tf_op jit(solution)/shard_map/meet/pallas_call | solution.py:169
  (36 shorter events, 8.5 us)
Async XLA Ops:
  4.3 22.1 %collective-permute-start = (bf16[256,2048]{1,0:T(8,128)(2,1)}, bf16[256,2048]{1,0:T(8,128)(2,1)S(1)}, u32[]{:S(2)}, u32[]{:S(2)}) collective-permute-start(bf16[256,2048]{1,0:T(8,128)(2,1)} %get-tuple-element.21), channel_id=1, source_target_pairs={{0,1},{1,0},{2,3},{3,2},{4,5},{5,4},{6,7},{7,6},{8,9},{9,8},{10,11... | collective-permute-start | bytes 3145736 | tf_op jit(solution)/shard_map/ppermute | solution.py:192
  7.5 18.8 %all-to-all-start = ((bf16[8,128,128]{2,1,0:T(8,128)(2,1)}), bf16[8,128,128]{2,1,0:T(8,128)(2,1)S(1)}, u32[]{:S(2)}, u32[]{:S(2)}) async-start(bf16[8,128,128]{2,1,0:T(8,128)(2,1)} %get-tuple-element.20), calls=%async_computation | async-start | bytes 524288 | tf_op jit(solution)/shard_map/all_to_all | solution.py:193
  17.2 1.7 %collective-permute-start.1 = (bf16[256,512]{1,0:T(8,128)(2,1)}, bf16[256,512]{1,0:T(8,128)(2,1)S(1)}, u32[]{:S(2)}, u32[]{:S(2)}) collective-permute-start(bf16[256,512]{1,0:T(8,128)(2,1)} %make_q.1.q_ref), channel_id=1, source_target_pairs={{0,1},{1,0},{2,3},{3,2},{4,5},{5,4},{6,7},{7,6},{8,9},{9,8},{10,11... | collective-permute-start | bytes 786440 | tf_op jit(solution)/shard_map/ppermute | solution.py:195
  18.9 7.4 %copy-start.5 = (bf16[256,512]{1,0:T(8,128)(2,1)}, bf16[256,512]{1,0:T(8,128)(2,1)S(1)}, u32[]{:S(2)}) copy-start(bf16[256,512]{1,0:T(8,128)(2,1)S(1)} %collective-permute-done.1.refs_1_.got_q_ref) | copy-start | bytes 786436
  26.3 0.7 copy-start.2
  27.0 1.0 copy-start.3
  34.9 72.0 %all-to-all-start.1 = ((bf16[16,8,128,128]{3,2,1,0:T(8,128)(2,1)}), bf16[16,8,128,128]{3,2,1,0:T(8,128)(2,1)}, u32[]{:S(2)}, u32[]{:S(2)}) async-start(bf16[16,8,128,128]{3,2,1,0:T(8,128)(2,1)} %spread.1.after_ref), calls=%async_computation.1 | async-start | bytes 8388608 | tf_op jit(solution)/shard_map/all_to_all | solution.py:199
  41.7 32.1 %copy-start.6 = (bf16[256,1024]{1,0:T(8,128)(2,1)S(1)}, bf16[256,1024]{1,0:T(8,128)(2,1)}, u32[]{:S(2)}) copy-start(bf16[256,1024]{1,0:T(8,128)(2,1)} %up_ref.3) | copy-start | bytes 1572868
  46.0 24.2 %collective-permute-start.10 = (bf16[2,128,512]{2,1,0:T(8,128)(2,1)}, bf16[2,128,512]{2,1,0:T(8,128)(2,1)S(1)}, u32[]{:S(2)}, u32[]{:S(2)}) collective-permute-start(bf16[2,128,512]{2,1,0:T(8,128)(2,1)} %get-tuple-element.34), channel_id=1, source_target_pairs={{0,4},{4,8},{8,12},{12,16},{16,20},{20,24},{24,28},{28,0},{1,5},{5... | collective-permute-start | bytes 786440 | tf_op jit(solution)/shard_map/ppermute | solution.py:205
  46.0 24.2 %collective-permute-start.11 = (bf16[2,128,512]{2,1,0:T(8,128)(2,1)}, bf16[2,128,512]{2,1,0:T(8,128)(2,1)S(1)}, u32[]{:S(2)}, u32[]{:S(2)}) collective-permute-start(bf16[2,128,512]{2,1,0:T(8,128)(2,1)} %get-tuple-element.35), channel_id=1, source_target_pairs={{0,28},{4,0},{8,4},{12,8},{16,12},{20,16},{24,20},{28,24},{1,29},{... | collective-permute-start | bytes 786440 | tf_op jit(solution)/shard_map/ppermute | solution.py:205
  48.6 25.1 %collective-permute-start.5 = (bf16[2,128,512]{2,1,0:T(8,128)(2,1)}, bf16[2,128,512]{2,1,0:T(8,128)(2,1)S(1)}, u32[]{:S(2)}, u32[]{:S(2)}) collective-permute-start(bf16[2,128,512]{2,1,0:T(8,128)(2,1)} %get-tuple-element.29), channel_id=1, source_target_pairs={{0,16},{4,20},{8,24},{12,28},{16,0},{20,4},{24,8},{28,12},{1,17},{... | collective-permute-start | bytes 786440 | tf_op jit(solution)/shard_map/ppermute | solution.py:205
  48.6 34.1 %collective-permute-start.6 = (bf16[2,128,512]{2,1,0:T(8,128)(2,1)}, bf16[2,128,512]{2,1,0:T(8,128)(2,1)S(1)}, u32[]{:S(2)}, u32[]{:S(2)}) collective-permute-start(bf16[2,128,512]{2,1,0:T(8,128)(2,1)} %get-tuple-element.30), channel_id=1, source_target_pairs={{0,12},{4,16},{8,20},{12,24},{16,28},{20,0},{24,4},{28,8},{1,13},{... | collective-permute-start | bytes 786440 | tf_op jit(solution)/shard_map/ppermute | solution.py:205
  51.6 31.1 %collective-permute-start.7 = (bf16[2,128,512]{2,1,0:T(8,128)(2,1)}, bf16[2,128,512]{2,1,0:T(8,128)(2,1)S(1)}, u32[]{:S(2)}, u32[]{:S(2)}) collective-permute-start(bf16[2,128,512]{2,1,0:T(8,128)(2,1)} %get-tuple-element.31), channel_id=1, source_target_pairs={{0,20},{4,24},{8,28},{12,0},{16,4},{20,8},{24,12},{28,16},{1,21},{... | collective-permute-start | bytes 786440 | tf_op jit(solution)/shard_map/ppermute | solution.py:205
  70.2 15.1 %collective-permute-start.8 = (bf16[2,128,512]{2,1,0:T(8,128)(2,1)}, bf16[2,128,512]{2,1,0:T(8,128)(2,1)S(1)}, u32[]{:S(2)}, u32[]{:S(2)}) collective-permute-start(bf16[2,128,512]{2,1,0:T(8,128)(2,1)} %get-tuple-element.32), channel_id=1, source_target_pairs={{0,8},{4,12},{8,16},{12,20},{16,24},{20,28},{24,0},{28,4},{1,9},{5... | collective-permute-start | bytes 786440 | tf_op jit(solution)/shard_map/ppermute | solution.py:205
  70.2 22.7 %collective-permute-start.9 = (bf16[2,128,512]{2,1,0:T(8,128)(2,1)}, bf16[2,128,512]{2,1,0:T(8,128)(2,1)S(1)}, u32[]{:S(2)}, u32[]{:S(2)}) collective-permute-start(bf16[2,128,512]{2,1,0:T(8,128)(2,1)} %get-tuple-element.33), channel_id=1, source_target_pairs={{0,24},{4,28},{8,0},{12,4},{16,8},{20,12},{24,16},{28,20},{1,25},{... | collective-permute-start | bytes 786440 | tf_op jit(solution)/shard_map/ppermute | solution.py:205
  73.8 39.2 %collective-permute-start.2 = (bf16[256,1024]{1,0:T(8,128)(2,1)S(1)}, bf16[256,1024]{1,0:T(8,128)(2,1)S(1)}, u32[]{:S(2)}, u32[]{:S(2)}) collective-permute-start(bf16[256,1024]{1,0:T(8,128)(2,1)S(1)} %copy-done.6), channel_id=1, source_target_pairs={{0,1},{1,0},{2,3},{3,2},{4,5},{5,4},{6,7},{7,6},{8,9},{9,8},{10,11... | collective-permute-start | bytes 1572872 | tf_op jit(solution)/shard_map/ppermute | solution.py:196
  106.9 15.2 %all-to-all-start.2 = ((bf16[16,16,512]{2,1,0:T(8,128)(2,1)}), bf16[16,16,512]{2,1,0:T(8,128)(2,1)S(1)}, u32[]{:S(2)}, u32[]{:S(2)}) async-start(bf16[16,16,512]{2,1,0:T(8,128)(2,1)} %bitcast.3), calls=%async_computation.2 | async-start | bytes 524288 | tf_op jit(solution)/shard_map/all_to_all | solution.py:208
  113.0 0.8 copy-start.7
  113.8 19.0 %copy-start = (f32[1024,512]{1,0:T(8,128)S(1)}, f32[1024,512]{1,0:T(8,128)}, u32[]{:S(2)}) copy-start(f32[1024,512]{1,0:T(8,128)} %proj_ref.1) | copy-start | bytes 6291460
  120.1 13.2 %copy-start.1 = (f32[128,1024]{1,0:T(8,128)S(1)}, f32[128,1024]{1,0:T(8,128)}, u32[]{:S(2)}) copy-start(f32[128,1024]{1,0:T(8,128)} %params_ref.1) | copy-start | bytes 1572868
  120.1 13.2 %copy-start.4 = (f32[128,1024]{1,0:T(8,128)S(1)}, f32[128,1024]{1,0:T(8,128)}, u32[]{:S(2)}) copy-start(f32[128,1024]{1,0:T(8,128)} %param.8) | copy-start | bytes 1572868
  120.1 21.3 %collective-permute-start.3 = (f32[256,1024]{1,0:T(8,128)}, f32[256,1024]{1,0:T(8,128)}, u32[]{:S(2)}, u32[]{:S(2)}) collective-permute-start(f32[256,1024]{1,0:T(8,128)} %get-tuple-element.23), channel_id=1, source_target_pairs={{0,1},{1,0},{2,3},{3,2},{4,5},{5,4},{6,7},{7,6},{8,9},{9,8},{10,11... | collective-permute-start | bytes 3145736 | tf_op jit(solution)/shard_map/ppermute | solution.py:222
  122.0 19.4 %collective-permute-start.4 = (bf16[256,2048]{1,0:T(8,128)(2,1)}, bf16[256,2048]{1,0:T(8,128)(2,1)}, u32[]{:S(2)}, u32[]{:S(2)}) collective-permute-start(bf16[256,2048]{1,0:T(8,128)(2,1)} %get-tuple-element.25), channel_id=1, source_target_pairs={{0,1},{1,0},{2,3},{3,2},{4,5},{5,4},{6,7},{7,6},{8,9},{9,8},{10,11... | collective-permute-start | bytes 3145736 | tf_op jit(solution)/shard_map/ppermute | solution.py:222

commit v5 on v2

--- a/solution.py
+++ b/solution.py
@@ -12,7 +12,7 @@
 
 ISLAND = ("y", "xl")
 FSDP = ("z", "xh", "c")
-PLANE = ("y", "xl", "xh")
+PLANE = ("xh", "y", "xl")
 F32, BF16 = jnp.float32, jnp.bfloat16
 LANES = 128
 VMEM = pl.BlockSpec(memory_space=pltpu.VMEM)
@@ -72,29 +72,26 @@
 
 
 def sketch_kernel(at_ref, tok_ref, got_ref, q_ref, got_q_ref, out_ref):
-    pieces, n_xh, _, part, proj = out_ref.shape
-    z = pl.program_id(0)
+    n_z, n_xh = out_ref.shape[:2]
     dims = (((0,), (0,)), ((), ()))
-    for h in range(n_xh):
-        k = z * n_xh + h
+    for k in range(n_z * n_xh):
         mine = tok_ref[:, pl.ds(pl.multiple_of((2 * k + at_ref[0]) * LANES, LANES), LANES)]
-        theirs = got_ref[:, pl.ds(pl.multiple_of(k * LANES, LANES), LANES)]
+        theirs = got_ref[:, k * LANES : (k + 1) * LANES]
         s = lax.dot_general(mine, q_ref[...], dims, preferred_element_type=F32)
         s += lax.dot_general(theirs, got_q_ref[...], dims, preferred_element_type=F32)
-        out_ref[:, h, 0] = s.astype(BF16).reshape(pieces, part, proj)
-
-
-def make_sketch(at, tokens, got, q, got_q, pieces, n_xh, n_z):
+        out_ref[k // n_xh, k % n_xh] = s.astype(BF16)
+
+
+def make_sketch(at, tokens, got, q, got_q, n_z, n_xh):
     proj = q.shape[1]
-    part = LANES // pieces
-    vm = pl.BlockSpec(memory_space=pltpu.VMEM)
     return pl.pallas_call(
         sketch_kernel,
-        grid=(n_z,),
-        out_shape=jax.ShapeDtypeStruct((pieces, n_xh, n_z, part, proj), BF16),
-        in_specs=[pl.BlockSpec(memory_space=pltpu.SMEM), vm, vm, vm, vm],
-        out_specs=pl.BlockSpec((pieces, n_xh, 1, part, proj), lambda z: (0, 0, z, 0, 0)),
-        cost_estimate=pl.CostEstimate(flops=8 * tokens.size * proj, bytes_accessed=16 * tokens.size, transcendentals=0),
+        out_shape=jax.ShapeDtypeStruct((n_z, n_xh, LANES, proj), BF16),
+        in_specs=[SMEM] + [VMEM] * 4,
+        out_specs=VMEM,
+        cost_estimate=pl.CostEstimate(
+            flops=8 * tokens.size * proj, bytes_accessed=16 * tokens.size, transcendentals=0
+        ),
         name="make_sketch",
     )(at, tokens, got, q, got_q)
 
@@ -149,7 +146,7 @@
     )(piece, after)
 
 
-def join_kernel(after_ref, *refs):
+def join_kernel(*refs):
     n = len(refs) // 3
     for a_ref, b_ref, out_ref in zip(refs[:n], refs[n : 2 * n], refs[2 * n :]):
         k = a_ref.shape[0]
@@ -157,12 +154,12 @@
         out_ref[k:] = b_ref[...]
 
 
-def join(held, more, after):
+def join(held, more):
     n = len(held)
     shapes = tuple(jax.ShapeDtypeStruct((2 * h.shape[0],) + h.shape[1:], BF16) for h in held)
     return pl.pallas_call(
-        join_kernel, out_shape=shapes, in_specs=[LEFT] + [VMEM] * (2 * n), out_specs=(VMEM,) * n, name="join"
-    )(after, *held, *more)
+        join_kernel, out_shape=shapes, in_specs=[VMEM] * (2 * n), out_specs=(VMEM,) * n, name="join"
+    )(*held, *more)
 
 
 def lanes(ref, blocks):
@@ -282,26 +279,22 @@
 
     q = make_q(upstream, projection)
     got_q = swap(q)
-    pair = make_sketch(at, tokens, got, q, got_q, n_isl, n_xh, n_z)
+    pair = make_sketch(at, tokens, got, q, got_q, n_z, n_xh)
+    along = lax.all_to_all(pair, "z", 0, 0, tiled=True)
     held = split(piece, pair)
-    held = join(held, [exchange(h, order[0]) for h, order in zip(held, GROUPS)], pair)
-    more = [exchange(h, order[1]) for h, order in zip(held, GROUPS)]
-    pair = pair.reshape(n_isl * n_xh, n_z * part, proj)
-    pair = lax.all_to_all(pair, PLANE, 0, 0, tiled=True)
-    plane = jnp.sum(pair.astype(F32), axis=0).astype(BF16)
-    held = join(held, more, plane)
-    more = [exchange(h, order[2]) for h, order in zip(held, GROUPS)]
-    plane = lax.all_to_all(plane.reshape(n_z, part, proj), "z", 0, 0, tiled=True)
-    total = jnp.sum(plane.astype(F32), axis=0).astype(BF16)
-    held = join(held, more, total)
+    for step in range(3):
+        held = join(held, [exchange(h, order[step]) for h, order in zip(held, GROUPS)])
     far = [exchange(h, order[3]) for h, order in zip(held, GROUPS)]
-    total = jnp.broadcast_to(total[None], (n_isl, part, proj))
-    total = lax.all_to_all(total, ISLAND, 0, 0, tiled=True).reshape(rows, proj)
-
     held = [*held, *(swap(h) for h in held)]
     acc, sums = near_products(at, tokens, upstream, held)
     far = [*far, *(swap(f) for f in far)]
     values, token_grads = far_products(at, tokens, upstream, acc, sums, far, inv_width)
+
+    along = jnp.sum(along.astype(F32), axis=0).astype(BF16)
+    plane = lax.all_to_all(along.reshape(n_xh * n_isl, part, proj), PLANE, 0, 0, tiled=True)
+    total = jnp.sum(plane.astype(F32), axis=0).astype(BF16)
+    total = jnp.broadcast_to(total[None], (n_isl, part, proj))
+    total = lax.all_to_all(total, ISLAND, 0, 0, tiled=True).reshape(rows, proj)
 
     dims = (((1,), (1,)), ((), ()))
     head, rest = two_parts(projection)

time: 145 us -> 124 us (0.86)
  blocking collectives: 13.2 us -> 0 us
  starting transfers between devices: 48.5 us -> 46.2 us
  waiting for transfers between devices: 33.1 us -> 31.1 us
  Pallas kernels: 37.9 us -> 36.1 us
    all_to_all x1 -> x0, blocking collectives: 13.2 us -> none  [step(): lax.all_to_all(plane.reshape(n_z, part, proj), 'z', 0, 0, tiled=True)]
    all_to_all x1, waiting for transfers between devices: 9.05 us -> 0.01 us  [step(): total = lax.all_to_all(total, ISLAND, 0, 0, tiled=True).reshape(rows, proj)]
    ppermute x4, waiting for transfers between devices: 10.6 us -> 3.44 us  [exchange(): return lax.ppermute(x, ('xl', 'xh'), [(0, 3), (3, 0), (1, 2), (2, 1)])]
    ppermute x8, waiting for transfers between devices: 11 us -> 17 us  [exchange(): return lax.ppermute(x, 'y', [(i, i ^ flip) for i in range(4)])]
    ppermute x4, waiting for transfers between devices: 0.01 us -> 5.76 us  [exchange(): return lax.ppermute(x, 'xl', [(0, 1), (1, 0)])]
    ppermute x4, starting transfers between devices: 7.51 us -> 3.75 us  [exchange(): return lax.ppermute(x, ('xl', 'xh'), [(0, 3), (3, 0), (1, 2), (2, 1)])]
    all_to_all x1, waiting for transfers between devices: 2.41 us -> 4.36 us  [step(): piece = lax.all_to_all(piece, 'z', 0, 0, tiled=True)]
    pallas_call x4, Pallas kernels: 13.6 us -> 11.6 us  [the longest x3 7 us: join(): pl.pallas_call(join_kernel, out_shape=shapes, in_specs=[VMEM] * (2 * n),...]
  transfers between devices with their start and end apart: 29 -> 30, of which waited for: 6 -> 14; matrix products, arithmetic and copies ran while one was open for 3% -> 1% of each run, Pallas kernels for 15% -> 27%
where the time goes in v5:
time: 124 us
  starting transfers between devices  46.2 us (37%)
  Pallas kernels  36.1 us (29%)
  waiting for transfers between devices  31.1 us (25%)
  local copies, waits for them, and re-layouts  5.74 us (5%)
  matrix products  2 us (2%)
  other arithmetic  1.69 us (1%)
    ppermute x8, waiting for transfers between devices, exchange(): return lax.ppermute(x, 'y', [(i, i ^ flip) for i in range(4)])  17 us
    pallas_call x1, Pallas kernels, far_products(): pl.pallas_call(functools.partial(far_kernel, scale=scale), out_shape=(jax...  8.82 us
    ppermute x8, starting transfers between devices, exchange(): return lax.ppermute(x, 'y', [(i, i ^ flip) for i in range(4)])  7.97 us
    ppermute x4, starting transfers between devices, step(): held = [*held, *(swap(h) for h in held)]  7.72 us
    pallas_call x1, Pallas kernels, near_products(): pl.pallas_call(near_kernel, out_shape=(jax.ShapeDtypeStruct((t, kv), F32)...  7.68 us
    pallas_call x3, Pallas kernels, join(): pl.pallas_call(join_kernel, out_shape=shapes, in_specs=[VMEM] * (2 * n),...  7 us
    all_to_all x1, starting transfers between devices, step(): piece = lax.all_to_all(piece, 'z', 0, 0, tiled=True)  6.48 us
    ppermute x4, waiting for transfers between devices, exchange(): return lax.ppermute(x, 'xl', [(0, 1), (1, 0)])  5.76 us
  transfers between devices with their start and end apart: 30, of which 14 were waited for; matrix products, arithmetic and copies ran while one was open for 1% of the time, Pallas kernels for 27%

profile of v5, /device:TPU:1, one launch (start us, length us, event | category | flops | bytes accessed | tf_op | source)
XLA Modules:
  0.0 123.7 jit_solution(4148091652786326881)
XLA Ops:
  1.2 3.0 %pick.1 = (bf16[256,2048]{1,0:T(8,128)(2,1)}, bf16[8,128,128]{2,1,0:T(8,128)(2,1)}) custom-call(s32[4]{0:T(128)} %pad_add_fusion.at_ref, bf16[256,4096]{1,0:T(8,128)(2,1)} %tok_ref.5, f32[128,1024]{1,0:T(8,128)} %params_ref.1), custom_call_target="tpu_custom_call" | custom-call | tf_op jit(solution)/shard_map/pick/pallas_call | solution.py:43
  4.3 3.2 %collective-permute-start = (bf16[256,2048]{1,0:T(8,128)(2,1)}, bf16[256,2048]{1,0:T(8,128)(2,1)S(1)}, u32[]{:S(2)}, u32[]{:S(2)}) collective-permute-start(bf16[256,2048]{1,0:T(8,128)(2,1)} %get-tuple-element.27), channel_id=1, source_target_pairs={{0,1},{1,0},{2,3},{3,2},{4,5},{5,4},{6,7},{7,6},{8,9},{9,8},{10,11... | collective-permute-start | bytes 3145736 | tf_op jit(solution)/shard_map/ppermute | solution.py:277
  7.5 3.2 %make_q.1.q_ref = bf16[256,512]{1,0:T(8,128)(2,1)} custom-call(bf16[256,1024]{1,0:T(8,128)(2,1)} %up_ref.5, f32[1024,512]{1,0:T(8,128)} %proj_ref.1), custom_call_target="tpu_custom_call" | custom-call | flops 1073741824 | bytes 3145728 | tf_op jit(solution)/shard_map/make_q/pallas_call | solution.py:64
  10.7 6.5 %all-to-all-start = ((bf16[8,128,128]{2,1,0:T(8,128)(2,1)}), bf16[8,128,128]{2,1,0:T(8,128)(2,1)S(1)}, u32[]{:S(2)}, u32[]{:S(2)}) async-start(bf16[8,128,128]{2,1,0:T(8,128)(2,1)} %get-tuple-element.26), calls=%async_computation | async-start | bytes 524288 | tf_op jit(solution)/shard_map/all_to_all | solution.py:278
  18.9 4.6 %make_sketch.1.after_ref = bf16[8,2,128,512]{3,2,1,0:T(8,128)(2,1)} custom-call(s32[4]{0:T(128)} %pad_add_fusion.at_ref, bf16[256,4096]{1,0:T(8,128)(2,1)} %tok_ref.5, bf16[256,2048]{1,0:T(8,128)(2,1)} %copy-done.18, bf16[256,512]{1,0:T(8,128)(2,1)} %make_q.1.q_ref, bf16[256,512]{1,0:T(8,128)(2,1)} %copy-done.22), custom_call_target="tpu_custom_call" | custom-call | flops 4294967296 | bytes 16777216 | tf_op jit(solution)/shard_map/make_sketch/pallas_call | solution.py:87
  23.5 4.4 %all-to-all-done.piece_ref = bf16[8,128,128]{2,1,0:T(8,128)(2,1)S(1)} async-done(((bf16[8,128,128]{2,1,0:T(8,128)(2,1)}), bf16[8,128,128]{2,1,0:T(8,128)(2,1)S(1)}, u32[]{:S(2)}, u32[]{:S(2)}) %all-to-all-start) | async-done | bytes 262176 | tf_op jit(solution)/shard_map/all_to_all | solution.py:278
  27.9 3.6 %all-to-all-start.1 = ((bf16[8,2,128,512]{3,2,1,0:T(8,128)(2,1)}), bf16[8,2,128,512]{3,2,1,0:T(8,128)(2,1)S(1)}, u32[]{:S(2)}, u32[]{:S(2)}) async-start(bf16[8,2,128,512]{3,2,1,0:T(8,128)(2,1)} %make_sketch.1.after_ref), calls=%async_computation.1 | async-start | bytes 4194304 | tf_op jit(solution)/shard_map/all_to_all | solution.py:283
  31.5 1.7 %split.1 = (bf16[2,128,128]{2,1,0:T(8,128)(2,1)}, bf16[2,128,128]{2,1,0:T(8,128)(2,1)}, bf16[2,128,128]{2,1,0:T(8,128)(2,1)}, bf16[2,128,128]{2,1,0:T(8,128)(2,1)}) custom-call(bf16[8,128,128]{2,1,0:T(8,128)(2,1)} %copy-done.2, bf16[8,2,128,512]{3,2,1,0:T(8,128)(2,1)} %make_sketch.1.after_ref), custom_call_target="tpu_custom_call" | custom-call | tf_op jit(solution)/shard_map/split/pallas_call | solution.py:140
  33.2 2.5 %collective-permute-start.2 = (bf16[2,128,128]{2,1,0:T(8,128)(2,1)}, bf16[2,128,128]{2,1,0:T(8,128)(2,1)S(1)}, u32[]{:S(2)}, u32[]{:S(2)}) collective-permute-start(bf16[2,128,128]{2,1,0:T(8,128)(2,1)} %get-tuple-element.28.refs_0_), channel_id=1, source_target_pairs={{0,34},{34,0},{2,32},{32,2},{1,35},{35,1},{3,33},{33,3},{4,38},{38... | collective-permute-start | bytes 196616 | tf_op jit(solution)/shard_map/ppermute | solution.py:105
  37.0 1.9 %collective-permute-start.5 = (bf16[2,128,128]{2,1,0:T(8,128)(2,1)}, bf16[2,128,128]{2,1,0:T(8,128)(2,1)S(1)}, u32[]{:S(2)}, u32[]{:S(2)}) collective-permute-start(bf16[2,128,128]{2,1,0:T(8,128)(2,1)} %get-tuple-element.31.refs_3_), channel_id=1, source_target_pairs={{0,192},{64,128},{128,64},{192,0},{1,193},{65,129},{129,65},{193,1... | collective-permute-start | bytes 196616 | tf_op jit(solution)/shard_map/ppermute | solution.py:109
  42.4 1.9 %join.3 = (bf16[4,128,128]{2,1,0:T(8,128)(2,1)}, bf16[4,128,128]{2,1,0:T(8,128)(2,1)}, bf16[4,128,128]{2,1,0:T(8,128)(2,1)}, bf16[4,128,128]{2,1,0:T(8,128)(2,1)}) custom-call(bf16[2,128,128]{2,1,0:T(8,128)(2,1)} %get-tuple-element.28.refs_0_, bf16[2,128,128]{2,1,0:T(8,128)(2,1)} %get-tuple-element.29.refs_1_, ...), custom_call_target="tpu_custom_call" | custom-call | tf_op jit(solution)/shard_map/join/pallas_call | solution.py:160
  45.8 1.9 %collective-permute-start.8 = (bf16[4,128,128]{2,1,0:T(8,128)(2,1)}, bf16[4,128,128]{2,1,0:T(8,128)(2,1)S(1)}, u32[]{:S(2)}, u32[]{:S(2)}) collective-permute-start(bf16[4,128,128]{2,1,0:T(8,128)(2,1)} %get-tuple-element.34.refs_2_), channel_id=1, source_target_pairs={{0,192},{64,128},{128,64},{192,0},{1,193},{65,129},{129,65},{193,1... | collective-permute-start | bytes 393224 | tf_op jit(solution)/shard_map/ppermute | solution.py:109
  48.7 2.7 %collective-permute-done.8.refs_6_ = bf16[4,128,128]{2,1,0:T(8,128)(2,1)S(1)} collective-permute-done((bf16[4,128,128]{2,1,0:T(8,128)(2,1)}, bf16[4,128,128]{2,1,0:T(8,128)(2,1)S(1)}, u32[]{:S(2)}, u32[]{:S(2)}) %collective-permute-start.8) | collective-permute-done | bytes 131104 | tf_op jit(solution)/shard_map/ppermute | solution.py:109
  51.3 1.7 %collective-permute-done.9.refs_7_ = bf16[4,128,128]{2,1,0:T(8,128)(2,1)S(1)} collective-permute-done((bf16[4,128,128]{2,1,0:T(8,128)(2,1)}, bf16[4,128,128]{2,1,0:T(8,128)(2,1)S(1)}, u32[]{:S(2)}, u32[]{:S(2)}) %collective-permute-start.9) | collective-permute-done | bytes 131104 | tf_op jit(solution)/shard_map/ppermute | solution.py:105
  53.7 2.3 %join.4 = (bf16[8,128,128]{2,1,0:T(8,128)(2,1)}, bf16[8,128,128]{2,1,0:T(8,128)(2,1)}, bf16[8,128,128]{2,1,0:T(8,128)(2,1)}, bf16[8,128,128]{2,1,0:T(8,128)(2,1)}) custom-call(bf16[4,128,128]{2,1,0:T(8,128)(2,1)} %get-tuple-element.32.refs_0_, bf16[4,128,128]{2,1,0:T(8,128)(2,1)} %get-tuple-element.33.refs_1_, ...), custom_call_target="tpu_custom_call" | custom-call | tf_op jit(solution)/shard_map/join/pallas_call | solution.py:160
  57.4 4.4 %collective-permute-done.10.refs_4_ = bf16[8,128,128]{2,1,0:T(8,128)(2,1)S(1)} collective-permute-done((bf16[8,128,128]{2,1,0:T(8,128)(2,1)}, bf16[8,128,128]{2,1,0:T(8,128)(2,1)S(1)}, u32[]{:S(2)}, u32[]{:S(2)}) %collective-permute-start.10) | collective-permute-done | bytes 262176 | tf_op jit(solution)/shard_map/ppermute | solution.py:107
  65.5 2.9 %join.5 = (bf16[16,128,128]{2,1,0:T(8,128)(2,1)}, bf16[16,128,128]{2,1,0:T(8,128)(2,1)}, bf16[16,128,128]{2,1,0:T(8,128)(2,1)}, bf16[16,128,128]{2,1,0:T(8,128)(2,1)}) custom-call(bf16[8,128,128]{2,1,0:T(8,128)(2,1)} %get-tuple-element.36.refs_0_, bf16[8,128,128]{2,1,0:T(8,128)(2,1)} %get-tuple-element.37.refs_1_, ...), custom_call_target="tpu_custom_call" | custom-call | tf_op jit(solution)/shard_map/join/pallas_call | solution.py:160
  68.3 6.3 %collective-permute-start.14 = (bf16[16,128,128]{2,1,0:T(8,128)(2,1)}, bf16[16,128,128]{2,1,0:T(8,128)(2,1)S(1)}, u32[]{:S(2)}, u32[]{:S(2)}) collective-permute-start(bf16[16,128,128]{2,1,0:T(8,128)(2,1)} %get-tuple-element.40.refs_0_), channel_id=1, source_target_pairs={{0,1},{1,0},{2,3},{3,2},{4,5},{5,4},{6,7},{7,6},{8,9},{9,8},{10,11... | collective-permute-start | bytes 1572872 | tf_op jit(solution)/shard_map/ppermute | solution.py:288
  75.2 1.7 %collective-permute-start.18 = (bf16[16,128,128]{2,1,0:T(8,128)(2,1)}, bf16[16,128,128]{2,1,0:T(8,128)(2,1)S(1)}, u32[]{:S(2)}, u32[]{:S(2)}) collective-permute-start(bf16[16,128,128]{2,1,0:T(8,128)(2,1)} %get-tuple-element.40.refs_0_), channel_id=1, source_target_pairs={{0,192},{64,128},{128,64},{192,0},{1,193},{65,129},{129,65},{193,1... | collective-permute-start | bytes 1572872 | tf_op jit(solution)/shard_map/ppermute | solution.py:109
  79.5 10.6 %collective-permute-done.18.refs_0_ = bf16[16,128,128]{2,1,0:T(8,128)(2,1)S(1)} collective-permute-done((bf16[16,128,128]{2,1,0:T(8,128)(2,1)}, bf16[16,128,128]{2,1,0:T(8,128)(2,1)S(1)}, u32[]{:S(2)}, u32[]{:S(2)}) %collective-permute-start.18) | collective-permute-done | bytes 524320 | tf_op jit(solution)/shard_map/ppermute | solution.py:109
  94.4 4.3 %all-to-all-start.2 = ((bf16[16,16,512]{2,1,0:T(8,128)(2,1)}), bf16[16,16,512]{2,1,0:T(8,128)(2,1)S(1)}, u32[]{:S(2)}, u32[]{:S(2)}) async-start(bf16[16,16,512]{2,1,0:T(8,128)(2,1)} %bitcast.4), calls=%async_computation.2 | async-start | bytes 524288 | tf_op jit(solution)/shard_map/all_to_all | solution.py:294
  98.7 7.7 %near_products.1 = (f32[256,1024]{1,0:T(8,128)}, f32[16,256,256]{2,1,0:T(8,128)}) custom-call(s32[4]{0:T(128)} %pad_add_fusion.at_ref, bf16[256,4096]{1,0:T(8,128)(2,1)} %tok_ref.5, bf16[256,1024]{1,0:T(8,128)(2,1)} %up_ref.5, bf16[16,128,128]{2,1,0:T(8,128)(2,1)} %get-tuple-element.40.refs_0_, bf16[16,128,128]{2,1,0:T(8,128)(2,1)} %get-tuple-element.41.refs_1_, ...), custom_call_target="tpu_custom_call" | custom-call | flops 2147483648 | bytes 4194304 | tf_op jit(solution)/shard_map/near_products/pallas_call | solution.py:235
  107.6 4.5 %all-to-all-start.3 = ((bf16[8,16,512]{2,1,0:T(8,128)(2,1)}), bf16[8,16,512]{2,1,0:T(8,128)(2,1)S(1)}, u32[]{:S(2)}, u32[]{:S(2)}) async-start(bf16[8,16,512]{2,1,0:T(8,128)(2,1)} %broadcast_in_dim.2), calls=%async_computation.3 | async-start | bytes 262144 | tf_op jit(solution)/shard_map/all_to_all | solution.py:297
  112.2 8.8 %far_products.1 = (bf16[256,1024]{1,0:T(8,128)(2,1)}, bf16[256,4096]{1,0:T(8,128)(2,1)}) custom-call(s32[4]{0:T(128)} %pad_add_fusion.at_ref, bf16[256,4096]{1,0:T(8,128)(2,1)} %tok_ref.5, bf16[256,1024]{1,0:T(8,128)(2,1)} %up_ref.5, f32[256,1024]{1,0:T(8,128)} %get-tuple-element.44.before_ref, f32[16,256,256]{2,1,0:T(8,128)} %get-tuple-element.45.sum_ref, ...), custom_call_target="tpu_custom_call" | custom-call | flops 2147483648 | bytes 4194304 | tf_op jit(solution)/shard_map/far_products/pallas_call | solution.py:252
  (97 shorter events, 26.6 us)
Async XLA Ops:
  4.3 12.9 %collective-permute-start = (bf16[256,2048]{1,0:T(8,128)(2,1)}, bf16[256,2048]{1,0:T(8,128)(2,1)S(1)}, u32[]{:S(2)}, u32[]{:S(2)}) collective-permute-start(bf16[256,2048]{1,0:T(8,128)(2,1)} %get-tuple-element.27), channel_id=1, source_target_pairs={{0,1},{1,0},{2,3},{3,2},{4,5},{5,4},{6,7},{7,6},{8,9},{9,8},{10,11... | collective-permute-start | bytes 3145736 | tf_op jit(solution)/shard_map/ppermute | solution.py:277
  10.7 6.5 %collective-permute-start.1 = (bf16[256,512]{1,0:T(8,128)(2,1)}, bf16[256,512]{1,0:T(8,128)(2,1)S(1)}, u32[]{:S(2)}, u32[]{:S(2)}) collective-permute-start(bf16[256,512]{1,0:T(8,128)(2,1)} %make_q.1.q_ref), channel_id=1, source_target_pairs={{0,1},{1,0},{2,3},{3,2},{4,5},{5,4},{6,7},{7,6},{8,9},{9,8},{10,11... | collective-permute-start | bytes 786440 | tf_op jit(solution)/shard_map/ppermute | solution.py:281
  10.7 17.2 %all-to-all-start = ((bf16[8,128,128]{2,1,0:T(8,128)(2,1)}), bf16[8,128,128]{2,1,0:T(8,128)(2,1)S(1)}, u32[]{:S(2)}, u32[]{:S(2)}) async-start(bf16[8,128,128]{2,1,0:T(8,128)(2,1)} %get-tuple-element.26), calls=%async_computation | async-start | bytes 524288 | tf_op jit(solution)/shard_map/all_to_all | solution.py:278
  27.9 65.4 %all-to-all-start.1 = ((bf16[8,2,128,512]{3,2,1,0:T(8,128)(2,1)}), bf16[8,2,128,512]{3,2,1,0:T(8,128)(2,1)S(1)}, u32[]{:S(2)}, u32[]{:S(2)}) async-start(bf16[8,2,128,512]{3,2,1,0:T(8,128)(2,1)} %make_sketch.1.after_ref), calls=%async_computation.1 | async-start | bytes 4194304 | tf_op jit(solution)/shard_map/all_to_all | solution.py:283
  33.2 5.7 %collective-permute-start.2 = (bf16[2,128,128]{2,1,0:T(8,128)(2,1)}, bf16[2,128,128]{2,1,0:T(8,128)(2,1)S(1)}, u32[]{:S(2)}, u32[]{:S(2)}) collective-permute-start(bf16[2,128,128]{2,1,0:T(8,128)(2,1)} %get-tuple-element.28.refs_0_), channel_id=1, source_target_pairs={{0,34},{34,0},{2,32},{32,2},{1,35},{35,1},{3,33},{33,3},{4,38},{38... | collective-permute-start | bytes 196616 | tf_op jit(solution)/shard_map/ppermute | solution.py:105
  37.0 4.8 %collective-permute-start.5 = (bf16[2,128,128]{2,1,0:T(8,128)(2,1)}, bf16[2,128,128]{2,1,0:T(8,128)(2,1)S(1)}, u32[]{:S(2)}, u32[]{:S(2)}) collective-permute-start(bf16[2,128,128]{2,1,0:T(8,128)(2,1)} %get-tuple-element.31.refs_3_), channel_id=1, source_target_pairs={{0,192},{64,128},{128,64},{192,0},{1,193},{65,129},{129,65},{193,1... | collective-permute-start | bytes 196616 | tf_op jit(solution)/shard_map/ppermute | solution.py:109
  45.8 5.5 %collective-permute-start.8 = (bf16[4,128,128]{2,1,0:T(8,128)(2,1)}, bf16[4,128,128]{2,1,0:T(8,128)(2,1)S(1)}, u32[]{:S(2)}, u32[]{:S(2)}) collective-permute-start(bf16[4,128,128]{2,1,0:T(8,128)(2,1)} %get-tuple-element.34.refs_2_), channel_id=1, source_target_pairs={{0,192},{64,128},{128,64},{192,0},{1,193},{65,129},{129,65},{193,1... | collective-permute-start | bytes 393224 | tf_op jit(solution)/shard_map/ppermute | solution.py:109
  47.7 5.4 %collective-permute-start.9 = (bf16[4,128,128]{2,1,0:T(8,128)(2,1)}, bf16[4,128,128]{2,1,0:T(8,128)(2,1)S(1)}, u32[]{:S(2)}, u32[]{:S(2)}) collective-permute-start(bf16[4,128,128]{2,1,0:T(8,128)(2,1)} %get-tuple-element.35.refs_3_), channel_id=1, source_target_pairs={{0,34},{34,0},{2,32},{32,2},{1,35},{35,1},{3,33},{33,3},{4,38},{38... | collective-permute-start | bytes 393224 | tf_op jit(solution)/shard_map/ppermute | solution.py:105
  56.0 5.7 %collective-permute-start.10 = (bf16[8,128,128]{2,1,0:T(8,128)(2,1)}, bf16[8,128,128]{2,1,0:T(8,128)(2,1)S(1)}, u32[]{:S(2)}, u32[]{:S(2)}) collective-permute-start(bf16[8,128,128]{2,1,0:T(8,128)(2,1)} %get-tuple-element.36.refs_0_), channel_id=1, source_target_pairs={{0,32},{32,0},{1,33},{33,1},{2,34},{34,2},{3,35},{35,3},{4,36},{36... | collective-permute-start | bytes 786440 | tf_op jit(solution)/shard_map/ppermute | solution.py:107
  56.0 7.0 %collective-permute-start.11 = (bf16[8,128,128]{2,1,0:T(8,128)(2,1)}, bf16[8,128,128]{2,1,0:T(8,128)(2,1)S(1)}, u32[]{:S(2)}, u32[]{:S(2)}) collective-permute-start(bf16[8,128,128]{2,1,0:T(8,128)(2,1)} %get-tuple-element.37.refs_1_), channel_id=1, source_target_pairs={{0,192},{64,128},{128,64},{192,0},{1,193},{65,129},{129,65},{193,1... | collective-permute-start | bytes 786440 | tf_op jit(solution)/shard_map/ppermute | solution.py:109
  57.2 6.9 %collective-permute-start.12 = (bf16[8,128,128]{2,1,0:T(8,128)(2,1)}, bf16[8,128,128]{2,1,0:T(8,128)(2,1)S(1)}, u32[]{:S(2)}, u32[]{:S(2)}) collective-permute-start(bf16[8,128,128]{2,1,0:T(8,128)(2,1)} %get-tuple-element.38.refs_2_), channel_id=1, source_target_pairs={{0,34},{34,0},{2,32},{32,2},{1,35},{35,1},{3,33},{33,3},{4,38},{38... | collective-permute-start | bytes 786440 | tf_op jit(solution)/shard_map/ppermute | solution.py:105
  57.4 6.7 %collective-permute-start.13 = (bf16[8,128,128]{2,1,0:T(8,128)(2,1)}, bf16[8,128,128]{2,1,0:T(8,128)(2,1)S(1)}, u32[]{:S(2)}, u32[]{:S(2)}) collective-permute-start(bf16[8,128,128]{2,1,0:T(8,128)(2,1)} %get-tuple-element.39.refs_3_), channel_id=1, source_target_pairs={{0,64},{64,0},{128,192},{192,128},{1,65},{65,1},{129,193},{193,129... | collective-permute-start | bytes 786440 | tf_op jit(solution)/shard_map/ppermute | solution.py:109
  68.3 9.7 %collective-permute-start.14 = (bf16[16,128,128]{2,1,0:T(8,128)(2,1)}, bf16[16,128,128]{2,1,0:T(8,128)(2,1)S(1)}, u32[]{:S(2)}, u32[]{:S(2)}) collective-permute-start(bf16[16,128,128]{2,1,0:T(8,128)(2,1)} %get-tuple-element.40.refs_0_), channel_id=1, source_target_pairs={{0,1},{1,0},{2,3},{3,2},{4,5},{5,4},{6,7},{7,6},{8,9},{9,8},{10,11... | collective-permute-start | bytes 1572872 | tf_op jit(solution)/shard_map/ppermute | solution.py:288
  75.2 14.9 %collective-permute-start.18 = (bf16[16,128,128]{2,1,0:T(8,128)(2,1)}, bf16[16,128,128]{2,1,0:T(8,128)(2,1)S(1)}, u32[]{:S(2)}, u32[]{:S(2)}) collective-permute-start(bf16[16,128,128]{2,1,0:T(8,128)(2,1)} %get-tuple-element.40.refs_0_), channel_id=1, source_target_pairs={{0,192},{64,128},{128,64},{192,0},{1,193},{65,129},{129,65},{193,1... | collective-permute-start | bytes 1572872 | tf_op jit(solution)/shard_map/ppermute | solution.py:109
  76.9 14.6 %collective-permute-start.19 = (bf16[16,128,128]{2,1,0:T(8,128)(2,1)}, bf16[16,128,128]{2,1,0:T(8,128)(2,1)S(1)}, u32[]{:S(2)}, u32[]{:S(2)}) collective-permute-start(bf16[16,128,128]{2,1,0:T(8,128)(2,1)} %get-tuple-element.41.refs_1_), channel_id=1, source_target_pairs={{0,34},{34,0},{2,32},{32,2},{1,35},{35,1},{3,33},{33,3},{4,38},{38... | collective-permute-start | bytes 1572872 | tf_op jit(solution)/shard_map/ppermute | solution.py:105
  78.0 14.7 %collective-permute-start.20 = (bf16[16,128,128]{2,1,0:T(8,128)(2,1)}, bf16[16,128,128]{2,1,0:T(8,128)(2,1)}, u32[]{:S(2)}, u32[]{:S(2)}) collective-permute-start(bf16[16,128,128]{2,1,0:T(8,128)(2,1)} %get-tuple-element.42.refs_2_), channel_id=1, source_target_pairs={{0,64},{64,0},{128,192},{192,128},{1,65},{65,1},{129,193},{193,129... | collective-permute-start | bytes 1572872 | tf_op jit(solution)/shard_map/ppermute | solution.py:109
  78.0 14.8 %collective-permute-start.21 = (bf16[16,128,128]{2,1,0:T(8,128)(2,1)}, bf16[16,128,128]{2,1,0:T(8,128)(2,1)}, u32[]{:S(2)}, u32[]{:S(2)}) collective-permute-start(bf16[16,128,128]{2,1,0:T(8,128)(2,1)} %get-tuple-element.43.refs_3_), channel_id=1, source_target_pairs={{0,32},{32,0},{1,33},{33,1},{2,34},{34,2},{3,35},{35,3},{4,36},{36... | collective-permute-start | bytes 1572872 | tf_op jit(solution)/shard_map/ppermute | solution.py:107
  78.6 20.0 %collective-permute-start.17 = (bf16[16,128,128]{2,1,0:T(8,128)(2,1)}, bf16[16,128,128]{2,1,0:T(8,128)(2,1)}, u32[]{:S(2)}, u32[]{:S(2)}) collective-permute-start(bf16[16,128,128]{2,1,0:T(8,128)(2,1)} %get-tuple-element.43.refs_3_), channel_id=1, source_target_pairs={{0,1},{1,0},{2,3},{3,2},{4,5},{5,4},{6,7},{7,6},{8,9},{9,8},{10,11... | collective-permute-start | bytes 1572872 | tf_op jit(solution)/shard_map/ppermute | solution.py:288
  90.1 22.0 %collective-permute-start.22 = (bf16[16,128,128]{2,1,0:T(8,128)(2,1)S(1)}, bf16[16,128,128]{2,1,0:T(8,128)(2,1)}, u32[]{:S(2)}, u32[]{:S(2)}) collective-permute-start(bf16[16,128,128]{2,1,0:T(8,128)(2,1)S(1)} %collective-permute-done.18.refs_0_), channel_id=1, source_target_pairs={{0,1},{1,0},{2,3},{3,2},{4,5},{5,4},{6,7},{7,6},{8,9},{9,8},{10,11... | collective-permute-start | bytes 1572872 | tf_op jit(solution)/shard_map/ppermute | solution.py:290
  91.6 20.6 %collective-permute-start.23 = (bf16[16,128,128]{2,1,0:T(8,128)(2,1)S(1)}, bf16[16,128,128]{2,1,0:T(8,128)(2,1)}, u32[]{:S(2)}, u32[]{:S(2)}) collective-permute-start(bf16[16,128,128]{2,1,0:T(8,128)(2,1)S(1)} %collective-permute-done.19.refs_1_), channel_id=1, source_target_pairs={{0,1},{1,0},{2,3},{3,2},{4,5},{5,4},{6,7},{7,6},{8,9},{9,8},{10,11... | collective-permute-start | bytes 1572872 | tf_op jit(solution)/shard_map/ppermute | solution.py:290
  92.7 19.4 %collective-permute-start.24 = (bf16[16,128,128]{2,1,0:T(8,128)(2,1)}, bf16[16,128,128]{2,1,0:T(8,128)(2,1)}, u32[]{:S(2)}, u32[]{:S(2)}) collective-permute-start(bf16[16,128,128]{2,1,0:T(8,128)(2,1)} %collective-permute-done.20.refs_2_), channel_id=1, source_target_pairs={{0,1},{1,0},{2,3},{3,2},{4,5},{5,4},{6,7},{7,6},{8,9},{9,8},{10,11... | collective-permute-start | bytes 1572872 | tf_op jit(solution)/shard_map/ppermute | solution.py:290
  92.8 19.3 %collective-permute-start.25 = (bf16[16,128,128]{2,1,0:T(8,128)(2,1)}, bf16[16,128,128]{2,1,0:T(8,128)(2,1)}, u32[]{:S(2)}, u32[]{:S(2)}) collective-permute-start(bf16[16,128,128]{2,1,0:T(8,128)(2,1)} %collective-permute-done.21.refs_3_), channel_id=1, source_target_pairs={{0,1},{1,0},{2,3},{3,2},{4,5},{5,4},{6,7},{7,6},{8,9},{9,8},{10,11... | collective-permute-start | bytes 1572872 | tf_op jit(solution)/shard_map/ppermute | solution.py:290
  94.4 12.5 %all-to-all-start.2 = ((bf16[16,16,512]{2,1,0:T(8,128)(2,1)}), bf16[16,16,512]{2,1,0:T(8,128)(2,1)S(1)}, u32[]{:S(2)}, u32[]{:S(2)}) async-start(bf16[16,16,512]{2,1,0:T(8,128)(2,1)} %bitcast.4), calls=%async_computation.2 | async-start | bytes 524288 | tf_op jit(solution)/shard_map/all_to_all | solution.py:294
  107.6 13.4 %all-to-all-start.3 = ((bf16[8,16,512]{2,1,0:T(8,128)(2,1)}), bf16[8,16,512]{2,1,0:T(8,128)(2,1)S(1)}, u32[]{:S(2)}, u32[]{:S(2)}) async-start(bf16[8,16,512]{2,1,0:T(8,128)(2,1)} %broadcast_in_dim.2), calls=%async_computation.3 | async-start | bytes 262144 | tf_op jit(solution)/shard_map/all_to_all | solution.py:297
  (29 other events, 137.9 us)

commit v6 on v5

v6 whole, which is shorter than its diff:
```python
import functools
import math

import jax
import jax.numpy as jnp
from jax import lax
from jax.experimental import pallas as pl
from jax.experimental.pallas import tpu as pltpu
from jax.sharding import Mesh
from jax.sharding import PartitionSpec as P


ISLAND = ("y", "xl")
FSDP = ("z", "xh", "c")
PLANE = ("xh", "y", "xl")
F32, BF16 = jnp.float32, jnp.bfloat16
LANES = 128
VMEM = pl.BlockSpec(memory_space=pltpu.VMEM)
SMEM = pl.BlockSpec(memory_space=pltpu.SMEM)
LEFT = pl.BlockSpec(memory_space=pl.ANY)


def two_parts(x):
    head = x.astype(BF16)
    return head, (x - head.astype(F32)).astype(BF16)


def piece_kernel(at_ref, params_ref, piece_ref):
    width = piece_ref.shape[2]
    block = 2 * at_ref[1] + at_ref[3]
    piece = params_ref[:, pl.ds(pl.multiple_of(block * width, width), width)].astype(BF16)
    for z in range(piece_ref.shape[0]):
        piece_ref[z] = piece


def make_piece(at, params, n_z, pieces):
    rows, kv = params.shape
    return pl.pallas_call(
        piece_kernel,
        out_shape=jax.ShapeDtypeStruct((n_z, rows, kv // pieces), BF16),
        in_specs=[SMEM, VMEM],
        out_specs=VMEM,
        name="make_piece",
    )(at, params)


def pick_kernel(at_ref, tokens_ref, after_ref, out_ref):
    skip = 1 - at_ref[0]
    for k in range(out_ref.shape[1] // LANES):
        at = pl.multiple_of((2 * k + skip) * LANES, LANES)
        out_ref[:, k * LANES : (k + 1) * LANES] = tokens_ref[:, pl.ds(at, LANES)]


def pick(at, tokens, after):
    t, d = tokens.shape
    return pl.pallas_call(
        pick_kernel,
        out_shape=jax.ShapeDtypeStruct((t, d // 2), BF16),
        in_specs=[SMEM, VMEM, LEFT],
        out_specs=VMEM,
        name="pick",
    )(at, tokens, after)


def q_kernel(up_ref, proj_ref, q_ref):
    head, rest = two_parts(proj_ref[...])
    q = jnp.dot(up_ref[...], head, preferred_element_type=F32)
    q += jnp.dot(up_ref[...], rest, preferred_element_type=F32)
    q_ref[...] = q.astype(BF16)


def make_q(upstream, projection):
    return pl.pallas_call(
        q_kernel,
        out_shape=jax.ShapeDtypeStruct((upstream.shape[0], projection.shape[1]), BF16),
        in_specs=[VMEM, VMEM],
        out_specs=VMEM,
        cost_estimate=pl.CostEstimate(
            flops=8 * upstream.size * projection.shape[1],
            bytes_accessed=4 * projection.size + 4 * upstream.size,
            transcendentals=0,
        ),
        name="make_q",
    )(upstream, projection)


def sketch_kernel(at_ref, tok_ref, got_ref, q_ref, got_q_ref, out_ref):
    n_z, n_xh = out_ref.shape[:2]
    dims = (((0,), (0,)), ((), ()))
    for k in range(n_z * n_xh):
        mine = tok_ref[:, pl.ds(pl.multiple_of((2 * k + at_ref[0]) * LANES, LANES), LANES)]
        theirs = got_ref[:, k * LANES : (k + 1) * LANES]
        s = lax.dot_general(mine, q_ref[...], dims, preferred_element_type=F32)
        s += lax.dot_general(theirs, got_q_ref[...], dims, preferred_element_type=F32)
        out_ref[k // n_xh, k % n_xh] = s.astype(BF16)


def make_sketch(at, tokens, got, q, got_q, n_z, n_xh):
    proj = q.shape[1]
    return pl.pallas_call(
        sketch_kernel,
        out_shape=jax.ShapeDtypeStruct((n_z, n_xh, LANES, proj), BF16),
        in_specs=[SMEM] + [VMEM] * 4,
        out_specs=VMEM,
        cost_estimate=pl.CostEstimate(
            flops=8 * tokens.size * proj, bytes_accessed=16 * tokens.size, transcendentals=0
        ),
        name="make_sketch",
    )(at, tokens, got, q, got_q)


ORDERS = (("XALB", "LBXA"), ("ALBX", "BXAL"))
GROUPS = len(ORDERS[0])
FLIP = {"X": (1, 0, 1), "L": (0, 0, 1), "A": (0, 1, 0), "B": (0, 3, 0)}


def exchange(x, group, step):
    def index(y, xl, xh, c):
        return ((y * 2 + xl) * 2 + xh) * 2 + c

    pairs = []
    for y in range(4):
        for xl in range(2):
            for xh in range(2):
                for c in range(2):
                    a, b, l = FLIP[ORDERS[c][group][step]]
                    pairs.append((index(y, xl, xh, c), index(y ^ b, xl ^ l, xh ^ a, c)))
    return lax.ppermute(x, ("y", "xl", "xh", "c"), pairs)


def places(core, group):
    order = ORDERS[core][group]
    held = [(0, 0, 0)]
    for kind in order[:3]:
        f = FLIP[kind]
        held = held + [(a ^ f[0], b ^ f[1], l ^ f[2]) for a, b, l in held]
    f = FLIP[order[3]]
    far = [(a ^ f[0], b ^ f[1], l ^ f[2]) for a, b, l in held]
    return {
        (half, a): sorted(((b, l), i) for i, (a_, b, l) in enumerate(part) if a_ == a)
        for half, part in enumerate((held, far))
        for a in range(2)
    }


def split_kernel(piece_ref, after_ref, *out_refs):
    each = out_refs[0].shape[0]
    for g, out_ref in enumerate(out_refs):
        out_ref[...] = piece_ref[g * each : (g + 1) * each]


def split(piece, after):
    n = GROUPS
    shape = (piece.shape[0] // n,) + piece.shape[1:]
    return pl.pallas_call(
        split_kernel,
        out_shape=(jax.ShapeDtypeStruct(shape, BF16),) * n,
        in_specs=[VMEM, LEFT],
        out_specs=(VMEM,) * n,
        name="split",
    )(piece, after)


def join_kernel(*refs):
    n = len(refs) // 3
    for a_ref, b_ref, out_ref in zip(refs[:n], refs[n : 2 * n], refs[2 * n :]):
        k = a_ref.shape[0]
        out_ref[:k] = a_ref[...]
        out_ref[k:] = b_ref[...]


def join(held, more):
    n = len(held)
    shapes = tuple(jax.ShapeDtypeStruct((2 * h.shape[0],) + h.shape[1:], BF16) for h in held)
    return pl.pallas_call(
        join_kernel, out_shape=shapes, in_specs=[VMEM] * (2 * n), out_specs=(VMEM,) * n, name="join"
    )(*held, *more)


def lanes(ref, blocks):
    return jnp.concatenate([ref[:, at] for at in blocks], axis=1)


def half_products(half, groups, core, at_ref, tok_ref, w_refs, acc_ref, up_rel, take):
    xh = at_ref[2]
    each = w_refs[0].shape[0] // 8
    for n, g in enumerate(groups):
        for o in range(2):
            table = places(core ^ o, g)
            w_ref = w_refs[len(groups) * o + n]
            for a in range(2):
                zs = range(g * each, (g + 1) * each)
                blocks = [
                    pl.ds(pl.multiple_of((2 * (2 * z + (xh ^ a)) + (core ^ o)) * LANES, LANES), LANES) for z in zs
                ]
                found = table[half, a]
                total = None
                if found:
                    w = jnp.concatenate(
                        [
                            jnp.concatenate([w_ref[i * each + k] for _, i in found], axis=1)
                            for k in range(each)
                        ],
                        axis=0,
                    )
                    here = [slice((2 * b + l) * LANES, (2 * b + l + 1) * LANES) for (b, l), _ in found]
                    part = jnp.dot(lanes(tok_ref, blocks), w, preferred_element_type=F32)
                    for i, at in enumerate(here):
                        acc_ref[:, at] += part[:, i * LANES : (i + 1) * LANES]
                    total = lax.dot_general(
                        lanes(up_rel, here), w, (((1,), (1,)), ((), ())), preferred_element_type=F32
                    )
                take(g, a, o, blocks, total)


def columns(at_ref):
    y, xl = at_ref[1], at_ref[3]
    return [
        pl.ds(pl.multiple_of((2 * (y ^ (r // 2)) + (xl ^ (r % 2))) * LANES, LANES), LANES) for r in range(8)
    ]


def arrange(at_ref, up_ref, up_rel):
    for r, at in enumerate(columns(at_ref)):
        up_rel[:, r * LANES : (r + 1) * LANES] = up_ref[:, at]


def near_kernel(at_ref, tok_ref, up_ref, *refs):
    w_refs, (acc_ref, sum_ref, up_rel) = refs[:-3], refs[-3:]
    acc_ref[...] = jnp.zeros(acc_ref.shape, F32)
    arrange(at_ref, up_ref, up_rel)

    def take(g, a, o, blocks, total):
        if total is not None:
            sum_ref[(2 * g + a) * 2 + o] = total

    for core in range(2):

        @pl.when(at_ref[0] == core)
        def _():
            half_products(0, range(GROUPS), core, at_ref, tok_ref, w_refs, acc_ref, up_rel, take)


def far_kernel(at_ref, tok_ref, up_ref, before_ref, sum_ref, *refs, group, scale, last):
    w_refs = refs[:2]
    if last:
        part_ref, values_ref, grads_ref, acc_ref, up_rel = refs[2:]
        done = part_ref.shape[1]
        grads_ref[:, :done] = part_ref[...]
    else:
        acc_ref, grads_ref, up_rel = refs[2:]
    acc_ref[...] = before_ref[...]
    arrange(at_ref, up_ref, up_rel)

    for core in range(2):

        def take(g, a, o, blocks, total, core=core):
            if places(core ^ o, g)[0, a]:
                before = sum_ref[(2 * g + a) * 2 + o]
                total = before if total is None else total + before
            grad = (total * scale).astype(BF16)
            for k, at in enumerate(blocks):
                grads_ref[:, at] = grad[:, k * LANES : (k + 1) * LANES]

        @pl.when(at_ref[0] == core)
        def _():
            half_products(1, (group,), core, at_ref, tok_ref, w_refs, acc_ref, up_rel, take)

    if last:
        for r, at in enumerate(columns(at_ref)):
            values_ref[:, at] = (acc_ref[:, r * LANES : (r + 1) * LANES] * scale).astype(BF16)


def near_products(at, tokens, upstream, weights):
    t, d = tokens.shape
    kv = upstream.shape[1]
    return pl.pallas_call(
        near_kernel,
        out_shape=(
            jax.ShapeDtypeStruct((t, kv), F32),
            jax.ShapeDtypeStruct((4 * GROUPS, t, d // (4 * GROUPS)), F32),
        ),
        in_specs=[SMEM] + [VMEM] * (2 + len(weights)),
        out_specs=(VMEM, VMEM),
        scratch_shapes=[pltpu.VMEM((t, kv), BF16)],
        cost_estimate=pl.CostEstimate(flops=2 * t * d * kv, bytes_accessed=d * kv, transcendentals=0),
        name="near_products",
    )(at, tokens, upstream, *weights)


def far_products(at, tokens, upstream, acc, sums, weights, scale, group, part=None):
    t, d = tokens.shape
    kv = upstream.shape[1]
    last = part is not None
    rel = pltpu.VMEM((t, kv), BF16)
    if last:
        shapes = (jax.ShapeDtypeStruct((t, kv), BF16), jax.ShapeDtypeStruct((t, d), BF16))
        extra, scratch = (part,), [pltpu.VMEM((t, kv), F32), rel]
    else:
        shapes = (jax.ShapeDtypeStruct((t, kv), F32), jax.ShapeDtypeStruct((t, d // GROUPS), BF16))
        extra, scratch = (), [rel]
    return pl.pallas_call(
        functools.partial(far_kernel, group=group, scale=scale, last=last),
        out_shape=shapes,
        in_specs=[SMEM] + [VMEM] * (6 + len(extra)),
        out_specs=(VMEM, VMEM),
        scratch_shapes=scratch,
        cost_estimate=pl.CostEstimate(flops=t * d * kv, bytes_accessed=d * kv, transcendentals=0),
        name="far_products",
    )(at, tokens, upstream, acc, sums, *weights, *extra)


def step(tokens, upstream, params, momentum, projection):
    rows, _ = params.shape
    n_z, n_xh, n_c = (lax.axis_size(a) for a in FSDP)
    n_isl = lax.axis_size("y") * lax.axis_size("xl")
    fsdp_count = n_z * n_xh * n_c
    width = tokens.shape[1]
    proj = projection.shape[1]
    part = rows // n_isl
    inv_width = 1.0 / math.sqrt(width)
    scale_tok = 1.0 / math.sqrt(tokens.shape[0] * fsdp_count)
    at = jnp.stack([lax.axis_index(a).astype(jnp.int32) for a in ("c", "y", "xh", "xl")])
    swap = functools.partial(lax.ppermute, axis_name="c", perm=[(0, 1), (1, 0)])

    piece = make_piece(at, params, n_z, n_isl)
    got = swap(pick(at, tokens, piece))
    piece = lax.all_to_all(piece, "z", 0, 0, tiled=True)

    q = make_q(upstream, projection)
    got_q = swap(q)
    pair = make_sketch(at, tokens, got, q, got_q, n_z, n_xh)
    along = lax.all_to_all(pair, "z", 0, 0, tiled=True)
    held = split(piece, pair)
    for step in range(3):
        held = join(held, [exchange(h, g, step) for g, h in enumerate(held)])
    far = [exchange(h, g, 3) for g, h in enumerate(held)]
    acc, sums = near_products(at, tokens, upstream, [*held, *(swap(h) for h in held)])
    acc, grads = far_products(at, tokens, upstream, acc, sums, (far[0], swap(far[0])), inv_width, 0)
    values, token_grads = far_products(
        at, tokens, upstream, acc, sums, (far[1], swap(far[1])), inv_width, 1, grads
    )

    along = jnp.sum(along.astype(F32), axis=0).astype(BF16)
    plane = lax.all_to_all(along.reshape(n_xh * n_isl, part, proj), PLANE, 0, 0, tiled=True)
    total = jnp.sum(plane.astype(F32), axis=0).astype(BF16)
    total = jnp.broadcast_to(total[None], (n_isl, part, proj))
    total = lax.all_to_all(total, ISLAND, 0, 0, tiled=True)
    total = total.reshape(rows, proj)

    dims = (((1,), (1,)), ((), ()))
    head, rest = two_parts(projection)
    outer = lax.dot_general(total, head, dims, preferred_element_type=F32)
    outer = outer + lax.dot_general(total, rest, dims, preferred_element_type=F32)
    outer = outer * (scale_tok / (proj * n_isl))
    new_momentum = 0.9 * momentum + outer
    new_params = params - 0.7 * (outer + 0.9 * new_momentum)

    return (values, token_grads, new_params, new_momentum)


def solution(mesh):
    fine = Mesh(mesh.devices.reshape(4, 2, 8, 2, 2), ISLAND + FSDP)
    both = ISLAND + FSDP
    in_specs = (P(both, None), P(both, None), P(FSDP, None), P(FSDP, None), P())
    out_specs = (P(both, None), P(both, None), P(FSDP, None), P(FSDP, None))
    return jax.shard_map(step, mesh=fine, in_specs=in_specs, out_specs=out_specs, check_vma=False)
```

time: 124 us -> 129 us (1.040)
  Pallas kernels: 36.1 us -> 43.8 us
  starting transfers between devices: 46.2 us -> 43.9 us
    pallas_call x2 -> x4, Pallas kernels: 11.9 us -> 19.2 us  [the longest x2 14.6 us: far_products(): pl.pallas_call(functools.partial(far_kernel, group=group, scale=scale, la...]
    ppermute x25 -> x13, starting transfers between devices: 27.4 us -> 24.9 us  [the longest x8 9.64 us: exchange(): return lax.ppermute(x, ('y', 'xl', 'xh', 'c'), pairs)]
    ppermute x25 -> x13, waiting for transfers between devices: 26.2 us -> 25.6 us  [the longest x8 25.6 us: exchange(): return lax.ppermute(x, ('y', 'xl', 'xh', 'c'), pairs)]
    unnamed x46 -> x26, local copies, waits for them, and re-layouts: 5.07 us -> 4.6 us
  transfers between devices with their start and end apart: 30 -> 18, of which waited for: 14 -> 8; matrix products, arithmetic and copies ran while one was open for 1% -> 1% of each run, Pallas kernels for 27% -> 31%
where the time goes in v6:
time: 129 us; the launch traced here: 128 us
  starting transfers between devices  43.9 us (34%)
  Pallas kernels  43.8 us (34%)
  waiting for transfers between devices  30 us (23%)
  local copies, waits for them, and re-layouts  5.27 us (4%)
  matrix products  2 us (2%)
  other arithmetic  1.74 us (1%)
    ppermute x8, waiting for transfers between devices, exchange(): return lax.ppermute(x, ('y', 'xl', 'xh', 'c'), pairs)  25.6 us
    pallas_call x2, Pallas kernels, far_products(): pl.pallas_call(functools.partial(far_kernel, group=group, scale=scale, la...  14.6 us
    ppermute x8, starting transfers between devices, exchange(): return lax.ppermute(x, ('y', 'xl', 'xh', 'c'), pairs)  9.64 us
    pallas_call x1, Pallas kernels, near_products(): pl.pallas_call(near_kernel, out_shape=(jax.ShapeDtypeStruct((t, kv), F32)...  8.06 us
    pallas_call x3, Pallas kernels, join(): pl.pallas_call(join_kernel, out_shape=shapes, in_specs=[VMEM] * (2 * n),...  7.03 us
    all_to_all x1, starting transfers between devices, step(): piece = lax.all_to_all(piece, 'z', 0, 0, tiled=True)  6.48 us
    ppermute x1, starting transfers between devices, step(): swap(far[0])  5.86 us
    ppermute x2, starting transfers between devices, step(): swap(h)  5.37 us
  transfers between devices with their start and end apart: 18, of which 8 were waited for; matrix products, arithmetic and copies ran while one was open for 1% of the time, Pallas kernels for 31%

profile of v6, /device:TPU:1, one launch (start us, length us, event | category | flops | bytes accessed | tf_op | source)
XLA Modules:
  0.0 127.5 jit_solution(7760015701162599285)
XLA Ops:
  3.1 2.9 %pick.1 = bf16[256,2048]{1,0:T(8,128)(2,1)} custom-call(s32[4]{0:T(128)} %pad_add_fusion.at_ref, bf16[256,4096]{1,0:T(8,128)(2,1)} %tok_ref.7, bf16[8,128,128]{2,1,0:T(8,128)(2,1)} %make_piece.1.after_ref), custom_call_target="tpu_custom_call" | custom-call | tf_op jit(solution)/shard_map/pick/pallas_call | solution.py:56
  5.9 3.2 %collective-permute-start = (bf16[256,2048]{1,0:T(8,128)(2,1)}, bf16[256,2048]{1,0:T(8,128)(2,1)S(1)}, u32[]{:S(2)}, u32[]{:S(2)}) collective-permute-start(bf16[256,2048]{1,0:T(8,128)(2,1)} %pick.1), channel_id=1, source_target_pairs={{0,1},{1,0},{2,3},{3,2},{4,5},{5,4},{6,7},{7,6},{8,9},{9,8},{10,11... | collective-permute-start | bytes 3145736 | tf_op jit(solution)/shard_map/ppermute | solution.py:327
  9.1 3.2 %make_q.1.q_ref = bf16[256,512]{1,0:T(8,128)(2,1)} custom-call(bf16[256,1024]{1,0:T(8,128)(2,1)} %up_ref.7, f32[1024,512]{1,0:T(8,128)} %proj_ref.1), custom_call_target="tpu_custom_call" | custom-call | flops 1073741824 | bytes 3145728 | tf_op jit(solution)/shard_map/make_q/pallas_call | solution.py:73
  12.3 6.5 %all-to-all-start = ((bf16[8,128,128]{2,1,0:T(8,128)(2,1)}), bf16[8,128,128]{2,1,0:T(8,128)(2,1)S(1)}, u32[]{:S(2)}, u32[]{:S(2)}) async-start(bf16[8,128,128]{2,1,0:T(8,128)(2,1)} %make_piece.1.after_ref), calls=%async_computation | async-start | bytes 524288 | tf_op jit(solution)/shard_map/all_to_all | solution.py:328
  20.5 4.6 %make_sketch.1.after_ref = bf16[8,2,128,512]{3,2,1,0:T(8,128)(2,1)} custom-call(s32[4]{0:T(128)} %pad_add_fusion.at_ref, bf16[256,4096]{1,0:T(8,128)(2,1)} %tok_ref.7, bf16[256,2048]{1,0:T(8,128)(2,1)} %copy-done.11, bf16[256,512]{1,0:T(8,128)(2,1)} %make_q.1.q_ref, bf16[256,512]{1,0:T(8,128)(2,1)} %copy-done.12), custom_call_target="tpu_custom_call" | custom-call | flops 4294967296 | bytes 16777216 | tf_op jit(solution)/shard_map/make_sketch/pallas_call | solution.py:100
  25.1 4.4 %all-to-all-done.piece_ref = bf16[8,128,128]{2,1,0:T(8,128)(2,1)S(1)} async-done(((bf16[8,128,128]{2,1,0:T(8,128)(2,1)}), bf16[8,128,128]{2,1,0:T(8,128)(2,1)S(1)}, u32[]{:S(2)}, u32[]{:S(2)}) %all-to-all-start) | async-done | bytes 262176 | tf_op jit(solution)/shard_map/all_to_all | solution.py:328
  29.6 3.6 %all-to-all-start.1 = ((bf16[8,2,128,512]{3,2,1,0:T(8,128)(2,1)}), bf16[8,2,128,512]{3,2,1,0:T(8,128)(2,1)S(1)}, u32[]{:S(2)}, u32[]{:S(2)}) async-start(bf16[8,2,128,512]{3,2,1,0:T(8,128)(2,1)} %make_sketch.1.after_ref), calls=%async_computation.1 | async-start | bytes 4194304 | tf_op jit(solution)/shard_map/all_to_all | solution.py:333
  36.1 1.9 %collective-permute-start.3 = (bf16[4,128,128]{2,1,0:T(8,128)(2,1)}, bf16[4,128,128]{2,1,0:T(8,128)(2,1)S(1)}, u32[]{:S(2)}, u32[]{:S(2)}) collective-permute-start(bf16[4,128,128]{2,1,0:T(8,128)(2,1)} %get-tuple-element.19.refs_1_), channel_id=1, source_target_pairs={{0,32},{1,193},{2,34},{3,195},{32,0},{33,225},{34,2},{35,227},{64,... | collective-permute-start | bytes 393224 | tf_op jit(solution)/shard_map/ppermute | solution.py:128
  39.2 2.5 %collective-permute-done.3.refs_3_ = bf16[4,128,128]{2,1,0:T(8,128)(2,1)S(1)} collective-permute-done((bf16[4,128,128]{2,1,0:T(8,128)(2,1)}, bf16[4,128,128]{2,1,0:T(8,128)(2,1)S(1)}, u32[]{:S(2)}, u32[]{:S(2)}) %collective-permute-start.3) | collective-permute-done | bytes 131104 | tf_op jit(solution)/shard_map/ppermute | solution.py:128
  42.3 1.9 %join.3 = (bf16[8,128,128]{2,1,0:T(8,128)(2,1)}, bf16[8,128,128]{2,1,0:T(8,128)(2,1)}) custom-call(bf16[4,128,128]{2,1,0:T(8,128)(2,1)} %get-tuple-element.18.refs_0_, bf16[4,128,128]{2,1,0:T(8,128)(2,1)} %get-tuple-element.19.refs_1_, bf16[4,128,128]{2,1,0:T(8,128)(2,1)} %copy-done.9, bf16[4,128,128]{2,1,0:T(8,128)(2,1)} %copy-done.10), custom_call_target="tpu_custom_call" | custom-call | tf_op jit(solution)/shard_map/join/pallas_call | solution.py:175
  46.9 3.0 %collective-permute-done.4.refs_2_ = bf16[8,128,128]{2,1,0:T(8,128)(2,1)S(1)} collective-permute-done((bf16[8,128,128]{2,1,0:T(8,128)(2,1)}, bf16[8,128,128]{2,1,0:T(8,128)(2,1)S(1)}, u32[]{:S(2)}, u32[]{:S(2)}) %collective-permute-start.4) | collective-permute-done | bytes 262176 | tf_op jit(solution)/shard_map/ppermute | solution.py:128
  50.0 2.1 %collective-permute-done.5.refs_3_ = bf16[8,128,128]{2,1,0:T(8,128)(2,1)S(1)} collective-permute-done((bf16[8,128,128]{2,1,0:T(8,128)(2,1)}, bf16[8,128,128]{2,1,0:T(8,128)(2,1)S(1)}, u32[]{:S(2)}, u32[]{:S(2)}) %collective-permute-start.5) | collective-permute-done | bytes 262176 | tf_op jit(solution)/shard_map/ppermute | solution.py:128
  52.8 2.2 %join.4 = (bf16[16,128,128]{2,1,0:T(8,128)(2,1)}, bf16[16,128,128]{2,1,0:T(8,128)(2,1)}) custom-call(bf16[8,128,128]{2,1,0:T(8,128)(2,1)} %get-tuple-element.20.refs_0_, bf16[8,128,128]{2,1,0:T(8,128)(2,1)} %get-tuple-element.21.refs_1_, bf16[8,128,128]{2,1,0:T(8,128)(2,1)} %copy-done.7, bf16[8,128,128]{2,1,0:T(8,128)(2,1)} %copy-done.8), custom_call_target="tpu_custom_call" | custom-call | tf_op jit(solution)/shard_map/join/pallas_call | solution.py:175
  55.0 1.9 %collective-permute-start.6 = (bf16[16,128,128]{2,1,0:T(8,128)(2,1)}, bf16[16,128,128]{2,1,0:T(8,128)(2,1)S(1)}, u32[]{:S(2)}, u32[]{:S(2)}) collective-permute-start(bf16[16,128,128]{2,1,0:T(8,128)(2,1)} %get-tuple-element.22.refs_0_), channel_id=1, source_target_pairs={{0,32},{1,193},{2,34},{3,195},{32,0},{33,225},{34,2},{35,227},{64,... | collective-permute-start | bytes 1572872 | tf_op jit(solution)/shard_map/ppermute | solution.py:128
  56.9 7.8 %collective-permute-done.6.refs_2_ = bf16[16,128,128]{2,1,0:T(8,128)(2,1)S(1)} collective-permute-done((bf16[16,128,128]{2,1,0:T(8,128)(2,1)}, bf16[16,128,128]{2,1,0:T(8,128)(2,1)S(1)}, u32[]{:S(2)}, u32[]{:S(2)}) %collective-permute-start.6) | collective-permute-done | bytes 524320 | tf_op jit(solution)/shard_map/ppermute | solution.py:128
  66.3 3.0 %join.5 = (bf16[32,128,128]{2,1,0:T(8,128)(2,1)}, bf16[32,128,128]{2,1,0:T(8,128)(2,1)}) custom-call(bf16[16,128,128]{2,1,0:T(8,128)(2,1)} %get-tuple-element.22.refs_0_, bf16[16,128,128]{2,1,0:T(8,128)(2,1)} %get-tuple-element.23.refs_1_, bf16[16,128,128]{2,1,0:T(8,128)(2,1)} %copy-done.5, bf16[16,128,128]{2,1,0:T(8,128)(2,1)} %copy-done.6), custom_call_target="tpu_custom_call" | custom-call | tf_op jit(solution)/shard_map/join/pallas_call | solution.py:175
  71.1 5.4 %collective-permute-start.8 = (bf16[32,128,128]{2,1,0:T(8,128)(2,1)}, bf16[32,128,128]{2,1,0:T(8,128)(2,1)}, u32[]{:S(2)}, u32[]{:S(2)}) collective-permute-start(bf16[32,128,128]{2,1,0:T(8,128)(2,1)} %get-tuple-element.24.refs_0_), channel_id=1, source_target_pairs={{0,1},{1,0},{2,3},{3,2},{4,5},{5,4},{6,7},{7,6},{8,9},{9,8},{10,11... | collective-permute-start | bytes 3145736 | tf_op jit(solution)/shard_map/ppermute | solution.py:338
  76.4 8.3 %collective-permute-done.10.refs_0_ = bf16[32,128,128]{2,1,0:T(8,128)(2,1)} collective-permute-done((bf16[32,128,128]{2,1,0:T(8,128)(2,1)}, bf16[32,128,128]{2,1,0:T(8,128)(2,1)}, u32[]{:S(2)}, u32[]{:S(2)}) %collective-permute-start.10) | collective-permute-done | bytes 1048608 | tf_op jit(solution)/shard_map/ppermute | solution.py:128
  84.7 5.9 %collective-permute-start.11 = (bf16[32,128,128]{2,1,0:T(8,128)(2,1)}, bf16[32,128,128]{2,1,0:T(8,128)(2,1)}, u32[]{:S(2)}, u32[]{:S(2)}) collective-permute-start(bf16[32,128,128]{2,1,0:T(8,128)(2,1)} %collective-permute-done.10.refs_0_), channel_id=1, source_target_pairs={{0,1},{1,0},{2,3},{3,2},{4,5},{5,4},{6,7},{7,6},{8,9},{9,8},{10,11... | collective-permute-start | bytes 3145736 | tf_op jit(solution)/shard_map/ppermute | solution.py:339
  92.5 3.8 %all-to-all-start.2 = ((bf16[16,16,512]{2,1,0:T(8,128)(2,1)}), bf16[16,16,512]{2,1,0:T(8,128)(2,1)S(1)}, u32[]{:S(2)}, u32[]{:S(2)}) async-start(bf16[16,16,512]{2,1,0:T(8,128)(2,1)} %bitcast.4), calls=%async_computation.2 | async-start | bytes 524288 | tf_op jit(solution)/shard_map/all_to_all | solution.py:345
  96.4 8.1 %near_products.1 = (f32[256,1024]{1,0:T(8,128)}, f32[8,256,512]{2,1,0:T(8,128)}) custom-call(s32[4]{0:T(128)} %pad_add_fusion.at_ref, bf16[256,4096]{1,0:T(8,128)(2,1)} %tok_ref.7, bf16[256,1024]{1,0:T(8,128)(2,1)} %up_ref.7, bf16[32,128,128]{2,1,0:T(8,128)(2,1)} %get-tuple-element.24.refs_0_, bf16[32,128,128]{2,1,0:T(8,128)(2,1)} %get-tuple-element.25.refs_1_, ...), custom_call_target="tpu_custom_call" | custom-call | flops 2147483648 | bytes 4194304 | tf_op jit(solution)/shard_map/near_products/pallas_call | solution.py:277
  105.2 5.0 %all-to-all-start.3 = ((bf16[8,16,512]{2,1,0:T(8,128)(2,1)}), bf16[8,16,512]{2,1,0:T(8,128)(2,1)S(1)}, u32[]{:S(2)}, u32[]{:S(2)}) async-start(bf16[8,16,512]{2,1,0:T(8,128)(2,1)} %broadcast_in_dim.2), calls=%async_computation.3 | async-start | bytes 262144 | tf_op jit(solution)/shard_map/all_to_all | solution.py:348
  110.2 6.9 %far_products.2 = (f32[256,1024]{1,0:T(8,128)}, bf16[256,2048]{1,0:T(8,128)(2,1)}) custom-call(s32[4]{0:T(128)} %pad_add_fusion.at_ref, bf16[256,4096]{1,0:T(8,128)(2,1)} %tok_ref.7, bf16[256,1024]{1,0:T(8,128)(2,1)} %up_ref.7, f32[256,1024]{1,0:T(8,128)} %get-tuple-element.26.before_ref, f32[8,256,512]{2,1,0:T(8,128)} %get-tuple-element.27.sum_ref, ...), custom_call_target="tpu_custom_call" | custom-call | flops 1073741824 | bytes 4194304 | tf_op jit(solution)/shard_map/far_products/pallas_call | solution.py:302
  117.2 7.6 %far_products.3 = (bf16[256,1024]{1,0:T(8,128)(2,1)}, bf16[256,4096]{1,0:T(8,128)(2,1)}) custom-call(s32[4]{0:T(128)} %pad_add_fusion.at_ref, bf16[256,4096]{1,0:T(8,128)(2,1)} %tok_ref.7, bf16[256,1024]{1,0:T(8,128)(2,1)} %up_ref.7, f32[256,1024]{1,0:T(8,128)} %get-tuple-element.28.before_ref, f32[8,256,512]{2,1,0:T(8,128)} %get-tuple-element.27.sum_ref, ...), custom_call_target="tpu_custom_call" | custom-call | flops 1073741824 | bytes 4194304 | tf_op jit(solution)/shard_map/far_products/pallas_call | solution.py:302
  (55 shorter events, 21.0 us)
Async XLA Ops:
  5.9 12.9 %collective-permute-start = (bf16[256,2048]{1,0:T(8,128)(2,1)}, bf16[256,2048]{1,0:T(8,128)(2,1)S(1)}, u32[]{:S(2)}, u32[]{:S(2)}) collective-permute-start(bf16[256,2048]{1,0:T(8,128)(2,1)} %pick.1), channel_id=1, source_target_pairs={{0,1},{1,0},{2,3},{3,2},{4,5},{5,4},{6,7},{7,6},{8,9},{9,8},{10,11... | collective-permute-start | bytes 3145736 | tf_op jit(solution)/shard_map/ppermute | solution.py:327
  12.3 6.5 %collective-permute-start.1 = (bf16[256,512]{1,0:T(8,128)(2,1)}, bf16[256,512]{1,0:T(8,128)(2,1)S(1)}, u32[]{:S(2)}, u32[]{:S(2)}) collective-permute-start(bf16[256,512]{1,0:T(8,128)(2,1)} %make_q.1.q_ref), channel_id=1, source_target_pairs={{0,1},{1,0},{2,3},{3,2},{4,5},{5,4},{6,7},{7,6},{8,9},{9,8},{10,11... | collective-permute-start | bytes 786440 | tf_op jit(solution)/shard_map/ppermute | solution.py:331
  12.3 17.2 %all-to-all-start = ((bf16[8,128,128]{2,1,0:T(8,128)(2,1)}), bf16[8,128,128]{2,1,0:T(8,128)(2,1)S(1)}, u32[]{:S(2)}, u32[]{:S(2)}) async-start(bf16[8,128,128]{2,1,0:T(8,128)(2,1)} %make_piece.1.after_ref), calls=%async_computation | async-start | bytes 524288 | tf_op jit(solution)/shard_map/all_to_all | solution.py:328
  29.6 3.6 %copy-start.2 = (bf16[8,128,128]{2,1,0:T(8,128)(2,1)}, bf16[8,128,128]{2,1,0:T(8,128)(2,1)S(1)}, u32[]{:S(2)}) copy-start(bf16[8,128,128]{2,1,0:T(8,128)(2,1)S(1)} %all-to-all-done.piece_ref) | copy-start | bytes 786436
  29.6 61.9 %all-to-all-start.1 = ((bf16[8,2,128,512]{3,2,1,0:T(8,128)(2,1)}), bf16[8,2,128,512]{3,2,1,0:T(8,128)(2,1)S(1)}, u32[]{:S(2)}, u32[]{:S(2)}) async-start(bf16[8,2,128,512]{3,2,1,0:T(8,128)(2,1)} %make_sketch.1.after_ref), calls=%async_computation.1 | async-start | bytes 4194304 | tf_op jit(solution)/shard_map/all_to_all | solution.py:333
  34.8 4.3 %collective-permute-start.2 = (bf16[4,128,128]{2,1,0:T(8,128)(2,1)}, bf16[4,128,128]{2,1,0:T(8,128)(2,1)S(1)}, u32[]{:S(2)}, u32[]{:S(2)}) collective-permute-start(bf16[4,128,128]{2,1,0:T(8,128)(2,1)} %get-tuple-element.18.refs_0_), channel_id=1, source_target_pairs={{0,34},{1,65},{2,32},{3,67},{32,2},{33,97},{34,0},{35,99},{64,98},... | collective-permute-start | bytes 393224 | tf_op jit(solution)/shard_map/ppermute | solution.py:128
  36.1 5.5 %collective-permute-start.3 = (bf16[4,128,128]{2,1,0:T(8,128)(2,1)}, bf16[4,128,128]{2,1,0:T(8,128)(2,1)S(1)}, u32[]{:S(2)}, u32[]{:S(2)}) collective-permute-start(bf16[4,128,128]{2,1,0:T(8,128)(2,1)} %get-tuple-element.19.refs_1_), channel_id=1, source_target_pairs={{0,32},{1,193},{2,34},{3,195},{32,0},{33,225},{34,2},{35,227},{64,... | collective-permute-start | bytes 393224 | tf_op jit(solution)/shard_map/ppermute | solution.py:128
  39.2 2.5 %copy-start.9 = (bf16[4,128,128]{2,1,0:T(8,128)(2,1)}, bf16[4,128,128]{2,1,0:T(8,128)(2,1)S(1)}, u32[]{:S(2)}) copy-start(bf16[4,128,128]{2,1,0:T(8,128)(2,1)S(1)} %collective-permute-done.2.refs_2_) | copy-start | bytes 393220
  44.2 5.7 %collective-permute-start.4 = (bf16[8,128,128]{2,1,0:T(8,128)(2,1)}, bf16[8,128,128]{2,1,0:T(8,128)(2,1)S(1)}, u32[]{:S(2)}, u32[]{:S(2)}) collective-permute-start(bf16[8,128,128]{2,1,0:T(8,128)(2,1)} %get-tuple-element.20.refs_0_), channel_id=1, source_target_pairs={{0,64},{1,33},{2,66},{3,35},{32,96},{33,1},{34,98},{35,3},{64,0},{... | collective-permute-start | bytes 786440 | tf_op jit(solution)/shard_map/ppermute | solution.py:128
  45.1 6.9 %collective-permute-start.5 = (bf16[8,128,128]{2,1,0:T(8,128)(2,1)}, bf16[8,128,128]{2,1,0:T(8,128)(2,1)S(1)}, u32[]{:S(2)}, u32[]{:S(2)}) collective-permute-start(bf16[8,128,128]{2,1,0:T(8,128)(2,1)} %get-tuple-element.21.refs_1_), channel_id=1, source_target_pairs={{0,192},{1,35},{2,194},{3,33},{32,224},{33,3},{34,226},{35,1},{64,... | collective-permute-start | bytes 786440 | tf_op jit(solution)/shard_map/ppermute | solution.py:128
  49.9 2.1 %copy-start.7 = (bf16[8,128,128]{2,1,0:T(8,128)(2,1)}, bf16[8,128,128]{2,1,0:T(8,128)(2,1)S(1)}, u32[]{:S(2)}) copy-start(bf16[8,128,128]{2,1,0:T(8,128)(2,1)S(1)} %collective-permute-done.4.refs_2_) | copy-start | bytes 786436
  55.0 9.7 %collective-permute-start.6 = (bf16[16,128,128]{2,1,0:T(8,128)(2,1)}, bf16[16,128,128]{2,1,0:T(8,128)(2,1)S(1)}, u32[]{:S(2)}, u32[]{:S(2)}) collective-permute-start(bf16[16,128,128]{2,1,0:T(8,128)(2,1)} %get-tuple-element.22.refs_0_), channel_id=1, source_target_pairs={{0,32},{1,193},{2,34},{3,195},{32,0},{33,225},{34,2},{35,227},{64,... | collective-permute-start | bytes 1572872 | tf_op jit(solution)/shard_map/ppermute | solution.py:128
  56.9 8.5 %collective-permute-start.7 = (bf16[16,128,128]{2,1,0:T(8,128)(2,1)}, bf16[16,128,128]{2,1,0:T(8,128)(2,1)S(1)}, u32[]{:S(2)}, u32[]{:S(2)}) collective-permute-start(bf16[16,128,128]{2,1,0:T(8,128)(2,1)} %get-tuple-element.23.refs_1_), channel_id=1, source_target_pairs={{0,34},{1,65},{2,32},{3,67},{32,2},{33,97},{34,0},{35,99},{64,98},... | collective-permute-start | bytes 1572872 | tf_op jit(solution)/shard_map/ppermute | solution.py:128
  69.2 15.5 %collective-permute-start.10 = (bf16[32,128,128]{2,1,0:T(8,128)(2,1)}, bf16[32,128,128]{2,1,0:T(8,128)(2,1)}, u32[]{:S(2)}, u32[]{:S(2)}) collective-permute-start(bf16[32,128,128]{2,1,0:T(8,128)(2,1)} %get-tuple-element.24.refs_0_), channel_id=1, source_target_pairs={{0,192},{1,35},{2,194},{3,33},{32,224},{33,3},{34,226},{35,1},{64,... | collective-permute-start | bytes 3145736 | tf_op jit(solution)/shard_map/ppermute | solution.py:128
  71.1 19.5 %collective-permute-start.12 = (bf16[32,128,128]{2,1,0:T(8,128)(2,1)}, bf16[32,128,128]{2,1,0:T(8,128)(2,1)S(1)}, u32[]{:S(2)}, u32[]{:S(2)}) collective-permute-start(bf16[32,128,128]{2,1,0:T(8,128)(2,1)} %get-tuple-element.25.refs_1_), channel_id=1, source_target_pairs={{0,64},{1,33},{2,66},{3,35},{32,96},{33,1},{34,98},{35,3},{64,0},{... | collective-permute-start | bytes 3145736 | tf_op jit(solution)/shard_map/ppermute | solution.py:128
  71.1 25.3 %collective-permute-start.8 = (bf16[32,128,128]{2,1,0:T(8,128)(2,1)}, bf16[32,128,128]{2,1,0:T(8,128)(2,1)}, u32[]{:S(2)}, u32[]{:S(2)}) collective-permute-start(bf16[32,128,128]{2,1,0:T(8,128)(2,1)} %get-tuple-element.24.refs_0_), channel_id=1, source_target_pairs={{0,1},{1,0},{2,3},{3,2},{4,5},{5,4},{6,7},{7,6},{8,9},{9,8},{10,11... | collective-permute-start | bytes 3145736 | tf_op jit(solution)/shard_map/ppermute | solution.py:338
  76.4 19.9 %collective-permute-start.9 = (bf16[32,128,128]{2,1,0:T(8,128)(2,1)}, bf16[32,128,128]{2,1,0:T(8,128)(2,1)}, u32[]{:S(2)}, u32[]{:S(2)}) collective-permute-start(bf16[32,128,128]{2,1,0:T(8,128)(2,1)} %get-tuple-element.25.refs_1_), channel_id=1, source_target_pairs={{0,1},{1,0},{2,3},{3,2},{4,5},{5,4},{6,7},{7,6},{8,9},{9,8},{10,11... | collective-permute-start | bytes 3145736 | tf_op jit(solution)/shard_map/ppermute | solution.py:338
  84.7 25.5 %collective-permute-start.11 = (bf16[32,128,128]{2,1,0:T(8,128)(2,1)}, bf16[32,128,128]{2,1,0:T(8,128)(2,1)}, u32[]{:S(2)}, u32[]{:S(2)}) collective-permute-start(bf16[32,128,128]{2,1,0:T(8,128)(2,1)} %collective-permute-done.10.refs_0_), channel_id=1, source_target_pairs={{0,1},{1,0},{2,3},{3,2},{4,5},{5,4},{6,7},{7,6},{8,9},{9,8},{10,11... | collective-permute-start | bytes 3145736 | tf_op jit(solution)/shard_map/ppermute | solution.py:339
  90.6 13.9 %copy-start.3 = (bf16[32,128,128]{2,1,0:T(8,128)(2,1)}, bf16[32,128,128]{2,1,0:T(8,128)(2,1)S(1)}, u32[]{:S(2)}) copy-start(bf16[32,128,128]{2,1,0:T(8,128)(2,1)S(1)} %collective-permute-done.12.refs_0_) | copy-start | bytes 3145732
  90.6 26.6 %collective-permute-start.13 = (bf16[32,128,128]{2,1,0:T(8,128)(2,1)S(1)}, bf16[32,128,128]{2,1,0:T(8,128)(2,1)}, u32[]{:S(2)}, u32[]{:S(2)}) collective-permute-start(bf16[32,128,128]{2,1,0:T(8,128)(2,1)S(1)} %collective-permute-done.12.refs_0_), channel_id=1, source_target_pairs={{0,1},{1,0},{2,3},{3,2},{4,5},{5,4},{6,7},{7,6},{8,9},{9,8},{10,11... | collective-permute-start | bytes 3145736 | tf_op jit(solution)/shard_map/ppermute | solution.py:341
  92.5 11.9 %all-to-all-start.2 = ((bf16[16,16,512]{2,1,0:T(8,128)(2,1)}), bf16[16,16,512]{2,1,0:T(8,128)(2,1)S(1)}, u32[]{:S(2)}, u32[]{:S(2)}) async-start(bf16[16,16,512]{2,1,0:T(8,128)(2,1)} %bitcast.4), calls=%async_computation.2 | async-start | bytes 524288 | tf_op jit(solution)/shard_map/all_to_all | solution.py:345
  105.2 19.7 %all-to-all-start.3 = ((bf16[8,16,512]{2,1,0:T(8,128)(2,1)}), bf16[8,16,512]{2,1,0:T(8,128)(2,1)S(1)}, u32[]{:S(2)}, u32[]{:S(2)}) async-start(bf16[8,16,512]{2,1,0:T(8,128)(2,1)} %broadcast_in_dim.2), calls=%async_computation.3 | async-start | bytes 262144 | tf_op jit(solution)/shard_map/all_to_all | solution.py:348
  117.2 7.7 %copy-start = (f32[1024,512]{1,0:T(8,128)S(1)}, f32[1024,512]{1,0:T(8,128)}, u32[]{:S(2)}) copy-start(f32[1024,512]{1,0:T(8,128)} %proj_ref.1) | copy-start | bytes 6291460
  124.8 1.2 copy-start.4
  (7 other events, 5.7 us)

commit v7 on v6

--- a/solution.py
+++ b/solution.py
@@ -159,22 +159,6 @@
         out_specs=(VMEM,) * n,
         name="split",
     )(piece, after)
-
-
-def join_kernel(*refs):
-    n = len(refs) // 3
-    for a_ref, b_ref, out_ref in zip(refs[:n], refs[n : 2 * n], refs[2 * n :]):
-        k = a_ref.shape[0]
-        out_ref[:k] = a_ref[...]
-        out_ref[k:] = b_ref[...]
-
-
-def join(held, more):
-    n = len(held)
-    shapes = tuple(jax.ShapeDtypeStruct((2 * h.shape[0],) + h.shape[1:], BF16) for h in held)
-    return pl.pallas_call(
-        join_kernel, out_shape=shapes, in_specs=[VMEM] * (2 * n), out_specs=(VMEM,) * n, name="join"
-    )(*held, *more)
 
 
 def lanes(ref, blocks):
@@ -226,13 +210,13 @@
 
 
 def near_kernel(at_ref, tok_ref, up_ref, *refs):
-    w_refs, (acc_ref, sum_ref, up_rel) = refs[:-3], refs[-3:]
+    w_refs, (acc_ref, *sum_refs, up_rel) = refs[: 2 * GROUPS], refs[2 * GROUPS :]
     acc_ref[...] = jnp.zeros(acc_ref.shape, F32)
     arrange(at_ref, up_ref, up_rel)
 
     def take(g, a, o, blocks, total):
         if total is not None:
-            sum_ref[(2 * g + a) * 2 + o] = total
+            sum_refs[g][2 * a + o] = total
 
     for core in range(2):
 
@@ -256,7 +240,7 @@
 
         def take(g, a, o, blocks, total, core=core):
             if places(core ^ o, g)[0, a]:
-                before = sum_ref[(2 * g + a) * 2 + o]
+                before = sum_ref[2 * a + o]
                 total = before if total is None else total + before
             grad = (total * scale).astype(BF16)
             for k, at in enumerate(blocks):
@@ -278,10 +262,10 @@
         near_kernel,
         out_shape=(
             jax.ShapeDtypeStruct((t, kv), F32),
-            jax.ShapeDtypeStruct((4 * GROUPS, t, d // (4 * GROUPS)), F32),
+            *[jax.ShapeDtypeStruct((4, t, d // (4 * GROUPS)), F32)] * GROUPS,
         ),
         in_specs=[SMEM] + [VMEM] * (2 + len(weights)),
-        out_specs=(VMEM, VMEM),
+        out_specs=(VMEM,) * (1 + GROUPS),
         scratch_shapes=[pltpu.VMEM((t, kv), BF16)],
         cost_estimate=pl.CostEstimate(flops=2 * t * d * kv, bytes_accessed=d * kv, transcendentals=0),
         name="near_products",
@@ -324,7 +308,8 @@
     swap = functools.partial(lax.ppermute, axis_name="c", perm=[(0, 1), (1, 0)])
 
     piece = make_piece(at, params, n_z, n_isl)
-    got = swap(pick(at, tokens, piece))
+    other = pick(at, tokens, piece)
+    got = swap(other)
     piece = lax.all_to_all(piece, "z", 0, 0, tiled=True)
 
     q = make_q(upstream, projection)
@@ -333,12 +318,14 @@
     along = lax.all_to_all(pair, "z", 0, 0, tiled=True)
     held = split(piece, pair)
     for step in range(3):
-        held = join(held, [exchange(h, g, step) for g, h in enumerate(held)])
+        held = [jnp.concatenate([h, exchange(h, g, step)], axis=0) for g, h in enumerate(held)]
     far = [exchange(h, g, 3) for g, h in enumerate(held)]
-    acc, sums = near_products(at, tokens, upstream, [*held, *(swap(h) for h in held)])
-    acc, grads = far_products(at, tokens, upstream, acc, sums, (far[0], swap(far[0])), inv_width, 0)
+    acc, *sums = near_products(at, tokens, upstream, [*held, *(swap(h) for h in held)])
+    acc, grads = far_products(
+        at, tokens, upstream, acc, sums[0], (far[0], swap(far[0])), inv_width, 0
+    )
     values, token_grads = far_products(
-        at, tokens, upstream, acc, sums, (far[1], swap(far[1])), inv_width, 1, grads
+        at, tokens, upstream, acc, sums[1], (far[1], swap(far[1])), inv_width, 1, grads
     )
 
     along = jnp.sum(along.astype(F32), axis=0).astype(BF16)

time: 129 us -> 125 us (0.969)
  waiting for transfers between devices: 30 us -> 20.2 us
  starting transfers between devices: 43.9 us -> 53.6 us
  Pallas kernels: 43.8 us -> 35.6 us
  other arithmetic: 1.74 us -> 4.61 us
  local copies, waits for them, and re-layouts: 5.27 us -> 7.05 us
    ppermute x8, waiting for transfers between devices: 25.6 us -> 15.6 us  [exchange(): return lax.ppermute(x, ('y', 'xl', 'xh', 'c'), pairs)]
    ppermute x1, starting transfers between devices: 0.86 us -> 8.5 us  [step(): swap(far[1])]
    pallas_call x3 -> x0, Pallas kernels: 7.03 us -> none  [join(): pl.pallas_call(join_kernel, out_shape=shapes, in_specs=[VMEM] * (2 * n),...]
    ppermute x1, starting transfers between devices: 5.86 us -> 0.01 us  [step(): swap(far[0])]
    ppermute x2, starting transfers between devices: 5.37 us -> 9.58 us  [step(): swap(h)]
    concatenate x0 -> x4, other arithmetic: none -> 2.87 us  [step(): jnp.concatenate([h, exchange(h, g, step)], axis=0)]
    ppermute x8, starting transfers between devices: 9.64 us -> 11.6 us  [exchange(): return lax.ppermute(x, ('y', 'xl', 'xh', 'c'), pairs)]
    all_to_all x1, starting transfers between devices: 3.85 us -> 5.68 us  [step(): lax.all_to_all(along.reshape(n_xh * n_isl, part, proj), PLANE, 0, 0, tile...]
  transfers between devices with their start and end apart: 18 -> 18, of which waited for: 8 -> 7; matrix products, arithmetic and copies ran while one was open for 1% -> 7% of each run, Pallas kernels for 31% -> 25%
where the time goes in v7:
time: 125 us; the launch traced here: 124 us
  starting transfers between devices  53.6 us (43%)
  Pallas kernels  35.6 us (28%)
  waiting for transfers between devices  20.2 us (16%)
  local copies, waits for them, and re-layouts  7.05 us (6%)
  other arithmetic  4.61 us (4%)
  matrix products  2 us (2%)
    ppermute x8, waiting for transfers between devices, exchange(): return lax.ppermute(x, ('y', 'xl', 'xh', 'c'), pairs)  15.6 us
    pallas_call x2, Pallas kernels, far_products(): pl.pallas_call(functools.partial(far_kernel, group=group, scale=scale, la...  13.4 us
    ppermute x8, starting transfers between devices, exchange(): return lax.ppermute(x, ('y', 'xl', 'xh', 'c'), pairs)  11.6 us
    ppermute x2, starting transfers between devices, step(): swap(h)  9.58 us
    ppermute x1, starting transfers between devices, step(): swap(far[1])  8.5 us
    pallas_call x1, Pallas kernels, near_products(): pl.pallas_call(near_kernel, out_shape=(jax.ShapeDtypeStruct((t, kv), F32)...  8.13 us
    all_to_all x1, starting transfers between devices, step(): piece = lax.all_to_all(piece, 'z', 0, 0, tiled=True)  6.48 us
    all_to_all x1, starting transfers between devices, step(): lax.all_to_all(along.reshape(n_xh * n_isl, part, proj), PLANE, 0, 0, tile...  5.68 us
  transfers between devices with their start and end apart: 18, of which 7 were waited for; matrix products, arithmetic and copies ran while one was open for 7% of the time, Pallas kernels for 25%

profile of v7, /device:TPU:1, one launch (start us, length us, event | category | flops | bytes accessed | tf_op | source)
XLA Modules:
  0.0 123.9 jit_solution(17193851537945192344)
XLA Ops:
  1.3 1.8 %make_piece.1.after_ref = bf16[8,128,128]{2,1,0:T(8,128)(2,1)} custom-call(s32[4]{0:T(128)} %pad_add_fusion.at_ref, f32[128,1024]{1,0:T(8,128)} %params_ref.1), custom_call_target="tpu_custom_call" | custom-call | tf_op jit(solution)/shard_map/make_piece/pallas_call | solution.py:38
  3.1 2.9 %pick.1 = bf16[256,2048]{1,0:T(8,128)(2,1)} custom-call(s32[4]{0:T(128)} %pad_add_fusion.at_ref, bf16[256,4096]{1,0:T(8,128)(2,1)} %tok_ref.7, bf16[8,128,128]{2,1,0:T(8,128)(2,1)} %make_piece.1.after_ref), custom_call_target="tpu_custom_call" | custom-call | tf_op jit(solution)/shard_map/pick/pallas_call | solution.py:56
  5.9 3.2 %collective-permute-start = (bf16[256,2048]{1,0:T(8,128)(2,1)}, bf16[256,2048]{1,0:T(8,128)(2,1)S(1)}, u32[]{:S(2)}, u32[]{:S(2)}) collective-permute-start(bf16[256,2048]{1,0:T(8,128)(2,1)} %pick.1), channel_id=1, source_target_pairs={{0,1},{1,0},{2,3},{3,2},{4,5},{5,4},{6,7},{7,6},{8,9},{9,8},{10,11... | collective-permute-start | bytes 3145736 | tf_op jit(solution)/shard_map/ppermute | solution.py:312
  9.1 3.2 %make_q.1.q_ref = bf16[256,512]{1,0:T(8,128)(2,1)} custom-call(bf16[256,1024]{1,0:T(8,128)(2,1)} %up_ref.7, f32[1024,512]{1,0:T(8,128)} %proj_ref.1), custom_call_target="tpu_custom_call" | custom-call | flops 1073741824 | bytes 3145728 | tf_op jit(solution)/shard_map/make_q/pallas_call | solution.py:73
  12.3 6.5 %all-to-all-start = ((bf16[8,128,128]{2,1,0:T(8,128)(2,1)}), bf16[8,128,128]{2,1,0:T(8,128)(2,1)S(1)}, u32[]{:S(2)}, u32[]{:S(2)}) async-start(bf16[8,128,128]{2,1,0:T(8,128)(2,1)} %make_piece.1.after_ref), calls=%async_computation | async-start | bytes 524288 | tf_op jit(solution)/shard_map/all_to_all | solution.py:313
  20.5 4.6 %make_sketch.1.after_ref = bf16[8,2,128,512]{3,2,1,0:T(8,128)(2,1)} custom-call(s32[4]{0:T(128)} %pad_add_fusion.at_ref, bf16[256,4096]{1,0:T(8,128)(2,1)} %tok_ref.7, bf16[256,2048]{1,0:T(8,128)(2,1)} %copy-done.6, bf16[256,512]{1,0:T(8,128)(2,1)} %make_q.1.q_ref, bf16[256,512]{1,0:T(8,128)(2,1)} %copy-done.7), custom_call_target="tpu_custom_call" | custom-call | flops 4294967296 | bytes 16777216 | tf_op jit(solution)/shard_map/make_sketch/pallas_call | solution.py:100
  25.2 4.4 %all-to-all-done.piece_ref = bf16[8,128,128]{2,1,0:T(8,128)(2,1)S(1)} async-done(((bf16[8,128,128]{2,1,0:T(8,128)(2,1)}), bf16[8,128,128]{2,1,0:T(8,128)(2,1)S(1)}, u32[]{:S(2)}, u32[]{:S(2)}) %all-to-all-start) | async-done | bytes 262176 | tf_op jit(solution)/shard_map/all_to_all | solution.py:313
  29.6 3.6 %all-to-all-start.1 = ((bf16[8,2,128,512]{3,2,1,0:T(8,128)(2,1)}), bf16[8,2,128,512]{3,2,1,0:T(8,128)(2,1)S(1)}, u32[]{:S(2)}, u32[]{:S(2)}) async-start(bf16[8,2,128,512]{3,2,1,0:T(8,128)(2,1)} %make_sketch.1.after_ref), calls=%async_computation.1 | async-start | bytes 4194304 | tf_op jit(solution)/shard_map/all_to_all | solution.py:318
  33.2 1.7 %split.1 = (bf16[4,128,128]{2,1,0:T(8,128)(2,1)}, bf16[4,128,128]{2,1,0:T(8,128)(2,1)}) custom-call(bf16[8,128,128]{2,1,0:T(8,128)(2,1)} %copy-done.3, bf16[8,2,128,512]{3,2,1,0:T(8,128)(2,1)} %make_sketch.1.after_ref), custom_call_target="tpu_custom_call" | custom-call | tf_op jit(solution)/shard_map/split/pallas_call | solution.py:155
  36.1 1.9 %collective-permute-start.5 = (bf16[4,128,128]{2,1,0:T(8,128)(2,1)}, bf16[4,128,128]{2,1,0:T(8,128)(2,1)S(1)}, u32[]{:S(2)}, u32[]{:S(2)}) collective-permute-start(bf16[4,128,128]{2,1,0:T(8,128)(2,1)} %get-tuple-element.14), channel_id=1, source_target_pairs={{0,32},{1,193},{2,34},{3,195},{32,0},{33,225},{34,2},{35,227},{64,... | collective-permute-start | bytes 393224 | tf_op jit(solution)/shard_map/ppermute | solution.py:128
  42.6 2.6 %collective-permute-start.6 = (bf16[8,128,128]{2,1,0:T(8,128)(2,1)S(1)}, bf16[8,128,128]{2,1,0:T(8,128)(2,1)S(1)}, u32[]{:S(2)}, u32[]{:S(2)}) collective-permute-start(bf16[8,128,128]{2,1,0:T(8,128)(2,1)S(1)} %pad_maximum_fusion.3), channel_id=1, source_target_pairs={{0,192},{1,35},{2,194},{3,33},{32,224},{33,3},{34,226},{35,1},{64,... | collective-permute-start | bytes 786440 | tf_op jit(solution)/shard_map/ppermute | solution.py:128
  45.2 1.6 %constant_dynamic-update-slice_fusion.3 = (bf16[32,128,128]{2,1,0:T(8,128)(2,1)S(1)}, bf16[32,128,128]{2,1,0:T(8,128)(2,1)}) fusion(bf16[4,128,128]{2,1,0:T(8,128)(2,1)} %get-tuple-element.13, bf16[4,128,128]{2,1,0:T(8,128)(2,1)} %get-tuple-element.14), kind=kLoop, calls=%fused_computation.15 | loop fusion | bytes 524288
  48.1 2.8 %collective-permute-start.4 = (bf16[16,128,128]{2,1,0:T(8,128)(2,1)S(1)}, bf16[16,128,128]{2,1,0:T(8,128)(2,1)S(1)}, u32[]{:S(2)}, u32[]{:S(2)}) collective-permute-start(bf16[16,128,128]{2,1,0:T(8,128)(2,1)S(1)} %pad_maximum_fusion), channel_id=1, source_target_pairs={{0,32},{1,193},{2,34},{3,195},{32,0},{33,225},{34,2},{35,227},{64,... | collective-permute-start | bytes 1572872 | tf_op jit(solution)/shard_map/ppermute | solution.py:128
  52.5 7.6 %collective-permute-done.4 = bf16[16,128,128]{2,1,0:T(8,128)(2,1)S(1)} collective-permute-done((bf16[16,128,128]{2,1,0:T(8,128)(2,1)S(1)}, bf16[16,128,128]{2,1,0:T(8,128)(2,1)S(1)}, u32[]{:S(2)}, u32[]{:S(2)}) %collective-permute-start.4) | collective-permute-done | bytes 524320 | tf_op jit(solution)/shard_map/ppermute | solution.py:128
  60.2 1.6 %collective-permute-start.10 = (bf16[32,128,128]{2,1,0:T(8,128)(2,1)S(1)}, bf16[32,128,128]{2,1,0:T(8,128)(2,1)}, u32[]{:S(2)}, u32[]{:S(2)}) collective-permute-start(bf16[32,128,128]{2,1,0:T(8,128)(2,1)S(1)} %constant_dynamic-update-slice_fusion.refs_0_), channel_id=1, source_target_pairs={{0,192},{1,35},{2,194},{3,33},{32,224},{33,3},{34,226},{35,1},{64,... | collective-permute-start | bytes 3145736 | tf_op jit(solution)/shard_map/ppermute | solution.py:128
  62.7 9.6 %collective-permute-start.9 = (bf16[32,128,128]{2,1,0:T(8,128)(2,1)}, bf16[32,128,128]{2,1,0:T(8,128)(2,1)}, u32[]{:S(2)}, u32[]{:S(2)}) collective-permute-start(bf16[32,128,128]{2,1,0:T(8,128)(2,1)} %constant_dynamic-update-slice_fusion.4.refs_1_), channel_id=1, source_target_pairs={{0,1},{1,0},{2,3},{3,2},{4,5},{5,4},{6,7},{7,6},{8,9},{9,8},{10,11... | collective-permute-start | bytes 3145736 | tf_op jit(solution)/shard_map/ppermute | solution.py:323
  72.3 6.3 %collective-permute-done.10.refs_0_ = bf16[32,128,128]{2,1,0:T(8,128)(2,1)} collective-permute-done((bf16[32,128,128]{2,1,0:T(8,128)(2,1)S(1)}, bf16[32,128,128]{2,1,0:T(8,128)(2,1)}, u32[]{:S(2)}, u32[]{:S(2)}) %collective-permute-start.10) | collective-permute-done | bytes 1048608 | tf_op jit(solution)/shard_map/ppermute | solution.py:128
  78.6 8.5 %collective-permute-start.13 = (bf16[32,128,128]{2,1,0:T(8,128)(2,1)}, bf16[32,128,128]{2,1,0:T(8,128)(2,1)}, u32[]{:S(2)}, u32[]{:S(2)}) collective-permute-start(bf16[32,128,128]{2,1,0:T(8,128)(2,1)} %collective-permute-done.12.refs_0_), channel_id=1, source_target_pairs={{0,1},{1,0},{2,3},{3,2},{4,5},{5,4},{6,7},{7,6},{8,9},{9,8},{10,11... | collective-permute-start | bytes 3145736 | tf_op jit(solution)/shard_map/ppermute | solution.py:328
  88.2 5.7 %all-to-all-start.2 = ((bf16[16,16,512]{2,1,0:T(8,128)(2,1)}), bf16[16,16,512]{2,1,0:T(8,128)(2,1)S(1)}, u32[]{:S(2)}, u32[]{:S(2)}) async-start(bf16[16,16,512]{2,1,0:T(8,128)(2,1)} %bitcast.4), calls=%async_computation.2 | async-start | bytes 524288 | tf_op jit(solution)/shard_map/all_to_all | solution.py:332
  93.9 8.1 %near_products.1 = (f32[256,1024]{1,0:T(8,128)}, f32[4,256,512]{2,1,0:T(8,128)}, f32[4,256,512]{2,1,0:T(8,128)}) custom-call(s32[4]{0:T(128)} %pad_add_fusion.at_ref, bf16[256,4096]{1,0:T(8,128)(2,1)} %tok_ref.7, bf16[256,1024]{1,0:T(8,128)(2,1)} %up_ref.7, bf16[32,128,128]{2,1,0:T(8,128)(2,1)} %copy-done.5, ...), custom_call_target="tpu_custom_call" | custom-call | flops 2147483648 | bytes 4194304 | tf_op jit(solution)/shard_map/near_products/pallas_call | solution.py:261
  102.8 4.9 %all-to-all-start.3 = ((bf16[8,16,512]{2,1,0:T(8,128)(2,1)}), bf16[8,16,512]{2,1,0:T(8,128)(2,1)S(1)}, u32[]{:S(2)}, u32[]{:S(2)}) async-start(bf16[8,16,512]{2,1,0:T(8,128)(2,1)} %broadcast_in_dim.2), calls=%async_computation.3 | async-start | bytes 262144 | tf_op jit(solution)/shard_map/all_to_all | solution.py:335
  107.8 6.3 %far_products.2 = (f32[256,1024]{1,0:T(8,128)}, bf16[256,2048]{1,0:T(8,128)(2,1)}) custom-call(s32[4]{0:T(128)} %pad_add_fusion.at_ref, bf16[256,4096]{1,0:T(8,128)(2,1)} %tok_ref.7, bf16[256,1024]{1,0:T(8,128)(2,1)} %up_ref.7, f32[256,1024]{1,0:T(8,128)} %get-tuple-element.15.before_ref, f32[4,256,512]{2,1,0:T(8,128)} %get-tuple-element.16.sum_ref, ...), custom_call_target="tpu_custom_call" | custom-call | flops 1073741824 | bytes 4194304 | tf_op jit(solution)/shard_map/far_products/pallas_call | solution.py:286
  114.1 7.0 %far_products.3 = (bf16[256,1024]{1,0:T(8,128)(2,1)}, bf16[256,4096]{1,0:T(8,128)(2,1)}) custom-call(s32[4]{0:T(128)} %pad_add_fusion.at_ref, bf16[256,4096]{1,0:T(8,128)(2,1)} %tok_ref.7, bf16[256,1024]{1,0:T(8,128)(2,1)} %up_ref.7, f32[256,1024]{1,0:T(8,128)} %get-tuple-element.17.before_ref, f32[4,256,512]{2,1,0:T(8,128)} %get-tuple-element.18.sum_ref, ...), custom_call_target="tpu_custom_call" | custom-call | flops 1073741824 | bytes 4194304 | tf_op jit(solution)/shard_map/far_products/pallas_call | solution.py:286
  122.3 1.5 %multiply_subtract_fusion = (f32[128,1024]{1,0:T(8,128)}, f32[128,1024]{1,0:T(8,128)}) fusion(f32[128,1024]{1,0:T(8,128)S(1)} %copy-done.1, f32[128,1024]{1,0:T(8,128)S(1)} %copy-done.4, f32[128,1024]{1,0:T(8,128)S(1)} %fusion.2, bf16[128,512]{1,0:T(8,128)(2,1)S(1)} %bitcast.9, f32[1024,512]{1,0:T(8,128)S(1)} %copy-done), kind=kOutput, calls=%fused_computation.5 | convolution fusion | flops 137363456 | bytes 4849664 | tf_op jit(solution)/shard_map/dot_general | solution.py:341
  (53 shorter events, 15.1 us)
Async XLA Ops:
  5.9 12.9 %collective-permute-start = (bf16[256,2048]{1,0:T(8,128)(2,1)}, bf16[256,2048]{1,0:T(8,128)(2,1)S(1)}, u32[]{:S(2)}, u32[]{:S(2)}) collective-permute-start(bf16[256,2048]{1,0:T(8,128)(2,1)} %pick.1), channel_id=1, source_target_pairs={{0,1},{1,0},{2,3},{3,2},{4,5},{5,4},{6,7},{7,6},{8,9},{9,8},{10,11... | collective-permute-start | bytes 3145736 | tf_op jit(solution)/shard_map/ppermute | solution.py:312
  12.3 6.5 %collective-permute-start.1 = (bf16[256,512]{1,0:T(8,128)(2,1)}, bf16[256,512]{1,0:T(8,128)(2,1)S(1)}, u32[]{:S(2)}, u32[]{:S(2)}) collective-permute-start(bf16[256,512]{1,0:T(8,128)(2,1)} %make_q.1.q_ref), channel_id=1, source_target_pairs={{0,1},{1,0},{2,3},{3,2},{4,5},{5,4},{6,7},{7,6},{8,9},{9,8},{10,11... | collective-permute-start | bytes 786440 | tf_op jit(solution)/shard_map/ppermute | solution.py:316
  12.3 17.2 %all-to-all-start = ((bf16[8,128,128]{2,1,0:T(8,128)(2,1)}), bf16[8,128,128]{2,1,0:T(8,128)(2,1)S(1)}, u32[]{:S(2)}, u32[]{:S(2)}) async-start(bf16[8,128,128]{2,1,0:T(8,128)(2,1)} %make_piece.1.after_ref), calls=%async_computation | async-start | bytes 524288 | tf_op jit(solution)/shard_map/all_to_all | solution.py:313
  29.6 3.6 %copy-start.3 = (bf16[8,128,128]{2,1,0:T(8,128)(2,1)}, bf16[8,128,128]{2,1,0:T(8,128)(2,1)S(1)}, u32[]{:S(2)}) copy-start(bf16[8,128,128]{2,1,0:T(8,128)(2,1)S(1)} %all-to-all-done.piece_ref) | copy-start | bytes 786436
  29.6 57.6 %all-to-all-start.1 = ((bf16[8,2,128,512]{3,2,1,0:T(8,128)(2,1)}), bf16[8,2,128,512]{3,2,1,0:T(8,128)(2,1)S(1)}, u32[]{:S(2)}, u32[]{:S(2)}) async-start(bf16[8,2,128,512]{3,2,1,0:T(8,128)(2,1)} %make_sketch.1.after_ref), calls=%async_computation.1 | async-start | bytes 4194304 | tf_op jit(solution)/shard_map/all_to_all | solution.py:318
  34.8 16.1 %copy-start.2 = (bf16[4,128,128]{2,1,0:T(8,128)(2,1)S(1)}, bf16[4,128,128]{2,1,0:T(8,128)(2,1)}, u32[]{:S(2)}) copy-start(bf16[4,128,128]{2,1,0:T(8,128)(2,1)} %get-tuple-element.14) | copy-start | bytes 393220
  34.8 4.3 %collective-permute-start.2 = (bf16[4,128,128]{2,1,0:T(8,128)(2,1)}, bf16[4,128,128]{2,1,0:T(8,128)(2,1)S(1)}, u32[]{:S(2)}, u32[]{:S(2)}) collective-permute-start(bf16[4,128,128]{2,1,0:T(8,128)(2,1)} %get-tuple-element.13), channel_id=1, source_target_pairs={{0,34},{1,65},{2,32},{3,67},{32,2},{33,97},{34,0},{35,99},{64,98},... | collective-permute-start | bytes 393224 | tf_op jit(solution)/shard_map/ppermute | solution.py:128
  36.1 5.5 %collective-permute-start.5 = (bf16[4,128,128]{2,1,0:T(8,128)(2,1)}, bf16[4,128,128]{2,1,0:T(8,128)(2,1)S(1)}, u32[]{:S(2)}, u32[]{:S(2)}) collective-permute-start(bf16[4,128,128]{2,1,0:T(8,128)(2,1)} %get-tuple-element.14), channel_id=1, source_target_pairs={{0,32},{1,193},{2,34},{3,195},{32,0},{33,225},{34,2},{35,227},{64,... | collective-permute-start | bytes 393224 | tf_op jit(solution)/shard_map/ppermute | solution.py:128
  40.1 7.0 %collective-permute-start.3 = (bf16[8,128,128]{2,1,0:T(8,128)(2,1)S(1)}, bf16[8,128,128]{2,1,0:T(8,128)(2,1)S(1)}, u32[]{:S(2)}, u32[]{:S(2)}) collective-permute-start(bf16[8,128,128]{2,1,0:T(8,128)(2,1)S(1)} %pad_maximum_fusion.2), channel_id=1, source_target_pairs={{0,64},{1,33},{2,66},{3,35},{32,96},{33,1},{34,98},{35,3},{64,0},{... | collective-permute-start | bytes 786440 | tf_op jit(solution)/shard_map/ppermute | solution.py:128
  42.6 8.3 %collective-permute-start.6 = (bf16[8,128,128]{2,1,0:T(8,128)(2,1)S(1)}, bf16[8,128,128]{2,1,0:T(8,128)(2,1)S(1)}, u32[]{:S(2)}, u32[]{:S(2)}) collective-permute-start(bf16[8,128,128]{2,1,0:T(8,128)(2,1)S(1)} %pad_maximum_fusion.3), channel_id=1, source_target_pairs={{0,192},{1,35},{2,194},{3,33},{32,224},{33,3},{34,226},{35,1},{64,... | collective-permute-start | bytes 786440 | tf_op jit(solution)/shard_map/ppermute | solution.py:128
  48.1 12.0 %collective-permute-start.4 = (bf16[16,128,128]{2,1,0:T(8,128)(2,1)S(1)}, bf16[16,128,128]{2,1,0:T(8,128)(2,1)S(1)}, u32[]{:S(2)}, u32[]{:S(2)}) collective-permute-start(bf16[16,128,128]{2,1,0:T(8,128)(2,1)S(1)} %pad_maximum_fusion), channel_id=1, source_target_pairs={{0,32},{1,193},{2,34},{3,195},{32,0},{33,225},{34,2},{35,227},{64,... | collective-permute-start | bytes 1572872 | tf_op jit(solution)/shard_map/ppermute | solution.py:128
  51.0 10.9 %collective-permute-start.7 = (bf16[16,128,128]{2,1,0:T(8,128)(2,1)S(1)}, bf16[16,128,128]{2,1,0:T(8,128)(2,1)S(1)}, u32[]{:S(2)}, u32[]{:S(2)}) collective-permute-start(bf16[16,128,128]{2,1,0:T(8,128)(2,1)S(1)} %pad_maximum_fusion.1), channel_id=1, source_target_pairs={{0,34},{1,65},{2,32},{3,67},{32,2},{33,97},{34,0},{35,99},{64,98},... | collective-permute-start | bytes 1572872 | tf_op jit(solution)/shard_map/ppermute | solution.py:128
  60.2 33.7 %copy-start.5 = (bf16[32,128,128]{2,1,0:T(8,128)(2,1)}, bf16[32,128,128]{2,1,0:T(8,128)(2,1)S(1)}, u32[]{:S(2)}) copy-start(bf16[32,128,128]{2,1,0:T(8,128)(2,1)S(1)} %constant_dynamic-update-slice_fusion.refs_0_) | copy-start | bytes 3145732
  60.2 18.4 %collective-permute-start.10 = (bf16[32,128,128]{2,1,0:T(8,128)(2,1)S(1)}, bf16[32,128,128]{2,1,0:T(8,128)(2,1)}, u32[]{:S(2)}, u32[]{:S(2)}) collective-permute-start(bf16[32,128,128]{2,1,0:T(8,128)(2,1)S(1)} %constant_dynamic-update-slice_fusion.refs_0_), channel_id=1, source_target_pairs={{0,192},{1,35},{2,194},{3,33},{32,224},{33,3},{34,226},{35,1},{64,... | collective-permute-start | bytes 3145736 | tf_op jit(solution)/shard_map/ppermute | solution.py:128
  62.7 15.9 %collective-permute-start.12 = (bf16[32,128,128]{2,1,0:T(8,128)(2,1)}, bf16[32,128,128]{2,1,0:T(8,128)(2,1)}, u32[]{:S(2)}, u32[]{:S(2)}) collective-permute-start(bf16[32,128,128]{2,1,0:T(8,128)(2,1)} %constant_dynamic-update-slice_fusion.4.refs_1_), channel_id=1, source_target_pairs={{0,64},{1,33},{2,66},{3,35},{32,96},{33,1},{34,98},{35,3},{64,0},{... | collective-permute-start | bytes 3145736 | tf_op jit(solution)/shard_map/ppermute | solution.py:128
  62.7 31.2 %collective-permute-start.9 = (bf16[32,128,128]{2,1,0:T(8,128)(2,1)}, bf16[32,128,128]{2,1,0:T(8,128)(2,1)}, u32[]{:S(2)}, u32[]{:S(2)}) collective-permute-start(bf16[32,128,128]{2,1,0:T(8,128)(2,1)} %constant_dynamic-update-slice_fusion.4.refs_1_), channel_id=1, source_target_pairs={{0,1},{1,0},{2,3},{3,2},{4,5},{5,4},{6,7},{7,6},{8,9},{9,8},{10,11... | collective-permute-start | bytes 3145736 | tf_op jit(solution)/shard_map/ppermute | solution.py:323
  72.2 21.6 %collective-permute-start.8 = (bf16[32,128,128]{2,1,0:T(8,128)(2,1)S(1)}, bf16[32,128,128]{2,1,0:T(8,128)(2,1)}, u32[]{:S(2)}, u32[]{:S(2)}) collective-permute-start(bf16[32,128,128]{2,1,0:T(8,128)(2,1)S(1)} %constant_dynamic-update-slice_fusion.refs_0_), channel_id=1, source_target_pairs={{0,1},{1,0},{2,3},{3,2},{4,5},{5,4},{6,7},{7,6},{8,9},{9,8},{10,11... | collective-permute-start | bytes 3145736 | tf_op jit(solution)/shard_map/ppermute | solution.py:323
  78.6 29.2 %collective-permute-start.11 = (bf16[32,128,128]{2,1,0:T(8,128)(2,1)}, bf16[32,128,128]{2,1,0:T(8,128)(2,1)}, u32[]{:S(2)}, u32[]{:S(2)}) collective-permute-start(bf16[32,128,128]{2,1,0:T(8,128)(2,1)} %collective-permute-done.10.refs_0_), channel_id=1, source_target_pairs={{0,1},{1,0},{2,3},{3,2},{4,5},{5,4},{6,7},{7,6},{8,9},{9,8},{10,11... | collective-permute-start | bytes 3145736 | tf_op jit(solution)/shard_map/ppermute | solution.py:325
  78.6 35.5 %collective-permute-start.13 = (bf16[32,128,128]{2,1,0:T(8,128)(2,1)}, bf16[32,128,128]{2,1,0:T(8,128)(2,1)}, u32[]{:S(2)}, u32[]{:S(2)}) collective-permute-start(bf16[32,128,128]{2,1,0:T(8,128)(2,1)} %collective-permute-done.12.refs_0_), channel_id=1, source_target_pairs={{0,1},{1,0},{2,3},{3,2},{4,5},{5,4},{6,7},{7,6},{8,9},{9,8},{10,11... | collective-permute-start | bytes 3145736 | tf_op jit(solution)/shard_map/ppermute | solution.py:328
  88.2 14.0 %all-to-all-start.2 = ((bf16[16,16,512]{2,1,0:T(8,128)(2,1)}), bf16[16,16,512]{2,1,0:T(8,128)(2,1)S(1)}, u32[]{:S(2)}, u32[]{:S(2)}) async-start(bf16[16,16,512]{2,1,0:T(8,128)(2,1)} %bitcast.4), calls=%async_computation.2 | async-start | bytes 524288 | tf_op jit(solution)/shard_map/all_to_all | solution.py:332
  102.8 18.3 %all-to-all-start.3 = ((bf16[8,16,512]{2,1,0:T(8,128)(2,1)}), bf16[8,16,512]{2,1,0:T(8,128)(2,1)S(1)}, u32[]{:S(2)}, u32[]{:S(2)}) async-start(bf16[8,16,512]{2,1,0:T(8,128)(2,1)} %broadcast_in_dim.2), calls=%async_computation.3 | async-start | bytes 262144 | tf_op jit(solution)/shard_map/all_to_all | solution.py:335
  114.1 7.1 %copy-start = (f32[1024,512]{1,0:T(8,128)S(1)}, f32[1024,512]{1,0:T(8,128)}, u32[]{:S(2)}) copy-start(f32[1024,512]{1,0:T(8,128)} %proj_ref.1) | copy-start | bytes 6291460
  121.1 1.0 copy-start.1
  121.1 1.2 copy-start.4
  (2 other events, 1.7 us)

commit v8 on v7

--- a/solution.py
+++ b/solution.py
@@ -84,24 +84,28 @@
     )(upstream, projection)
 
 
-def sketch_kernel(at_ref, tok_ref, got_ref, q_ref, got_q_ref, out_ref):
-    n_z, n_xh = out_ref.shape[:2]
+def sketch_kernel(at_ref, tok_ref, got_ref, q_ref, got_q_ref, *out_refs):
+    n_z = len(out_refs)
+    n_xh = out_refs[0].shape[0]
     dims = (((0,), (0,)), ((), ()))
-    for k in range(n_z * n_xh):
-        mine = tok_ref[:, pl.ds(pl.multiple_of((2 * k + at_ref[0]) * LANES, LANES), LANES)]
-        theirs = got_ref[:, k * LANES : (k + 1) * LANES]
-        s = lax.dot_general(mine, q_ref[...], dims, preferred_element_type=F32)
-        s += lax.dot_general(theirs, got_q_ref[...], dims, preferred_element_type=F32)
-        out_ref[k // n_xh, k % n_xh] = s.astype(BF16)
+    for r, out_ref in enumerate(out_refs):
+        z = lax.rem(at_ref[4] + r, n_z)
+        for h in range(n_xh):
+            k = z * n_xh + h
+            mine = tok_ref[:, pl.ds(pl.multiple_of((2 * k + at_ref[0]) * LANES, LANES), LANES)]
+            theirs = got_ref[:, pl.ds(pl.multiple_of(k * LANES, LANES), LANES)]
+            s = lax.dot_general(mine, q_ref[...], dims, preferred_element_type=F32)
+            s += lax.dot_general(theirs, got_q_ref[...], dims, preferred_element_type=F32)
+            out_ref[h] = s.astype(BF16)
 
 
 def make_sketch(at, tokens, got, q, got_q, n_z, n_xh):
     proj = q.shape[1]
     return pl.pallas_call(
         sketch_kernel,
-        out_shape=jax.ShapeDtypeStruct((n_z, n_xh, LANES, proj), BF16),
+        out_shape=(jax.ShapeDtypeStruct((n_xh, LANES, proj), BF16),) * n_z,
         in_specs=[SMEM] + [VMEM] * 4,
-        out_specs=VMEM,
+        out_specs=(VMEM,) * n_z,
         cost_estimate=pl.CostEstimate(
             flops=8 * tokens.size * proj, bytes_accessed=16 * tokens.size, transcendentals=0
         ),
@@ -225,14 +229,9 @@
             half_products(0, range(GROUPS), core, at_ref, tok_ref, w_refs, acc_ref, up_rel, take)
 
 
-def far_kernel(at_ref, tok_ref, up_ref, before_ref, sum_ref, *refs, group, scale, last):
-    w_refs = refs[:2]
-    if last:
-        part_ref, values_ref, grads_ref, acc_ref, up_rel = refs[2:]
-        done = part_ref.shape[1]
-        grads_ref[:, :done] = part_ref[...]
-    else:
-        acc_ref, grads_ref, up_rel = refs[2:]
+def far_kernel(at_ref, tok_ref, up_ref, before_ref, *refs, scale):
+    sum_refs, w_refs = refs[:GROUPS], refs[GROUPS : 3 * GROUPS]
+    values_ref, grads_ref, acc_ref, up_rel = refs[3 * GROUPS :]
     acc_ref[...] = before_ref[...]
     arrange(at_ref, up_ref, up_rel)
 
@@ -240,7 +239,7 @@
 
         def take(g, a, o, blocks, total, core=core):
             if places(core ^ o, g)[0, a]:
-                before = sum_ref[2 * a + o]
+                before = sum_refs[g][2 * a + o]
                 total = before if total is None else total + before
             grad = (total * scale).astype(BF16)
             for k, at in enumerate(blocks):
@@ -248,11 +247,10 @@
 
         @pl.when(at_ref[0] == core)
         def _():
-            half_products(1, (group,), core, at_ref, tok_ref, w_refs, acc_ref, up_rel, take)
-
-    if last:
-        for r, at in enumerate(columns(at_ref)):
-            values_ref[:, at] = (acc_ref[:, r * LANES : (r + 1) * LANES] * scale).astype(BF16)
+            half_products(1, range(GROUPS), core, at_ref, tok_ref, w_refs, acc_ref, up_rel, take)
+
+    for r, at in enumerate(columns(at_ref)):
+        values_ref[:, at] = (acc_ref[:, r * LANES : (r + 1) * LANES] * scale).astype(BF16)
 
 
 def near_products(at, tokens, upstream, weights):
@@ -272,26 +270,18 @@
     )(at, tokens, upstream, *weights)
 
 
-def far_products(at, tokens, upstream, acc, sums, weights, scale, group, part=None):
+def far_products(at, tokens, upstream, acc, sums, weights, scale):
     t, d = tokens.shape
     kv = upstream.shape[1]
-    last = part is not None
-    rel = pltpu.VMEM((t, kv), BF16)
-    if last:
-        shapes = (jax.ShapeDtypeStruct((t, kv), BF16), jax.ShapeDtypeStruct((t, d), BF16))
-        extra, scratch = (part,), [pltpu.VMEM((t, kv), F32), rel]
-    else:
-        shapes = (jax.ShapeDtypeStruct((t, kv), F32), jax.ShapeDtypeStruct((t, d // GROUPS), BF16))
-        extra, scratch = (), [rel]
-    return pl.pallas_call(
-        functools.partial(far_kernel, group=group, scale=scale, last=last),
-        out_shape=shapes,
-        in_specs=[SMEM] + [VMEM] * (6 + len(extra)),
+    return pl.pallas_call(
+        functools.partial(far_kernel, scale=scale),
+        out_shape=(jax.ShapeDtypeStruct((t, kv), BF16), jax.ShapeDtypeStruct((t, d), BF16)),
+        in_specs=[SMEM] + [VMEM] * (3 + len(sums) + len(weights)),
         out_specs=(VMEM, VMEM),
-        scratch_shapes=scratch,
-        cost_estimate=pl.CostEstimate(flops=t * d * kv, bytes_accessed=d * kv, transcendentals=0),
+        scratch_shapes=[pltpu.VMEM((t, kv), F32), pltpu.VMEM((t, kv), BF16)],
+        cost_estimate=pl.CostEstimate(flops=2 * t * d * kv, bytes_accessed=d * kv, transcendentals=0),
         name="far_products",
-    )(at, tokens, upstream, acc, sums, *weights, *extra)
+    )(at, tokens, upstream, acc, *sums, *weights)
 
 
 def step(tokens, upstream, params, momentum, projection):
@@ -304,7 +294,7 @@
     part = rows // n_isl
     inv_width = 1.0 / math.sqrt(width)
     scale_tok = 1.0 / math.sqrt(tokens.shape[0] * fsdp_count)
-    at = jnp.stack([lax.axis_index(a).astype(jnp.int32) for a in ("c", "y", "xh", "xl")])
+    at = jnp.stack([lax.axis_index(a).astype(jnp.int32) for a in ("c", "y", "xh", "xl", "z")])
     swap = functools.partial(lax.ppermute, axis_name="c", perm=[(0, 1), (1, 0)])
 
     piece = make_piece(at, params, n_z, n_isl)
@@ -315,20 +305,31 @@
     q = make_q(upstream, projection)
     got_q = swap(q)
     pair = make_sketch(at, tokens, got, q, got_q, n_z, n_xh)
-    along = lax.all_to_all(pair, "z", 0, 0, tiled=True)
-    held = split(piece, pair)
+
+    def shift(x, k):
+        return lax.ppermute(x, "z", [(i, (i + k) % n_z) for i in range(n_z)])
+
+    half_way = n_z // 2
+    near_by = half_way + 1
+    relayed = shift(pair[half_way], n_z - 1)
+    along = pair[0].astype(F32)
+    for k in range(half_way - 1, 0, -1):
+        along += shift(pair[k], k).astype(F32)
+        if k < half_way - 1:
+            along += shift(pair[n_z - k], n_z - k).astype(F32)
+    joined = (pair[near_by].astype(F32) + relayed.astype(F32)).astype(BF16)
+    along += shift(joined, near_by).astype(F32)
+    held = split(piece, pair[0])
     for step in range(3):
-        held = [jnp.concatenate([h, exchange(h, g, step)], axis=0) for g, h in enumerate(held)]
+        more = [exchange(h, g, step) for g, h in enumerate(held)]
+        held = [jnp.concatenate(both, axis=0) for both in zip(held, more)]
     far = [exchange(h, g, 3) for g, h in enumerate(held)]
     acc, *sums = near_products(at, tokens, upstream, [*held, *(swap(h) for h in held)])
-    acc, grads = far_products(
-        at, tokens, upstream, acc, sums[0], (far[0], swap(far[0])), inv_width, 0
+    values, token_grads = far_products(
+        at, tokens, upstream, acc, sums, [*far, *(swap(f) for f in far)], inv_width
     )
-    values, token_grads = far_products(
-        at, tokens, upstream, acc, sums[1], (far[1], swap(far[1])), inv_width, 1, grads
-    )
-
-    along = jnp.sum(along.astype(F32), axis=0).astype(BF16)
+
+    along = along.astype(BF16)
     plane = lax.all_to_all(along.reshape(n_xh * n_isl, part, proj), PLANE, 0, 0, tiled=True)
     total = jnp.sum(plane.astype(F32), axis=0).astype(BF16)
     total = jnp.broadcast_to(total[None], (n_isl, part, proj))

time: 125 us -> 157 us (1.26)
  the two profiles are of different devices: /device:TPU:1 before, /device:TPU:32 now
where the time goes in v8:
time: 157 us; the launch traced here: 156 us
  waiting for transfers between devices  60.2 us (38%)
  starting transfers between devices  40.3 us (26%)
  Pallas kernels  30.7 us (20%)
  local copies, waits for them, and re-layouts  9.19 us (6%)
  blocking collectives  9.08 us (6%)
  other arithmetic  3.92 us (2%)
  matrix products  2.02 us (1%)
    ppermute x7, waiting for transfers between devices, shift(): return lax.ppermute(x, 'z', [(i, (i + k) % n_z) for i in range(n_z)])  39.7 us
    ppermute x8, starting transfers between devices, exchange(): return lax.ppermute(x, ('y', 'xl', 'xh', 'c'), pairs)  15.2 us
    ppermute x7, starting transfers between devices, shift(): return lax.ppermute(x, 'z', [(i, (i + k) % n_z) for i in range(n_z)])  10.5 us
    pallas_call x1, Pallas kernels, far_products(): pl.pallas_call(functools.partial(far_kernel, scale=scale), out_shape=(jax...  9.14 us
    all_to_all x1, blocking collectives, step(): total = lax.all_to_all(total, ISLAND, 0, 0, tiled=True)  9.08 us
    all_to_all x1, starting transfers between devices, step(): piece = lax.all_to_all(piece, 'z', 0, 0, tiled=True)  8.57 us
    all_to_all x1, waiting for transfers between devices, step(): lax.all_to_all(along.reshape(n_xh * n_isl, part, proj), PLANE, 0, 0, tile...  8.08 us
    pallas_call x1, Pallas kernels, near_products(): pl.pallas_call(near_kernel, out_shape=(jax.ShapeDtypeStruct((t, kv), F32)...  7.9 us
  transfers between devices with their start and end apart: 23, of which 10 were waited for; matrix products, arithmetic and copies ran while one was open for 8% of the time, Pallas kernels for 10%

profile of v8, /device:TPU:32, one launch (start us, length us, event | category | flops | bytes accessed | tf_op | source)
XLA Modules:
  0.0 156.2 jit_solution(4873956167243265903)
XLA Ops:
  3.0 2.9 %pick.1 = bf16[256,2048]{1,0:T(8,128)(2,1)} custom-call(s32[5]{0:T(128)} %stack.23.at_ref, bf16[256,4096]{1,0:T(8,128)(2,1)} %tok_ref.5, bf16[8,128,128]{2,1,0:T(8,128)(2,1)} %make_piece.1.after_ref), custom_call_target="tpu_custom_call" | custom-call | tf_op jit(solution)/shard_map/pick/pallas_call | solution.py:56
  5.9 3.2 %make_q.1.q_ref = bf16[256,512]{1,0:T(8,128)(2,1)} custom-call(bf16[256,1024]{1,0:T(8,128)(2,1)} %up_ref.5, f32[1024,512]{1,0:T(8,128)} %proj_ref.1), custom_call_target="tpu_custom_call" | custom-call | flops 1073741824 | bytes 3145728 | tf_op jit(solution)/shard_map/make_q/pallas_call | solution.py:73
  9.6 8.6 %all-to-all-start = ((bf16[8,128,128]{2,1,0:T(8,128)(2,1)}), bf16[8,128,128]{2,1,0:T(8,128)(2,1)S(1)}, u32[]{:S(2)}, u32[]{:S(2)}) async-start(bf16[8,128,128]{2,1,0:T(8,128)(2,1)} %make_piece.1.after_ref), calls=%async_computation | async-start | bytes 524288 | tf_op jit(solution)/shard_map/all_to_all | solution.py:303
  19.8 4.2 %make_sketch.1 = (bf16[2,128,512]{2,1,0:T(8,128)(2,1)}, bf16[2,128,512]{2,1,0:T(8,128)(2,1)}, bf16[2,128,512]{2,1,0:T(8,128)(2,1)}, bf16[2,128,512]{2,1,0:T(8,12...) custom-call(s32[5]{0:T(128)} %stack.23.at_ref, ...), custom_call_target="tpu_custom_call" | custom-call | flops 4294967296 | bytes 16777216 | tf_op jit(solution)/shard_map/make_sketch/pallas_call | solution.py:104
  24.0 4.7 %all-to-all-done.piece_ref = bf16[8,128,128]{2,1,0:T(8,128)(2,1)S(1)} async-done(((bf16[8,128,128]{2,1,0:T(8,128)(2,1)}), bf16[8,128,128]{2,1,0:T(8,128)(2,1)S(1)}, u32[]{:S(2)}, u32[]{:S(2)}) %all-to-all-start) | async-done | bytes 262176 | tf_op jit(solution)/shard_map/all_to_all | solution.py:303
  32.6 2.1 %collective-permute-start.2 = (bf16[4,128,128]{2,1,0:T(8,128)(2,1)}, bf16[4,128,128]{2,1,0:T(8,128)(2,1)S(1)}, u32[]{:S(2)}, u32[]{:S(2)}) collective-permute-start(bf16[4,128,128]{2,1,0:T(8,128)(2,1)} %get-tuple-element.20), channel_id=1, source_target_pairs={{0,34},{1,65},{2,32},{3,67},{32,2},{33,97},{34,0},{35,99},{64,98},... | collective-permute-start | bytes 393224 | tf_op jit(solution)/shard_map/ppermute | solution.py:132
  37.2 3.1 %collective-permute-start.6 = (bf16[8,128,128]{2,1,0:T(8,128)(2,1)S(1)}, bf16[8,128,128]{2,1,0:T(8,128)(2,1)S(1)}, u32[]{:S(2)}, u32[]{:S(2)}) collective-permute-start(bf16[8,128,128]{2,1,0:T(8,128)(2,1)S(1)} %pad_maximum_fusion.3), channel_id=1, source_target_pairs={{0,192},{1,35},{2,194},{3,33},{32,224},{33,3},{34,226},{35,1},{64,... | collective-permute-start | bytes 786440 | tf_op jit(solution)/shard_map/ppermute | solution.py:132
  46.3 2.4 %collective-permute-start.7 = (bf16[16,128,128]{2,1,0:T(8,128)(2,1)S(1)}, bf16[16,128,128]{2,1,0:T(8,128)(2,1)S(1)}, u32[]{:S(2)}, u32[]{:S(2)}) collective-permute-start(bf16[16,128,128]{2,1,0:T(8,128)(2,1)S(1)} %pad_maximum_fusion.1), channel_id=1, source_target_pairs={{0,34},{1,65},{2,32},{3,67},{32,2},{33,97},{34,0},{35,99},{64,98},... | collective-permute-start | bytes 1572872 | tf_op jit(solution)/shard_map/ppermute | solution.py:132
  53.8 3.0 %collective-permute-done.7 = bf16[16,128,128]{2,1,0:T(8,128)(2,1)S(1)} collective-permute-done((bf16[16,128,128]{2,1,0:T(8,128)(2,1)S(1)}, bf16[16,128,128]{2,1,0:T(8,128)(2,1)S(1)}, u32[]{:S(2)}, u32[]{:S(2)}) %collective-permute-start.7) | collective-permute-done | bytes 524320 | tf_op jit(solution)/shard_map/ppermute | solution.py:132
  58.8 2.1 %collective-permute-done.4 = bf16[16,128,128]{2,1,0:T(8,128)(2,1)S(1)} collective-permute-done((bf16[16,128,128]{2,1,0:T(8,128)(2,1)S(1)}, bf16[16,128,128]{2,1,0:T(8,128)(2,1)S(1)}, u32[]{:S(2)}, u32[]{:S(2)}) %collective-permute-start.4) | collective-permute-done | bytes 524320 | tf_op jit(solution)/shard_map/ppermute | solution.py:132
  61.8 2.0 %collective-permute-start.10 = (bf16[32,128,128]{2,1,0:T(8,128)(2,1)}, bf16[32,128,128]{2,1,0:T(8,128)(2,1)}, u32[]{:S(2)}, u32[]{:S(2)}) collective-permute-start(bf16[32,128,128]{2,1,0:T(8,128)(2,1)} %constant_dynamic-update-slice_fusion.refs_0_), channel_id=1, source_target_pairs={{0,192},{1,35},{2,194},{3,33},{32,224},{33,3},{34,226},{35,1},{64,... | collective-permute-start | bytes 3145736 | tf_op jit(solution)/shard_map/ppermute | solution.py:132
  63.8 2.3 %collective-permute-start.15 = (bf16[2,128,512]{2,1,0:T(8,128)(2,1)S(1)}, bf16[2,128,512]{2,1,0:T(8,128)(2,1)S(1)}, u32[]{:S(2)}, u32[]{:S(2)}) collective-permute-start(bf16[2,128,512]{2,1,0:T(8,128)(2,1)S(1)} %copy-done.11), channel_id=1, source_target_pairs={{0,8},{4,12},{8,16},{12,20},{16,24},{20,28},{24,0},{28,4},{1,9},{5... | collective-permute-start | bytes 786440 | tf_op jit(solution)/shard_map/ppermute | solution.py:310
  66.1 1.9 %collective-permute-start.16 = (bf16[2,128,512]{2,1,0:T(8,128)(2,1)S(1)}, bf16[2,128,512]{2,1,0:T(8,128)(2,1)S(1)}, u32[]{:S(2)}, u32[]{:S(2)}) collective-permute-start(bf16[2,128,512]{2,1,0:T(8,128)(2,1)S(1)} %copy-done.10), channel_id=1, source_target_pairs={{0,24},{4,28},{8,0},{12,4},{16,8},{20,12},{24,16},{28,20},{1,25},{... | collective-permute-start | bytes 786440 | tf_op jit(solution)/shard_map/ppermute | solution.py:310
  68.1 15.2 %collective-permute-done.14 = bf16[2,128,512]{2,1,0:T(8,128)(2,1)S(1)} collective-permute-done((bf16[2,128,512]{2,1,0:T(8,128)(2,1)S(1)}, bf16[2,128,512]{2,1,0:T(8,128)(2,1)S(1)}, u32[]{:S(2)}, u32[]{:S(2)}) %collective-permute-start.14) | collective-permute-done | bytes 262176 | tf_op jit(solution)/shard_map/ppermute | solution.py:310
  83.3 2.0 %collective-permute-start.17 = (bf16[2,128,512]{2,1,0:T(8,128)(2,1)S(1)}, bf16[2,128,512]{2,1,0:T(8,128)(2,1)S(1)}, u32[]{:S(2)}, u32[]{:S(2)}) collective-permute-start(bf16[2,128,512]{2,1,0:T(8,128)(2,1)S(1)} %copy-done.9), channel_id=1, source_target_pairs={{0,4},{4,8},{8,12},{12,16},{16,20},{20,24},{24,28},{28,0},{1,5},{5... | collective-permute-start | bytes 786440 | tf_op jit(solution)/shard_map/ppermute | solution.py:310
  85.3 7.1 %collective-permute-done.15 = bf16[2,128,512]{2,1,0:T(8,128)(2,1)S(1)} collective-permute-done((bf16[2,128,512]{2,1,0:T(8,128)(2,1)S(1)}, bf16[2,128,512]{2,1,0:T(8,128)(2,1)S(1)}, u32[]{:S(2)}, u32[]{:S(2)}) %collective-permute-start.15) | collective-permute-done | bytes 262176 | tf_op jit(solution)/shard_map/ppermute | solution.py:310
  92.4 3.6 %collective-permute-start.20 = (bf16[2,128,512]{2,1,0:T(8,128)(2,1)S(1)}, bf16[2,128,512]{2,1,0:T(8,128)(2,1)S(1)}, u32[]{:S(2)}, u32[]{:S(2)}) collective-permute-start(bf16[2,128,512]{2,1,0:T(8,128)(2,1)S(1)} %add_convert_fusion.1), channel_id=1, source_target_pairs={{0,20},{4,24},{8,28},{12,0},{16,4},{20,8},{24,12},{28,16},{1,21},{... | collective-permute-start | bytes 786440 | tf_op jit(solution)/shard_map/ppermute | solution.py:310
  96.0 6.4 %collective-permute-done.18 = bf16[2,128,512]{2,1,0:T(8,128)(2,1)S(1)} collective-permute-done((bf16[2,128,512]{2,1,0:T(8,128)(2,1)S(1)}, bf16[2,128,512]{2,1,0:T(8,128)(2,1)S(1)}, u32[]{:S(2)}, u32[]{:S(2)}) %collective-permute-start.18) | collective-permute-done | bytes 262176 | tf_op jit(solution)/shard_map/ppermute | solution.py:310
  102.4 11.0 %collective-permute-done.20 = bf16[2,128,512]{2,1,0:T(8,128)(2,1)S(1)} collective-permute-done((bf16[2,128,512]{2,1,0:T(8,128)(2,1)S(1)}, bf16[2,128,512]{2,1,0:T(8,128)(2,1)S(1)}, u32[]{:S(2)}, u32[]{:S(2)}) %collective-permute-start.20) | collective-permute-done | bytes 262176 | tf_op jit(solution)/shard_map/ppermute | solution.py:310
  114.3 4.9 %all-to-all-start.1 = ((bf16[16,16,512]{2,1,0:T(8,128)(2,1)}), bf16[16,16,512]{2,1,0:T(8,128)(2,1)S(1)}, u32[]{:S(2)}, u32[]{:S(2)}) async-start(bf16[16,16,512]{2,1,0:T(8,128)(2,1)} %bitcast.5), calls=%async_computation.1 | async-start | bytes 524288 | tf_op jit(solution)/shard_map/all_to_all | solution.py:333
  119.9 8.1 %all-to-all-done.1 = bf16[16,16,512]{2,1,0:T(8,128)(2,1)S(1)} async-done(((bf16[16,16,512]{2,1,0:T(8,128)(2,1)}), bf16[16,16,512]{2,1,0:T(8,128)(2,1)S(1)}, u32[]{:S(2)}, u32[]{:S(2)}) %all-to-all-start.1) | async-done | bytes 262176 | tf_op jit(solution)/shard_map/all_to_all | solution.py:333
  128.0 9.1 %all_to_all.15 = bf16[8,16,512]{2,1,0:T(8,128)(2,1)S(1)} all-to-all(bf16[8,16,512]{2,1,0:T(8,128)(2,1)S(1)} %broadcast_in_dim.2), channel_id=1, replica_groups=mesh['y'=4,'xl'=2,'z'=8,'xh'=2,'c'=2] {'y','xl'}, dimensions={0} | all-to-all | bytes 262144 | tf_op jit(solution)/shard_map/all_to_all | solution.py:336
  139.2 7.9 %near_products.1 = (f32[256,1024]{1,0:T(8,128)}, f32[4,256,512]{2,1,0:T(8,128)}, f32[4,256,512]{2,1,0:T(8,128)}) custom-call(s32[5]{0:T(128)} %stack.23.at_ref, bf16[256,4096]{1,0:T(8,128)(2,1)} %tok_ref.5, bf16[256,1024]{1,0:T(8,128)(2,1)} %up_ref.5, bf16[32,128,128]{2,1,0:T(8,128)(2,1)} %constant_dynamic-update-slice_fusion.refs_0_, ...), custom_call_target="tpu_custom_call" | custom-call | flops 2147483648 | bytes 4194304 | tf_op jit(solution)/shard_map/near_products/pallas_call | solution.py:259
  147.1 9.1 %far_products.1 = (bf16[256,1024]{1,0:T(8,128)(2,1)}, bf16[256,4096]{1,0:T(8,128)(2,1)}) custom-call(s32[5]{0:T(128)} %stack.23.at_ref, bf16[256,4096]{1,0:T(8,128)(2,1)} %tok_ref.5, bf16[256,1024]{1,0:T(8,128)(2,1)} %up_ref.5, f32[256,1024]{1,0:T(8,128)} %get-tuple-element.22.before_ref, f32[4,256,512]{2,1,0:T(8,128)} %get-tuple-element.23.refs_0_, ...), custom_call_target="tpu_custom_call" | custom-call | flops 2147483648 | bytes 4194304 | tf_op jit(solution)/shard_map/far_products/pallas_call | solution.py:276
  (76 shorter events, 28.6 us)
Async XLA Ops:
  5.9 12.3 %collective-permute-start = (bf16[256,2048]{1,0:T(8,128)(2,1)}, bf16[256,2048]{1,0:T(8,128)(2,1)S(1)}, u32[]{:S(2)}, u32[]{:S(2)}) collective-permute-start(bf16[256,2048]{1,0:T(8,128)(2,1)} %pick.1), channel_id=1, source_target_pairs={{0,1},{1,0},{2,3},{3,2},{4,5},{5,4},{6,7},{7,6},{8,9},{9,8},{10,11... | collective-permute-start | bytes 3145736 | tf_op jit(solution)/shard_map/ppermute | solution.py:302
  9.1 9.1 %collective-permute-start.1 = (bf16[256,512]{1,0:T(8,128)(2,1)}, bf16[256,512]{1,0:T(8,128)(2,1)S(1)}, u32[]{:S(2)}, u32[]{:S(2)}) collective-permute-start(bf16[256,512]{1,0:T(8,128)(2,1)} %make_q.1.q_ref), channel_id=1, source_target_pairs={{0,1},{1,0},{2,3},{3,2},{4,5},{5,4},{6,7},{7,6},{8,9},{9,8},{10,11... | collective-permute-start | bytes 786440 | tf_op jit(solution)/shard_map/ppermute | solution.py:306
  9.6 19.2 %all-to-all-start = ((bf16[8,128,128]{2,1,0:T(8,128)(2,1)}), bf16[8,128,128]{2,1,0:T(8,128)(2,1)S(1)}, u32[]{:S(2)}, u32[]{:S(2)}) async-start(bf16[8,128,128]{2,1,0:T(8,128)(2,1)} %make_piece.1.after_ref), calls=%async_computation | async-start | bytes 524288 | tf_op jit(solution)/shard_map/all_to_all | solution.py:303
  31.1 5.2 %collective-permute-start.5 = (bf16[4,128,128]{2,1,0:T(8,128)(2,1)}, bf16[4,128,128]{2,1,0:T(8,128)(2,1)S(1)}, u32[]{:S(2)}, u32[]{:S(2)}) collective-permute-start(bf16[4,128,128]{2,1,0:T(8,128)(2,1)} %get-tuple-element.21), channel_id=1, source_target_pairs={{0,32},{1,193},{2,34},{3,195},{32,0},{33,225},{34,2},{35,227},{64,... | collective-permute-start | bytes 393224 | tf_op jit(solution)/shard_map/ppermute | solution.py:132
  32.6 7.7 %collective-permute-start.2 = (bf16[4,128,128]{2,1,0:T(8,128)(2,1)}, bf16[4,128,128]{2,1,0:T(8,128)(2,1)S(1)}, u32[]{:S(2)}, u32[]{:S(2)}) collective-permute-start(bf16[4,128,128]{2,1,0:T(8,128)(2,1)} %get-tuple-element.20), channel_id=1, source_target_pairs={{0,34},{1,65},{2,32},{3,67},{32,2},{33,97},{34,0},{35,99},{64,98},... | collective-permute-start | bytes 393224 | tf_op jit(solution)/shard_map/ppermute | solution.py:132
  37.2 8.1 %collective-permute-start.6 = (bf16[8,128,128]{2,1,0:T(8,128)(2,1)S(1)}, bf16[8,128,128]{2,1,0:T(8,128)(2,1)S(1)}, u32[]{:S(2)}, u32[]{:S(2)}) collective-permute-start(bf16[8,128,128]{2,1,0:T(8,128)(2,1)S(1)} %pad_maximum_fusion.3), channel_id=1, source_target_pairs={{0,192},{1,35},{2,194},{3,33},{32,224},{33,3},{34,226},{35,1},{64,... | collective-permute-start | bytes 786440 | tf_op jit(solution)/shard_map/ppermute | solution.py:132
  41.3 8.4 %collective-permute-start.3 = (bf16[8,128,128]{2,1,0:T(8,128)(2,1)S(1)}, bf16[8,128,128]{2,1,0:T(8,128)(2,1)S(1)}, u32[]{:S(2)}, u32[]{:S(2)}) collective-permute-start(bf16[8,128,128]{2,1,0:T(8,128)(2,1)S(1)} %pad_maximum_fusion.2), channel_id=1, source_target_pairs={{0,64},{1,33},{2,66},{3,35},{32,96},{33,1},{34,98},{35,3},{64,0},{... | collective-permute-start | bytes 786440 | tf_op jit(solution)/shard_map/ppermute | solution.py:132
  43.0 23.1 %collective-permute-start.19 = (bf16[2,128,512]{2,1,0:T(8,128)(2,1)}, bf16[2,128,512]{2,1,0:T(8,128)(2,1)S(1)}, u32[]{:S(2)}, u32[]{:S(2)}) collective-permute-start(bf16[2,128,512]{2,1,0:T(8,128)(2,1)} %get-tuple-element.33), channel_id=1, source_target_pairs={{0,28},{4,0},{8,4},{12,8},{16,12},{20,16},{24,20},{28,24},{1,29},{... | collective-permute-start | bytes 786440 | tf_op jit(solution)/shard_map/ppermute | solution.py:310
  46.3 10.5 %collective-permute-start.7 = (bf16[16,128,128]{2,1,0:T(8,128)(2,1)S(1)}, bf16[16,128,128]{2,1,0:T(8,128)(2,1)S(1)}, u32[]{:S(2)}, u32[]{:S(2)}) collective-permute-start(bf16[16,128,128]{2,1,0:T(8,128)(2,1)S(1)} %pad_maximum_fusion.1), channel_id=1, source_target_pairs={{0,34},{1,65},{2,32},{3,67},{32,2},{33,97},{34,0},{35,99},{64,98},... | collective-permute-start | bytes 1572872 | tf_op jit(solution)/shard_map/ppermute | solution.py:132
  49.8 11.2 %collective-permute-start.4 = (bf16[16,128,128]{2,1,0:T(8,128)(2,1)S(1)}, bf16[16,128,128]{2,1,0:T(8,128)(2,1)S(1)}, u32[]{:S(2)}, u32[]{:S(2)}) collective-permute-start(bf16[16,128,128]{2,1,0:T(8,128)(2,1)S(1)} %pad_maximum_fusion), channel_id=1, source_target_pairs={{0,32},{1,193},{2,34},{3,195},{32,0},{33,225},{34,2},{35,227},{64,... | collective-permute-start | bytes 1572872 | tf_op jit(solution)/shard_map/ppermute | solution.py:132
  57.6 61.6 %collective-permute-start.11 = (bf16[32,128,128]{2,1,0:T(8,128)(2,1)}, bf16[32,128,128]{2,1,0:T(8,128)(2,1)}, u32[]{:S(2)}, u32[]{:S(2)}) collective-permute-start(bf16[32,128,128]{2,1,0:T(8,128)(2,1)} %constant_dynamic-update-slice_fusion.4.refs_1_), channel_id=1, source_target_pairs={{0,64},{1,33},{2,66},{3,35},{32,96},{33,1},{34,98},{35,3},{64,0},{... | collective-permute-start | bytes 3145736 | tf_op jit(solution)/shard_map/ppermute | solution.py:132
  61.8 75.3 %copy-start = (f32[1024,512]{1,0:T(8,128)S(1)}, f32[1024,512]{1,0:T(8,128)}, u32[]{:S(2)}) copy-start(f32[1024,512]{1,0:T(8,128)} %proj_ref.1) | copy-start | bytes 6291460
  61.8 57.6 %collective-permute-start.10 = (bf16[32,128,128]{2,1,0:T(8,128)(2,1)}, bf16[32,128,128]{2,1,0:T(8,128)(2,1)}, u32[]{:S(2)}, u32[]{:S(2)}) collective-permute-start(bf16[32,128,128]{2,1,0:T(8,128)(2,1)} %constant_dynamic-update-slice_fusion.refs_0_), channel_id=1, source_target_pairs={{0,192},{1,35},{2,194},{3,33},{32,224},{33,3},{34,226},{35,1},{64,... | collective-permute-start | bytes 3145736 | tf_op jit(solution)/shard_map/ppermute | solution.py:132
  63.8 19.5 %collective-permute-start.14 = (bf16[2,128,512]{2,1,0:T(8,128)(2,1)S(1)}, bf16[2,128,512]{2,1,0:T(8,128)(2,1)S(1)}, u32[]{:S(2)}, u32[]{:S(2)}) collective-permute-start(bf16[2,128,512]{2,1,0:T(8,128)(2,1)S(1)} %copy-done.12), channel_id=1, source_target_pairs={{0,12},{4,16},{8,20},{12,24},{16,28},{20,0},{24,4},{28,8},{1,13},{... | collective-permute-start | bytes 786440 | tf_op jit(solution)/shard_map/ppermute | solution.py:310
  63.8 28.6 %collective-permute-start.15 = (bf16[2,128,512]{2,1,0:T(8,128)(2,1)S(1)}, bf16[2,128,512]{2,1,0:T(8,128)(2,1)S(1)}, u32[]{:S(2)}, u32[]{:S(2)}) collective-permute-start(bf16[2,128,512]{2,1,0:T(8,128)(2,1)S(1)} %copy-done.11), channel_id=1, source_target_pairs={{0,8},{4,12},{8,16},{12,20},{16,24},{20,28},{24,0},{28,4},{1,9},{5... | collective-permute-start | bytes 786440 | tf_op jit(solution)/shard_map/ppermute | solution.py:310
  66.1 26.4 %collective-permute-start.16 = (bf16[2,128,512]{2,1,0:T(8,128)(2,1)S(1)}, bf16[2,128,512]{2,1,0:T(8,128)(2,1)S(1)}, u32[]{:S(2)}, u32[]{:S(2)}) collective-permute-start(bf16[2,128,512]{2,1,0:T(8,128)(2,1)S(1)} %copy-done.10), channel_id=1, source_target_pairs={{0,24},{4,28},{8,0},{12,4},{16,8},{20,12},{24,16},{28,20},{1,25},{... | collective-permute-start | bytes 786440 | tf_op jit(solution)/shard_map/ppermute | solution.py:310
  83.3 12.7 %collective-permute-start.17 = (bf16[2,128,512]{2,1,0:T(8,128)(2,1)S(1)}, bf16[2,128,512]{2,1,0:T(8,128)(2,1)S(1)}, u32[]{:S(2)}, u32[]{:S(2)}) collective-permute-start(bf16[2,128,512]{2,1,0:T(8,128)(2,1)S(1)} %copy-done.9), channel_id=1, source_target_pairs={{0,4},{4,8},{8,12},{12,16},{16,20},{20,24},{24,28},{28,0},{1,5},{5... | collective-permute-start | bytes 786440 | tf_op jit(solution)/shard_map/ppermute | solution.py:310
  92.4 10.1 %collective-permute-start.18 = (bf16[2,128,512]{2,1,0:T(8,128)(2,1)S(1)}, bf16[2,128,512]{2,1,0:T(8,128)(2,1)S(1)}, u32[]{:S(2)}, u32[]{:S(2)}) collective-permute-start(bf16[2,128,512]{2,1,0:T(8,128)(2,1)S(1)} %copy-done.8), channel_id=1, source_target_pairs={{0,28},{4,0},{8,4},{12,8},{16,12},{20,16},{24,20},{28,24},{1,29},{... | collective-permute-start | bytes 786440 | tf_op jit(solution)/shard_map/ppermute | solution.py:310
  92.4 21.0 %collective-permute-start.20 = (bf16[2,128,512]{2,1,0:T(8,128)(2,1)S(1)}, bf16[2,128,512]{2,1,0:T(8,128)(2,1)S(1)}, u32[]{:S(2)}, u32[]{:S(2)}) collective-permute-start(bf16[2,128,512]{2,1,0:T(8,128)(2,1)S(1)} %add_convert_fusion.1), channel_id=1, source_target_pairs={{0,20},{4,24},{8,28},{12,0},{16,4},{20,8},{24,12},{28,16},{1,21},{... | collective-permute-start | bytes 786440 | tf_op jit(solution)/shard_map/ppermute | solution.py:310
  96.0 43.2 %collective-permute-start.9 = (bf16[32,128,128]{2,1,0:T(8,128)(2,1)}, bf16[32,128,128]{2,1,0:T(8,128)(2,1)}, u32[]{:S(2)}, u32[]{:S(2)}) collective-permute-start(bf16[32,128,128]{2,1,0:T(8,128)(2,1)} %constant_dynamic-update-slice_fusion.4.refs_1_), channel_id=1, source_target_pairs={{0,1},{1,0},{2,3},{3,2},{4,5},{5,4},{6,7},{7,6},{8,9},{9,8},{10,11... | collective-permute-start | bytes 3145736 | tf_op jit(solution)/shard_map/ppermute | solution.py:327
  102.4 36.8 %collective-permute-start.8 = (bf16[32,128,128]{2,1,0:T(8,128)(2,1)}, bf16[32,128,128]{2,1,0:T(8,128)(2,1)}, u32[]{:S(2)}, u32[]{:S(2)}) collective-permute-start(bf16[32,128,128]{2,1,0:T(8,128)(2,1)} %constant_dynamic-update-slice_fusion.refs_0_), channel_id=1, source_target_pairs={{0,1},{1,0},{2,3},{3,2},{4,5},{5,4},{6,7},{7,6},{8,9},{9,8},{10,11... | collective-permute-start | bytes 3145736 | tf_op jit(solution)/shard_map/ppermute | solution.py:327
  114.3 13.6 %all-to-all-start.1 = ((bf16[16,16,512]{2,1,0:T(8,128)(2,1)}), bf16[16,16,512]{2,1,0:T(8,128)(2,1)S(1)}, u32[]{:S(2)}, u32[]{:S(2)}) async-start(bf16[16,16,512]{2,1,0:T(8,128)(2,1)} %bitcast.5), calls=%async_computation.1 | async-start | bytes 524288 | tf_op jit(solution)/shard_map/all_to_all | solution.py:333
  119.3 27.8 %collective-permute-start.13 = (bf16[32,128,128]{2,1,0:T(8,128)(2,1)}, bf16[32,128,128]{2,1,0:T(8,128)(2,1)}, u32[]{:S(2)}, u32[]{:S(2)}) collective-permute-start(bf16[32,128,128]{2,1,0:T(8,128)(2,1)} %collective-permute-done.11.refs_3_), channel_id=1, source_target_pairs={{0,1},{1,0},{2,3},{3,2},{4,5},{5,4},{6,7},{7,6},{8,9},{9,8},{10,11... | collective-permute-start | bytes 3145736 | tf_op jit(solution)/shard_map/ppermute | solution.py:329
  119.4 27.7 %collective-permute-start.12 = (bf16[32,128,128]{2,1,0:T(8,128)(2,1)}, bf16[32,128,128]{2,1,0:T(8,128)(2,1)}, u32[]{:S(2)}, u32[]{:S(2)}) collective-permute-start(bf16[32,128,128]{2,1,0:T(8,128)(2,1)} %collective-permute-done.10.refs_2_), channel_id=1, source_target_pairs={{0,1},{1,0},{2,3},{3,2},{4,5},{5,4},{6,7},{7,6},{8,9},{9,8},{10,11... | collective-permute-start | bytes 3145736 | tf_op jit(solution)/shard_map/ppermute | solution.py:329
  (13 other events, 264.2 us)

commit v9 on v8

--- a/solution.py
+++ b/solution.py
@@ -145,24 +145,6 @@
         for half, part in enumerate((held, far))
         for a in range(2)
     }
-
-
-def split_kernel(piece_ref, after_ref, *out_refs):
-    each = out_refs[0].shape[0]
-    for g, out_ref in enumerate(out_refs):
-        out_ref[...] = piece_ref[g * each : (g + 1) * each]
-
-
-def split(piece, after):
-    n = GROUPS
-    shape = (piece.shape[0] // n,) + piece.shape[1:]
-    return pl.pallas_call(
-        split_kernel,
-        out_shape=(jax.ShapeDtypeStruct(shape, BF16),) * n,
-        in_specs=[VMEM, LEFT],
-        out_specs=(VMEM,) * n,
-        name="split",
-    )(piece, after)
 
 
 def lanes(ref, blocks):
@@ -319,7 +301,8 @@
             along += shift(pair[n_z - k], n_z - k).astype(F32)
     joined = (pair[near_by].astype(F32) + relayed.astype(F32)).astype(BF16)
     along += shift(joined, near_by).astype(F32)
-    held = split(piece, pair[0])
+    each = n_z // GROUPS
+    held = [piece[g * each : (g + 1) * each] for g in range(GROUPS)]
     for step in range(3):
         more = [exchange(h, g, step) for g, h in enumerate(held)]
         held = [jnp.concatenate(both, axis=0) for both in zip(held, more)]

time: 157 us -> 137 us (0.87)
  the two profiles are of different devices: /device:TPU:32 before, /device:TPU:1 now
where the time goes in v9:
time: 137 us; the launch traced here: 134 us
  starting transfers between devices  47 us (34%)
  waiting for transfers between devices  42.3 us (31%)
  Pallas kernels  29.1 us (21%)
  blocking collectives  8.13 us (6%)
  other arithmetic  3.35 us (2%)
  matrix products  2.01 us (1%)
  local copies, waits for them, and re-layouts  1.44 us (1%)
    ppermute x7, waiting for transfers between devices, shift(): return lax.ppermute(x, 'z', [(i, (i + k) % n_z) for i in range(n_z)])  21.9 us
    ppermute x2, starting transfers between devices, step(): swap(h)  15 us
    pallas_call x1, Pallas kernels, far_products(): pl.pallas_call(functools.partial(far_kernel, scale=scale), out_shape=(jax...  9.09 us
    all_to_all x1, starting transfers between devices, step(): piece = lax.all_to_all(piece, 'z', 0, 0, tiled=True)  9 us
    all_to_all x1, blocking collectives, step(): total = lax.all_to_all(total, ISLAND, 0, 0, tiled=True)  8.13 us
    pallas_call x1, Pallas kernels, near_products(): pl.pallas_call(near_kernel, out_shape=(jax.ShapeDtypeStruct((t, kv), F32)...  7.97 us
    ppermute x8, starting transfers between devices, exchange(): return lax.ppermute(x, ('y', 'xl', 'xh', 'c'), pairs)  7.94 us
    all_to_all x1, waiting for transfers between devices, step(): lax.all_to_all(along.reshape(n_xh * n_isl, part, proj), PLANE, 0, 0, tile...  7.59 us
  transfers between devices with their start and end apart: 23, of which 10 were waited for; matrix products, arithmetic and copies ran while one was open for 4% of the time, Pallas kernels for 14%

profile of v9, /device:TPU:1, one launch (start us, length us, event | category | flops | bytes accessed | tf_op | source)
XLA Modules:
  0.0 134.2 jit_solution(14682333558768528376)
XLA Ops:
  1.3 1.8 %make_piece.1.after_ref = bf16[8,128,128]{2,1,0:T(8,128)(2,1)} custom-call(s32[5]{0:T(128)} %stack.23.at_ref, f32[128,1024]{1,0:T(8,128)} %params_ref.1), custom_call_target="tpu_custom_call" | custom-call | tf_op jit(solution)/shard_map/make_piece/pallas_call | solution.py:38
  3.1 9.0 %all-to-all-start = ((bf16[8,128,128]{2,1,0:T(8,128)(2,1)}), bf16[8,128,128]{2,1,0:T(8,128)(2,1)S(1)}, u32[]{:S(2)}, u32[]{:S(2)}) async-start(bf16[8,128,128]{2,1,0:T(8,128)(2,1)} %make_piece.1.after_ref), calls=%async_computation | async-start | bytes 524288 | tf_op jit(solution)/shard_map/all_to_all | solution.py:285
  12.1 2.9 %pick.1 = bf16[256,2048]{1,0:T(8,128)(2,1)} custom-call(s32[5]{0:T(128)} %stack.23.at_ref, bf16[256,4096]{1,0:T(8,128)(2,1)} %tok_ref.5, bf16[8,128,128]{2,1,0:T(8,128)(2,1)} %make_piece.1.after_ref), custom_call_target="tpu_custom_call" | custom-call | tf_op jit(solution)/shard_map/pick/pallas_call | solution.py:56
  15.9 6.7 %all-to-all-done = bf16[8,128,128]{2,1,0:T(8,128)(2,1)S(1)} async-done(((bf16[8,128,128]{2,1,0:T(8,128)(2,1)}), bf16[8,128,128]{2,1,0:T(8,128)(2,1)S(1)}, u32[]{:S(2)}, u32[]{:S(2)}) %all-to-all-start) | async-done | bytes 262176 | tf_op jit(solution)/shard_map/all_to_all | solution.py:285
  22.6 1.4 %collective-permute-start = (bf16[4,128,128]{2,1,0:T(8,128)(2,1)S(1)}, bf16[4,128,128]{2,1,0:T(8,128)(2,1)S(1)}, u32[]{:S(2)}, u32[]{:S(2)}) collective-permute-start(bf16[4,128,128]{2,1,0:T(8,128)(2,1)S(1)} %get-tuple-element.33), channel_id=1, source_target_pairs={{0,34},{1,65},{2,32},{3,67},{32,2},{33,97},{34,0},{35,99},{64,98},... | collective-permute-start | bytes 393224 | tf_op jit(solution)/shard_map/ppermute | solution.py:132
  24.0 1.9 %collective-permute-start.3 = (bf16[4,128,128]{2,1,0:T(8,128)(2,1)S(1)}, bf16[4,128,128]{2,1,0:T(8,128)(2,1)S(1)}, u32[]{:S(2)}, u32[]{:S(2)}) collective-permute-start(bf16[4,128,128]{2,1,0:T(8,128)(2,1)S(1)} %get-tuple-element.32), channel_id=1, source_target_pairs={{0,32},{1,193},{2,34},{3,195},{32,0},{33,225},{34,2},{35,227},{64,... | collective-permute-start | bytes 393224 | tf_op jit(solution)/shard_map/ppermute | solution.py:132
  26.5 1.3 collective-permute-start.1
  29.1 2.6 %collective-permute-start.4 = (bf16[8,128,128]{2,1,0:T(8,128)(2,1)S(1)}, bf16[8,128,128]{2,1,0:T(8,128)(2,1)S(1)}, u32[]{:S(2)}, u32[]{:S(2)}) collective-permute-start(bf16[8,128,128]{2,1,0:T(8,128)(2,1)S(1)} %pad_maximum_fusion.5), channel_id=1, source_target_pairs={{0,192},{1,35},{2,194},{3,33},{32,224},{33,3},{34,226},{35,1},{64,... | collective-permute-start | bytes 786440 | tf_op jit(solution)/shard_map/ppermute | solution.py:132
  31.6 3.2 %make_q.1.q_ref = bf16[256,512]{1,0:T(8,128)(2,1)} custom-call(bf16[256,1024]{1,0:T(8,128)(2,1)} %up_ref.5, f32[1024,512]{1,0:T(8,128)} %proj_ref.1), custom_call_target="tpu_custom_call" | custom-call | flops 1073741824 | bytes 3145728 | tf_op jit(solution)/shard_map/make_q/pallas_call | solution.py:73
  34.8 5.5 %collective-permute-start.13 = (bf16[256,512]{1,0:T(8,128)(2,1)}, bf16[256,512]{1,0:T(8,128)(2,1)S(1)}, u32[]{:S(2)}, u32[]{:S(2)}) collective-permute-start(bf16[256,512]{1,0:T(8,128)(2,1)} %make_q.1.q_ref), channel_id=1, source_target_pairs={{0,1},{1,0},{2,3},{3,2},{4,5},{5,4},{6,7},{7,6},{8,9},{9,8},{10,11... | collective-permute-start | bytes 786440 | tf_op jit(solution)/shard_map/ppermute | solution.py:288
  42.4 4.2 %make_sketch.1 = (bf16[2,128,512]{2,1,0:T(8,128)(2,1)}, bf16[2,128,512]{2,1,0:T(8,128)(2,1)}, bf16[2,128,512]{2,1,0:T(8,128)(2,1)}, bf16[2,128,512]{2,1,0:T(8,12...) custom-call(s32[5]{0:T(128)} %stack.23.at_ref, ...), custom_call_target="tpu_custom_call" | custom-call | flops 4294967296 | bytes 16777216 | tf_op jit(solution)/shard_map/make_sketch/pallas_call | solution.py:104
  46.7 3.3 %collective-permute-done.2 = bf16[16,128,128]{2,1,0:T(8,128)(2,1)S(1)} collective-permute-done((bf16[16,128,128]{2,1,0:T(8,128)(2,1)S(1)}, bf16[16,128,128]{2,1,0:T(8,128)(2,1)S(1)}, u32[]{:S(2)}, u32[]{:S(2)}) %collective-permute-start.2) | collective-permute-done | bytes 524320 | tf_op jit(solution)/shard_map/ppermute | solution.py:132
  52.8 1.4 %collective-permute-start.17 = (bf16[2,128,512]{2,1,0:T(8,128)(2,1)S(1)}, bf16[2,128,512]{2,1,0:T(8,128)(2,1)S(1)}, u32[]{:S(2)}, u32[]{:S(2)}) collective-permute-start(bf16[2,128,512]{2,1,0:T(8,128)(2,1)S(1)} %copy-done.8), channel_id=1, source_target_pairs={{0,4},{4,8},{8,12},{12,16},{16,20},{20,24},{24,28},{28,0},{1,5},{5... | collective-permute-start | bytes 786440 | tf_op jit(solution)/shard_map/ppermute | solution.py:292
  54.4 5.6 %collective-permute-done.18 = bf16[2,128,512]{2,1,0:T(8,128)(2,1)S(1)} collective-permute-done((bf16[2,128,512]{2,1,0:T(8,128)(2,1)S(1)}, bf16[2,128,512]{2,1,0:T(8,128)(2,1)S(1)}, u32[]{:S(2)}, u32[]{:S(2)}) %collective-permute-start.18) | collective-permute-done | bytes 262176 | tf_op jit(solution)/shard_map/ppermute | solution.py:292
  61.6 9.0 %collective-permute-done.16 = bf16[2,128,512]{2,1,0:T(8,128)(2,1)S(1)} collective-permute-done((bf16[2,128,512]{2,1,0:T(8,128)(2,1)S(1)}, bf16[2,128,512]{2,1,0:T(8,128)(2,1)S(1)}, u32[]{:S(2)}, u32[]{:S(2)}) %collective-permute-start.16) | collective-permute-done | bytes 262176 | tf_op jit(solution)/shard_map/ppermute | solution.py:292
  70.6 6.0 %collective-permute-done.15 = bf16[2,128,512]{2,1,0:T(8,128)(2,1)S(1)} collective-permute-done((bf16[2,128,512]{2,1,0:T(8,128)(2,1)S(1)}, bf16[2,128,512]{2,1,0:T(8,128)(2,1)S(1)}, u32[]{:S(2)}, u32[]{:S(2)}) %collective-permute-start.15) | collective-permute-done | bytes 262176 | tf_op jit(solution)/shard_map/ppermute | solution.py:292
  76.6 7.5 %collective-permute-start.6 = (bf16[32,128,128]{2,1,0:T(8,128)(2,1)}, bf16[32,128,128]{2,1,0:T(8,128)(2,1)}, u32[]{:S(2)}, u32[]{:S(2)}) collective-permute-start(bf16[32,128,128]{2,1,0:T(8,128)(2,1)} %pad_maximum_fusion.refs_0_), channel_id=1, source_target_pairs={{0,1},{1,0},{2,3},{3,2},{4,5},{5,4},{6,7},{7,6},{8,9},{9,8},{10,11... | collective-permute-start | bytes 3145736 | tf_op jit(solution)/shard_map/ppermute | solution.py:310
  84.1 7.5 %collective-permute-start.7 = (bf16[32,128,128]{2,1,0:T(8,128)(2,1)}, bf16[32,128,128]{2,1,0:T(8,128)(2,1)}, u32[]{:S(2)}, u32[]{:S(2)}) collective-permute-start(bf16[32,128,128]{2,1,0:T(8,128)(2,1)} %pad_maximum_fusion.1.refs_1_), channel_id=1, source_target_pairs={{0,1},{1,0},{2,3},{3,2},{4,5},{5,4},{6,7},{7,6},{8,9},{9,8},{10,11... | collective-permute-start | bytes 3145736 | tf_op jit(solution)/shard_map/ppermute | solution.py:310
  92.6 6.1 %all-to-all-start.1 = ((bf16[16,16,512]{2,1,0:T(8,128)(2,1)}), bf16[16,16,512]{2,1,0:T(8,128)(2,1)S(1)}, u32[]{:S(2)}, u32[]{:S(2)}) async-start(bf16[16,16,512]{2,1,0:T(8,128)(2,1)} %bitcast.5), calls=%async_computation.1 | async-start | bytes 524288 | tf_op jit(solution)/shard_map/all_to_all | solution.py:316
  99.3 7.6 %all-to-all-done.1 = bf16[16,16,512]{2,1,0:T(8,128)(2,1)S(1)} async-done(((bf16[16,16,512]{2,1,0:T(8,128)(2,1)}), bf16[16,16,512]{2,1,0:T(8,128)(2,1)S(1)}, u32[]{:S(2)}, u32[]{:S(2)}) %all-to-all-start.1) | async-done | bytes 262176 | tf_op jit(solution)/shard_map/all_to_all | solution.py:316
  106.9 8.1 %all_to_all.15 = bf16[8,16,512]{2,1,0:T(8,128)(2,1)S(1)} all-to-all(bf16[8,16,512]{2,1,0:T(8,128)(2,1)S(1)} %broadcast_in_dim.2), channel_id=1, replica_groups=mesh['y'=4,'xl'=2,'z'=8,'xh'=2,'c'=2] {'y','xl'}, dimensions={0} | all-to-all | bytes 262144 | tf_op jit(solution)/shard_map/all_to_all | solution.py:319
  115.6 1.5 %multiply_subtract_fusion = (f32[128,1024]{1,0:T(8,128)}, f32[128,1024]{1,0:T(8,128)}) fusion(f32[128,1024]{1,0:T(8,128)S(1)} %copy-done.1, f32[128,1024]{1,0:T(8,128)S(1)} %copy-done.2, f32[128,1024]{1,0:T(8,128)S(1)} %fusion.2, bf16[128,512]{1,0:T(8,128)(2,1)S(1)} %bitcast.10, f32[1024,512]{1,0:T(8,128)S(1)} %copy-done), kind=kOutput, calls=%fused_computation.7 | convolution fusion | flops 137363456 | bytes 4849664 | tf_op jit(solution)/shard_map/dot_general | solution.py:325
  117.1 8.0 %near_products.1 = (f32[256,1024]{1,0:T(8,128)}, f32[4,256,512]{2,1,0:T(8,128)}, f32[4,256,512]{2,1,0:T(8,128)}) custom-call(s32[5]{0:T(128)} %stack.23.at_ref, bf16[256,4096]{1,0:T(8,128)(2,1)} %tok_ref.5, bf16[256,1024]{1,0:T(8,128)(2,1)} %up_ref.5, bf16[32,128,128]{2,1,0:T(8,128)(2,1)} %pad_maximum_fusion.refs_0_, ...), custom_call_target="tpu_custom_call" | custom-call | flops 2147483648 | bytes 4194304 | tf_op jit(solution)/shard_map/near_products/pallas_call | solution.py:241
  125.1 9.1 %far_products.1 = (bf16[256,1024]{1,0:T(8,128)(2,1)}, bf16[256,4096]{1,0:T(8,128)(2,1)}) custom-call(s32[5]{0:T(128)} %stack.23.at_ref, bf16[256,4096]{1,0:T(8,128)(2,1)} %tok_ref.5, bf16[256,1024]{1,0:T(8,128)(2,1)} %up_ref.5, f32[256,1024]{1,0:T(8,128)} %get-tuple-element.17.before_ref, f32[4,256,512]{2,1,0:T(8,128)} %get-tuple-element.18.refs_0_, ...), custom_call_target="tpu_custom_call" | custom-call | flops 2147483648 | bytes 4194304 | tf_op jit(solution)/shard_map/far_products/pallas_call | solution.py:258
  (65 shorter events, 12.3 us)
Async XLA Ops:
  3.1 19.5 %all-to-all-start = ((bf16[8,128,128]{2,1,0:T(8,128)(2,1)}), bf16[8,128,128]{2,1,0:T(8,128)(2,1)S(1)}, u32[]{:S(2)}, u32[]{:S(2)}) async-start(bf16[8,128,128]{2,1,0:T(8,128)(2,1)} %make_piece.1.after_ref), calls=%async_computation | async-start | bytes 524288 | tf_op jit(solution)/shard_map/all_to_all | solution.py:285
  14.9 26.7 %collective-permute-start.12 = (bf16[256,2048]{1,0:T(8,128)(2,1)}, bf16[256,2048]{1,0:T(8,128)(2,1)}, u32[]{:S(2)}, u32[]{:S(2)}) collective-permute-start(bf16[256,2048]{1,0:T(8,128)(2,1)} %pick.1), channel_id=1, source_target_pairs={{0,1},{1,0},{2,3},{3,2},{4,5},{5,4},{6,7},{7,6},{8,9},{9,8},{10,11... | collective-permute-start | bytes 3145736 | tf_op jit(solution)/shard_map/ppermute | solution.py:284
  22.6 3.9 %collective-permute-start = (bf16[4,128,128]{2,1,0:T(8,128)(2,1)S(1)}, bf16[4,128,128]{2,1,0:T(8,128)(2,1)S(1)}, u32[]{:S(2)}, u32[]{:S(2)}) collective-permute-start(bf16[4,128,128]{2,1,0:T(8,128)(2,1)S(1)} %get-tuple-element.33), channel_id=1, source_target_pairs={{0,34},{1,65},{2,32},{3,67},{32,2},{33,97},{34,0},{35,99},{64,98},... | collective-permute-start | bytes 393224 | tf_op jit(solution)/shard_map/ppermute | solution.py:132
  24.0 5.0 %collective-permute-start.3 = (bf16[4,128,128]{2,1,0:T(8,128)(2,1)S(1)}, bf16[4,128,128]{2,1,0:T(8,128)(2,1)S(1)}, u32[]{:S(2)}, u32[]{:S(2)}) collective-permute-start(bf16[4,128,128]{2,1,0:T(8,128)(2,1)S(1)} %get-tuple-element.32), channel_id=1, source_target_pairs={{0,32},{1,193},{2,34},{3,195},{32,0},{33,225},{34,2},{35,227},{64,... | collective-permute-start | bytes 393224 | tf_op jit(solution)/shard_map/ppermute | solution.py:132
  26.5 13.7 %collective-permute-start.1 = (bf16[8,128,128]{2,1,0:T(8,128)(2,1)S(1)}, bf16[8,128,128]{2,1,0:T(8,128)(2,1)S(1)}, u32[]{:S(2)}, u32[]{:S(2)}) collective-permute-start(bf16[8,128,128]{2,1,0:T(8,128)(2,1)S(1)} %pad_maximum_fusion.4), channel_id=1, source_target_pairs={{0,64},{1,33},{2,66},{3,35},{32,96},{33,1},{34,98},{35,3},{64,0},{... | collective-permute-start | bytes 786440 | tf_op jit(solution)/shard_map/ppermute | solution.py:132
  29.1 11.4 %collective-permute-start.4 = (bf16[8,128,128]{2,1,0:T(8,128)(2,1)S(1)}, bf16[8,128,128]{2,1,0:T(8,128)(2,1)S(1)}, u32[]{:S(2)}, u32[]{:S(2)}) collective-permute-start(bf16[8,128,128]{2,1,0:T(8,128)(2,1)S(1)} %pad_maximum_fusion.5), channel_id=1, source_target_pairs={{0,192},{1,35},{2,194},{3,33},{32,224},{33,3},{34,226},{35,1},{64,... | collective-permute-start | bytes 786440 | tf_op jit(solution)/shard_map/ppermute | solution.py:132
  34.8 6.8 %collective-permute-start.13 = (bf16[256,512]{1,0:T(8,128)(2,1)}, bf16[256,512]{1,0:T(8,128)(2,1)S(1)}, u32[]{:S(2)}, u32[]{:S(2)}) collective-permute-start(bf16[256,512]{1,0:T(8,128)(2,1)} %make_q.1.q_ref), channel_id=1, source_target_pairs={{0,1},{1,0},{2,3},{3,2},{4,5},{5,4},{6,7},{7,6},{8,9},{9,8},{10,11... | collective-permute-start | bytes 786440 | tf_op jit(solution)/shard_map/ppermute | solution.py:288
  40.4 9.6 %collective-permute-start.2 = (bf16[16,128,128]{2,1,0:T(8,128)(2,1)S(1)}, bf16[16,128,128]{2,1,0:T(8,128)(2,1)S(1)}, u32[]{:S(2)}, u32[]{:S(2)}) collective-permute-start(bf16[16,128,128]{2,1,0:T(8,128)(2,1)S(1)} %pad_maximum_fusion.2), channel_id=1, source_target_pairs={{0,32},{1,193},{2,34},{3,195},{32,0},{33,225},{34,2},{35,227},{64,... | collective-permute-start | bytes 1572872 | tf_op jit(solution)/shard_map/ppermute | solution.py:132
  40.5 11.1 %collective-permute-start.5 = (bf16[16,128,128]{2,1,0:T(8,128)(2,1)S(1)}, bf16[16,128,128]{2,1,0:T(8,128)(2,1)S(1)}, u32[]{:S(2)}, u32[]{:S(2)}) collective-permute-start(bf16[16,128,128]{2,1,0:T(8,128)(2,1)S(1)} %pad_maximum_fusion.3), channel_id=1, source_target_pairs={{0,34},{1,65},{2,32},{3,67},{32,2},{33,97},{34,0},{35,99},{64,98},... | collective-permute-start | bytes 1572872 | tf_op jit(solution)/shard_map/ppermute | solution.py:132
  46.6 7.7 %collective-permute-start.19 = (bf16[2,128,512]{2,1,0:T(8,128)(2,1)}, bf16[2,128,512]{2,1,0:T(8,128)(2,1)S(1)}, u32[]{:S(2)}, u32[]{:S(2)}) collective-permute-start(bf16[2,128,512]{2,1,0:T(8,128)(2,1)} %get-tuple-element.29), channel_id=1, source_target_pairs={{0,28},{4,0},{8,4},{12,8},{16,12},{20,16},{24,20},{28,24},{1,29},{... | collective-permute-start | bytes 786440 | tf_op jit(solution)/shard_map/ppermute | solution.py:292
  51.0 47.6 %collective-permute-start.8 = (bf16[32,128,128]{2,1,0:T(8,128)(2,1)}, bf16[32,128,128]{2,1,0:T(8,128)(2,1)}, u32[]{:S(2)}, u32[]{:S(2)}) collective-permute-start(bf16[32,128,128]{2,1,0:T(8,128)(2,1)} %pad_maximum_fusion.refs_0_), channel_id=1, source_target_pairs={{0,192},{1,35},{2,194},{3,33},{32,224},{33,3},{34,226},{35,1},{64,... | collective-permute-start | bytes 3145736 | tf_op jit(solution)/shard_map/ppermute | solution.py:132
  52.7 62.3 %copy-start = (f32[1024,512]{1,0:T(8,128)S(1)}, f32[1024,512]{1,0:T(8,128)}, u32[]{:S(2)}) copy-start(f32[1024,512]{1,0:T(8,128)} %proj_ref.1) | copy-start | bytes 6291460
  52.7 46.4 %collective-permute-start.9 = (bf16[32,128,128]{2,1,0:T(8,128)(2,1)}, bf16[32,128,128]{2,1,0:T(8,128)(2,1)}, u32[]{:S(2)}, u32[]{:S(2)}) collective-permute-start(bf16[32,128,128]{2,1,0:T(8,128)(2,1)} %pad_maximum_fusion.1.refs_1_), channel_id=1, source_target_pairs={{0,64},{1,33},{2,66},{3,35},{32,96},{33,1},{34,98},{35,3},{64,0},{... | collective-permute-start | bytes 3145736 | tf_op jit(solution)/shard_map/ppermute | solution.py:132
  52.7 7.2 %collective-permute-start.18 = (bf16[2,128,512]{2,1,0:T(8,128)(2,1)S(1)}, bf16[2,128,512]{2,1,0:T(8,128)(2,1)S(1)}, u32[]{:S(2)}, u32[]{:S(2)}) collective-permute-start(bf16[2,128,512]{2,1,0:T(8,128)(2,1)S(1)} %copy-done.9), channel_id=1, source_target_pairs={{0,28},{4,0},{8,4},{12,8},{16,12},{20,16},{24,20},{28,24},{1,29},{... | collective-permute-start | bytes 786440 | tf_op jit(solution)/shard_map/ppermute | solution.py:292
  52.8 8.4 %collective-permute-start.17 = (bf16[2,128,512]{2,1,0:T(8,128)(2,1)S(1)}, bf16[2,128,512]{2,1,0:T(8,128)(2,1)S(1)}, u32[]{:S(2)}, u32[]{:S(2)}) collective-permute-start(bf16[2,128,512]{2,1,0:T(8,128)(2,1)S(1)} %copy-done.8), channel_id=1, source_target_pairs={{0,4},{4,8},{8,12},{12,16},{16,20},{20,24},{24,28},{28,0},{1,5},{5... | collective-permute-start | bytes 786440 | tf_op jit(solution)/shard_map/ppermute | solution.py:292
  54.3 16.3 %collective-permute-start.16 = (bf16[2,128,512]{2,1,0:T(8,128)(2,1)S(1)}, bf16[2,128,512]{2,1,0:T(8,128)(2,1)S(1)}, u32[]{:S(2)}, u32[]{:S(2)}) collective-permute-start(bf16[2,128,512]{2,1,0:T(8,128)(2,1)S(1)} %copy-done.7), channel_id=1, source_target_pairs={{0,24},{4,28},{8,0},{12,4},{16,8},{20,12},{24,16},{28,20},{1,25},{... | collective-permute-start | bytes 786440 | tf_op jit(solution)/shard_map/ppermute | solution.py:292
  60.0 16.6 %collective-permute-start.15 = (bf16[2,128,512]{2,1,0:T(8,128)(2,1)S(1)}, bf16[2,128,512]{2,1,0:T(8,128)(2,1)S(1)}, u32[]{:S(2)}, u32[]{:S(2)}) collective-permute-start(bf16[2,128,512]{2,1,0:T(8,128)(2,1)S(1)} %copy-done.6), channel_id=1, source_target_pairs={{0,8},{4,12},{8,16},{12,20},{16,24},{20,28},{24,0},{28,4},{1,9},{5... | collective-permute-start | bytes 786440 | tf_op jit(solution)/shard_map/ppermute | solution.py:292
  61.2 22.9 %collective-permute-start.14 = (bf16[2,128,512]{2,1,0:T(8,128)(2,1)S(1)}, bf16[2,128,512]{2,1,0:T(8,128)(2,1)S(1)}, u32[]{:S(2)}, u32[]{:S(2)}) collective-permute-start(bf16[2,128,512]{2,1,0:T(8,128)(2,1)S(1)} %copy-done.5), channel_id=1, source_target_pairs={{0,12},{4,16},{8,20},{12,24},{16,28},{20,0},{24,4},{28,8},{1,13},{... | collective-permute-start | bytes 786440 | tf_op jit(solution)/shard_map/ppermute | solution.py:292
  70.6 21.1 %collective-permute-start.20 = (bf16[2,128,512]{2,1,0:T(8,128)(2,1)S(1)}, bf16[2,128,512]{2,1,0:T(8,128)(2,1)S(1)}, u32[]{:S(2)}, u32[]{:S(2)}) collective-permute-start(bf16[2,128,512]{2,1,0:T(8,128)(2,1)S(1)} %add_convert_fusion.1), channel_id=1, source_target_pairs={{0,20},{4,24},{8,28},{12,0},{16,4},{20,8},{24,12},{28,16},{1,21},{... | collective-permute-start | bytes 786440 | tf_op jit(solution)/shard_map/ppermute | solution.py:292
  76.6 40.5 %collective-permute-start.6 = (bf16[32,128,128]{2,1,0:T(8,128)(2,1)}, bf16[32,128,128]{2,1,0:T(8,128)(2,1)}, u32[]{:S(2)}, u32[]{:S(2)}) collective-permute-start(bf16[32,128,128]{2,1,0:T(8,128)(2,1)} %pad_maximum_fusion.refs_0_), channel_id=1, source_target_pairs={{0,1},{1,0},{2,3},{3,2},{4,5},{5,4},{6,7},{7,6},{8,9},{9,8},{10,11... | collective-permute-start | bytes 3145736 | tf_op jit(solution)/shard_map/ppermute | solution.py:310
  84.1 33.0 %collective-permute-start.7 = (bf16[32,128,128]{2,1,0:T(8,128)(2,1)}, bf16[32,128,128]{2,1,0:T(8,128)(2,1)}, u32[]{:S(2)}, u32[]{:S(2)}) collective-permute-start(bf16[32,128,128]{2,1,0:T(8,128)(2,1)} %pad_maximum_fusion.1.refs_1_), channel_id=1, source_target_pairs={{0,1},{1,0},{2,3},{3,2},{4,5},{5,4},{6,7},{7,6},{8,9},{9,8},{10,11... | collective-permute-start | bytes 3145736 | tf_op jit(solution)/shard_map/ppermute | solution.py:310
  92.6 14.3 %all-to-all-start.1 = ((bf16[16,16,512]{2,1,0:T(8,128)(2,1)}), bf16[16,16,512]{2,1,0:T(8,128)(2,1)S(1)}, u32[]{:S(2)}, u32[]{:S(2)}) async-start(bf16[16,16,512]{2,1,0:T(8,128)(2,1)} %bitcast.5), calls=%async_computation.1 | async-start | bytes 524288 | tf_op jit(solution)/shard_map/all_to_all | solution.py:316
  98.7 26.4 %collective-permute-start.10 = (bf16[32,128,128]{2,1,0:T(8,128)(2,1)}, bf16[32,128,128]{2,1,0:T(8,128)(2,1)}, u32[]{:S(2)}, u32[]{:S(2)}) collective-permute-start(bf16[32,128,128]{2,1,0:T(8,128)(2,1)} %collective-permute-done.8.refs_2_), channel_id=1, source_target_pairs={{0,1},{1,0},{2,3},{3,2},{4,5},{5,4},{6,7},{7,6},{8,9},{9,8},{10,11... | collective-permute-start | bytes 3145736 | tf_op jit(solution)/shard_map/ppermute | solution.py:312
  99.1 26.0 %collective-permute-start.11 = (bf16[32,128,128]{2,1,0:T(8,128)(2,1)}, bf16[32,128,128]{2,1,0:T(8,128)(2,1)}, u32[]{:S(2)}, u32[]{:S(2)}) collective-permute-start(bf16[32,128,128]{2,1,0:T(8,128)(2,1)} %collective-permute-done.9.refs_3_), channel_id=1, source_target_pairs={{0,1},{1,0},{2,3},{3,2},{4,5},{5,4},{6,7},{7,6},{8,9},{9,8},{10,11... | collective-permute-start | bytes 3145736 | tf_op jit(solution)/shard_map/ppermute | solution.py:312
  (10 other events, 147.6 us)

commit v10 on v9

--- a/solution.py
+++ b/solution.py
@@ -151,13 +151,37 @@
     return jnp.concatenate([ref[:, at] for at in blocks], axis=1)
 
 
-def half_products(half, groups, core, at_ref, tok_ref, w_refs, acc_ref, up_rel, take):
+class Loads:
+    def __init__(self, sources, targets, sems):
+        self.targets = targets
+        self.copies = [
+            pltpu.make_async_copy(a, b, sems.at[i]) for i, (a, b) in enumerate(zip(sources, targets))
+        ]
+        for copy in self.copies:
+            copy.start()
+        self.left = None
+
+    def begin(self):
+        self.left = set(range(len(self.copies)))
+
+    def get(self, i):
+        if i in self.left:
+            self.left.remove(i)
+            self.copies[i].wait()
+        return self.targets[i]
+
+    def finish(self):
+        for i in sorted(self.left):
+            self.get(i)
+
+
+def half_products(half, groups, core, at_ref, tok_ref, get_w, acc_ref, up_rel, take):
     xh = at_ref[2]
-    each = w_refs[0].shape[0] // 8
+    each = tok_ref.shape[1] // (4 * LANES * GROUPS)
     for n, g in enumerate(groups):
         for o in range(2):
             table = places(core ^ o, g)
-            w_ref = w_refs[len(groups) * o + n]
+            w_ref = get_w(len(groups) * o + n)
             for a in range(2):
                 zs = range(g * each, (g + 1) * each)
                 blocks = [
@@ -196,7 +220,9 @@
 
 
 def near_kernel(at_ref, tok_ref, up_ref, *refs):
-    w_refs, (acc_ref, *sum_refs, up_rel) = refs[: 2 * GROUPS], refs[2 * GROUPS :]
+    n = 2 * GROUPS
+    w_refs, (acc_ref, *sum_refs), (up_rel, *held, sems) = refs[:n], refs[n : n + 1 + GROUPS], refs[n + 1 + GROUPS :]
+    loads = Loads(w_refs, held, sems)
     acc_ref[...] = jnp.zeros(acc_ref.shape, F32)
     arrange(at_ref, up_ref, up_rel)
 
@@ -206,14 +232,17 @@
 
     for core in range(2):
 
-        @pl.when(at_ref[0] == core)
+        @pl.when(lax.axis_index("c") == core)
         def _():
-            half_products(0, range(GROUPS), core, at_ref, tok_ref, w_refs, acc_ref, up_rel, take)
+            loads.begin()
+            half_products(0, range(GROUPS), core, at_ref, tok_ref, loads.get, acc_ref, up_rel, take)
+            loads.finish()
 
 
 def far_kernel(at_ref, tok_ref, up_ref, before_ref, *refs, scale):
-    sum_refs, w_refs = refs[:GROUPS], refs[GROUPS : 3 * GROUPS]
-    values_ref, grads_ref, acc_ref, up_rel = refs[3 * GROUPS :]
+    n = 3 * GROUPS
+    values_ref, grads_ref, acc_ref, up_rel, *held, sems = refs[n:]
+    loads = Loads(refs[:n], held, sems)
     acc_ref[...] = before_ref[...]
     arrange(at_ref, up_ref, up_rel)
 
@@ -221,18 +250,24 @@
 
         def take(g, a, o, blocks, total, core=core):
             if places(core ^ o, g)[0, a]:
-                before = sum_refs[g][2 * a + o]
+                before = loads.get(2 * GROUPS + g)[2 * a + o]
                 total = before if total is None else total + before
             grad = (total * scale).astype(BF16)
             for k, at in enumerate(blocks):
                 grads_ref[:, at] = grad[:, k * LANES : (k + 1) * LANES]
 
-        @pl.when(at_ref[0] == core)
+        @pl.when(lax.axis_index("c") == core)
         def _():
-            half_products(1, range(GROUPS), core, at_ref, tok_ref, w_refs, acc_ref, up_rel, take)
+            loads.begin()
+            half_products(1, range(GROUPS), core, at_ref, tok_ref, loads.get, acc_ref, up_rel, take)
+            loads.finish()
 
     for r, at in enumerate(columns(at_ref)):
         values_ref[:, at] = (acc_ref[:, r * LANES : (r + 1) * LANES] * scale).astype(BF16)
+
+
+def loaded(arrays):
+    return [*(pltpu.VMEM(a.shape, a.dtype) for a in arrays), pltpu.SemaphoreType.DMA((len(arrays),))]
 
 
 def near_products(at, tokens, upstream, weights):
@@ -244,9 +279,9 @@
             jax.ShapeDtypeStruct((t, kv), F32),
             *[jax.ShapeDtypeStruct((4, t, d // (4 * GROUPS)), F32)] * GROUPS,
         ),
-        in_specs=[SMEM] + [VMEM] * (2 + len(weights)),
+        in_specs=[SMEM, VMEM, VMEM] + [LEFT] * len(weights),
         out_specs=(VMEM,) * (1 + GROUPS),
-        scratch_shapes=[pltpu.VMEM((t, kv), BF16)],
+        scratch_shapes=[pltpu.VMEM((t, kv), BF16), *loaded(weights)],
         cost_estimate=pl.CostEstimate(flops=2 * t * d * kv, bytes_accessed=d * kv, transcendentals=0),
         name="near_products",
     )(at, tokens, upstream, *weights)
@@ -258,12 +293,12 @@
     return pl.pallas_call(
         functools.partial(far_kernel, scale=scale),
         out_shape=(jax.ShapeDtypeStruct((t, kv), BF16), jax.ShapeDtypeStruct((t, d), BF16)),
-        in_specs=[SMEM] + [VMEM] * (3 + len(sums) + len(weights)),
+        in_specs=[SMEM, VMEM, VMEM, VMEM] + [LEFT] * (len(sums) + len(weights)),
         out_specs=(VMEM, VMEM),
-        scratch_shapes=[pltpu.VMEM((t, kv), F32), pltpu.VMEM((t, kv), BF16)],
+        scratch_shapes=[pltpu.VMEM((t, kv), F32), pltpu.VMEM((t, kv), BF16), *loaded([*weights, *sums])],
         cost_estimate=pl.CostEstimate(flops=2 * t * d * kv, bytes_accessed=d * kv, transcendentals=0),
         name="far_products",
-    )(at, tokens, upstream, acc, *sums, *weights)
+    )(at, tokens, upstream, acc, *weights, *sums)
 
 
 def step(tokens, upstream, params, momentum, projection):
@@ -308,9 +343,8 @@
         held = [jnp.concatenate(both, axis=0) for both in zip(held, more)]
     far = [exchange(h, g, 3) for g, h in enumerate(held)]
     acc, *sums = near_products(at, tokens, upstream, [*held, *(swap(h) for h in held)])
-    values, token_grads = far_products(
-        at, tokens, upstream, acc, sums, [*far, *(swap(f) for f in far)], inv_width
-    )
+    swapped = [swap(f) for f in far]
+    values, token_grads = far_products(at, tokens, upstream, acc, sums, [*far, *swapped], inv_width)
 
     along = along.astype(BF16)
     plane = lax.all_to_all(along.reshape(n_xh * n_isl, part, proj), PLANE, 0, 0, tiled=True)

time: 137 us -> 138 us (level)
  no operation moved by 1% of the time
where the time goes in v10:
time: 138 us; the launch traced here: 136 us
  starting transfers between devices  47 us (34%)
  waiting for transfers between devices  42.3 us (31%)
  Pallas kernels  30.3 us (22%)
  blocking collectives  8.13 us (6%)
  other arithmetic  3.35 us (2%)
  matrix products  2.01 us (1%)
  local copies, waits for them, and re-layouts  1.44 us (1%)
    ppermute x7, waiting for transfers between devices, shift(): return lax.ppermute(x, 'z', [(i, (i + k) % n_z) for i in range(n_z)])  21.9 us
    ppermute x2, starting transfers between devices, step(): swap(h)  15 us
    pallas_call x1, Pallas kernels, far_products(): pl.pallas_call(functools.partial(far_kernel, scale=scale), out_shape=(jax...  10 us
    all_to_all x1, starting transfers between devices, step(): piece = lax.all_to_all(piece, 'z', 0, 0, tiled=True)  9 us
    pallas_call x1, Pallas kernels, near_products(): pl.pallas_call(near_kernel, out_shape=(jax.ShapeDtypeStruct((t, kv), F32)...  8.25 us
    all_to_all x1, blocking collectives, step(): total = lax.all_to_all(total, ISLAND, 0, 0, tiled=True)  8.13 us
    ppermute x8, starting transfers between devices, exchange(): return lax.ppermute(x, ('y', 'xl', 'xh', 'c'), pairs)  7.94 us
    all_to_all x1, waiting for transfers between devices, step(): lax.all_to_all(along.reshape(n_xh * n_isl, part, proj), PLANE, 0, 0, tile...  7.59 us
  transfers between devices with their start and end apart: 23, of which 10 were waited for; matrix products, arithmetic and copies ran while one was open for 4% of the time, Pallas kernels for 14%

profile of v10, /device:TPU:1, one launch (start us, length us, event | category | flops | bytes accessed | tf_op | source)
XLA Modules:
  0.0 135.6 jit_solution(14574882303341785471)
XLA Ops:
  1.3 1.8 %make_piece.1.after_ref = bf16[8,128,128]{2,1,0:T(8,128)(2,1)} custom-call(s32[5]{0:T(128)} %stack.23.at_ref, f32[128,1024]{1,0:T(8,128)} %params_ref.1), custom_call_target="tpu_custom_call" | custom-call | tf_op jit(solution)/shard_map/make_piece/pallas_call | solution.py:38
  3.1 9.0 %all-to-all-start = ((bf16[8,128,128]{2,1,0:T(8,128)(2,1)}), bf16[8,128,128]{2,1,0:T(8,128)(2,1)S(1)}, u32[]{:S(2)}, u32[]{:S(2)}) async-start(bf16[8,128,128]{2,1,0:T(8,128)(2,1)} %make_piece.1.after_ref), calls=%async_computation | async-start | bytes 524288 | tf_op jit(solution)/shard_map/all_to_all | solution.py:320
  12.1 2.9 %pick.1 = bf16[256,2048]{1,0:T(8,128)(2,1)} custom-call(s32[5]{0:T(128)} %stack.23.at_ref, bf16[256,4096]{1,0:T(8,128)(2,1)} %tok_ref.5, bf16[8,128,128]{2,1,0:T(8,128)(2,1)} %make_piece.1.after_ref), custom_call_target="tpu_custom_call" | custom-call | tf_op jit(solution)/shard_map/pick/pallas_call | solution.py:56
  15.9 6.7 %all-to-all-done = bf16[8,128,128]{2,1,0:T(8,128)(2,1)S(1)} async-done(((bf16[8,128,128]{2,1,0:T(8,128)(2,1)}), bf16[8,128,128]{2,1,0:T(8,128)(2,1)S(1)}, u32[]{:S(2)}, u32[]{:S(2)}) %all-to-all-start) | async-done | bytes 262176 | tf_op jit(solution)/shard_map/all_to_all | solution.py:320
  22.6 1.4 %collective-permute-start = (bf16[4,128,128]{2,1,0:T(8,128)(2,1)S(1)}, bf16[4,128,128]{2,1,0:T(8,128)(2,1)S(1)}, u32[]{:S(2)}, u32[]{:S(2)}) collective-permute-start(bf16[4,128,128]{2,1,0:T(8,128)(2,1)S(1)} %get-tuple-element.33), channel_id=1, source_target_pairs={{0,34},{1,65},{2,32},{3,67},{32,2},{33,97},{34,0},{35,99},{64,98},... | collective-permute-start | bytes 393224 | tf_op jit(solution)/shard_map/ppermute | solution.py:132
  24.0 1.9 %collective-permute-start.3 = (bf16[4,128,128]{2,1,0:T(8,128)(2,1)S(1)}, bf16[4,128,128]{2,1,0:T(8,128)(2,1)S(1)}, u32[]{:S(2)}, u32[]{:S(2)}) collective-permute-start(bf16[4,128,128]{2,1,0:T(8,128)(2,1)S(1)} %get-tuple-element.32), channel_id=1, source_target_pairs={{0,32},{1,193},{2,34},{3,195},{32,0},{33,225},{34,2},{35,227},{64,... | collective-permute-start | bytes 393224 | tf_op jit(solution)/shard_map/ppermute | solution.py:132
  26.5 1.3 collective-permute-start.1
  29.1 2.6 %collective-permute-start.4 = (bf16[8,128,128]{2,1,0:T(8,128)(2,1)S(1)}, bf16[8,128,128]{2,1,0:T(8,128)(2,1)S(1)}, u32[]{:S(2)}, u32[]{:S(2)}) collective-permute-start(bf16[8,128,128]{2,1,0:T(8,128)(2,1)S(1)} %pad_maximum_fusion.5), channel_id=1, source_target_pairs={{0,192},{1,35},{2,194},{3,33},{32,224},{33,3},{34,226},{35,1},{64,... | collective-permute-start | bytes 786440 | tf_op jit(solution)/shard_map/ppermute | solution.py:132
  31.6 3.2 %make_q.1.q_ref = bf16[256,512]{1,0:T(8,128)(2,1)} custom-call(bf16[256,1024]{1,0:T(8,128)(2,1)} %up_ref.5, f32[1024,512]{1,0:T(8,128)} %proj_ref.1), custom_call_target="tpu_custom_call" | custom-call | flops 1073741824 | bytes 3145728 | tf_op jit(solution)/shard_map/make_q/pallas_call | solution.py:73
  34.8 5.5 %collective-permute-start.13 = (bf16[256,512]{1,0:T(8,128)(2,1)}, bf16[256,512]{1,0:T(8,128)(2,1)S(1)}, u32[]{:S(2)}, u32[]{:S(2)}) collective-permute-start(bf16[256,512]{1,0:T(8,128)(2,1)} %make_q.1.q_ref), channel_id=1, source_target_pairs={{0,1},{1,0},{2,3},{3,2},{4,5},{5,4},{6,7},{7,6},{8,9},{9,8},{10,11... | collective-permute-start | bytes 786440 | tf_op jit(solution)/shard_map/ppermute | solution.py:323
  42.4 4.2 %make_sketch.1 = (bf16[2,128,512]{2,1,0:T(8,128)(2,1)}, bf16[2,128,512]{2,1,0:T(8,128)(2,1)}, bf16[2,128,512]{2,1,0:T(8,128)(2,1)}, bf16[2,128,512]{2,1,0:T(8,12...) custom-call(s32[5]{0:T(128)} %stack.23.at_ref, ...), custom_call_target="tpu_custom_call" | custom-call | flops 4294967296 | bytes 16777216 | tf_op jit(solution)/shard_map/make_sketch/pallas_call | solution.py:104
  46.7 3.3 %collective-permute-done.2 = bf16[16,128,128]{2,1,0:T(8,128)(2,1)S(1)} collective-permute-done((bf16[16,128,128]{2,1,0:T(8,128)(2,1)S(1)}, bf16[16,128,128]{2,1,0:T(8,128)(2,1)S(1)}, u32[]{:S(2)}, u32[]{:S(2)}) %collective-permute-start.2) | collective-permute-done | bytes 524320 | tf_op jit(solution)/shard_map/ppermute | solution.py:132
  52.8 1.4 %collective-permute-start.17 = (bf16[2,128,512]{2,1,0:T(8,128)(2,1)S(1)}, bf16[2,128,512]{2,1,0:T(8,128)(2,1)S(1)}, u32[]{:S(2)}, u32[]{:S(2)}) collective-permute-start(bf16[2,128,512]{2,1,0:T(8,128)(2,1)S(1)} %copy-done.8), channel_id=1, source_target_pairs={{0,4},{4,8},{8,12},{12,16},{16,20},{20,24},{24,28},{28,0},{1,5},{5... | collective-permute-start | bytes 786440 | tf_op jit(solution)/shard_map/ppermute | solution.py:327
  54.4 5.6 %collective-permute-done.18 = bf16[2,128,512]{2,1,0:T(8,128)(2,1)S(1)} collective-permute-done((bf16[2,128,512]{2,1,0:T(8,128)(2,1)S(1)}, bf16[2,128,512]{2,1,0:T(8,128)(2,1)S(1)}, u32[]{:S(2)}, u32[]{:S(2)}) %collective-permute-start.18) | collective-permute-done | bytes 262176 | tf_op jit(solution)/shard_map/ppermute | solution.py:327
  61.6 9.0 %collective-permute-done.16 = bf16[2,128,512]{2,1,0:T(8,128)(2,1)S(1)} collective-permute-done((bf16[2,128,512]{2,1,0:T(8,128)(2,1)S(1)}, bf16[2,128,512]{2,1,0:T(8,128)(2,1)S(1)}, u32[]{:S(2)}, u32[]{:S(2)}) %collective-permute-start.16) | collective-permute-done | bytes 262176 | tf_op jit(solution)/shard_map/ppermute | solution.py:327
  70.6 6.0 %collective-permute-done.15 = bf16[2,128,512]{2,1,0:T(8,128)(2,1)S(1)} collective-permute-done((bf16[2,128,512]{2,1,0:T(8,128)(2,1)S(1)}, bf16[2,128,512]{2,1,0:T(8,128)(2,1)S(1)}, u32[]{:S(2)}, u32[]{:S(2)}) %collective-permute-start.15) | collective-permute-done | bytes 262176 | tf_op jit(solution)/shard_map/ppermute | solution.py:327
  76.6 7.5 %collective-permute-start.6 = (bf16[32,128,128]{2,1,0:T(8,128)(2,1)}, bf16[32,128,128]{2,1,0:T(8,128)(2,1)}, u32[]{:S(2)}, u32[]{:S(2)}) collective-permute-start(bf16[32,128,128]{2,1,0:T(8,128)(2,1)} %pad_maximum_fusion.refs_0_), channel_id=1, source_target_pairs={{0,1},{1,0},{2,3},{3,2},{4,5},{5,4},{6,7},{7,6},{8,9},{9,8},{10,11... | collective-permute-start | bytes 3145736 | tf_op jit(solution)/shard_map/ppermute | solution.py:345
  84.1 7.5 %collective-permute-start.7 = (bf16[32,128,128]{2,1,0:T(8,128)(2,1)}, bf16[32,128,128]{2,1,0:T(8,128)(2,1)}, u32[]{:S(2)}, u32[]{:S(2)}) collective-permute-start(bf16[32,128,128]{2,1,0:T(8,128)(2,1)} %pad_maximum_fusion.1.refs_1_), channel_id=1, source_target_pairs={{0,1},{1,0},{2,3},{3,2},{4,5},{5,4},{6,7},{7,6},{8,9},{9,8},{10,11... | collective-permute-start | bytes 3145736 | tf_op jit(solution)/shard_map/ppermute | solution.py:345
  92.6 6.1 %all-to-all-start.1 = ((bf16[16,16,512]{2,1,0:T(8,128)(2,1)}), bf16[16,16,512]{2,1,0:T(8,128)(2,1)S(1)}, u32[]{:S(2)}, u32[]{:S(2)}) async-start(bf16[16,16,512]{2,1,0:T(8,128)(2,1)} %bitcast.5), calls=%async_computation.1 | async-start | bytes 524288 | tf_op jit(solution)/shard_map/all_to_all | solution.py:350
  99.3 7.6 %all-to-all-done.1 = bf16[16,16,512]{2,1,0:T(8,128)(2,1)S(1)} async-done(((bf16[16,16,512]{2,1,0:T(8,128)(2,1)}), bf16[16,16,512]{2,1,0:T(8,128)(2,1)S(1)}, u32[]{:S(2)}, u32[]{:S(2)}) %all-to-all-start.1) | async-done | bytes 262176 | tf_op jit(solution)/shard_map/all_to_all | solution.py:350
  106.9 8.1 %all_to_all.15 = bf16[8,16,512]{2,1,0:T(8,128)(2,1)S(1)} all-to-all(bf16[8,16,512]{2,1,0:T(8,128)(2,1)S(1)} %broadcast_in_dim.2), channel_id=1, replica_groups=mesh['y'=4,'xl'=2,'z'=8,'xh'=2,'c'=2] {'y','xl'}, dimensions={0} | all-to-all | bytes 262144 | tf_op jit(solution)/shard_map/all_to_all | solution.py:353
  115.6 1.5 %multiply_subtract_fusion = (f32[128,1024]{1,0:T(8,128)}, f32[128,1024]{1,0:T(8,128)}) fusion(f32[128,1024]{1,0:T(8,128)S(1)} %copy-done.1, f32[128,1024]{1,0:T(8,128)S(1)} %copy-done.2, f32[128,1024]{1,0:T(8,128)S(1)} %fusion.2, bf16[128,512]{1,0:T(8,128)(2,1)S(1)} %bitcast.10, f32[1024,512]{1,0:T(8,128)S(1)} %copy-done), kind=kOutput, calls=%fused_computation.7 | convolution fusion | flops 137363456 | bytes 4849664 | tf_op jit(solution)/shard_map/dot_general | solution.py:359
  117.1 8.2 %near_products.1 = (f32[256,1024]{1,0:T(8,128)}, f32[4,256,512]{2,1,0:T(8,128)}, f32[4,256,512]{2,1,0:T(8,128)}) custom-call(s32[5]{0:T(128)} %stack.23.at_ref, bf16[256,4096]{1,0:T(8,128)(2,1)} %tok_ref.5, bf16[256,1024]{1,0:T(8,128)(2,1)} %up_ref.5, bf16[32,128,128]{2,1,0:T(8,128)(2,1)} %pad_maximum_fusion.refs_0_, ...), custom_call_target="tpu_custom_call" | custom-call | flops 2147483648 | bytes 4194304 | tf_op jit(solution)/shard_map/near_products/pallas_call | solution.py:276
  125.4 10.0 %far_products.1 = (bf16[256,1024]{1,0:T(8,128)(2,1)}, bf16[256,4096]{1,0:T(8,128)(2,1)}) custom-call(s32[5]{0:T(128)} %stack.23.at_ref, bf16[256,4096]{1,0:T(8,128)(2,1)} %tok_ref.5, bf16[256,1024]{1,0:T(8,128)(2,1)} %up_ref.5, f32[256,1024]{1,0:T(8,128)} %get-tuple-element.17.before_ref, bf16[32,128,128]{2,1,0:T(8,128)(2,1)} %collective-permute-done.8.refs_0_, ...), custom_call_target="tpu_custom_call" | custom-call | flops 2147483648 | bytes 4194304 | tf_op jit(solution)/shard_map/far_products/pallas_call | solution.py:293
  (65 shorter events, 12.3 us)
Async XLA Ops:
  3.1 19.5 %all-to-all-start = ((bf16[8,128,128]{2,1,0:T(8,128)(2,1)}), bf16[8,128,128]{2,1,0:T(8,128)(2,1)S(1)}, u32[]{:S(2)}, u32[]{:S(2)}) async-start(bf16[8,128,128]{2,1,0:T(8,128)(2,1)} %make_piece.1.after_ref), calls=%async_computation | async-start | bytes 524288 | tf_op jit(solution)/shard_map/all_to_all | solution.py:320
  14.9 26.7 %collective-permute-start.12 = (bf16[256,2048]{1,0:T(8,128)(2,1)}, bf16[256,2048]{1,0:T(8,128)(2,1)}, u32[]{:S(2)}, u32[]{:S(2)}) collective-permute-start(bf16[256,2048]{1,0:T(8,128)(2,1)} %pick.1), channel_id=1, source_target_pairs={{0,1},{1,0},{2,3},{3,2},{4,5},{5,4},{6,7},{7,6},{8,9},{9,8},{10,11... | collective-permute-start | bytes 3145736 | tf_op jit(solution)/shard_map/ppermute | solution.py:319
  22.6 3.9 %collective-permute-start = (bf16[4,128,128]{2,1,0:T(8,128)(2,1)S(1)}, bf16[4,128,128]{2,1,0:T(8,128)(2,1)S(1)}, u32[]{:S(2)}, u32[]{:S(2)}) collective-permute-start(bf16[4,128,128]{2,1,0:T(8,128)(2,1)S(1)} %get-tuple-element.33), channel_id=1, source_target_pairs={{0,34},{1,65},{2,32},{3,67},{32,2},{33,97},{34,0},{35,99},{64,98},... | collective-permute-start | bytes 393224 | tf_op jit(solution)/shard_map/ppermute | solution.py:132
  24.0 5.0 %collective-permute-start.3 = (bf16[4,128,128]{2,1,0:T(8,128)(2,1)S(1)}, bf16[4,128,128]{2,1,0:T(8,128)(2,1)S(1)}, u32[]{:S(2)}, u32[]{:S(2)}) collective-permute-start(bf16[4,128,128]{2,1,0:T(8,128)(2,1)S(1)} %get-tuple-element.32), channel_id=1, source_target_pairs={{0,32},{1,193},{2,34},{3,195},{32,0},{33,225},{34,2},{35,227},{64,... | collective-permute-start | bytes 393224 | tf_op jit(solution)/shard_map/ppermute | solution.py:132
  26.5 13.7 %collective-permute-start.1 = (bf16[8,128,128]{2,1,0:T(8,128)(2,1)S(1)}, bf16[8,128,128]{2,1,0:T(8,128)(2,1)S(1)}, u32[]{:S(2)}, u32[]{:S(2)}) collective-permute-start(bf16[8,128,128]{2,1,0:T(8,128)(2,1)S(1)} %pad_maximum_fusion.4), channel_id=1, source_target_pairs={{0,64},{1,33},{2,66},{3,35},{32,96},{33,1},{34,98},{35,3},{64,0},{... | collective-permute-start | bytes 786440 | tf_op jit(solution)/shard_map/ppermute | solution.py:132
  29.1 11.4 %collective-permute-start.4 = (bf16[8,128,128]{2,1,0:T(8,128)(2,1)S(1)}, bf16[8,128,128]{2,1,0:T(8,128)(2,1)S(1)}, u32[]{:S(2)}, u32[]{:S(2)}) collective-permute-start(bf16[8,128,128]{2,1,0:T(8,128)(2,1)S(1)} %pad_maximum_fusion.5), channel_id=1, source_target_pairs={{0,192},{1,35},{2,194},{3,33},{32,224},{33,3},{34,226},{35,1},{64,... | collective-permute-start | bytes 786440 | tf_op jit(solution)/shard_map/ppermute | solution.py:132
  34.8 6.8 %collective-permute-start.13 = (bf16[256,512]{1,0:T(8,128)(2,1)}, bf16[256,512]{1,0:T(8,128)(2,1)S(1)}, u32[]{:S(2)}, u32[]{:S(2)}) collective-permute-start(bf16[256,512]{1,0:T(8,128)(2,1)} %make_q.1.q_ref), channel_id=1, source_target_pairs={{0,1},{1,0},{2,3},{3,2},{4,5},{5,4},{6,7},{7,6},{8,9},{9,8},{10,11... | collective-permute-start | bytes 786440 | tf_op jit(solution)/shard_map/ppermute | solution.py:323
  40.4 9.6 %collective-permute-start.2 = (bf16[16,128,128]{2,1,0:T(8,128)(2,1)S(1)}, bf16[16,128,128]{2,1,0:T(8,128)(2,1)S(1)}, u32[]{:S(2)}, u32[]{:S(2)}) collective-permute-start(bf16[16,128,128]{2,1,0:T(8,128)(2,1)S(1)} %pad_maximum_fusion.2), channel_id=1, source_target_pairs={{0,32},{1,193},{2,34},{3,195},{32,0},{33,225},{34,2},{35,227},{64,... | collective-permute-start | bytes 1572872 | tf_op jit(solution)/shard_map/ppermute | solution.py:132
  40.5 11.1 %collective-permute-start.5 = (bf16[16,128,128]{2,1,0:T(8,128)(2,1)S(1)}, bf16[16,128,128]{2,1,0:T(8,128)(2,1)S(1)}, u32[]{:S(2)}, u32[]{:S(2)}) collective-permute-start(bf16[16,128,128]{2,1,0:T(8,128)(2,1)S(1)} %pad_maximum_fusion.3), channel_id=1, source_target_pairs={{0,34},{1,65},{2,32},{3,67},{32,2},{33,97},{34,0},{35,99},{64,98},... | collective-permute-start | bytes 1572872 | tf_op jit(solution)/shard_map/ppermute | solution.py:132
  46.6 7.7 %collective-permute-start.19 = (bf16[2,128,512]{2,1,0:T(8,128)(2,1)}, bf16[2,128,512]{2,1,0:T(8,128)(2,1)S(1)}, u32[]{:S(2)}, u32[]{:S(2)}) collective-permute-start(bf16[2,128,512]{2,1,0:T(8,128)(2,1)} %get-tuple-element.29), channel_id=1, source_target_pairs={{0,28},{4,0},{8,4},{12,8},{16,12},{20,16},{24,20},{28,24},{1,29},{... | collective-permute-start | bytes 786440 | tf_op jit(solution)/shard_map/ppermute | solution.py:327
  51.0 47.6 %collective-permute-start.8 = (bf16[32,128,128]{2,1,0:T(8,128)(2,1)}, bf16[32,128,128]{2,1,0:T(8,128)(2,1)}, u32[]{:S(2)}, u32[]{:S(2)}) collective-permute-start(bf16[32,128,128]{2,1,0:T(8,128)(2,1)} %pad_maximum_fusion.refs_0_), channel_id=1, source_target_pairs={{0,192},{1,35},{2,194},{3,33},{32,224},{33,3},{34,226},{35,1},{64,... | collective-permute-start | bytes 3145736 | tf_op jit(solution)/shard_map/ppermute | solution.py:132
  52.7 62.3 %copy-start = (f32[1024,512]{1,0:T(8,128)S(1)}, f32[1024,512]{1,0:T(8,128)}, u32[]{:S(2)}) copy-start(f32[1024,512]{1,0:T(8,128)} %proj_ref.1) | copy-start | bytes 6291460
  52.7 46.4 %collective-permute-start.9 = (bf16[32,128,128]{2,1,0:T(8,128)(2,1)}, bf16[32,128,128]{2,1,0:T(8,128)(2,1)}, u32[]{:S(2)}, u32[]{:S(2)}) collective-permute-start(bf16[32,128,128]{2,1,0:T(8,128)(2,1)} %pad_maximum_fusion.1.refs_1_), channel_id=1, source_target_pairs={{0,64},{1,33},{2,66},{3,35},{32,96},{33,1},{34,98},{35,3},{64,0},{... | collective-permute-start | bytes 3145736 | tf_op jit(solution)/shard_map/ppermute | solution.py:132
  52.7 7.2 %collective-permute-start.18 = (bf16[2,128,512]{2,1,0:T(8,128)(2,1)S(1)}, bf16[2,128,512]{2,1,0:T(8,128)(2,1)S(1)}, u32[]{:S(2)}, u32[]{:S(2)}) collective-permute-start(bf16[2,128,512]{2,1,0:T(8,128)(2,1)S(1)} %copy-done.9), channel_id=1, source_target_pairs={{0,28},{4,0},{8,4},{12,8},{16,12},{20,16},{24,20},{28,24},{1,29},{... | collective-permute-start | bytes 786440 | tf_op jit(solution)/shard_map/ppermute | solution.py:327
  52.8 8.4 %collective-permute-start.17 = (bf16[2,128,512]{2,1,0:T(8,128)(2,1)S(1)}, bf16[2,128,512]{2,1,0:T(8,128)(2,1)S(1)}, u32[]{:S(2)}, u32[]{:S(2)}) collective-permute-start(bf16[2,128,512]{2,1,0:T(8,128)(2,1)S(1)} %copy-done.8), channel_id=1, source_target_pairs={{0,4},{4,8},{8,12},{12,16},{16,20},{20,24},{24,28},{28,0},{1,5},{5... | collective-permute-start | bytes 786440 | tf_op jit(solution)/shard_map/ppermute | solution.py:327
  54.3 16.3 %collective-permute-start.16 = (bf16[2,128,512]{2,1,0:T(8,128)(2,1)S(1)}, bf16[2,128,512]{2,1,0:T(8,128)(2,1)S(1)}, u32[]{:S(2)}, u32[]{:S(2)}) collective-permute-start(bf16[2,128,512]{2,1,0:T(8,128)(2,1)S(1)} %copy-done.7), channel_id=1, source_target_pairs={{0,24},{4,28},{8,0},{12,4},{16,8},{20,12},{24,16},{28,20},{1,25},{... | collective-permute-start | bytes 786440 | tf_op jit(solution)/shard_map/ppermute | solution.py:327
  60.0 16.6 %collective-permute-start.15 = (bf16[2,128,512]{2,1,0:T(8,128)(2,1)S(1)}, bf16[2,128,512]{2,1,0:T(8,128)(2,1)S(1)}, u32[]{:S(2)}, u32[]{:S(2)}) collective-permute-start(bf16[2,128,512]{2,1,0:T(8,128)(2,1)S(1)} %copy-done.6), channel_id=1, source_target_pairs={{0,8},{4,12},{8,16},{12,20},{16,24},{20,28},{24,0},{28,4},{1,9},{5... | collective-permute-start | bytes 786440 | tf_op jit(solution)/shard_map/ppermute | solution.py:327
  61.2 22.9 %collective-permute-start.14 = (bf16[2,128,512]{2,1,0:T(8,128)(2,1)S(1)}, bf16[2,128,512]{2,1,0:T(8,128)(2,1)S(1)}, u32[]{:S(2)}, u32[]{:S(2)}) collective-permute-start(bf16[2,128,512]{2,1,0:T(8,128)(2,1)S(1)} %copy-done.5), channel_id=1, source_target_pairs={{0,12},{4,16},{8,20},{12,24},{16,28},{20,0},{24,4},{28,8},{1,13},{... | collective-permute-start | bytes 786440 | tf_op jit(solution)/shard_map/ppermute | solution.py:327
  70.6 21.1 %collective-permute-start.20 = (bf16[2,128,512]{2,1,0:T(8,128)(2,1)S(1)}, bf16[2,128,512]{2,1,0:T(8,128)(2,1)S(1)}, u32[]{:S(2)}, u32[]{:S(2)}) collective-permute-start(bf16[2,128,512]{2,1,0:T(8,128)(2,1)S(1)} %add_convert_fusion.1), channel_id=1, source_target_pairs={{0,20},{4,24},{8,28},{12,0},{16,4},{20,8},{24,12},{28,16},{1,21},{... | collective-permute-start | bytes 786440 | tf_op jit(solution)/shard_map/ppermute | solution.py:327
  76.6 40.5 %collective-permute-start.6 = (bf16[32,128,128]{2,1,0:T(8,128)(2,1)}, bf16[32,128,128]{2,1,0:T(8,128)(2,1)}, u32[]{:S(2)}, u32[]{:S(2)}) collective-permute-start(bf16[32,128,128]{2,1,0:T(8,128)(2,1)} %pad_maximum_fusion.refs_0_), channel_id=1, source_target_pairs={{0,1},{1,0},{2,3},{3,2},{4,5},{5,4},{6,7},{7,6},{8,9},{9,8},{10,11... | collective-permute-start | bytes 3145736 | tf_op jit(solution)/shard_map/ppermute | solution.py:345
  84.1 33.0 %collective-permute-start.7 = (bf16[32,128,128]{2,1,0:T(8,128)(2,1)}, bf16[32,128,128]{2,1,0:T(8,128)(2,1)}, u32[]{:S(2)}, u32[]{:S(2)}) collective-permute-start(bf16[32,128,128]{2,1,0:T(8,128)(2,1)} %pad_maximum_fusion.1.refs_1_), channel_id=1, source_target_pairs={{0,1},{1,0},{2,3},{3,2},{4,5},{5,4},{6,7},{7,6},{8,9},{9,8},{10,11... | collective-permute-start | bytes 3145736 | tf_op jit(solution)/shard_map/ppermute | solution.py:345
  92.6 14.3 %all-to-all-start.1 = ((bf16[16,16,512]{2,1,0:T(8,128)(2,1)}), bf16[16,16,512]{2,1,0:T(8,128)(2,1)S(1)}, u32[]{:S(2)}, u32[]{:S(2)}) async-start(bf16[16,16,512]{2,1,0:T(8,128)(2,1)} %bitcast.5), calls=%async_computation.1 | async-start | bytes 524288 | tf_op jit(solution)/shard_map/all_to_all | solution.py:350
  98.7 26.7 %collective-permute-start.10 = (bf16[32,128,128]{2,1,0:T(8,128)(2,1)}, bf16[32,128,128]{2,1,0:T(8,128)(2,1)}, u32[]{:S(2)}, u32[]{:S(2)}) collective-permute-start(bf16[32,128,128]{2,1,0:T(8,128)(2,1)} %collective-permute-done.8.refs_0_), channel_id=1, source_target_pairs={{0,1},{1,0},{2,3},{3,2},{4,5},{5,4},{6,7},{7,6},{8,9},{9,8},{10,11... | collective-permute-start | bytes 3145736 | tf_op jit(solution)/shard_map/ppermute | solution.py:346
  99.1 26.3 %collective-permute-start.11 = (bf16[32,128,128]{2,1,0:T(8,128)(2,1)}, bf16[32,128,128]{2,1,0:T(8,128)(2,1)}, u32[]{:S(2)}, u32[]{:S(2)}) collective-permute-start(bf16[32,128,128]{2,1,0:T(8,128)(2,1)} %collective-permute-done.9.refs_1_), channel_id=1, source_target_pairs={{0,1},{1,0},{2,3},{3,2},{4,5},{5,4},{6,7},{7,6},{8,9},{9,8},{10,11... | collective-permute-start | bytes 3145736 | tf_op jit(solution)/shard_map/ppermute | solution.py:346
  (10 other events, 147.6 us)

commit v11 on v9

--- a/solution.py
+++ b/solution.py
@@ -211,9 +211,14 @@
             half_products(0, range(GROUPS), core, at_ref, tok_ref, w_refs, acc_ref, up_rel, take)
 
 
-def far_kernel(at_ref, tok_ref, up_ref, before_ref, *refs, scale):
-    sum_refs, w_refs = refs[:GROUPS], refs[GROUPS : 3 * GROUPS]
-    values_ref, grads_ref, acc_ref, up_rel = refs[3 * GROUPS :]
+def far_kernel(at_ref, tok_ref, up_ref, before_ref, sum_ref, *refs, group, scale, last):
+    w_refs = refs[:2]
+    if last:
+        part_ref, values_ref, grads_ref, acc_ref, up_rel = refs[2:]
+        done = part_ref.shape[1]
+        grads_ref[:, :done] = part_ref[...]
+    else:
+        acc_ref, grads_ref, up_rel = refs[2:]
     acc_ref[...] = before_ref[...]
     arrange(at_ref, up_ref, up_rel)
 
@@ -221,7 +226,7 @@
 
         def take(g, a, o, blocks, total, core=core):
             if places(core ^ o, g)[0, a]:
-                before = sum_refs[g][2 * a + o]
+                before = sum_ref[2 * a + o]
                 total = before if total is None else total + before
             grad = (total * scale).astype(BF16)
             for k, at in enumerate(blocks):
@@ -229,10 +234,11 @@
 
         @pl.when(at_ref[0] == core)
         def _():
-            half_products(1, range(GROUPS), core, at_ref, tok_ref, w_refs, acc_ref, up_rel, take)
-
-    for r, at in enumerate(columns(at_ref)):
-        values_ref[:, at] = (acc_ref[:, r * LANES : (r + 1) * LANES] * scale).astype(BF16)
+            half_products(1, (group,), core, at_ref, tok_ref, w_refs, acc_ref, up_rel, take)
+
+    if last:
+        for r, at in enumerate(columns(at_ref)):
+            values_ref[:, at] = (acc_ref[:, r * LANES : (r + 1) * LANES] * scale).astype(BF16)
 
 
 def near_products(at, tokens, upstream, weights):
@@ -252,18 +258,26 @@
     )(at, tokens, upstream, *weights)
 
 
-def far_products(at, tokens, upstream, acc, sums, weights, scale):
+def far_products(at, tokens, upstream, acc, sums, weights, scale, group, part=None):
     t, d = tokens.shape
     kv = upstream.shape[1]
-    return pl.pallas_call(
-        functools.partial(far_kernel, scale=scale),
-        out_shape=(jax.ShapeDtypeStruct((t, kv), BF16), jax.ShapeDtypeStruct((t, d), BF16)),
-        in_specs=[SMEM] + [VMEM] * (3 + len(sums) + len(weights)),
+    last = part is not None
+    rel = pltpu.VMEM((t, kv), BF16)
+    if last:
+        shapes = (jax.ShapeDtypeStruct((t, kv), BF16), jax.ShapeDtypeStruct((t, d), BF16))
+        extra, scratch = (part,), [pltpu.VMEM((t, kv), F32), rel]
+    else:
+        shapes = (jax.ShapeDtypeStruct((t, kv), F32), jax.ShapeDtypeStruct((t, d // GROUPS), BF16))
+        extra, scratch = (), [rel]
+    return pl.pallas_call(
+        functools.partial(far_kernel, group=group, scale=scale, last=last),
+        out_shape=shapes,
+        in_specs=[SMEM] + [VMEM] * (6 + len(extra)),
         out_specs=(VMEM, VMEM),
-        scratch_shapes=[pltpu.VMEM((t, kv), F32), pltpu.VMEM((t, kv), BF16)],
-        cost_estimate=pl.CostEstimate(flops=2 * t * d * kv, bytes_accessed=d * kv, transcendentals=0),
+        scratch_shapes=scratch,
+        cost_estimate=pl.CostEstimate(flops=t * d * kv, bytes_accessed=d * kv, transcendentals=0),
         name="far_products",
-    )(at, tokens, upstream, acc, *sums, *weights)
+    )(at, tokens, upstream, acc, sums, *weights, *extra)
 
 
 def step(tokens, upstream, params, momentum, projection):
@@ -308,8 +322,10 @@
         held = [jnp.concatenate(both, axis=0) for both in zip(held, more)]
     far = [exchange(h, g, 3) for g, h in enumerate(held)]
     acc, *sums = near_products(at, tokens, upstream, [*held, *(swap(h) for h in held)])
+    far = [(f, swap(f)) for f in far]
+    acc, grads = far_products(at, tokens, upstream, acc, sums[0], far[0], inv_width, 0)
     values, token_grads = far_products(
-        at, tokens, upstream, acc, sums, [*far, *(swap(f) for f in far)], inv_width
+        at, tokens, upstream, acc, sums[1], far[1], inv_width, 1, grads
     )
 
     along = along.astype(BF16)

time: 137 us -> 141 us (1.029)
  the two profiles are of different devices: /device:TPU:1 before, /device:TPU:32 now
where the time goes in v11:
time: 141 us
  waiting for transfers between devices  58.7 us (42%)
  starting transfers between devices  40.3 us (29%)
  Pallas kernels  33.5 us (24%)
  other arithmetic  3.43 us (2%)
  local copies, waits for them, and re-layouts  2.08 us (1%)
  matrix products  2 us (1%)
    ppermute x7, waiting for transfers between devices, shift(): return lax.ppermute(x, 'z', [(i, (i + k) % n_z) for i in range(n_z)])  32.2 us
    ppermute x8, starting transfers between devices, exchange(): return lax.ppermute(x, ('y', 'xl', 'xh', 'c'), pairs)  14.3 us
    pallas_call x2, Pallas kernels, far_products(): pl.pallas_call(functools.partial(far_kernel, group=group, scale=scale, la...  13.5 us
    all_to_all x1, waiting for transfers between devices, step(): lax.all_to_all(along.reshape(n_xh * n_isl, part, proj), PLANE, 0, 0, tile...  9.03 us
    all_to_all x1, starting transfers between devices, step(): piece = lax.all_to_all(piece, 'z', 0, 0, tiled=True)  8.57 us
    pallas_call x1, Pallas kernels, near_products(): pl.pallas_call(near_kernel, out_shape=(jax.ShapeDtypeStruct((t, kv), F32)...  7.96 us
    ppermute x7, starting transfers between devices, shift(): return lax.ppermute(x, 'z', [(i, (i + k) % n_z) for i in range(n_z)])  7.91 us
    all_to_all x1, waiting for transfers between devices, step(): piece = lax.all_to_all(piece, 'z', 0, 0, tiled=True)  7.56 us
  transfers between devices with their start and end apart: 24, of which 10 were waited for; matrix products, arithmetic and copies ran while one was open for 4% of the time, Pallas kernels for 18%

profile of v11, /device:TPU:32, one launch (start us, length us, event | category | flops | bytes accessed | tf_op | source)
XLA Modules:
  0.0 140.8 jit_solution(16695597307707909104)
XLA Ops:
  1.3 1.8 %make_piece.1.after_ref = bf16[8,128,128]{2,1,0:T(8,128)(2,1)} custom-call(s32[5]{0:T(128)} %stack.23.at_ref, f32[128,1024]{1,0:T(8,128)} %params_ref.1), custom_call_target="tpu_custom_call" | custom-call | tf_op jit(solution)/shard_map/make_piece/pallas_call | solution.py:38
  3.1 8.6 %all-to-all-start = ((bf16[8,128,128]{2,1,0:T(8,128)(2,1)}), bf16[8,128,128]{2,1,0:T(8,128)(2,1)S(1)}, u32[]{:S(2)}, u32[]{:S(2)}) async-start(bf16[8,128,128]{2,1,0:T(8,128)(2,1)} %make_piece.1.after_ref), calls=%async_computation | async-start | bytes 524288 | tf_op jit(solution)/shard_map/all_to_all | solution.py:299
  11.7 2.9 %pick.1 = bf16[256,2048]{1,0:T(8,128)(2,1)} custom-call(s32[5]{0:T(128)} %stack.23.at_ref, bf16[256,4096]{1,0:T(8,128)(2,1)} %tok_ref.7, bf16[8,128,128]{2,1,0:T(8,128)(2,1)} %make_piece.1.after_ref), custom_call_target="tpu_custom_call" | custom-call | tf_op jit(solution)/shard_map/pick/pallas_call | solution.py:56
  14.5 7.6 %all-to-all-done = bf16[8,128,128]{2,1,0:T(8,128)(2,1)S(1)} async-done(((bf16[8,128,128]{2,1,0:T(8,128)(2,1)}), bf16[8,128,128]{2,1,0:T(8,128)(2,1)S(1)}, u32[]{:S(2)}, u32[]{:S(2)}) %all-to-all-start) | async-done | bytes 262176 | tf_op jit(solution)/shard_map/all_to_all | solution.py:299
  22.1 2.8 %collective-permute-start = (bf16[4,128,128]{2,1,0:T(8,128)(2,1)S(1)}, bf16[4,128,128]{2,1,0:T(8,128)(2,1)S(1)}, u32[]{:S(2)}, u32[]{:S(2)}) collective-permute-start(bf16[4,128,128]{2,1,0:T(8,128)(2,1)S(1)} %get-tuple-element.37), channel_id=1, source_target_pairs={{0,34},{1,65},{2,32},{3,67},{32,2},{33,97},{34,0},{35,99},{64,98},... | collective-permute-start | bytes 393224 | tf_op jit(solution)/shard_map/ppermute | solution.py:132
  25.2 3.2 %collective-permute-done = bf16[4,128,128]{2,1,0:T(8,128)(2,1)S(1)} collective-permute-done((bf16[4,128,128]{2,1,0:T(8,128)(2,1)S(1)}, bf16[4,128,128]{2,1,0:T(8,128)(2,1)S(1)}, u32[]{:S(2)}, u32[]{:S(2)}) %collective-permute-start) | collective-permute-done | bytes 131104 | tf_op jit(solution)/shard_map/ppermute | solution.py:132
  30.3 3.1 %collective-permute-start.4 = (bf16[8,128,128]{2,1,0:T(8,128)(2,1)S(1)}, bf16[8,128,128]{2,1,0:T(8,128)(2,1)S(1)}, u32[]{:S(2)}, u32[]{:S(2)}) collective-permute-start(bf16[8,128,128]{2,1,0:T(8,128)(2,1)S(1)} %pad_maximum_fusion.5), channel_id=1, source_target_pairs={{0,192},{1,35},{2,194},{3,33},{32,224},{33,3},{34,226},{35,1},{64,... | collective-permute-start | bytes 786440 | tf_op jit(solution)/shard_map/ppermute | solution.py:132
  33.4 3.2 %make_q.1.q_ref = bf16[256,512]{1,0:T(8,128)(2,1)} custom-call(bf16[256,1024]{1,0:T(8,128)(2,1)} %up_ref.7, f32[1024,512]{1,0:T(8,128)} %proj_ref.1), custom_call_target="tpu_custom_call" | custom-call | flops 1073741824 | bytes 3145728 | tf_op jit(solution)/shard_map/make_q/pallas_call | solution.py:73
  38.1 2.9 %collective-permute-start.5 = (bf16[16,128,128]{2,1,0:T(8,128)(2,1)S(1)}, bf16[16,128,128]{2,1,0:T(8,128)(2,1)S(1)}, u32[]{:S(2)}, u32[]{:S(2)}) collective-permute-start(bf16[16,128,128]{2,1,0:T(8,128)(2,1)S(1)} %pad_maximum_fusion.3), channel_id=1, source_target_pairs={{0,34},{1,65},{2,32},{3,67},{32,2},{33,97},{34,0},{35,99},{64,98},... | collective-permute-start | bytes 1572872 | tf_op jit(solution)/shard_map/ppermute | solution.py:132
  41.6 4.2 %make_sketch.1 = (bf16[2,128,512]{2,1,0:T(8,128)(2,1)}, bf16[2,128,512]{2,1,0:T(8,128)(2,1)}, bf16[2,128,512]{2,1,0:T(8,128)(2,1)}, bf16[2,128,512]{2,1,0:T(8,12...) custom-call(s32[5]{0:T(128)} %stack.23.at_ref, ...), custom_call_target="tpu_custom_call" | custom-call | flops 4294967296 | bytes 16777216 | tf_op jit(solution)/shard_map/make_sketch/pallas_call | solution.py:104
  47.1 2.0 %collective-permute-start.17 = (bf16[2,128,512]{2,1,0:T(8,128)(2,1)}, bf16[2,128,512]{2,1,0:T(8,128)(2,1)S(1)}, u32[]{:S(2)}, u32[]{:S(2)}) collective-permute-start(bf16[2,128,512]{2,1,0:T(8,128)(2,1)} %get-tuple-element.30), channel_id=1, source_target_pairs={{0,4},{4,8},{8,12},{12,16},{16,20},{20,24},{24,28},{28,0},{1,5},{5... | collective-permute-start | bytes 786440 | tf_op jit(solution)/shard_map/ppermute | solution.py:306
  51.8 2.2 %collective-permute-start.8 = (bf16[32,128,128]{2,1,0:T(8,128)(2,1)}, bf16[32,128,128]{2,1,0:T(8,128)(2,1)}, u32[]{:S(2)}, u32[]{:S(2)}) collective-permute-start(bf16[32,128,128]{2,1,0:T(8,128)(2,1)} %pad_maximum_fusion.refs_0_), channel_id=1, source_target_pairs={{0,192},{1,35},{2,194},{3,33},{32,224},{33,3},{34,226},{35,1},{64,... | collective-permute-start | bytes 3145736 | tf_op jit(solution)/shard_map/ppermute | solution.py:132
  56.1 9.7 %collective-permute-done.18 = bf16[2,128,512]{2,1,0:T(8,128)(2,1)S(1)} collective-permute-done((bf16[2,128,512]{2,1,0:T(8,128)(2,1)}, bf16[2,128,512]{2,1,0:T(8,128)(2,1)S(1)}, u32[]{:S(2)}, u32[]{:S(2)}) %collective-permute-start.18) | collective-permute-done | bytes 262176 | tf_op jit(solution)/shard_map/ppermute | solution.py:306
  65.9 3.3 %collective-permute-done.16 = bf16[2,128,512]{2,1,0:T(8,128)(2,1)S(1)} collective-permute-done((bf16[2,128,512]{2,1,0:T(8,128)(2,1)}, bf16[2,128,512]{2,1,0:T(8,128)(2,1)S(1)}, u32[]{:S(2)}, u32[]{:S(2)}) %collective-permute-start.16) | collective-permute-done | bytes 262176 | tf_op jit(solution)/shard_map/ppermute | solution.py:306
  69.2 3.0 %collective-permute-start.20 = (bf16[2,128,512]{2,1,0:T(8,128)(2,1)S(1)}, bf16[2,128,512]{2,1,0:T(8,128)(2,1)S(1)}, u32[]{:S(2)}, u32[]{:S(2)}) collective-permute-start(bf16[2,128,512]{2,1,0:T(8,128)(2,1)S(1)} %add_convert_fusion.1), channel_id=1, source_target_pairs={{0,20},{4,24},{8,28},{12,0},{16,4},{20,8},{24,12},{28,16},{1,21},{... | collective-permute-start | bytes 786440 | tf_op jit(solution)/shard_map/ppermute | solution.py:306
  72.3 12.2 %collective-permute-done.15 = bf16[2,128,512]{2,1,0:T(8,128)(2,1)S(1)} collective-permute-done((bf16[2,128,512]{2,1,0:T(8,128)(2,1)S(1)}, bf16[2,128,512]{2,1,0:T(8,128)(2,1)S(1)}, u32[]{:S(2)}, u32[]{:S(2)}) %collective-permute-start.15) | collective-permute-done | bytes 262176 | tf_op jit(solution)/shard_map/ppermute | solution.py:306
  84.4 6.1 %collective-permute-done.14 = bf16[2,128,512]{2,1,0:T(8,128)(2,1)S(1)} collective-permute-done((bf16[2,128,512]{2,1,0:T(8,128)(2,1)S(1)}, bf16[2,128,512]{2,1,0:T(8,128)(2,1)S(1)}, u32[]{:S(2)}, u32[]{:S(2)}) %collective-permute-start.14) | collective-permute-done | bytes 262176 | tf_op jit(solution)/shard_map/ppermute | solution.py:306
  91.5 5.8 %all-to-all-start.1 = ((bf16[16,16,512]{2,1,0:T(8,128)(2,1)}), bf16[16,16,512]{2,1,0:T(8,128)(2,1)S(1)}, u32[]{:S(2)}, u32[]{:S(2)}) async-start(bf16[16,16,512]{2,1,0:T(8,128)(2,1)} %bitcast.5), calls=%async_computation.1 | async-start | bytes 524288 | tf_op jit(solution)/shard_map/all_to_all | solution.py:332
  97.6 9.0 %all-to-all-done.1 = bf16[16,16,512]{2,1,0:T(8,128)(2,1)S(1)} async-done(((bf16[16,16,512]{2,1,0:T(8,128)(2,1)}), bf16[16,16,512]{2,1,0:T(8,128)(2,1)S(1)}, u32[]{:S(2)}, u32[]{:S(2)}) %all-to-all-start.1) | async-done | bytes 262176 | tf_op jit(solution)/shard_map/all_to_all | solution.py:332
  107.3 3.4 %all-to-all-start.2 = ((bf16[8,16,512]{2,1,0:T(8,128)(2,1)}), bf16[8,16,512]{2,1,0:T(8,128)(2,1)S(1)}, u32[]{:S(2)}, u32[]{:S(2)}) async-start(bf16[8,16,512]{2,1,0:T(8,128)(2,1)} %broadcast_in_dim.2), calls=%async_computation.2 | async-start | bytes 262144 | tf_op jit(solution)/shard_map/all_to_all | solution.py:335
  110.8 6.5 %all-to-all-done.2 = bf16[8,16,512]{2,1,0:T(8,128)(2,1)S(1)} async-done(((bf16[8,16,512]{2,1,0:T(8,128)(2,1)}), bf16[8,16,512]{2,1,0:T(8,128)(2,1)S(1)}, u32[]{:S(2)}, u32[]{:S(2)}) %all-to-all-start.2) | async-done | bytes 131104 | tf_op jit(solution)/shard_map/all_to_all | solution.py:335
  119.3 8.0 %near_products.1 = (f32[256,1024]{1,0:T(8,128)}, f32[4,256,512]{2,1,0:T(8,128)}, f32[4,256,512]{2,1,0:T(8,128)}) custom-call(s32[5]{0:T(128)} %stack.23.at_ref, bf16[256,4096]{1,0:T(8,128)(2,1)} %tok_ref.7, bf16[256,1024]{1,0:T(8,128)(2,1)} %up_ref.7, bf16[32,128,128]{2,1,0:T(8,128)(2,1)} %pad_maximum_fusion.refs_0_, ...), custom_call_target="tpu_custom_call" | custom-call | flops 2147483648 | bytes 4194304 | tf_op jit(solution)/shard_map/near_products/pallas_call | solution.py:247
  127.3 6.7 %far_products.2 = (f32[256,1024]{1,0:T(8,128)}, bf16[256,2048]{1,0:T(8,128)(2,1)}) custom-call(s32[5]{0:T(128)} %stack.23.at_ref, bf16[256,4096]{1,0:T(8,128)(2,1)} %tok_ref.7, bf16[256,1024]{1,0:T(8,128)(2,1)} %up_ref.7, f32[256,1024]{1,0:T(8,128)} %get-tuple-element.19.before_ref, f32[4,256,512]{2,1,0:T(8,128)} %get-tuple-element.20.sum_ref, ...), custom_call_target="tpu_custom_call" | custom-call | flops 1073741824 | bytes 4194304 | tf_op jit(solution)/shard_map/far_products/pallas_call | solution.py:272
  134.0 6.9 %far_products.3 = (bf16[256,1024]{1,0:T(8,128)(2,1)}, bf16[256,4096]{1,0:T(8,128)(2,1)}) custom-call(s32[5]{0:T(128)} %stack.23.at_ref, bf16[256,4096]{1,0:T(8,128)(2,1)} %tok_ref.7, bf16[256,1024]{1,0:T(8,128)(2,1)} %up_ref.7, f32[256,1024]{1,0:T(8,128)} %get-tuple-element.21.before_ref, f32[4,256,512]{2,1,0:T(8,128)} %get-tuple-element.22.sum_ref, ...), custom_call_target="tpu_custom_call" | custom-call | flops 1073741824 | bytes 4194304 | tf_op jit(solution)/shard_map/far_products/pallas_call | solution.py:272
  (61 shorter events, 15.3 us)
Async XLA Ops:
  3.1 19.0 %all-to-all-start = ((bf16[8,128,128]{2,1,0:T(8,128)(2,1)}), bf16[8,128,128]{2,1,0:T(8,128)(2,1)S(1)}, u32[]{:S(2)}, u32[]{:S(2)}) async-start(bf16[8,128,128]{2,1,0:T(8,128)(2,1)} %make_piece.1.after_ref), calls=%async_computation | async-start | bytes 524288 | tf_op jit(solution)/shard_map/all_to_all | solution.py:299
  14.5 26.4 %collective-permute-start.12 = (bf16[256,2048]{1,0:T(8,128)(2,1)}, bf16[256,2048]{1,0:T(8,128)(2,1)}, u32[]{:S(2)}, u32[]{:S(2)}) collective-permute-start(bf16[256,2048]{1,0:T(8,128)(2,1)} %pick.1), channel_id=1, source_target_pairs={{0,1},{1,0},{2,3},{3,2},{4,5},{5,4},{6,7},{7,6},{8,9},{9,8},{10,11... | collective-permute-start | bytes 3145736 | tf_op jit(solution)/shard_map/ppermute | solution.py:298
  22.1 6.3 %collective-permute-start = (bf16[4,128,128]{2,1,0:T(8,128)(2,1)S(1)}, bf16[4,128,128]{2,1,0:T(8,128)(2,1)S(1)}, u32[]{:S(2)}, u32[]{:S(2)}) collective-permute-start(bf16[4,128,128]{2,1,0:T(8,128)(2,1)S(1)} %get-tuple-element.37), channel_id=1, source_target_pairs={{0,34},{1,65},{2,32},{3,67},{32,2},{33,97},{34,0},{35,99},{64,98},... | collective-permute-start | bytes 393224 | tf_op jit(solution)/shard_map/ppermute | solution.py:132
  24.9 5.3 %collective-permute-start.3 = (bf16[4,128,128]{2,1,0:T(8,128)(2,1)S(1)}, bf16[4,128,128]{2,1,0:T(8,128)(2,1)S(1)}, u32[]{:S(2)}, u32[]{:S(2)}) collective-permute-start(bf16[4,128,128]{2,1,0:T(8,128)(2,1)S(1)} %get-tuple-element.36), channel_id=1, source_target_pairs={{0,32},{1,193},{2,34},{3,195},{32,0},{33,225},{34,2},{35,227},{64,... | collective-permute-start | bytes 393224 | tf_op jit(solution)/shard_map/ppermute | solution.py:132
  28.4 8.2 %collective-permute-start.1 = (bf16[8,128,128]{2,1,0:T(8,128)(2,1)S(1)}, bf16[8,128,128]{2,1,0:T(8,128)(2,1)S(1)}, u32[]{:S(2)}, u32[]{:S(2)}) collective-permute-start(bf16[8,128,128]{2,1,0:T(8,128)(2,1)S(1)} %pad_maximum_fusion.4), channel_id=1, source_target_pairs={{0,64},{1,33},{2,66},{3,35},{32,96},{33,1},{34,98},{35,3},{64,0},{... | collective-permute-start | bytes 786440 | tf_op jit(solution)/shard_map/ppermute | solution.py:132
  30.3 7.8 %collective-permute-start.4 = (bf16[8,128,128]{2,1,0:T(8,128)(2,1)S(1)}, bf16[8,128,128]{2,1,0:T(8,128)(2,1)S(1)}, u32[]{:S(2)}, u32[]{:S(2)}) collective-permute-start(bf16[8,128,128]{2,1,0:T(8,128)(2,1)S(1)} %pad_maximum_fusion.5), channel_id=1, source_target_pairs={{0,192},{1,35},{2,194},{3,33},{32,224},{33,3},{34,226},{35,1},{64,... | collective-permute-start | bytes 786440 | tf_op jit(solution)/shard_map/ppermute | solution.py:132
  36.6 4.4 %collective-permute-start.13 = (bf16[256,512]{1,0:T(8,128)(2,1)}, bf16[256,512]{1,0:T(8,128)(2,1)S(1)}, u32[]{:S(2)}, u32[]{:S(2)}) collective-permute-start(bf16[256,512]{1,0:T(8,128)(2,1)} %make_q.1.q_ref), channel_id=1, source_target_pairs={{0,1},{1,0},{2,3},{3,2},{4,5},{5,4},{6,7},{7,6},{8,9},{9,8},{10,11... | collective-permute-start | bytes 786440 | tf_op jit(solution)/shard_map/ppermute | solution.py:302
  36.6 12.4 %collective-permute-start.2 = (bf16[16,128,128]{2,1,0:T(8,128)(2,1)S(1)}, bf16[16,128,128]{2,1,0:T(8,128)(2,1)S(1)}, u32[]{:S(2)}, u32[]{:S(2)}) collective-permute-start(bf16[16,128,128]{2,1,0:T(8,128)(2,1)S(1)} %pad_maximum_fusion.2), channel_id=1, source_target_pairs={{0,32},{1,193},{2,34},{3,195},{32,0},{33,225},{34,2},{35,227},{64,... | collective-permute-start | bytes 1572872 | tf_op jit(solution)/shard_map/ppermute | solution.py:132
  38.1 13.7 %collective-permute-start.5 = (bf16[16,128,128]{2,1,0:T(8,128)(2,1)S(1)}, bf16[16,128,128]{2,1,0:T(8,128)(2,1)S(1)}, u32[]{:S(2)}, u32[]{:S(2)}) collective-permute-start(bf16[16,128,128]{2,1,0:T(8,128)(2,1)S(1)} %pad_maximum_fusion.3), channel_id=1, source_target_pairs={{0,34},{1,65},{2,32},{3,67},{32,2},{33,97},{34,0},{35,99},{64,98},... | collective-permute-start | bytes 1572872 | tf_op jit(solution)/shard_map/ppermute | solution.py:132
  45.8 10.2 %collective-permute-start.19 = (bf16[2,128,512]{2,1,0:T(8,128)(2,1)}, bf16[2,128,512]{2,1,0:T(8,128)(2,1)S(1)}, u32[]{:S(2)}, u32[]{:S(2)}) collective-permute-start(bf16[2,128,512]{2,1,0:T(8,128)(2,1)} %get-tuple-element.33), channel_id=1, source_target_pairs={{0,28},{4,0},{8,4},{12,8},{16,12},{20,16},{24,20},{28,24},{1,29},{... | collective-permute-start | bytes 786440 | tf_op jit(solution)/shard_map/ppermute | solution.py:306
  47.0 18.8 %collective-permute-start.18 = (bf16[2,128,512]{2,1,0:T(8,128)(2,1)}, bf16[2,128,512]{2,1,0:T(8,128)(2,1)S(1)}, u32[]{:S(2)}, u32[]{:S(2)}) collective-permute-start(bf16[2,128,512]{2,1,0:T(8,128)(2,1)} %get-tuple-element.31), channel_id=1, source_target_pairs={{0,28},{4,0},{8,4},{12,8},{16,12},{20,16},{24,20},{28,24},{1,29},{... | collective-permute-start | bytes 786440 | tf_op jit(solution)/shard_map/ppermute | solution.py:306
  47.1 18.8 %collective-permute-start.17 = (bf16[2,128,512]{2,1,0:T(8,128)(2,1)}, bf16[2,128,512]{2,1,0:T(8,128)(2,1)S(1)}, u32[]{:S(2)}, u32[]{:S(2)}) collective-permute-start(bf16[2,128,512]{2,1,0:T(8,128)(2,1)} %get-tuple-element.30), channel_id=1, source_target_pairs={{0,4},{4,8},{8,12},{12,16},{16,20},{20,24},{24,28},{28,0},{1,5},{5... | collective-permute-start | bytes 786440 | tf_op jit(solution)/shard_map/ppermute | solution.py:306
  49.0 20.2 %collective-permute-start.16 = (bf16[2,128,512]{2,1,0:T(8,128)(2,1)}, bf16[2,128,512]{2,1,0:T(8,128)(2,1)S(1)}, u32[]{:S(2)}, u32[]{:S(2)}) collective-permute-start(bf16[2,128,512]{2,1,0:T(8,128)(2,1)} %get-tuple-element.29), channel_id=1, source_target_pairs={{0,24},{4,28},{8,0},{12,4},{16,8},{20,12},{24,16},{28,20},{1,25},{... | collective-permute-start | bytes 786440 | tf_op jit(solution)/shard_map/ppermute | solution.py:306
  51.8 45.5 %collective-permute-start.8 = (bf16[32,128,128]{2,1,0:T(8,128)(2,1)}, bf16[32,128,128]{2,1,0:T(8,128)(2,1)}, u32[]{:S(2)}, u32[]{:S(2)}) collective-permute-start(bf16[32,128,128]{2,1,0:T(8,128)(2,1)} %pad_maximum_fusion.refs_0_), channel_id=1, source_target_pairs={{0,192},{1,35},{2,194},{3,33},{32,224},{33,3},{34,226},{35,1},{64,... | collective-permute-start | bytes 3145736 | tf_op jit(solution)/shard_map/ppermute | solution.py:132
  56.0 54.7 %collective-permute-start.10 = (bf16[32,128,128]{2,1,0:T(8,128)(2,1)}, bf16[32,128,128]{2,1,0:T(8,128)(2,1)}, u32[]{:S(2)}, u32[]{:S(2)}) collective-permute-start(bf16[32,128,128]{2,1,0:T(8,128)(2,1)} %pad_maximum_fusion.1.refs_1_), channel_id=1, source_target_pairs={{0,64},{1,33},{2,66},{3,35},{32,96},{33,1},{34,98},{35,3},{64,0},{... | collective-permute-start | bytes 3145736 | tf_op jit(solution)/shard_map/ppermute | solution.py:132
  65.8 18.6 %collective-permute-start.15 = (bf16[2,128,512]{2,1,0:T(8,128)(2,1)S(1)}, bf16[2,128,512]{2,1,0:T(8,128)(2,1)S(1)}, u32[]{:S(2)}, u32[]{:S(2)}) collective-permute-start(bf16[2,128,512]{2,1,0:T(8,128)(2,1)S(1)} %copy-done.6), channel_id=1, source_target_pairs={{0,8},{4,12},{8,16},{12,20},{16,24},{20,28},{24,0},{28,4},{1,9},{5... | collective-permute-start | bytes 786440 | tf_op jit(solution)/shard_map/ppermute | solution.py:306
  65.9 24.7 %collective-permute-start.14 = (bf16[2,128,512]{2,1,0:T(8,128)(2,1)S(1)}, bf16[2,128,512]{2,1,0:T(8,128)(2,1)S(1)}, u32[]{:S(2)}, u32[]{:S(2)}) collective-permute-start(bf16[2,128,512]{2,1,0:T(8,128)(2,1)S(1)} %copy-done.5), channel_id=1, source_target_pairs={{0,12},{4,16},{8,20},{12,24},{16,28},{20,0},{24,4},{28,8},{1,13},{... | collective-permute-start | bytes 786440 | tf_op jit(solution)/shard_map/ppermute | solution.py:306
  69.2 21.3 %collective-permute-start.20 = (bf16[2,128,512]{2,1,0:T(8,128)(2,1)S(1)}, bf16[2,128,512]{2,1,0:T(8,128)(2,1)S(1)}, u32[]{:S(2)}, u32[]{:S(2)}) collective-permute-start(bf16[2,128,512]{2,1,0:T(8,128)(2,1)S(1)} %add_convert_fusion.1), channel_id=1, source_target_pairs={{0,20},{4,24},{8,28},{12,0},{16,4},{20,8},{24,12},{28,16},{1,21},{... | collective-permute-start | bytes 786440 | tf_op jit(solution)/shard_map/ppermute | solution.py:306
  84.4 34.9 %collective-permute-start.6 = (bf16[32,128,128]{2,1,0:T(8,128)(2,1)}, bf16[32,128,128]{2,1,0:T(8,128)(2,1)}, u32[]{:S(2)}, u32[]{:S(2)}) collective-permute-start(bf16[32,128,128]{2,1,0:T(8,128)(2,1)} %pad_maximum_fusion.refs_0_), channel_id=1, source_target_pairs={{0,1},{1,0},{2,3},{3,2},{4,5},{5,4},{6,7},{7,6},{8,9},{9,8},{10,11... | collective-permute-start | bytes 3145736 | tf_op jit(solution)/shard_map/ppermute | solution.py:324
  90.5 28.8 %collective-permute-start.7 = (bf16[32,128,128]{2,1,0:T(8,128)(2,1)}, bf16[32,128,128]{2,1,0:T(8,128)(2,1)}, u32[]{:S(2)}, u32[]{:S(2)}) collective-permute-start(bf16[32,128,128]{2,1,0:T(8,128)(2,1)} %pad_maximum_fusion.1.refs_1_), channel_id=1, source_target_pairs={{0,1},{1,0},{2,3},{3,2},{4,5},{5,4},{6,7},{7,6},{8,9},{9,8},{10,11... | collective-permute-start | bytes 3145736 | tf_op jit(solution)/shard_map/ppermute | solution.py:324
  91.5 15.1 %all-to-all-start.1 = ((bf16[16,16,512]{2,1,0:T(8,128)(2,1)}), bf16[16,16,512]{2,1,0:T(8,128)(2,1)S(1)}, u32[]{:S(2)}, u32[]{:S(2)}) async-start(bf16[16,16,512]{2,1,0:T(8,128)(2,1)} %bitcast.5), calls=%async_computation.1 | async-start | bytes 524288 | tf_op jit(solution)/shard_map/all_to_all | solution.py:332
  97.3 30.0 %collective-permute-start.9 = (bf16[32,128,128]{2,1,0:T(8,128)(2,1)}, bf16[32,128,128]{2,1,0:T(8,128)(2,1)}, u32[]{:S(2)}, u32[]{:S(2)}) collective-permute-start(bf16[32,128,128]{2,1,0:T(8,128)(2,1)} %collective-permute-done.8.refs_0_), channel_id=1, source_target_pairs={{0,1},{1,0},{2,3},{3,2},{4,5},{5,4},{6,7},{7,6},{8,9},{9,8},{10,11... | collective-permute-start | bytes 3145736 | tf_op jit(solution)/shard_map/ppermute | solution.py:325
  107.3 10.0 %all-to-all-start.2 = ((bf16[8,16,512]{2,1,0:T(8,128)(2,1)}), bf16[8,16,512]{2,1,0:T(8,128)(2,1)S(1)}, u32[]{:S(2)}, u32[]{:S(2)}) async-start(bf16[8,16,512]{2,1,0:T(8,128)(2,1)} %broadcast_in_dim.2), calls=%async_computation.2 | async-start | bytes 262144 | tf_op jit(solution)/shard_map/all_to_all | solution.py:335
  110.7 23.3 %collective-permute-start.11 = (bf16[32,128,128]{2,1,0:T(8,128)(2,1)}, bf16[32,128,128]{2,1,0:T(8,128)(2,1)}, u32[]{:S(2)}, u32[]{:S(2)}) collective-permute-start(bf16[32,128,128]{2,1,0:T(8,128)(2,1)} %collective-permute-done.10.refs_0_), channel_id=1, source_target_pairs={{0,1},{1,0},{2,3},{3,2},{4,5},{5,4},{6,7},{7,6},{8,9},{9,8},{10,11... | collective-permute-start | bytes 3145736 | tf_op jit(solution)/shard_map/ppermute | solution.py:325
  (8 other events, 197.8 us)

commit v12 on v9

--- a/solution.py
+++ b/solution.py
@@ -20,11 +20,6 @@
 LEFT = pl.BlockSpec(memory_space=pl.ANY)
 
 
-def two_parts(x):
-    head = x.astype(BF16)
-    return head, (x - head.astype(F32)).astype(BF16)
-
-
 def piece_kernel(at_ref, params_ref, piece_ref):
     width = piece_ref.shape[2]
     block = 2 * at_ref[1] + at_ref[3]
@@ -63,9 +58,7 @@
 
 
 def q_kernel(up_ref, proj_ref, q_ref):
-    head, rest = two_parts(proj_ref[...])
-    q = jnp.dot(up_ref[...], head, preferred_element_type=F32)
-    q += jnp.dot(up_ref[...], rest, preferred_element_type=F32)
+    q = jnp.dot(up_ref[...], proj_ref[...].astype(BF16), preferred_element_type=F32)
     q_ref[...] = q.astype(BF16)
 
 
@@ -308,9 +301,8 @@
         held = [jnp.concatenate(both, axis=0) for both in zip(held, more)]
     far = [exchange(h, g, 3) for g, h in enumerate(held)]
     acc, *sums = near_products(at, tokens, upstream, [*held, *(swap(h) for h in held)])
-    values, token_grads = far_products(
-        at, tokens, upstream, acc, sums, [*far, *(swap(f) for f in far)], inv_width
-    )
+    swapped = [swap(f) for f in far]
+    values, token_grads = far_products(at, tokens, upstream, acc, sums, [*far, *swapped], inv_width)
 
     along = along.astype(BF16)
     plane = lax.all_to_all(along.reshape(n_xh * n_isl, part, proj), PLANE, 0, 0, tiled=True)
@@ -320,9 +312,7 @@
     total = total.reshape(rows, proj)
 
     dims = (((1,), (1,)), ((), ()))
-    head, rest = two_parts(projection)
-    outer = lax.dot_general(total, head, dims, preferred_element_type=F32)
-    outer = outer + lax.dot_general(total, rest, dims, preferred_element_type=F32)
+    outer = lax.dot_general(total, projection.astype(BF16), dims, preferred_element_type=F32)
     outer = outer * (scale_tok / (proj * n_isl))
     new_momentum = 0.9 * momentum + outer
     new_params = params - 0.7 * (outer + 0.9 * new_momentum)

time: 137 us -> 147 us (1.073)
  the two profiles are of different devices: /device:TPU:1 before, /device:TPU:64 now
where the time goes in v12:
time: 147 us; the launch traced here: 146 us
  blocking collectives  43 us (29%)
  waiting for transfers between devices  38.8 us (26%)
  Pallas kernels  28.8 us (20%)
  starting transfers between devices  27.8 us (19%)
  other arithmetic  4.55 us (3%)
  matrix products  1.52 us (1%)
    ppermute x7, waiting for transfers between devices, shift(): return lax.ppermute(x, 'z', [(i, (i + k) % n_z) for i in range(n_z)])  31.4 us
    all_to_all x1, blocking collectives, step(): piece = lax.all_to_all(piece, 'z', 0, 0, tiled=True)  17.1 us
    all_to_all x1, blocking collectives, step(): lax.all_to_all(along.reshape(n_xh * n_isl, part, proj), PLANE, 0, 0, tile...  16.8 us
    ppermute x7, starting transfers between devices, shift(): return lax.ppermute(x, 'z', [(i, (i + k) % n_z) for i in range(n_z)])  14.4 us
    ppermute x8, starting transfers between devices, exchange(): return lax.ppermute(x, ('y', 'xl', 'xh', 'c'), pairs)  12.8 us
    pallas_call x1, Pallas kernels, far_products(): pl.pallas_call(functools.partial(far_kernel, scale=scale), out_shape=(jax...  9.14 us
    all_to_all x1, blocking collectives, step(): total = lax.all_to_all(total, ISLAND, 0, 0, tiled=True)  9.08 us
    pallas_call x1, Pallas kernels, near_products(): pl.pallas_call(near_kernel, out_shape=(jax.ShapeDtypeStruct((t, kv), F32)...  7.92 us
  transfers between devices with their start and end apart: 21, of which 10 were waited for; matrix products, arithmetic and copies ran while one was open for 4% of the time, Pallas kernels for 12%

profile of v12, /device:TPU:64, one launch (start us, length us, event | category | flops | bytes accessed | tf_op | source)
XLA Modules:
  0.0 146.5 jit_solution(4643700169866716201)
XLA Ops:
  1.2 1.8 %make_piece.1.after_ref = bf16[8,128,128]{2,1,0:T(8,128)(2,1)} custom-call(s32[5]{0:T(128)} %stack.23.at_ref, f32[128,1024]{1,0:T(8,128)} %params_ref.1), custom_call_target="tpu_custom_call" | custom-call | tf_op jit(solution)/shard_map/make_piece/pallas_call | solution.py:33
  3.0 17.1 %all_to_all.15 = bf16[8,128,128]{2,1,0:T(8,128)(2,1)S(1)} all-to-all(bf16[8,128,128]{2,1,0:T(8,128)(2,1)} %make_piece.1.after_ref), channel_id=1, replica_groups=mesh['y'=4,'xl'=2,'z'=8,'xh'=2,'c'=2] {'z'}, dimensions={0} | all-to-all | bytes 524288 | tf_op jit(solution)/shard_map/all_to_all | solution.py:278
  20.1 2.8 %collective-permute-start = (bf16[4,128,128]{2,1,0:T(8,128)(2,1)S(1)}, bf16[4,128,128]{2,1,0:T(8,128)(2,1)S(1)}, u32[]{:S(2)}, u32[]{:S(2)}) collective-permute-start(bf16[4,128,128]{2,1,0:T(8,128)(2,1)S(1)} %get-tuple-element.33), channel_id=1, source_target_pairs={{0,34},{1,65},{2,32},{3,67},{32,2},{33,97},{34,0},{35,99},{64,98},... | collective-permute-start | bytes 393224 | tf_op jit(solution)/shard_map/ppermute | solution.py:125
  23.2 3.2 %collective-permute-done = bf16[4,128,128]{2,1,0:T(8,128)(2,1)S(1)} collective-permute-done((bf16[4,128,128]{2,1,0:T(8,128)(2,1)S(1)}, bf16[4,128,128]{2,1,0:T(8,128)(2,1)S(1)}, u32[]{:S(2)}, u32[]{:S(2)}) %collective-permute-start) | collective-permute-done | bytes 131104 | tf_op jit(solution)/shard_map/ppermute | solution.py:125
  28.6 3.1 %collective-permute-start.4 = (bf16[8,128,128]{2,1,0:T(8,128)(2,1)S(1)}, bf16[8,128,128]{2,1,0:T(8,128)(2,1)S(1)}, u32[]{:S(2)}, u32[]{:S(2)}) collective-permute-start(bf16[8,128,128]{2,1,0:T(8,128)(2,1)S(1)} %pad_maximum_fusion.5), channel_id=1, source_target_pairs={{0,192},{1,35},{2,194},{3,33},{32,224},{33,3},{34,226},{35,1},{64,... | collective-permute-start | bytes 786440 | tf_op jit(solution)/shard_map/ppermute | solution.py:125
  31.7 2.8 %pick.1 = bf16[256,2048]{1,0:T(8,128)(2,1)} custom-call(s32[5]{0:T(128)} %stack.23.at_ref, bf16[256,4096]{1,0:T(8,128)(2,1)} %tok_ref.5, bf16[8,128,128]{2,1,0:T(8,128)(2,1)} %make_piece.1.after_ref), custom_call_target="tpu_custom_call" | custom-call | tf_op jit(solution)/shard_map/pick/pallas_call | solution.py:51
  36.4 2.3 %collective-permute-start.5 = (bf16[16,128,128]{2,1,0:T(8,128)(2,1)S(1)}, bf16[16,128,128]{2,1,0:T(8,128)(2,1)S(1)}, u32[]{:S(2)}, u32[]{:S(2)}) collective-permute-start(bf16[16,128,128]{2,1,0:T(8,128)(2,1)S(1)} %pad_maximum_fusion.3), channel_id=1, source_target_pairs={{0,34},{1,65},{2,32},{3,67},{32,2},{33,97},{34,0},{35,99},{64,98},... | collective-permute-start | bytes 1572872 | tf_op jit(solution)/shard_map/ppermute | solution.py:125
  38.7 2.9 %make_q.1.q_ref = bf16[256,512]{1,0:T(8,128)(2,1)} custom-call(bf16[256,1024]{1,0:T(8,128)(2,1)} %up_ref.5, f32[1024,512]{1,0:T(8,128)} %proj_ref.1), custom_call_target="tpu_custom_call" | custom-call | flops 1073741824 | bytes 3145728 | tf_op jit(solution)/shard_map/make_q/pallas_call | solution.py:66
  41.6 2.3 %collective-permute-done.2 = bf16[16,128,128]{2,1,0:T(8,128)(2,1)S(1)} collective-permute-done((bf16[16,128,128]{2,1,0:T(8,128)(2,1)S(1)}, bf16[16,128,128]{2,1,0:T(8,128)(2,1)S(1)}, u32[]{:S(2)}, u32[]{:S(2)}) %collective-permute-start.2) | collective-permute-done | bytes 524320 | tf_op jit(solution)/shard_map/ppermute | solution.py:125
  49.0 4.2 %make_sketch.1 = (bf16[2,128,512]{2,1,0:T(8,128)(2,1)}, bf16[2,128,512]{2,1,0:T(8,128)(2,1)}, bf16[2,128,512]{2,1,0:T(8,128)(2,1)}, bf16[2,128,512]{2,1,0:T(8,12...) custom-call(s32[5]{0:T(128)} %stack.23.at_ref, ...), custom_call_target="tpu_custom_call" | custom-call | flops 4294967296 | bytes 16777216 | tf_op jit(solution)/shard_map/make_sketch/pallas_call | solution.py:97
  53.2 1.7 %collective-permute-start.19 = (bf16[2,128,512]{2,1,0:T(8,128)(2,1)}, bf16[2,128,512]{2,1,0:T(8,128)(2,1)S(1)}, u32[]{:S(2)}, u32[]{:S(2)}) collective-permute-start(bf16[2,128,512]{2,1,0:T(8,128)(2,1)} %get-tuple-element.29), channel_id=1, source_target_pairs={{0,28},{4,0},{8,4},{12,8},{16,12},{20,16},{24,20},{28,24},{1,29},{... | collective-permute-start | bytes 786440 | tf_op jit(solution)/shard_map/ppermute | solution.py:285
  54.9 2.3 %collective-permute-start.18 = (bf16[2,128,512]{2,1,0:T(8,128)(2,1)}, bf16[2,128,512]{2,1,0:T(8,128)(2,1)S(1)}, u32[]{:S(2)}, u32[]{:S(2)}) collective-permute-start(bf16[2,128,512]{2,1,0:T(8,128)(2,1)} %get-tuple-element.27), channel_id=1, source_target_pairs={{0,28},{4,0},{8,4},{12,8},{16,12},{20,16},{24,20},{28,24},{1,29},{... | collective-permute-start | bytes 786440 | tf_op jit(solution)/shard_map/ppermute | solution.py:285
  57.3 5.4 %collective-permute-done.19 = bf16[2,128,512]{2,1,0:T(8,128)(2,1)S(1)} collective-permute-done((bf16[2,128,512]{2,1,0:T(8,128)(2,1)}, bf16[2,128,512]{2,1,0:T(8,128)(2,1)S(1)}, u32[]{:S(2)}, u32[]{:S(2)}) %collective-permute-start.19) | collective-permute-done | bytes 262176 | tf_op jit(solution)/shard_map/ppermute | solution.py:285
  62.7 3.4 %collective-permute-start.16 = (bf16[2,128,512]{2,1,0:T(8,128)(2,1)}, bf16[2,128,512]{2,1,0:T(8,128)(2,1)S(1)}, u32[]{:S(2)}, u32[]{:S(2)}) collective-permute-start(bf16[2,128,512]{2,1,0:T(8,128)(2,1)} %get-tuple-element.25), channel_id=1, source_target_pairs={{0,24},{4,28},{8,0},{12,4},{16,8},{20,12},{24,16},{28,20},{1,25},{... | collective-permute-start | bytes 786440 | tf_op jit(solution)/shard_map/ppermute | solution.py:285
  66.1 4.5 %collective-permute-done.18 = bf16[2,128,512]{2,1,0:T(8,128)(2,1)S(1)} collective-permute-done((bf16[2,128,512]{2,1,0:T(8,128)(2,1)}, bf16[2,128,512]{2,1,0:T(8,128)(2,1)S(1)}, u32[]{:S(2)}, u32[]{:S(2)}) %collective-permute-start.18) | collective-permute-done | bytes 262176 | tf_op jit(solution)/shard_map/ppermute | solution.py:285
  70.6 5.0 %collective-permute-start.15 = (bf16[2,128,512]{2,1,0:T(8,128)(2,1)}, bf16[2,128,512]{2,1,0:T(8,128)(2,1)S(1)}, u32[]{:S(2)}, u32[]{:S(2)}) collective-permute-start(bf16[2,128,512]{2,1,0:T(8,128)(2,1)} %get-tuple-element.24), channel_id=1, source_target_pairs={{0,8},{4,12},{8,16},{12,20},{16,24},{20,28},{24,0},{28,4},{1,9},{5... | collective-permute-start | bytes 786440 | tf_op jit(solution)/shard_map/ppermute | solution.py:285
  76.6 3.2 %collective-permute-done.16 = bf16[2,128,512]{2,1,0:T(8,128)(2,1)S(1)} collective-permute-done((bf16[2,128,512]{2,1,0:T(8,128)(2,1)}, bf16[2,128,512]{2,1,0:T(8,128)(2,1)S(1)}, u32[]{:S(2)}, u32[]{:S(2)}) %collective-permute-start.16) | collective-permute-done | bytes 262176 | tf_op jit(solution)/shard_map/ppermute | solution.py:285
  79.8 1.9 %collective-permute-start.20 = (bf16[2,128,512]{2,1,0:T(8,128)(2,1)S(1)}, bf16[2,128,512]{2,1,0:T(8,128)(2,1)S(1)}, u32[]{:S(2)}, u32[]{:S(2)}) collective-permute-start(bf16[2,128,512]{2,1,0:T(8,128)(2,1)S(1)} %add_convert_fusion.1), channel_id=1, source_target_pairs={{0,20},{4,24},{8,28},{12,0},{16,4},{20,8},{24,12},{28,16},{1,21},{... | collective-permute-start | bytes 786440 | tf_op jit(solution)/shard_map/ppermute | solution.py:285
  81.7 2.6 %collective-permute-done.15 = bf16[2,128,512]{2,1,0:T(8,128)(2,1)S(1)} collective-permute-done((bf16[2,128,512]{2,1,0:T(8,128)(2,1)}, bf16[2,128,512]{2,1,0:T(8,128)(2,1)S(1)}, u32[]{:S(2)}, u32[]{:S(2)}) %collective-permute-start.15) | collective-permute-done | bytes 262176 | tf_op jit(solution)/shard_map/ppermute | solution.py:285
  84.3 15.8 %collective-permute-done.14 = bf16[2,128,512]{2,1,0:T(8,128)(2,1)S(1)} collective-permute-done((bf16[2,128,512]{2,1,0:T(8,128)(2,1)}, bf16[2,128,512]{2,1,0:T(8,128)(2,1)S(1)}, u32[]{:S(2)}, u32[]{:S(2)}) %collective-permute-start.14) | collective-permute-done | bytes 262176 | tf_op jit(solution)/shard_map/ppermute | solution.py:285
  101.9 16.8 %all_to_all.16 = bf16[16,16,512]{2,1,0:T(8,128)(2,1)S(1)} all-to-all(bf16[16,16,512]{2,1,0:T(8,128)(2,1)S(1)} %bitcast.8), channel_id=1, replica_groups=mesh['y'=4,'xl'=2,'z'=8,'xh'=2,'c'=2] {'xh','y','xl'}, dimensions={0} | all-to-all | bytes 524288 | tf_op jit(solution)/shard_map/all_to_all | solution.py:308
  118.8 9.1 %all_to_all.17 = bf16[8,16,512]{2,1,0:T(8,128)(2,1)S(1)} all-to-all(bf16[8,16,512]{2,1,0:T(8,128)(2,1)S(1)} %broadcast_in_dim.2), channel_id=1, replica_groups=mesh['y'=4,'xl'=2,'z'=8,'xh'=2,'c'=2] {'y','xl'}, dimensions={0} | all-to-all | bytes 262144 | tf_op jit(solution)/shard_map/all_to_all | solution.py:311
  129.4 7.9 %near_products.1 = (f32[256,1024]{1,0:T(8,128)}, f32[4,256,512]{2,1,0:T(8,128)}, f32[4,256,512]{2,1,0:T(8,128)}) custom-call(s32[5]{0:T(128)} %stack.23.at_ref, bf16[256,4096]{1,0:T(8,128)(2,1)} %tok_ref.5, bf16[256,1024]{1,0:T(8,128)(2,1)} %up_ref.5, bf16[32,128,128]{2,1,0:T(8,128)(2,1)} %pad_maximum_fusion.refs_0_, ...), custom_call_target="tpu_custom_call" | custom-call | flops 2147483648 | bytes 4194304 | tf_op jit(solution)/shard_map/near_products/pallas_call | solution.py:234
  137.3 9.1 %far_products.1 = (bf16[256,1024]{1,0:T(8,128)(2,1)}, bf16[256,4096]{1,0:T(8,128)(2,1)}) custom-call(s32[5]{0:T(128)} %stack.23.at_ref, bf16[256,4096]{1,0:T(8,128)(2,1)} %tok_ref.5, bf16[256,1024]{1,0:T(8,128)(2,1)} %up_ref.5, f32[256,1024]{1,0:T(8,128)} %get-tuple-element.17.before_ref, f32[4,256,512]{2,1,0:T(8,128)} %get-tuple-element.18.refs_0_, ...), custom_call_target="tpu_custom_call" | custom-call | flops 2147483648 | bytes 4194304 | tf_op jit(solution)/shard_map/far_products/pallas_call | solution.py:251
  (48 shorter events, 14.4 us)
Async XLA Ops:
  20.1 6.3 %collective-permute-start = (bf16[4,128,128]{2,1,0:T(8,128)(2,1)S(1)}, bf16[4,128,128]{2,1,0:T(8,128)(2,1)S(1)}, u32[]{:S(2)}, u32[]{:S(2)}) collective-permute-start(bf16[4,128,128]{2,1,0:T(8,128)(2,1)S(1)} %get-tuple-element.33), channel_id=1, source_target_pairs={{0,34},{1,65},{2,32},{3,67},{32,2},{33,97},{34,0},{35,99},{64,98},... | collective-permute-start | bytes 393224 | tf_op jit(solution)/shard_map/ppermute | solution.py:125
  23.0 5.7 %collective-permute-start.3 = (bf16[4,128,128]{2,1,0:T(8,128)(2,1)S(1)}, bf16[4,128,128]{2,1,0:T(8,128)(2,1)S(1)}, u32[]{:S(2)}, u32[]{:S(2)}) collective-permute-start(bf16[4,128,128]{2,1,0:T(8,128)(2,1)S(1)} %get-tuple-element.32), channel_id=1, source_target_pairs={{0,32},{1,193},{2,34},{3,195},{32,0},{33,225},{34,2},{35,227},{64,... | collective-permute-start | bytes 393224 | tf_op jit(solution)/shard_map/ppermute | solution.py:125
  26.4 8.2 %collective-permute-start.1 = (bf16[8,128,128]{2,1,0:T(8,128)(2,1)S(1)}, bf16[8,128,128]{2,1,0:T(8,128)(2,1)S(1)}, u32[]{:S(2)}, u32[]{:S(2)}) collective-permute-start(bf16[8,128,128]{2,1,0:T(8,128)(2,1)S(1)} %pad_maximum_fusion.4), channel_id=1, source_target_pairs={{0,64},{1,33},{2,66},{3,35},{32,96},{33,1},{34,98},{35,3},{64,0},{... | collective-permute-start | bytes 786440 | tf_op jit(solution)/shard_map/ppermute | solution.py:125
  28.6 7.7 %collective-permute-start.4 = (bf16[8,128,128]{2,1,0:T(8,128)(2,1)S(1)}, bf16[8,128,128]{2,1,0:T(8,128)(2,1)S(1)}, u32[]{:S(2)}, u32[]{:S(2)}) collective-permute-start(bf16[8,128,128]{2,1,0:T(8,128)(2,1)S(1)} %pad_maximum_fusion.5), channel_id=1, source_target_pairs={{0,192},{1,35},{2,194},{3,33},{32,224},{33,3},{34,226},{35,1},{64,... | collective-permute-start | bytes 786440 | tf_op jit(solution)/shard_map/ppermute | solution.py:125
  34.6 13.7 %collective-permute-start.12 = (bf16[256,2048]{1,0:T(8,128)(2,1)}, bf16[256,2048]{1,0:T(8,128)(2,1)}, u32[]{:S(2)}, u32[]{:S(2)}) collective-permute-start(bf16[256,2048]{1,0:T(8,128)(2,1)} %pick.1), channel_id=1, source_target_pairs={{0,1},{1,0},{2,3},{3,2},{4,5},{5,4},{6,7},{7,6},{8,9},{9,8},{10,11... | collective-permute-start | bytes 3145736 | tf_op jit(solution)/shard_map/ppermute | solution.py:277
  34.6 9.3 %collective-permute-start.2 = (bf16[16,128,128]{2,1,0:T(8,128)(2,1)S(1)}, bf16[16,128,128]{2,1,0:T(8,128)(2,1)S(1)}, u32[]{:S(2)}, u32[]{:S(2)}) collective-permute-start(bf16[16,128,128]{2,1,0:T(8,128)(2,1)S(1)} %pad_maximum_fusion.2), channel_id=1, source_target_pairs={{0,32},{1,193},{2,34},{3,195},{32,0},{33,225},{34,2},{35,227},{64,... | collective-permute-start | bytes 1572872 | tf_op jit(solution)/shard_map/ppermute | solution.py:125
  36.4 10.5 %collective-permute-start.5 = (bf16[16,128,128]{2,1,0:T(8,128)(2,1)S(1)}, bf16[16,128,128]{2,1,0:T(8,128)(2,1)S(1)}, u32[]{:S(2)}, u32[]{:S(2)}) collective-permute-start(bf16[16,128,128]{2,1,0:T(8,128)(2,1)S(1)} %pad_maximum_fusion.3), channel_id=1, source_target_pairs={{0,34},{1,65},{2,32},{3,67},{32,2},{33,97},{34,0},{35,99},{64,98},... | collective-permute-start | bytes 1572872 | tf_op jit(solution)/shard_map/ppermute | solution.py:125
  41.6 6.7 %collective-permute-start.13 = (bf16[256,512]{1,0:T(8,128)(2,1)}, bf16[256,512]{1,0:T(8,128)(2,1)S(1)}, u32[]{:S(2)}, u32[]{:S(2)}) collective-permute-start(bf16[256,512]{1,0:T(8,128)(2,1)} %make_q.1.q_ref), channel_id=1, source_target_pairs={{0,1},{1,0},{2,3},{3,2},{4,5},{5,4},{6,7},{7,6},{8,9},{9,8},{10,11... | collective-permute-start | bytes 786440 | tf_op jit(solution)/shard_map/ppermute | solution.py:281
  45.0 55.1 %collective-permute-start.8 = (bf16[32,128,128]{2,1,0:T(8,128)(2,1)}, bf16[32,128,128]{2,1,0:T(8,128)(2,1)}, u32[]{:S(2)}, u32[]{:S(2)}) collective-permute-start(bf16[32,128,128]{2,1,0:T(8,128)(2,1)} %pad_maximum_fusion.refs_0_), channel_id=1, source_target_pairs={{0,192},{1,35},{2,194},{3,33},{32,224},{33,3},{34,226},{35,1},{64,... | collective-permute-start | bytes 3145736 | tf_op jit(solution)/shard_map/ppermute | solution.py:125
  47.9 52.7 %collective-permute-start.9 = (bf16[32,128,128]{2,1,0:T(8,128)(2,1)}, bf16[32,128,128]{2,1,0:T(8,128)(2,1)}, u32[]{:S(2)}, u32[]{:S(2)}) collective-permute-start(bf16[32,128,128]{2,1,0:T(8,128)(2,1)} %pad_maximum_fusion.1.refs_1_), channel_id=1, source_target_pairs={{0,64},{1,33},{2,66},{3,35},{32,96},{33,1},{34,98},{35,3},{64,0},{... | collective-permute-start | bytes 3145736 | tf_op jit(solution)/shard_map/ppermute | solution.py:125
  53.2 74.7 %copy-start = (f32[128,1024]{1,0:T(8,128)S(1)}, f32[128,1024]{1,0:T(8,128)}, u32[]{:S(2)}) copy-start(f32[128,1024]{1,0:T(8,128)} %params_ref.1) | copy-start | bytes 1572868
  53.2 74.7 %copy-start.1 = (f32[1024,512]{1,0:T(8,128)S(1)}, f32[1024,512]{1,0:T(8,128)}, u32[]{:S(2)}) copy-start(f32[1024,512]{1,0:T(8,128)} %proj_ref.1) | copy-start | bytes 6291460
  53.2 74.7 %copy-start.2 = (f32[128,1024]{1,0:T(8,128)S(1)}, f32[128,1024]{1,0:T(8,128)}, u32[]{:S(2)}) copy-start(f32[128,1024]{1,0:T(8,128)} %param.8) | copy-start | bytes 1572868
  53.2 9.5 %collective-permute-start.19 = (bf16[2,128,512]{2,1,0:T(8,128)(2,1)}, bf16[2,128,512]{2,1,0:T(8,128)(2,1)S(1)}, u32[]{:S(2)}, u32[]{:S(2)}) collective-permute-start(bf16[2,128,512]{2,1,0:T(8,128)(2,1)} %get-tuple-element.29), channel_id=1, source_target_pairs={{0,28},{4,0},{8,4},{12,8},{16,12},{20,16},{24,20},{28,24},{1,29},{... | collective-permute-start | bytes 786440 | tf_op jit(solution)/shard_map/ppermute | solution.py:285
  54.9 15.7 %collective-permute-start.18 = (bf16[2,128,512]{2,1,0:T(8,128)(2,1)}, bf16[2,128,512]{2,1,0:T(8,128)(2,1)S(1)}, u32[]{:S(2)}, u32[]{:S(2)}) collective-permute-start(bf16[2,128,512]{2,1,0:T(8,128)(2,1)} %get-tuple-element.27), channel_id=1, source_target_pairs={{0,28},{4,0},{8,4},{12,8},{16,12},{20,16},{24,20},{28,24},{1,29},{... | collective-permute-start | bytes 786440 | tf_op jit(solution)/shard_map/ppermute | solution.py:285
  57.3 18.3 %collective-permute-start.17 = (bf16[2,128,512]{2,1,0:T(8,128)(2,1)}, bf16[2,128,512]{2,1,0:T(8,128)(2,1)S(1)}, u32[]{:S(2)}, u32[]{:S(2)}) collective-permute-start(bf16[2,128,512]{2,1,0:T(8,128)(2,1)} %get-tuple-element.26), channel_id=1, source_target_pairs={{0,4},{4,8},{8,12},{12,16},{16,20},{20,24},{24,28},{28,0},{1,5},{5... | collective-permute-start | bytes 786440 | tf_op jit(solution)/shard_map/ppermute | solution.py:285
  62.7 17.1 %collective-permute-start.16 = (bf16[2,128,512]{2,1,0:T(8,128)(2,1)}, bf16[2,128,512]{2,1,0:T(8,128)(2,1)S(1)}, u32[]{:S(2)}, u32[]{:S(2)}) collective-permute-start(bf16[2,128,512]{2,1,0:T(8,128)(2,1)} %get-tuple-element.25), channel_id=1, source_target_pairs={{0,24},{4,28},{8,0},{12,4},{16,8},{20,12},{24,16},{28,20},{1,25},{... | collective-permute-start | bytes 786440 | tf_op jit(solution)/shard_map/ppermute | solution.py:285
  70.6 13.7 %collective-permute-start.15 = (bf16[2,128,512]{2,1,0:T(8,128)(2,1)}, bf16[2,128,512]{2,1,0:T(8,128)(2,1)S(1)}, u32[]{:S(2)}, u32[]{:S(2)}) collective-permute-start(bf16[2,128,512]{2,1,0:T(8,128)(2,1)} %get-tuple-element.24), channel_id=1, source_target_pairs={{0,8},{4,12},{8,16},{12,20},{16,24},{20,28},{24,0},{28,4},{1,9},{5... | collective-permute-start | bytes 786440 | tf_op jit(solution)/shard_map/ppermute | solution.py:285
  75.6 24.5 %collective-permute-start.14 = (bf16[2,128,512]{2,1,0:T(8,128)(2,1)}, bf16[2,128,512]{2,1,0:T(8,128)(2,1)S(1)}, u32[]{:S(2)}, u32[]{:S(2)}) collective-permute-start(bf16[2,128,512]{2,1,0:T(8,128)(2,1)} %get-tuple-element.23), channel_id=1, source_target_pairs={{0,12},{4,16},{8,20},{12,24},{16,28},{20,0},{24,4},{28,8},{1,13},{... | collective-permute-start | bytes 786440 | tf_op jit(solution)/shard_map/ppermute | solution.py:285
  79.8 20.9 %collective-permute-start.20 = (bf16[2,128,512]{2,1,0:T(8,128)(2,1)S(1)}, bf16[2,128,512]{2,1,0:T(8,128)(2,1)S(1)}, u32[]{:S(2)}, u32[]{:S(2)}) collective-permute-start(bf16[2,128,512]{2,1,0:T(8,128)(2,1)S(1)} %add_convert_fusion.1), channel_id=1, source_target_pairs={{0,20},{4,24},{8,28},{12,0},{16,4},{20,8},{24,12},{28,16},{1,21},{... | collective-permute-start | bytes 786440 | tf_op jit(solution)/shard_map/ppermute | solution.py:285
  84.3 45.1 %collective-permute-start.6 = (bf16[32,128,128]{2,1,0:T(8,128)(2,1)}, bf16[32,128,128]{2,1,0:T(8,128)(2,1)}, u32[]{:S(2)}, u32[]{:S(2)}) collective-permute-start(bf16[32,128,128]{2,1,0:T(8,128)(2,1)} %pad_maximum_fusion.refs_0_), channel_id=1, source_target_pairs={{0,1},{1,0},{2,3},{3,2},{4,5},{5,4},{6,7},{7,6},{8,9},{9,8},{10,11... | collective-permute-start | bytes 3145736 | tf_op jit(solution)/shard_map/ppermute | solution.py:303
  100.1 29.3 %collective-permute-start.7 = (bf16[32,128,128]{2,1,0:T(8,128)(2,1)}, bf16[32,128,128]{2,1,0:T(8,128)(2,1)}, u32[]{:S(2)}, u32[]{:S(2)}) collective-permute-start(bf16[32,128,128]{2,1,0:T(8,128)(2,1)} %pad_maximum_fusion.1.refs_1_), channel_id=1, source_target_pairs={{0,1},{1,0},{2,3},{3,2},{4,5},{5,4},{6,7},{7,6},{8,9},{9,8},{10,11... | collective-permute-start | bytes 3145736 | tf_op jit(solution)/shard_map/ppermute | solution.py:303
  100.1 37.2 %collective-permute-start.10 = (bf16[32,128,128]{2,1,0:T(8,128)(2,1)}, bf16[32,128,128]{2,1,0:T(8,128)(2,1)}, u32[]{:S(2)}, u32[]{:S(2)}) collective-permute-start(bf16[32,128,128]{2,1,0:T(8,128)(2,1)} %collective-permute-done.8.refs_2_), channel_id=1, source_target_pairs={{0,1},{1,0},{2,3},{3,2},{4,5},{5,4},{6,7},{7,6},{8,9},{9,8},{10,11... | collective-permute-start | bytes 3145736 | tf_op jit(solution)/shard_map/ppermute | solution.py:304
  100.6 36.7 %collective-permute-start.11 = (bf16[32,128,128]{2,1,0:T(8,128)(2,1)}, bf16[32,128,128]{2,1,0:T(8,128)(2,1)}, u32[]{:S(2)}, u32[]{:S(2)}) collective-permute-start(bf16[32,128,128]{2,1,0:T(8,128)(2,1)} %collective-permute-done.9.refs_3_), channel_id=1, source_target_pairs={{0,1},{1,0},{2,3},{3,2},{4,5},{5,4},{6,7},{7,6},{8,9},{9,8},{10,11... | collective-permute-start | bytes 3145736 | tf_op jit(solution)/shard_map/ppermute | solution.py:304
  (1 other events, 0.7 us)
